TPU v7x, 256 devices: a whole 4x4x8 slice. The times are simulated.
256 devices in a mesh: tiles: 64 (over z, y, core), chan: 4 (over x).
Axes of the slice: x: 4, y: 4, z: 8, core: 2. Of those that a mesh axis runs over, the one named last changes fastest.
Arguments:
- x_scan: bfloat16 [1024, 192, 256], P('tiles', 'chan'), may hold values from -40 to 40
- slot_owner: int32 [1024], P('tiles'), may hold values from 0 to 512, as said below
- adjacency: int32 [512, 8], P('tiles'), may hold values from 0 to 512, as said below
- cotangent: bfloat16 [512, 192, 256], P('tiles', 'chan'), may hold values from -6 to 6
- dw_weight: float32 [192, 49], P('chan'), may hold values from -0.875 to 0.875
- ln_gain: bfloat16 [192], P('chan'), may hold values from 0.25 to 1.75
- w_in: bfloat16 [192, 768], P(None, 'chan'), may hold values from -0.4375 to 0.4375
- b_in: bfloat16 [768], P('chan'), may hold values from -3 to 3
- w_out: bfloat16 [768, 192], P('chan'), may hold values from -0.21875 to 0.21875
- layer_scale: float32 [192], P('chan'), may hold values from 0.3 to 1.5
Outputs:
- output: bfloat16 [512, 192, 256], P('tiles', 'chan')
- grad_in: bfloat16 [512, 192, 256], P('tiles', 'chan')
- grad_dw: float32 [192, 49], P('chan')
- grad_w1: float32 [192, 768], P(None, 'chan')
- grad_w2: float32 [768, 192], P('chan')
Inputs may be any that keep to these rules, and one draw needn't show every extreme that they name: `slot_owner`: slots run in scan order over a grid of tiles with 16 columns, one grid row for each device along tiles. A tissue slot holds its tile's owner-order index, a background slot holds 512. Tissue tiles are numbered in scan order, and owner-order index q belongs to device q // 8. Grid rows 2k and 2k + 1 hold 4 to 12 tissue tiles each and 16 together, so a device's tissue tiles belong to it or to the device whose index differs in the lowest bit, and at most 4 of them, a number reached in every draw, to the latter. `adjacency`: entry k of a tissue tile is the owner-order index of the grid cell at row and column offsets (-1,-1), (-1,0), (-1,1), (0,-1), (0,1), (1,-1), (1,0), (1,1) from it, 512 where that cell is background or off the grid. Every neighbour of a tile owned by device o is owned by one of the devices o - 3 to o + 3, a distance reached in every draw.
All inputs are finite; a program needn't handle non-finite values.
Results may differ from a plain program's by a relative error of at most 0.015.
Values may be sent and summed in bfloat16 or wider, within the bound.
No kernel may reach another device: no remote copies, remote signals or barrier semaphores. Data moves between devices by JAX's collectives and lax.ppermute only.
A program may use at most 128 MiB of HBM per device.

v0:
```python
import math

import jax
import jax.numpy as jnp
from jax import lax
from jax.sharding import PartitionSpec as P

CHANNEL_COUNT = 192
P_SIZE = 16
REACH = 3
PIX = 256


EPSILON = 1e-06
GELU_SCALE = 0.7978845608
GELU_CUBIC = 0.044715


def from_partner(value, axis, distance):
    return lax.ppermute(value, axis, [(i, i ^ 1 << distance) for i in range(lax.axis_size(axis))])


def passed_along(value, axis, by):
    length = lax.axis_size(axis)
    pairs = [(i, i + by) for i in range(length) if 0 <= i + by < length]
    return lax.ppermute(value, axis, pairs)


def strips(tile_field):
    side_len = tile_field.shape[-1]
    top_rows = tile_field[:, :, :3, :]
    bottom_rows = tile_field[:, :, side_len - 3 :, :]
    left_cols = jnp.swapaxes(tile_field[:, :, :, :3], 2, 3)
    right_cols = jnp.swapaxes(tile_field[:, :, :, side_len - 3 :], 2, 3)
    return jnp.stack([top_rows, bottom_rows, left_cols, right_cols], axis=2)


def assemble(tile_field, around):
    side_len = tile_field.shape[-1]
    upper_band = jnp.concatenate(
        [around[:, 0, :, 1, :, side_len - 3 :], around[:, 1, :, 1], around[:, 2, :, 1, :, :3]],
        axis=3,
    )
    middle = jnp.concatenate(
        [
            jnp.swapaxes(around[:, 3, :, 3], 2, 3),
            tile_field,
            jnp.swapaxes(around[:, 4, :, 2], 2, 3),
        ],
        axis=3,
    )
    lower_band = jnp.concatenate(
        [around[:, 5, :, 0, :, side_len - 3 :], around[:, 6, :, 0], around[:, 7, :, 0, :, :3]],
        axis=3,
    )
    return jnp.concatenate([upper_band, middle, lower_band], axis=2)


def depthwise(padded, kernel):
    tile_count = padded.shape[0]
    channels = padded.shape[1]
    wide_len = padded.shape[3]
    side_len = wide_len - 6
    span_len = side_len * wide_len
    flat_pad = jnp.pad(
        padded.astype(jnp.float32).reshape(tile_count, channels, wide_len * wide_len),
        ((0, 0), (0, 0), (0, 8)),
    )
    result = jnp.zeros((tile_count, channels, span_len), jnp.float32)
    for row_tap in range(7):
        for col_tap in range(7):
            offset = row_tap * wide_len + col_tap
            result = (
                result
                + kernel[:, row_tap * 7 + col_tap][None, :, None]
                * flat_pad[:, :, offset : offset + span_len]
            )
    return result.reshape(tile_count, channels, side_len, wide_len)[:, :, :, :side_len]


def kernel_grad(grad_tiles, padded):
    tile_count = grad_tiles.shape[0]
    channels = grad_tiles.shape[1]
    side_len = grad_tiles.shape[3]
    wide_len = side_len + 6
    span_len = side_len * wide_len
    flat_pad = jnp.pad(
        padded.astype(jnp.float32).reshape(tile_count, channels, wide_len * wide_len),
        ((0, 0), (0, 0), (0, 8)),
    )
    spread = jnp.pad(grad_tiles.astype(jnp.float32), ((0, 0), (0, 0), (0, 0), (0, 6))).reshape(
        tile_count, channels, span_len
    )
    columns = []
    for row_tap in range(7):
        for col_tap in range(7):
            offset = row_tap * wide_len + col_tap
            columns.append(
                jnp.sum(spread * flat_pad[:, :, offset : offset + span_len], axis=(0, 2))
            )
    return jnp.stack(columns, axis=1)


def gelu_parts(preact):
    tanh_arg = GELU_SCALE * (preact + GELU_CUBIC * preact * preact * preact)
    tangent = jnp.tanh(tanh_arg)
    values = 0.5 * preact * (1.0 + tangent)
    slopes = 0.5 * (1.0 + tangent) + 0.5 * preact * (1.0 - tangent * tangent) * GELU_SCALE * (
        1.0 + 3.0 * GELU_CUBIC * preact * preact
    )
    return (values, slopes)


def relay_tiles(x_scan, slot_owner, tile_count):
    my_index = lax.axis_index("tiles")
    partner = jnp.bitwise_xor(my_index, 1)
    owner_dev = slot_owner // tile_count
    position = slot_owner % tile_count
    slot_rows = x_scan.reshape(x_scan.shape[0], x_scan.shape[1] * x_scan.shape[2])
    targets = jnp.arange(tile_count, dtype=jnp.int32)
    staying = owner_dev == my_index
    keep_map = ((position[None, :] == targets[:, None]) & staying[None, :]).astype(jnp.bfloat16)
    kept_rows = jnp.dot(keep_map, slot_rows, preferred_element_type=jnp.float32)
    leaving = owner_dev == partner
    leave_rank = jnp.cumsum(leaving.astype(jnp.int32)) - 1
    outgoing = (
        leave_rank[None, :] == jnp.arange(tile_count // 2, dtype=jnp.int32)[:, None]
    ) & leaving[None, :]
    sent_rows = jnp.dot(
        outgoing.astype(jnp.bfloat16), slot_rows, preferred_element_type=jnp.float32
    ).astype(jnp.bfloat16)
    filled = jnp.any(outgoing, axis=1)
    sent_place = jnp.where(
        filled, jnp.sum(jnp.where(outgoing, position[None, :], 0), axis=1), tile_count
    )
    arrived_rows, arrived_place = from_partner((sent_rows, sent_place), "tiles", 0)
    settle_map = (arrived_place[None, :] == targets[:, None]).astype(jnp.bfloat16)
    merged = kept_rows + jnp.dot(settle_map, arrived_rows, preferred_element_type=jnp.float32)
    return merged.astype(jnp.bfloat16).reshape(tile_count, x_scan.shape[1], x_scan.shape[2])


def neighbour_rims(tile_field, adjacency, tile_count):
    rims = strips(tile_field)
    rim_shape = rims.shape
    rim_rows = rims.reshape(rim_shape[0], rim_shape[1] * rim_shape[2] * rim_shape[3] * rim_shape[4])
    pieces = []
    for offset in range(-REACH, REACH + 1):
        if offset == 0:
            pieces.append(rim_rows)
        else:
            pieces.append(passed_along(rim_rows, "tiles", -offset))
    rim_table = jnp.concatenate(pieces, axis=0)
    my_index = lax.axis_index("tiles")
    local_ids = adjacency - (my_index - REACH) * tile_count
    valid = (
        (adjacency < tile_count * lax.axis_size("tiles"))
        & (local_ids >= 0)
        & (local_ids < rim_table.shape[0])
    )
    found = jnp.take(rim_table, jnp.clip(local_ids, 0, rim_table.shape[0] - 1), axis=0)
    found = jnp.where(valid[:, :, None], found, jnp.zeros((), found.dtype))
    return found.reshape(rim_shape[0], 8, rim_shape[1], rim_shape[2], rim_shape[3], rim_shape[4])


def body(
    x_scan, slot_owner, adjacency, cotangent, dw_weight, ln_gain, w_in, b_in, w_out, layer_scale
):
    tile_count = adjacency.shape[0]
    channels = x_scan.shape[1]
    owned_tiles = relay_tiles(x_scan, slot_owner, tile_count)
    tile_field = owned_tiles.reshape(tile_count, channels, P_SIZE, P_SIZE)
    padded = assemble(tile_field, neighbour_rims(tile_field, adjacency, tile_count))
    mixed_tiles = (
        depthwise(padded, dw_weight).astype(jnp.bfloat16).reshape(tile_count, channels, PIX)
    )
    scale_col = layer_scale[None, :, None]
    mixed_f = mixed_tiles.astype(jnp.float32)
    moments = lax.psum((jnp.sum(mixed_f, axis=1), jnp.sum(mixed_f * mixed_f, axis=1)), "chan")
    row_mean = moments[0] / CHANNEL_COUNT
    inverse_deviation = lax.rsqrt(moments[1] / CHANNEL_COUNT - row_mean * row_mean + EPSILON)
    centered_input = (mixed_f - row_mean[:, None, :]) * inverse_deviation[:, None, :]
    gain_float = ln_gain.astype(jnp.float32)
    normed = (centered_input * gain_float[None, :, None]).astype(jnp.bfloat16)
    all_normed = lax.all_gather(normed, "chan", axis=1, tiled=True)
    preact = (
        jnp.einsum("tcp,ch->thp", all_normed, w_in, preferred_element_type=jnp.float32)
        + b_in.astype(jnp.float32)[None, :, None]
    )
    values, slopes = gelu_parts(preact)
    activated = values.astype(jnp.bfloat16)
    partial_out = jnp.einsum("thp,hc->tcp", activated, w_out, preferred_element_type=jnp.float32)
    branch = lax.psum_scatter(
        partial_out.astype(jnp.bfloat16), "chan", scatter_dimension=1, tiled=True
    )
    output = (owned_tiles.astype(jnp.float32) + scale_col * branch.astype(jnp.float32)).astype(
        jnp.bfloat16
    )
    dbranch = (cotangent.astype(jnp.float32) * scale_col).astype(jnp.bfloat16)
    all_dbranch = lax.all_gather(dbranch, "chan", axis=1, tiled=True)
    act_grad = jnp.einsum("tcp,hc->thp", all_dbranch, w_out, preferred_element_type=jnp.float32)
    pre_grad = (act_grad * slopes).astype(jnp.bfloat16)
    raw_w2 = jnp.einsum("thp,tcp->hc", activated, all_dbranch, preferred_element_type=jnp.float32)
    raw_w1 = jnp.einsum("tcp,thp->ch", all_normed, pre_grad, preferred_element_type=jnp.float32)
    partial_in = jnp.einsum("thp,ch->tcp", pre_grad, w_in, preferred_element_type=jnp.float32)
    normed_gradient = lax.psum_scatter(
        partial_in.astype(jnp.bfloat16), "chan", scatter_dimension=1, tiled=True
    ).astype(jnp.float32)
    centered_input_gradient = normed_gradient * gain_float[None, :, None]
    gradient_moments = lax.psum(
        (
            jnp.sum(centered_input_gradient, axis=1),
            jnp.sum(centered_input_gradient * centered_input, axis=1),
        ),
        "chan",
    )
    mixed_gradient = (
        inverse_deviation[:, None, :]
        * (
            centered_input_gradient
            - gradient_moments[0][:, None, :] / CHANNEL_COUNT
            - centered_input * gradient_moments[1][:, None, :] / CHANNEL_COUNT
        )
    ).astype(jnp.bfloat16)
    grad_field = mixed_gradient.reshape(tile_count, channels, P_SIZE, P_SIZE)
    dpadded = assemble(grad_field, neighbour_rims(grad_field, adjacency, tile_count))
    backflow = depthwise(dpadded, dw_weight[:, ::-1]).reshape(tile_count, channels, PIX)
    grad_in = (cotangent.astype(jnp.float32) + backflow).astype(jnp.bfloat16)
    local_dw = kernel_grad(grad_field, padded)
    totals = lax.psum((local_dw, raw_w1, raw_w2), "tiles")
    factor = 1.0 / math.sqrt(tile_count * lax.axis_size("tiles") * PIX)
    return (output, grad_in, totals[0] * factor, totals[1] * factor, totals[2] * factor)


def solution(mesh):
    in_specs = (
        P("tiles", "chan", None),
        P("tiles"),
        P("tiles", None),
        P("tiles", "chan", None),
        P("chan", None),
        P("chan"),
        P(None, "chan"),
        P("chan"),
        P("chan", None),
        P("chan"),
    )
    out_specs = (
        P("tiles", "chan", None),
        P("tiles", "chan", None),
        P("chan", None),
        P(None, "chan"),
        P("chan", None),
    )
    return jax.shard_map(body, mesh=mesh, in_specs=in_specs, out_specs=out_specs, check_vma=False)
```

profile of v0, /device:TPU:128, one launch (start us, length us, event | category | flops | bytes accessed | tf_op | source)
XLA Modules:
  0.0 768.5 jit_solution(2011883109561665990)
XLA Ops:
  16.9 1.9 slice_bitcast_fusion.1
  18.8 4.3 copy.189
  23.1 4.2 copy.190
  27.3 6.4 pad_maximum_fusion
  33.7 10.7 %copy.145 = bf16[8,48,4,3,16]{4,3,2,1,0:T(4,128)(2,1)S(1)} copy(bf16[8,48,4,3,16]{3,4,1,0,2:T(8,128)(2,1)} %pad_maximum_fusion) | data formatting | bytes 294912 | tf_op jit(solution)/shard_map/stack | solution.py:35
  44.4 2.0 reshape.207
  46.4 3.2 collective-permute-start.2
  52.0 6.0 collective-permute-start.7
  58.0 2.4 collective-permute-start.6
  60.4 2.2 collective-permute-start.5
  62.6 2.1 collective-permute-start.4
  64.7 3.7 collective-permute-start.3
  68.4 7.8 %collective-permute-done.3 = bf16[8,9216]{1,0:T(8,128)(2,1)S(1)} collective-permute-done((bf16[8,9216]{1,0:T(8,128)(2,1)}, bf16[8,9216]{1,0:T(8,128)(2,1)S(1)}, u32[]{:S(2)}, u32[]{:S(2)}) %collective-permute-start.3) | collective-permute-done | bytes 147488 | tf_op jit(solution)/shard_map/ppermute | solution.py:26
  76.4 2.3 gather_fusion
  80.2 13.5 %reshape.208 = bf16[8,8,48,4,3,16]{5,4,3,2,1,0:T(4,128)(2,1)} reshape(bf16[8,8,9216]{2,1,0:T(8,128)(2,1)S(1)} %fusion.114) | data formatting | bytes 2359296 | tf_op jit(solution)/shard_map/reshape | solution.py:162
  93.7 3.0 slice_bitcast_fusion.6
  96.8 2.9 slice_bitcast_fusion.7
  104.6 4.2 copy.191
  108.8 3.3 copy.192
  112.1 3.3 pad_maximum_fusion.1
  118.4 11.1 %add_convert_fusion = bf16[8,48,352]{1,0,2:T(8,128)(2,1)S(1)} fusion(f32[8,48,484]{1,0,2:T(8,128)S(1)} %bitcast_convert_fusion.1, f32[48]{0:T(128)S(1)} %copy-done.56, f32[48]{0:T(128)S(1)} %copy-done.58, f32[48]{0:T(128)S(1)} %get-tuple-element.85, f32[48]{0:T(128)S(1)} %get-tuple-element.86, f32[48]{0:T(128)S(1)} %get-tuple-element.87, ...), kind=kLoop, calls=%fused_computation.228 | loop fusion | flops 13246464 | bytes 64272704 | tf_op jit(solution)/shard_map/convert.9
  133.0 17.2 %all-reduce.5 = (f32[8,256]{1,0:T(8,128)S(1)}, f32[8,256]{1,0:T(8,128)S(1)}) all-reduce(f32[8,256]{1,0:T(8,128)S(1)} %copy.158, f32[8,256]{1,0:T(8,128)S(1)} %copy.156), channel_id=1, replica_groups=mesh['tiles'=64,'chan'=4] {'chan'}, use_global_device_ids=true, to_apply=%region_6.8 | all-reduce | flops 4096 | bytes 32768 | tf_op jit(solution)/shard_map/psum | solution.py:178
  150.3 13.3 %all_gather.6 = bf16[8,192,256]{2,1,0:T(8,128)(2,1)S(1)} all-gather(bf16[8,48,256]{2,1,0:T(8,128)(2,1)S(1)} %multiply_convert_fusion.2), channel_id=1, replica_groups=mesh['tiles'=64,'chan'=4] {'chan'}, dimensions={1}, use_global_device_ids=true | all-gather | bytes 983040 | tf_op jit(solution)/shard_map/all_gather | solution.py:184
  166.1 1.6 fusion.111
  168.6 21.6 %reduce-scatter.3.cloned.1.call-done = bf16[8,48,256]{2,1,0:T(8,128)(2,1)} async-done(((bf16[8,192,256]{2,1,0:T(8,128)(2,1)}), bf16[8,48,256]{2,1,0:T(8,128)(2,1)}) %reduce-scatter.3.cloned.1.call-update) | async-done | bytes 196624 | tf_op jit(solution)/shard_map/reduce_scatter | solution.py:192
  190.2 2.2 fusion.116
  192.4 14.0 %all_gather.7 = bf16[8,192,256]{2,1,0:T(8,128)(2,1)S(1)} all-gather(bf16[8,48,256]{2,1,0:T(8,128)(2,1)S(1)} %get-tuple-element.171), channel_id=1, replica_groups=mesh['tiles'=64,'chan'=4] {'chan'}, dimensions={1}, use_global_device_ids=true | all-gather | bytes 983040 | tf_op jit(solution)/shard_map/all_gather | solution.py:199
  210.9 2.4 fusion.112
  213.3 176.5 %all-reduce.8.cloned.1.call-done = (f32[192,192]{1,0:T(8,128)}, f32[192,192]{1,0:T(8,128)}) async-done(((f32[192,192]{1,0:T(8,128)}, f32[192,192]{1,0:T(8,128)}), (f32[192,192]{1,0:T(8,128)}, f32[192,192]{1,0:T(8,128)})) %all-reduce.8.cloned.1.call-update) | async-done | bytes 294928 | tf_op jit(solution)/shard_map/psum | solution.py:229
  389.8 1.8 broadcast_multiply_fusion
  391.6 26.2 %reduce-scatter.5.cloned.1.call-done = bf16[8,48,256]{2,1,0:T(8,128)(2,1)} async-done(((bf16[8,192,256]{2,1,0:T(8,128)(2,1)}), bf16[8,48,256]{2,1,0:T(8,128)(2,1)}) %reduce-scatter.5.cloned.1.call-update) | async-done | bytes 196624 | tf_op jit(solution)/shard_map/reduce_scatter | solution.py:205
  418.9 14.7 %all-reduce.4 = (f32[8,256]{1,0:T(8,128)S(1)}, f32[8,256]{1,0:T(8,128)S(1)}) all-reduce(f32[8,256]{1,0:T(8,128)S(1)} %get-tuple-element.83, f32[8,256]{1,0:T(8,128)S(1)} %get-tuple-element.82), channel_id=1, replica_groups=mesh['tiles'=64,'chan'=4] {'chan'}, use_global_device_ids=true, to_apply=%region_12.14 | all-reduce | flops 4096 | bytes 32768 | tf_op jit(solution)/shard_map/psum | solution.py:209
  437.5 2.2 fusion.108
  439.7 2.8 fusion.109
  442.5 2.8 fusion.110
  445.9 2.3 copy.165
  449.5 1.9 collective-permute-start.13
  451.5 4.6 collective-permute-start.12
  456.0 2.7 collective-permute-start.11
  458.8 1.9 collective-permute-start.10
  460.7 4.3 collective-permute-start.8
  465.1 249.8 %psum.53 = f32[48,49]{0,1:T(8,128)S(1)} all-reduce(f32[48,49]{0,1:T(8,128)S(1)} %stack.239), channel_id=1, replica_groups=mesh['tiles'=64,'chan'=4] {'tiles'}, use_global_device_ids=true, to_apply=%region_62.64 | all-reduce | flops 2352 | bytes 18816 | tf_op jit(solution)/shard_map/psum | solution.py:229
  715.6 2.2 collective-permute-start.9
  717.8 8.2 %collective-permute-done.9 = bf16[8,9216]{1,0:T(8,128)(2,1)S(1)} collective-permute-done((bf16[8,9216]{1,0:T(8,128)(2,1)S(1)}, bf16[8,9216]{1,0:T(8,128)(2,1)S(1)}, u32[]{:S(2)}, u32[]{:S(2)}) %collective-permute-start.9) | collective-permute-done | bytes 147488 | tf_op jit(solution)/shard_map/ppermute | solution.py:26
  727.6 13.5 %reshape.212 = bf16[8,8,48,4,3,16]{5,4,3,2,1,0:T(4,128)(2,1)} reshape(bf16[8,8,9216]{2,1,0:T(8,128)(2,1)S(1)} %fusion.113) | data formatting | bytes 2359296 | tf_op jit(solution)/shard_map/reshape | solution.py:162
  741.2 2.0 fusion.134
  743.2 2.1 fusion.133
  748.9 11.0 %fusion.14 = f32[8,48,352]{1,0,2:T(8,128)S(1)} fusion(f32[8,48,484]{1,0,2:T(8,128)S(1)} %bitcast_convert_fusion, f32[48]{0:T(128)S(1)} %copy-done.57, f32[48]{0:T(128)S(1)} %copy-done.59, f32[48]{0:T(128)S(1)} %get-tuple-element.85, f32[48]{0:T(128)S(1)} %get-tuple-element.86, f32[48]{0:T(128)S(1)} %get-tuple-element.87, f32[48]{0:T(128)S(1)} %copy-done.13, ...), kind=kLoop, calls=%fused_computation.39 | loop fusion | flops 13111296 | bytes 64544960 | tf_op jit(solution)/shard_map/add | solution.py:74
  (301 shorter events, 46.3 us)
Async XLA Ops:
  7.2 158.9 %copy-start = (bf16[192,192]{1,0:T(8,128)(2,1)S(1)}, bf16[192,192]{1,0:T(8,128)(2,1)}, u32[]{:S(2)}) copy-start(bf16[192,192]{1,0:T(8,128)(2,1)} %param.20) | copy-start | bytes 221188
  7.2 4.7 copy-start.2
  7.2 183.0 %reduce-scatter.3.cloned.1.call-start = ((), (), s32[]{:S(2)}) async-start(), calls=%async_computation.2 | async-start | bytes 983040 | tf_op jit(solution)/shard_map/reduce_scatter | solution.py:192
  9.1 5.1 collective-permute-start
  10.5 3.7 collective-permute-start.1
  44.4 5.3 copy-start.94
  44.4 5.8 copy-start.95
  46.4 29.9 %copy-start.9 = (bf16[8,9216]{1,0:T(8,128)(2,1)S(1)}, bf16[8,9216]{1,0:T(8,128)(2,1)}, u32[]{:S(2)}) copy-start(bf16[8,9216]{1,0:T(8,128)(2,1)} %reshape.207) | copy-start | bytes 442372
  46.4 18.3 %collective-permute-start.2 = (bf16[8,9216]{1,0:T(8,128)(2,1)}, bf16[8,9216]{1,0:T(8,128)(2,1)S(1)}, u32[]{:S(2)}, u32[]{:S(2)}) collective-permute-start(bf16[8,9216]{1,0:T(8,128)(2,1)} %reshape.207), channel_id=1, source_target_pairs={{0,12},{4,16},{8,20},{12,24},{16,28},{20,32},{24,36},{28,40},{32,4... | collective-permute-start | bytes 442376 | tf_op jit(solution)/shard_map/ppermute | solution.py:26
  52.0 66.0 %copy-start.60 = (f32[48]{0:T(128)}, f32[48]{0:T(128)S(1)}, u32[]{:S(2)}) copy-start(f32[48]{0:T(128)S(1)} %get-tuple-element.103) | copy-start | bytes 580
  52.0 24.4 %collective-permute-start.7 = (bf16[8,9216]{1,0:T(8,128)(2,1)}, bf16[8,9216]{1,0:T(8,128)(2,1)S(1)}, u32[]{:S(2)}, u32[]{:S(2)}) collective-permute-start(bf16[8,9216]{1,0:T(8,128)(2,1)} %reshape.207), channel_id=1, source_target_pairs={{12,0},{16,4},{20,8},{24,12},{28,16},{32,20},{36,24},{40,28},{44,3... | collective-permute-start | bytes 442376 | tf_op jit(solution)/shard_map/ppermute | solution.py:26
  58.0 18.4 %collective-permute-start.6 = (bf16[8,9216]{1,0:T(8,128)(2,1)}, bf16[8,9216]{1,0:T(8,128)(2,1)S(1)}, u32[]{:S(2)}, u32[]{:S(2)}) collective-permute-start(bf16[8,9216]{1,0:T(8,128)(2,1)} %reshape.207), channel_id=1, source_target_pairs={{8,0},{12,4},{16,8},{20,12},{24,16},{28,20},{32,24},{36,28},{40,32... | collective-permute-start | bytes 442376 | tf_op jit(solution)/shard_map/ppermute | solution.py:26
  60.4 16.0 %collective-permute-start.5 = (bf16[8,9216]{1,0:T(8,128)(2,1)}, bf16[8,9216]{1,0:T(8,128)(2,1)S(1)}, u32[]{:S(2)}, u32[]{:S(2)}) collective-permute-start(bf16[8,9216]{1,0:T(8,128)(2,1)} %reshape.207), channel_id=1, source_target_pairs={{4,0},{8,4},{12,8},{16,12},{20,16},{24,20},{28,24},{32,28},{36,32}... | collective-permute-start | bytes 442376 | tf_op jit(solution)/shard_map/ppermute | solution.py:26
  62.6 13.7 %collective-permute-start.4 = (bf16[8,9216]{1,0:T(8,128)(2,1)}, bf16[8,9216]{1,0:T(8,128)(2,1)S(1)}, u32[]{:S(2)}, u32[]{:S(2)}) collective-permute-start(bf16[8,9216]{1,0:T(8,128)(2,1)} %reshape.207), channel_id=1, source_target_pairs={{0,4},{4,8},{8,12},{12,16},{16,20},{20,24},{24,28},{28,32},{32,36}... | collective-permute-start | bytes 442376 | tf_op jit(solution)/shard_map/ppermute | solution.py:26
  64.7 11.5 %collective-permute-start.3 = (bf16[8,9216]{1,0:T(8,128)(2,1)}, bf16[8,9216]{1,0:T(8,128)(2,1)S(1)}, u32[]{:S(2)}, u32[]{:S(2)}) collective-permute-start(bf16[8,9216]{1,0:T(8,128)(2,1)} %reshape.207), channel_id=1, source_target_pairs={{0,8},{4,12},{8,16},{12,20},{16,24},{20,28},{24,32},{28,36},{32,40... | collective-permute-start | bytes 442376 | tf_op jit(solution)/shard_map/ppermute | solution.py:26
  103.4 5.4 copy-start.7
  115.4 1.7 copy-start.11
  115.5 1.7 copy-start.12
  117.4 0.7 copy-start.17
  117.4 0.7 copy-start.20
  117.5 0.7 copy-start.32
  117.6 0.7 copy-start.64
  117.7 0.7 copy-start.80
  130.2 20.0 %copy-start.90 = (f32[48]{0:T(128)S(1)}, f32[48]{0:T(128)}, u32[]{:S(2)}) copy-start(f32[48]{0:T(128)} %convert_element_type.107) | copy-start | bytes 580
  131.4 32.2 %copy-start.92 = (f32[192]{0:T(256)S(1)}, f32[192]{0:T(256)}, u32[]{:S(2)}) copy-start(f32[192]{0:T(256)} %convert_element_type.109) | copy-start | bytes 2308
  164.9 1.2 copy-start.5
  166.1 24.1 %copy-start.93 = (f32[48]{0:T(128)S(1)}, f32[48]{0:T(128)}, u32[]{:S(2)}) copy-start(f32[48]{0:T(128)} %param.21) | copy-start | bytes 580
  167.8 222.0 %all-reduce.8.cloned.1.call-start = ((), (), s32[]{:S(2)}) async-start(), calls=%async_computation.4 | async-start | bytes 786432 | tf_op jit(solution)/shard_map/psum | solution.py:229
  190.2 16.2 %copy-start.6 = (f32[8,256,192]{1,2,0:T(8,128)S(1)}, f32[8,256,192]{1,2,0:T(8,128)}, u32[]{:S(2)}) copy-start(f32[8,256,192]{1,2,0:T(8,128)} %copy-done.5) | copy-start | bytes 4718596
  208.8 0.9 copy-start.3
  209.7 1.1 copy-start.10
  210.8 207.0 %reduce-scatter.5.cloned.1.call-start = ((), (), s32[]{:S(2)}) async-start(), calls=%async_computation.3 | async-start | bytes 983040 | tf_op jit(solution)/shard_map/reduce_scatter | solution.py:205
  213.2 220.3 %copy-start.91 = (f32[48]{0:T(128)S(1)}, f32[48]{0:T(128)}, u32[]{:S(2)}) copy-start(f32[48]{0:T(128)} %convert_element_type.107) | copy-start | bytes 580
  449.5 276.6 %collective-permute-start.13 = (bf16[8,9216]{1,0:T(8,128)(2,1)S(1)}, bf16[8,9216]{1,0:T(8,128)(2,1)S(1)}, u32[]{:S(2)}, u32[]{:S(2)}) collective-permute-start(bf16[8,9216]{1,0:T(8,128)(2,1)S(1)} %reshape.211), channel_id=1, source_target_pairs={{12,0},{16,4},{20,8},{24,12},{28,16},{32,20},{36,24},{40,28},{44,3... | collective-permute-start | bytes 442376 | tf_op jit(solution)/shard_map/ppermute | solution.py:26
  451.5 274.6 %collective-permute-start.12 = (bf16[8,9216]{1,0:T(8,128)(2,1)S(1)}, bf16[8,9216]{1,0:T(8,128)(2,1)S(1)}, u32[]{:S(2)}, u32[]{:S(2)}) collective-permute-start(bf16[8,9216]{1,0:T(8,128)(2,1)S(1)} %reshape.211), channel_id=1, source_target_pairs={{8,0},{12,4},{16,8},{20,12},{24,16},{28,20},{32,24},{36,28},{40,32... | collective-permute-start | bytes 442376 | tf_op jit(solution)/shard_map/ppermute | solution.py:26
  456.0 270.0 %collective-permute-start.11 = (bf16[8,9216]{1,0:T(8,128)(2,1)S(1)}, bf16[8,9216]{1,0:T(8,128)(2,1)S(1)}, u32[]{:S(2)}, u32[]{:S(2)}) collective-permute-start(bf16[8,9216]{1,0:T(8,128)(2,1)S(1)} %reshape.211), channel_id=1, source_target_pairs={{4,0},{8,4},{12,8},{16,12},{20,16},{24,20},{28,24},{32,28},{36,32}... | collective-permute-start | bytes 442376 | tf_op jit(solution)/shard_map/ppermute | solution.py:26
  458.8 267.2 %collective-permute-start.10 = (bf16[8,9216]{1,0:T(8,128)(2,1)S(1)}, bf16[8,9216]{1,0:T(8,128)(2,1)S(1)}, u32[]{:S(2)}, u32[]{:S(2)}) collective-permute-start(bf16[8,9216]{1,0:T(8,128)(2,1)S(1)} %reshape.211), channel_id=1, source_target_pairs={{0,4},{4,8},{8,12},{12,16},{16,20},{20,24},{24,28},{28,32},{32,36}... | collective-permute-start | bytes 442376 | tf_op jit(solution)/shard_map/ppermute | solution.py:26
  460.7 254.9 %collective-permute-start.8 = (bf16[8,9216]{1,0:T(8,128)(2,1)S(1)}, bf16[8,9216]{1,0:T(8,128)(2,1)S(1)}, u32[]{:S(2)}, u32[]{:S(2)}) collective-permute-start(bf16[8,9216]{1,0:T(8,128)(2,1)S(1)} %reshape.211), channel_id=1, source_target_pairs={{0,12},{4,16},{8,20},{12,24},{16,28},{20,32},{24,36},{28,40},{32,4... | collective-permute-start | bytes 442376 | tf_op jit(solution)/shard_map/ppermute | solution.py:26
  715.6 10.3 %collective-permute-start.9 = (bf16[8,9216]{1,0:T(8,128)(2,1)S(1)}, bf16[8,9216]{1,0:T(8,128)(2,1)S(1)}, u32[]{:S(2)}, u32[]{:S(2)}) collective-permute-start(bf16[8,9216]{1,0:T(8,128)(2,1)S(1)} %reshape.211), channel_id=1, source_target_pairs={{0,8},{4,12},{8,16},{12,20},{16,24},{20,28},{24,32},{28,36},{32,40... | collective-permute-start | bytes 442376 | tf_op jit(solution)/shard_map/ppermute | solution.py:26
  745.8 1.6 copy-start.4
  747.8 0.7 copy-start.21
  747.9 0.7 copy-start.33
  748.0 0.7 copy-start.65
  748.1 0.7 copy-start.81
  748.2 0.7 copy-start.86
  748.2 0.7 copy-start.88
  759.9 0.9 copy-start.8
  759.9 1.6 copy-start.1
  (65 other events, 43.3 us)
Sparse Core Ops, SparseCore 0:
  167.9 22.2 reduce-scatter.2
  210.9 178.7 all-reduce.7
  392.5 25.2 reduce-scatter.4
where the time goes:
time: 776 us; the launch traced here: 768 us
  blocking collectives  309 us (40%)
  waiting for transfers between devices  240 us (31%)
  local copies, waits for them, and re-layouts  100 us (13%)
  other arithmetic  55.9 us (7%)
  starting transfers between devices  38 us (5%)
  between operations  15.6 us (2%)
  matrix products  9.38 us (1%)
    psum x1, blocking collectives, body(): totals = lax.psum((local_dw, raw_w1, raw_w2), 'tiles')  250 us
    psum x1, waiting for transfers between devices, body(): totals = lax.psum((local_dw, raw_w1, raw_w2), 'tiles')  176 us
    ppermute x12, starting transfers between devices, passed_along(): return lax.ppermute(value, axis, pairs)  37.2 us
    reshape x2, local copies, waits for them, and re-layouts, neighbour_rims(): found.reshape(rim_shape[0], 8, rim_shape[1], rim_shape[2], rim_shape[3],...  27.1 us
    reduce_scatter x1, waiting for transfers between devices, body(): lax.psum_scatter(partial_in.astype(jnp.bfloat16), 'chan', scatter_dimensi...  26.2 us
    unnamed x218, local copies, waits for them, and re-layouts  23.7 us
    reduce_scatter x1, waiting for transfers between devices, body(): lax.psum_scatter(partial_out.astype(jnp.bfloat16), 'chan', scatter_dimens...  21.6 us
    psum x1, blocking collectives, body(): lax.psum((jnp.sum(mixed_f, axis=1), jnp.sum(mixed_f * mixed_f, axis=1)),...  17.2 us
  transfers between devices with their start and end apart: 17, of which 5 were waited for; matrix products, arithmetic and copies ran while one was open for 2% of the time, Pallas kernels for 0%

commit v1 on v0

v1 whole, which is shorter than its diff:
```python
import functools
import math

import jax
import jax.numpy as jnp
import numpy as np
from jax import lax
from jax.experimental import pallas as pl
from jax.experimental.pallas import tpu as pltpu
from jax.sharding import PartitionSpec as P

CHANNELS = 192
SIDE = 16
PIX = 256
WIDE = 24
EPSILON = 1e-06
GELU_SCALE = 0.7978845608
GELU_CUBIC = 0.044715

F32 = jnp.float32
BF16 = jnp.bfloat16
NT = (((1,), (1,)), ((), ()))
NN = (((1,), (0,)), ((), ()))


def dot(a, b, dims):
    return lax.dot_general(a, b, dims, preferred_element_type=F32)


def placement_tables():
    up = np.zeros((72, 384), np.float32)
    mid = np.zeros((384, 768), np.float32)
    down = np.zeros((72, 384), np.float32)
    for j in range(22):
        if j < 3:
            side, col = 0, 13 + j
        elif j < 19:
            side, col = 1, j - 3
        else:
            side, col = 2, j - 19
        for i in range(3):
            up[i * WIDE + j, 128 * side + 16 * (13 + i) + col - 128] = 1
            down[i * WIDE + j, 128 * side + 16 * i + col] = 1
        for i in range(16):
            block = (1, 0, 2)[side]
            mid[i * WIDE + j, 256 * block + 16 * i + col] = 1
    return up.astype(jnp.bfloat16), mid.astype(jnp.bfloat16), down.astype(jnp.bfloat16)


def column(row):
    n = row.shape[1]
    same = lax.broadcasted_iota(jnp.int32, (n, n), 0) == lax.broadcasted_iota(jnp.int32, (n, n), 1)
    return jnp.sum(jnp.where(same, jnp.broadcast_to(row, (n, n)), 0.0), axis=1, keepdims=True)


def eye(n):
    same = lax.broadcasted_iota(jnp.int32, (n, n), 0) == lax.broadcasted_iota(jnp.int32, (n, n), 1)
    return same.astype(F32).astype(BF16)


def swap_halves(value):
    return pltpu.roll(value.astype(F32), 64, 1)


def low_lanes(shape):
    return lax.broadcasted_iota(jnp.int32, shape, 1) < 64


def pack_pair(natural, other, natural_low):
    shape = natural.shape
    keep = low_lanes(shape) if natural_low else jnp.logical_not(low_lanes(shape))
    return jnp.where(keep, natural.astype(F32), swap_halves(other)).astype(BF16)


def prepare_kernel(x_ref, cot_ref, scale_ref, strips_ref, d0, d1, d2, d3):
    odd = lax.axis_index("tiles") & 1
    mine = lax.axis_index("chan")

    @pl.when(odd == 1)
    def _():
        for s in range(8):
            strips_ref[s] = pack_pair(x_ref[s, :, 128:256], x_ref[s + 8, :, 128:256], False)

    @pl.when(odd == 0)
    def _():
        for s in range(8):
            strips_ref[s] = pack_pair(x_ref[s, :, 0:128], x_ref[s + 8, :, 0:128], True)

    scale = column(scale_ref[...])
    for j, out in enumerate((d0, d1, d2, d3)):
        first = 2 * ((mine + j) & 3)
        for i in range(2):
            out[i] = (cot_ref[first + i].astype(F32) * scale).astype(BF16)


def gather_tile(table, up_g, mid_g, down_g, t, center, entries):
    rows = pl.ds(48 * t, 48)
    mid_g[rows, 0:256] = table[center]
    mid_g[rows, 256:512] = table[entries[3]]
    mid_g[rows, 512:768] = table[entries[4]]
    for k in range(3):
        up_g[rows, 128 * k : 128 * k + 128] = table[entries[k], :, 128:256]
        down_g[rows, 128 * k : 128 * k + 128] = table[entries[5 + k], :, 0:128]


def build_padded(pad, up_g, mid_g, down_g, up_p, mid_p, down_p):
    pad[0:3] = dot(up_p[...], up_g[...], NT).reshape(3, WIDE, 384)
    pad[3:19] = dot(mid_p[...], mid_g[...], NT).reshape(16, WIDE, 384)
    pad[19:22] = dot(down_p[...], down_g[...], NT).reshape(3, WIDE, 384)


def convolve(pad, taps, result, flip):
    def lane_block(block, carry):
        lanes = pl.ds(pl.multiple_of(block * 128, 128), 128)
        acc = [jnp.zeros((16, 128), F32) for _ in range(16)]
        for b in range(7):
            weights = []
            for a in range(7):
                tap = 7 * a + b
                weights.append(taps[pl.ds(48 - tap if flip else tap, 1), lanes])
            for r in range(22):
                line = pad[r, pl.ds(b, 16), lanes]
                for a in range(7):
                    i = r - a
                    if 0 <= i < 16:
                        acc[i] = acc[i] + line * weights[a]
        for i in range(16):
            result[pl.ds(16 * i, 16), lanes] = acc[i]
        return carry

    lax.fori_loop(0, 3, lane_block, 0)


OFFSETS = (-17, -16, -15, -1, 1, 15, 16, 17)


def mix_kernel(
    own_slots, par_slots, adj, x_ref, par_ref, sa_ref, sb_ref, taps, up_p, mid_p, down_p,
    owned_ref, pad_out, m0, m1, m2, m3,
    place, table, up_g, mid_g, down_g, pad, result, flat,
):
    me = lax.axis_index("tiles")
    odd = me & 1
    mine = lax.axis_index("chan")
    base = 8 * me
    for t in range(8):
        place[t] = 0
    for s in range(16):
        for slots, row in ((own_slots, odd), (par_slots, 1 - odd)):
            t = slots[s] - base

            @pl.when((t >= 0) & (t < 8))
            def _():
                place[t] = 16 + 16 * row + s

    table[pl.ds(16 + 16 * odd, 16)] = x_ref[...]
    table[pl.ds(32 - 16 * odd, 16)] = par_ref[...]
    table[64] = jnp.zeros((48, 256), BF16)

    def halo_rows(above, below):
        for s in range(8):
            up = above[s]
            table[s, :, 128:256] = up
            table[s + 8, :, 128:256] = swap_halves(up).astype(BF16)
            down = below[s]
            table[48 + s, :, 0:128] = down
            table[56 + s, :, 0:128] = swap_halves(down).astype(BF16)

    @pl.when(odd == 0)
    def _():
        halo_rows(sa_ref, sb_ref)

    @pl.when(odd == 1)
    def _():
        halo_rows(sb_ref, sa_ref)

    for t in range(8):
        center = place[t]
        entries = [jnp.where(adj[t, k] < 512, center + OFFSETS[k], 64) for k in range(8)]
        gather_tile(table, up_g, mid_g, down_g, t, center, entries)
    owned_ref[...] = mid_g[:, 0:256].reshape(8, 48, 256)
    build_padded(pad, up_g, mid_g, down_g, up_p, mid_p, down_p)
    pad_out[...] = pad[...].astype(BF16)
    convolve(pad, taps, result, False)
    flat[...] = result[...].T.astype(BF16).reshape(8, 48, 256)
    for j, out in enumerate((m0, m1, m2, m3)):
        first = 2 * ((mine + j) & 3)
        out[0] = flat[first]
        out[1] = flat[first + 1]


def weights_kernel(w0, w1, w2, w3, in_t, out_t, bias, gain):
    mine = lax.axis_index("chan")
    unit = eye(192)
    for j, ref in enumerate((w0, w1, w2, w3)):
        in_t[j] = dot(unit, ref[0:192], NT).astype(BF16)
        out_t[j] = dot(unit, ref[192:384], NT).astype(BF16)
        cols = dot(unit, ref[384:400], NT)
        bias[j] = jnp.broadcast_to(cols[:, 0:1], (192, 128))
        gain[(mine + 4 - j) & 3] = jnp.broadcast_to(cols[0:48, 1:2], (48, 128))


def across(col_block):
    return jnp.concatenate([col_block] * 4, axis=1)


def mlp_kernel(
    m0, m1, m2, m3, b0, b1, b2, b3, w0, w1, w2, w3, in_t, out_t, bias, gain,
    g0, g1, g2, g3, r0, r1, r2, r3, v0, v1, v2, v3,
    mixed_s, dbranch_s, back_s, branch_s,
):
    mine = lax.axis_index("chan")
    for j, (m_ref, b_ref) in enumerate(((m0, b0), (m1, b1), (m2, b2), (m3, b3))):
        a = (mine + 4 - j) & 3
        for i in range(2):
            mixed_s[a, :, 256 * i : 256 * i + 256] = m_ref[i]
            dbranch_s[a, :, 256 * i : 256 * i + 256] = b_ref[i]
    mixed = mixed_s[...].reshape(192, 512).astype(F32)
    dbranch = dbranch_s[...].reshape(192, 512)
    mean = jnp.sum(mixed, axis=0, keepdims=True) / CHANNELS
    inv = lax.rsqrt(
        jnp.sum(mixed * mixed, axis=0, keepdims=True) / CHANNELS - mean * mean + EPSILON
    )
    x_hat = (mixed - mean) * inv
    gain_full = across(gain[...].reshape(192, 128))
    normed = (x_hat * gain_full).astype(BF16)
    branch = jnp.zeros((192, 512), F32)
    dnormed = jnp.zeros((192, 512), F32)
    for j, (w_ref, v_ref) in enumerate(((w0, v0), (w1, v1), (w2, v2), (w3, v3))):
        preact = dot(in_t[j], normed, NN) + across(bias[j])
        square = preact * preact
        tangent = jnp.tanh(GELU_SCALE * (preact + GELU_CUBIC * square * preact))
        half = 0.5 * (1.0 + tangent)
        act = (preact * half).astype(BF16)
        slope = half + 0.5 * preact * (1.0 - tangent * tangent) * (
            GELU_SCALE * (1.0 + 3.0 * GELU_CUBIC * square)
        )
        branch = branch + dot(out_t[j], act, NN)
        pre_grad = (dot(w_ref[192:384], dbranch, NN) * slope).astype(BF16)
        dnormed = dnormed + dot(w_ref[0:192], pre_grad, NN)
        v_ref[0:192] = dot(normed, pre_grad, NT).astype(BF16)
        v_ref[192:384] = dot(act, dbranch, NT).astype(BF16)
    xhat_grad = dnormed * gain_full
    first = jnp.sum(xhat_grad, axis=0, keepdims=True) / CHANNELS
    second = jnp.sum(xhat_grad * x_hat, axis=0, keepdims=True) / CHANNELS
    dmixed = (inv * (xhat_grad - first - x_hat * second)).astype(BF16)
    back_s[...] = dmixed.reshape(4, 48, 512)
    branch_s[...] = branch.astype(BF16).reshape(4, 48, 512)
    for j, (g_ref, r_ref) in enumerate(((g0, r0), (g1, r1), (g2, r2), (g3, r3))):
        a = (mine + j) & 3
        for i in range(2):
            g_ref[i] = back_s[a, :, 256 * i : 256 * i + 256]
            r_ref[i] = branch_s[a, :, 256 * i : 256 * i + 256]


def collect_kernel(g0, g1, g2, g3, grad_ref, top_ref, bottom_ref):
    mine = lax.axis_index("chan")
    for j, ref in enumerate((g0, g1, g2, g3)):
        grad_ref[pl.ds(2 * ((mine + 4 - j) & 3), 2)] = ref[...]
    for t in range(4):
        top_ref[t] = pack_pair(grad_ref[t, :, 0:128], grad_ref[t + 4, :, 0:128], True)
        bottom_ref[t] = pack_pair(grad_ref[t, :, 128:256], grad_ref[t + 4, :, 128:256], False)


def taps_kernel(grad_ref, pad_ref, fold, v0, v1, v2, v3, out_ref, pad, grad_t, sums):
    pad[...] = pad_ref[...].astype(F32)
    grad_t[...] = grad_ref[...].reshape(384, 256).astype(F32).T
    sums[...] = jnp.zeros((64, 384), F32)

    def lane_block(block, carry):
        lanes = pl.ds(pl.multiple_of(block * 128, 128), 128)
        lines = [grad_t[pl.ds(16 * i, 16), lanes] for i in range(16)]
        for b in range(7):
            acc = [jnp.zeros((16, 128), F32) for _ in range(7)]
            for r in range(22):
                line = pad[r, pl.ds(b, 16), lanes]
                for a in range(7):
                    i = r - a
                    if 0 <= i < 16:
                        acc[a] = acc[a] + line * lines[i]
            for a in range(7):
                sums[pl.ds(7 * a + b, 1), lanes] = jnp.sum(acc[a], axis=0, keepdims=True)
        return carry

    lax.fori_loop(0, 3, lane_block, 0)
    total = jnp.zeros((384, 192), F32)
    for ref in (v0, v1, v2, v3):
        total = total + ref[...].astype(F32)
    for q in range(6):
        out_ref[:, 128 * q : 128 * q + 128] = total[64 * q : 64 * q + 64, 0:128].astype(BF16)
    for q in range(3):
        both = jnp.concatenate(
            [total[128 * q : 128 * q + 64, 128:192], total[128 * q + 64 : 128 * q + 128, 128:192]],
            axis=1,
        )
        out_ref[:, 768 + 128 * q : 896 + 128 * q] = both.astype(BF16)
    folded = lax.dot_general(
        sums[...], fold[...], NN, precision=lax.Precision.HIGHEST, preferred_element_type=F32
    )
    out_ref[:, 1152:1280] = folded.astype(BF16)


def total_kernel(factor, in_ref, out_ref):
    total = jnp.sum(in_ref[...].astype(F32), axis=0, keepdims=True) * factor
    out_ref[...] = jnp.broadcast_to(total, in_ref.shape).astype(out_ref.dtype)


def finish_kernel(in_ref, dw_ref, w1_ref, w2_ref):
    for q in range(6):
        out, row = (w1_ref, 64 * q) if q < 3 else (w2_ref, 64 * q - 192)
        out[row : row + 64, 0:128] = in_ref[:, 128 * q : 128 * q + 128].astype(F32)
        lo = 768 + 128 * (q // 2) + 64 * (q % 2)
        out[row : row + 64, 128:192] = in_ref[:, lo : lo + 64].astype(F32)
    dw_ref[...] = in_ref[:, 1152:1280].astype(F32).T[0:48, 0:49]


def unmix_kernel(
    adj, grad_ref, par_ref, us, uc, ds_, dc, cot_ref, taps, up_p, mid_p, down_p,
    owned_ref, scale_ref, r0, r1, r2, r3,
    out_ref, gin_ref,
    table, up_g, mid_g, down_g, pad, result,
):
    me = lax.axis_index("tiles")
    odd = me & 1
    mine = lax.axis_index("chan")
    start = 16 * (me // 2) - 16
    table[pl.ds(16 + 8 * odd, 8)] = grad_ref[...]
    table[pl.ds(24 - 8 * odd, 8)] = par_ref[...]
    table[48] = jnp.zeros((48, 256), BF16)
    for t in range(4):
        for ref, side in ((us, odd), (uc, 1 - odd)):
            up = ref[t]
            table[8 * side + t, :, 128:256] = up
            table[8 * side + t + 4, :, 128:256] = swap_halves(up).astype(BF16)
        for ref, side in ((ds_, odd), (dc, 1 - odd)):
            down = ref[t]
            table[32 + 8 * side + t, :, 0:128] = down
            table[32 + 8 * side + t + 4, :, 0:128] = swap_halves(down).astype(BF16)
    for t in range(8):
        center = 16 + 8 * odd + t
        entries = [jnp.where(adj[t, k] < 512, adj[t, k] - start, 48) for k in range(8)]
        gather_tile(table, up_g, mid_g, down_g, t, center, entries)
    build_padded(pad, up_g, mid_g, down_g, up_p, mid_p, down_p)
    convolve(pad, taps, result, True)
    back = result[...].T.reshape(8, 48, 256)
    gin_ref[...] = (cot_ref[...].astype(F32) + back).astype(BF16)
    scale = column(scale_ref[...])
    for j, ref in enumerate((r0, r1, r2, r3)):
        first = 2 * ((mine + 4 - j) & 3)
        for i in range(2):
            out_ref[first + i] = (
                owned_ref[first + i].astype(F32) + scale * ref[i].astype(F32)
            ).astype(BF16)


def call(kernel, shapes, scratch=(), smem=0, n_in=0, name=None):
    vmem = pl.BlockSpec(memory_space=pltpu.VMEM)
    scalar = pl.BlockSpec(memory_space=pltpu.SMEM)
    many = isinstance(shapes, (list, tuple))
    return pl.pallas_call(
        kernel,
        out_shape=shapes,
        in_specs=[scalar] * smem + [vmem] * (n_in - smem),
        out_specs=[vmem] * len(shapes) if many else vmem,
        scratch_shapes=list(scratch),
        name=name,
    )


def shape(*dims, dtype=BF16):
    return jax.ShapeDtypeStruct(dims, dtype)


def along_chan(values):
    got = [values[0]]
    for j in range(1, 4):
        got.append(lax.ppermute(values[j], "chan", [(i, (i + j) % 4) for i in range(4)]))
    return got


def body(
    x_scan, slot_owner, adjacency, cotangent, dw_weight, ln_gain, w_in, b_in, w_out, layer_scale
):
    devices = lax.axis_size("tiles")
    up_p, mid_p, down_p = (jnp.asarray(v) for v in placement_tables())
    fold = jnp.asarray((np.arange(384)[:, None] % 48 == np.arange(128)[None, :]).astype(np.float32))
    scale_row = layer_scale.reshape(1, 48)

    def hop(value, target):
        pairs = [(i, target(i)) for i in range(devices)]
        return lax.ppermute(value, "tiles", [p for p in pairs if 0 <= p[1] < devices])

    tile_chunk = shape(2, 48, 256)
    prep = call(prepare_kernel, [shape(8, 48, 128)] + [tile_chunk] * 4, n_in=3, name="prepare")
    strips, *dbranch = prep(x_scan, cotangent, scale_row)
    par_x = hop(x_scan, lambda i: i ^ 1)
    par_slots = hop(slot_owner, lambda i: i ^ 1)
    near = hop(strips, lambda i: i + 1 if i & 1 else i - 1)
    far = hop(strips, lambda i: i + 2 if i & 1 else i - 2)
    taps = jnp.tile(dw_weight.T, (1, 8))

    small = jnp.zeros((16, 192), BF16).at[0].set(b_in).at[1, 0:48].set(ln_gain)
    packed = jnp.concatenate([w_in, w_out, small], axis=0)
    all_dbranch = along_chan(dbranch)
    all_weights = along_chan([packed] * 4)

    grid_scratch = lambda entries: [
        pltpu.VMEM((entries, 48, 256), BF16),
        pltpu.VMEM((384, 384), BF16),
        pltpu.VMEM((384, 768), BF16),
        pltpu.VMEM((384, 384), BF16),
        pltpu.VMEM((22, WIDE, 384), F32),
        pltpu.VMEM((256, 384), F32),
    ]
    mix = call(
        mix_kernel,
        [shape(8, 48, 256), shape(22, WIDE, 384)] + [tile_chunk] * 4,
        scratch=[pltpu.SMEM((8,), jnp.int32)] + grid_scratch(65) + [pltpu.VMEM((8, 48, 256), BF16)],
        smem=3,
        n_in=11,
        name="mix",
    )
    owned, padded, *mixed = mix(
        slot_owner, par_slots, adjacency, x_scan, par_x, near, far, taps, up_p, mid_p, down_p
    )
    all_mixed = along_chan(mixed)

    turn = call(
        weights_kernel,
        [
            shape(4, 192, 192),
            shape(4, 192, 192),
            shape(4, 192, 128, dtype=F32),
            shape(4, 48, 128, dtype=F32),
        ],
        n_in=4,
        name="turn",
    )
    turned = turn(*all_weights)

    mlp = call(
        mlp_kernel,
        [tile_chunk] * 8 + [shape(384, 192)] * 4,
        scratch=[pltpu.VMEM((4, 48, 512), BF16)] * 4,
        n_in=16,
        name="mlp",
    )
    results = mlp(*all_mixed, *all_dbranch, *all_weights, *turned)
    all_back = along_chan(results[0:4])
    collect = call(
        collect_kernel,
        [shape(8, 48, 256), shape(4, 48, 128), shape(4, 48, 128)],
        n_in=4,
        name="collect",
    )
    grads, top, bottom = collect(*all_back)
    par_grads = hop(grads, lambda i: i ^ 1)
    from_up = hop(bottom, lambda i: i + 2)
    from_up_cross = hop(bottom, lambda i: (i ^ 1) + 2)
    from_down = hop(top, lambda i: i - 2)
    from_down_cross = hop(top, lambda i: (i ^ 1) - 2)

    partials = results[8:12]
    all_partials = [partials[0]]
    for j in range(1, 4):
        all_partials.append(
            lax.ppermute(partials[j], "chan", [(i, (i - j) % 4) for i in range(4)])
        )
    all_branch = along_chan(results[4:8])

    tap_sums = call(
        taps_kernel,
        shape(64, 1280),
        scratch=[
            pltpu.VMEM((22, WIDE, 384), F32),
            pltpu.VMEM((256, 384), F32),
            pltpu.VMEM((64, 384), F32),
        ],
        n_in=7,
        name="tap_sums",
    )
    pieces = tap_sums(grads, padded, fold, *all_partials)
    arrived = lax.all_to_all(pieces, "tiles", 0, 0, tiled=True)
    factor = 1.0 / math.sqrt(adjacency.shape[0] * devices * PIX)
    totals = call(
        functools.partial(total_kernel, factor), shape(64, 1280), n_in=1, name="totals"
    )(arrived)
    spread = lax.all_to_all(totals, "tiles", 0, 0, tiled=True)

    unmix = call(
        unmix_kernel,
        [shape(8, 48, 256), shape(8, 48, 256)],
        scratch=grid_scratch(49),
        smem=1,
        n_in=18,
        name="unmix",
    )
    output, grad_in = unmix(
        adjacency, grads, par_grads, from_up, from_up_cross, from_down, from_down_cross,
        cotangent, taps, up_p, mid_p, down_p, owned, scale_row, *all_branch
    )
    grad_dw, grad_w1, grad_w2 = call(
        finish_kernel,
        [shape(48, 49, dtype=F32), shape(192, 192, dtype=F32), shape(192, 192, dtype=F32)],
        n_in=1,
        name="finish",
    )(spread)
    return (output, grad_in, grad_dw, grad_w1, grad_w2)


def solution(mesh):
    in_specs = (
        P("tiles", "chan", None),
        P("tiles"),
        P("tiles", None),
        P("tiles", "chan", None),
        P("chan", None),
        P("chan"),
        P(None, "chan"),
        P("chan"),
        P("chan", None),
        P("chan"),
    )
    out_specs = (
        P("tiles", "chan", None),
        P("tiles", "chan", None),
        P("chan", None),
        P(None, "chan"),
        P("chan", None),
    )
    return jax.shard_map(body, mesh=mesh, in_specs=in_specs, out_specs=out_specs, check_vma=False)
```

time: 776 us -> 141 us (0.18)
  the two profiles are of different devices: /device:TPU:128 before, /device:TPU:123 now
where the time goes in v1:
time: 141 us
  starting transfers between devices  55.5 us (39%)
  Pallas kernels  33 us (23%)
  blocking collectives  23.8 us (17%)
  waiting for transfers between devices  15.8 us (11%)
  local copies, waits for them, and re-layouts  7.9 us (6%)
  other arithmetic  3.25 us (2%)
    all_to_all x1, blocking collectives, body(): arrived = lax.all_to_all(pieces, 'tiles', 0, 0, tiled=True)  23.8 us
    ppermute x9, starting transfers between devices, hop(): lax.ppermute(value, 'tiles', [p for p in pairs if 0 <= p[1] < devices])  23.3 us
    ppermute x15, starting transfers between devices, along_chan(): lax.ppermute(values[j], 'chan', [(i, (i + j) % 4) for i in range(4)])  18.8 us
    ppermute x9, waiting for transfers between devices, hop(): lax.ppermute(value, 'tiles', [p for p in pairs if 0 <= p[1] < devices])  9.51 us
    all_to_all x1, starting transfers between devices, body(): spread = lax.all_to_all(totals, 'tiles', 0, 0, tiled=True)  8.97 us
    pallas_call x1, Pallas kernels, body(): unmix(adjacency, grads, par_grads, from_up, from_up_cross, from_down, fro...  6.73 us
    pallas_call x1, Pallas kernels, body(): mix(slot_owner, par_slots, adjacency, x_scan, par_x, near, far, taps, up_...  6.67 us
    unnamed x94, local copies, waits for them, and re-layouts  6.44 us
  transfers between devices with their start and end apart: 28, of which 6 were waited for; matrix products, arithmetic and copies ran while one was open for 1% of the time, Pallas kernels for 14%

profile of v1, /device:TPU:123, one launch (start us, length us, event | category | flops | bytes accessed | tf_op | source)
XLA Modules:
  0.0 140.5 jit_solution(14265094309477087030)
XLA Ops:
  0.6 0.8 collective-permute-start.1
  1.4 2.0 %prepare.1 = (bf16[8,48,128]{2,1,0:T(8,128)(2,1)}, bf16[2,48,256]{2,1,0:T(8,128)(2,1)}, bf16[2,48,256]{2,1,0:T(8,128)(2,1)}, bf16[2,48,256]{2,1,0:T(8,128)(2,1)}, bf16[2,48,256]{2,1,0:T(8,128)(2,1)}) custom-call(bf16[16,48,256]{2,1,0:T(8,128)(2,1)} %x_ref.3, bf16[8,48,256]{2,1,0:T(8,128)(2,1)} %cot_ref.3, f32[1,48]{1,0:T(1,128)} %bitcast.16), custom_call_target="tpu_custom_call" | custom-call | tf_op jit(solution)/shard_map/prepare/pallas_call | solution.py:395
  3.4 4.5 %collective-permute-start.2 = (bf16[8,48,128]{2,1,0:T(8,128)(2,1)}, bf16[8,48,128]{2,1,0:T(8,128)(2,1)S(1)}, u32[]{:S(2)}, u32[]{:S(2)}) collective-permute-start(bf16[8,48,128]{2,1,0:T(8,128)(2,1)} %get-tuple-element.64), channel_id=1, source_target_pairs={{4,8},{8,4},{12,16},{16,12},{20,24},{24,20},{28,32},{32,28},{36,40... | collective-permute-start | bytes 294920 | tf_op jit(solution)/shard_map/ppermute | solution.py:391
  7.9 0.6 copy-done.33
  8.8 1.3 collective-permute-start.10
  10.0 0.8 collective-permute-start.11
  10.9 1.1 collective-permute-done.par_slots
  12.0 1.9 %collective-permute-start.12 = (bf16[400,192]{1,0:T(8,128)(2,1)S(1)}, bf16[400,192]{1,0:T(8,128)(2,1)S(1)}, u32[]{:S(2)}, u32[]{:S(2)}) collective-permute-start(bf16[400,192]{1,0:T(8,128)(2,1)S(1)} %pad_maximum_fusion.w0), channel_id=1, source_target_pairs={{0,3},{1,0},{2,1},{3,2},{4,7},{5,4},{6,5},{7,6},{8,11},{9,8},{10,9... | collective-permute-start | bytes 460808 | tf_op jit(solution)/shard_map/ppermute | solution.py:377
  13.9 4.9 %collective-permute-start.3 = (bf16[8,48,128]{2,1,0:T(8,128)(2,1)S(1)}, bf16[8,48,128]{2,1,0:T(8,128)(2,1)S(1)}, u32[]{:S(2)}, u32[]{:S(2)}) collective-permute-start(bf16[8,48,128]{2,1,0:T(8,128)(2,1)S(1)} %copy-done.34), channel_id=1, source_target_pairs={{4,12},{8,0},{12,20},{16,8},{20,28},{24,16},{28,36},{32,24},{36,44... | collective-permute-start | bytes 294920 | tf_op jit(solution)/shard_map/ppermute | solution.py:391
  18.8 1.6 %collective-permute-done.3.sb_ref = bf16[8,48,128]{2,1,0:T(8,128)(2,1)S(1)} collective-permute-done((bf16[8,48,128]{2,1,0:T(8,128)(2,1)S(1)}, bf16[8,48,128]{2,1,0:T(8,128)(2,1)S(1)}, u32[]{:S(2)}, u32[]{:S(2)}) %collective-permute-start.3) | collective-permute-done | bytes 98336 | tf_op jit(solution)/shard_map/ppermute | solution.py:391
  20.6 0.8 tile.10.taps
  21.4 3.0 %collective-permute-start.8 = (bf16[2,48,256]{2,1,0:T(8,128)(2,1)S(1)}, bf16[2,48,256]{2,1,0:T(8,128)(2,1)S(1)}, u32[]{:S(2)}, u32[]{:S(2)}) collective-permute-start(bf16[2,48,256]{2,1,0:T(8,128)(2,1)S(1)} %copy-done.39), channel_id=1, source_target_pairs={{0,2},{1,3},{2,0},{3,1},{4,6},{5,7},{6,4},{7,5},{8,10},{9,11},{10,... | collective-permute-start | bytes 147464 | tf_op jit(solution)/shard_map/ppermute | solution.py:377
  24.4 6.7 %mix.1 = (bf16[8,48,256]{2,1,0:T(8,128)(2,1)}, bf16[22,24,384]{2,1,0:T(8,128)(2,1)}, bf16[2,48,256]{2,1,0:T(8,128)(2,1)}, bf16[2,48,256]{2,1,0:T(8,128)(2,1)}, b...) custom-call(s32[16]{0:T(128)} %own_slots.1, s32[16]{0:T(128)} %copy-done.32, s32[8,8]{1,0:T(8,128)} %adj.3, ...), custom_call_target="tpu_custom_call" | custom-call | tf_op jit(solution)/shard_map/mix/pallas_call | solution.py:423
  31.2 1.4 %collective-permute-start.4 = (bf16[2,48,256]{2,1,0:T(8,128)(2,1)}, bf16[2,48,256]{2,1,0:T(8,128)(2,1)S(1)}, u32[]{:S(2)}, u32[]{:S(2)}) collective-permute-start(bf16[2,48,256]{2,1,0:T(8,128)(2,1)} %get-tuple-element.66), channel_id=1, source_target_pairs={{0,1},{1,2},{2,3},{3,0},{4,5},{5,6},{6,7},{7,4},{8,9},{9,10},{10,1... | collective-permute-start | bytes 147464 | tf_op jit(solution)/shard_map/ppermute | solution.py:377
  32.6 1.8 %collective-permute-start.5 = (bf16[2,48,256]{2,1,0:T(8,128)(2,1)}, bf16[2,48,256]{2,1,0:T(8,128)(2,1)S(1)}, u32[]{:S(2)}, u32[]{:S(2)}) collective-permute-start(bf16[2,48,256]{2,1,0:T(8,128)(2,1)} %get-tuple-element.67), channel_id=1, source_target_pairs={{0,2},{1,3},{2,0},{3,1},{4,6},{5,7},{6,4},{7,5},{8,10},{9,11},{10,... | collective-permute-start | bytes 147464 | tf_op jit(solution)/shard_map/ppermute | solution.py:377
  34.5 0.6 copy-done.3
  35.1 2.7 %turn.1 = (bf16[4,192,192]{2,1,0:T(8,128)(2,1)}, bf16[4,192,192]{2,1,0:T(8,128)(2,1)}, f32[4,192,128]{2,1,0:T(8,128)}, f32[4,48,128]{2,1,0:T(8,128)}) custom-call(bf16[400,192]{1,0:T(8,128)(2,1)} %copy-done, bf16[400,192]{1,0:T(8,128)(2,1)} %copy-done.1, bf16[400,192]{1,0:T(8,128)(2,1)} %copy-done.2, bf16[400,192]{1,0:T(8,128)(2,1)} %copy-done.3), custom_call_target="tpu_custom_call" | custom-call | tf_op jit(solution)/shard_map/turn/pallas_call | solution.py:439
  38.6 5.1 %mlp.1 = (bf16[2,48,256]{2,1,0:T(8,128)(2,1)}, bf16[2,48,256]{2,1,0:T(8,128)(2,1)}, bf16[2,48,256]{2,1,0:T(8,128)(2,1)}, bf16[2,48,256]{2,1,0:T(8,128)(2,1)}, bf...) custom-call(bf16[2,48,256]{2,1,0:T(8,128)(2,1)} %get-tuple-element.6, ...), custom_call_target="tpu_custom_call" | custom-call | tf_op jit(solution)/shard_map/mlp/pallas_call | solution.py:448
  43.7 1.4 %collective-permute-start.24 = (bf16[384,192]{1,0:T(8,128)(2,1)}, bf16[384,192]{1,0:T(8,128)(2,1)S(1)}, u32[]{:S(2)}, u32[]{:S(2)}) collective-permute-start(bf16[384,192]{1,0:T(8,128)(2,1)} %get-tuple-element.93), channel_id=1, source_target_pairs={{0,3},{1,0},{2,1},{3,2},{4,7},{5,4},{6,5},{7,6},{8,11},{9,8},{10,9... | collective-permute-start | bytes 442376 | tf_op jit(solution)/shard_map/ppermute | solution.py:467
  45.1 1.2 collective-permute-start.25
  46.2 2.0 %collective-permute-start.26 = (bf16[384,192]{1,0:T(8,128)(2,1)}, bf16[384,192]{1,0:T(8,128)(2,1)S(1)}, u32[]{:S(2)}, u32[]{:S(2)}) collective-permute-start(bf16[384,192]{1,0:T(8,128)(2,1)} %get-tuple-element.95), channel_id=1, source_target_pairs={{0,1},{1,2},{2,3},{3,0},{4,5},{5,6},{6,7},{7,4},{8,9},{9,10},{10,1... | collective-permute-start | bytes 442376 | tf_op jit(solution)/shard_map/ppermute | solution.py:467
  48.3 1.2 collective-permute-start.14
  49.5 3.7 %collective-permute-done.13.g1 = bf16[2,48,256]{2,1,0:T(8,128)(2,1)S(1)} collective-permute-done((bf16[2,48,256]{2,1,0:T(8,128)(2,1)}, bf16[2,48,256]{2,1,0:T(8,128)(2,1)S(1)}, u32[]{:S(2)}, u32[]{:S(2)}) %collective-permute-start.13) | collective-permute-done | bytes 49184 | tf_op jit(solution)/shard_map/ppermute | solution.py:377
  53.2 2.4 %collective-permute-start.15 = (bf16[2,48,256]{2,1,0:T(8,128)(2,1)}, bf16[2,48,256]{2,1,0:T(8,128)(2,1)S(1)}, u32[]{:S(2)}, u32[]{:S(2)}) collective-permute-start(bf16[2,48,256]{2,1,0:T(8,128)(2,1)} %get-tuple-element.80), channel_id=1, source_target_pairs={{0,3},{1,0},{2,1},{3,2},{4,7},{5,4},{6,5},{7,6},{8,11},{9,8},{10,9... | collective-permute-start | bytes 147464 | tf_op jit(solution)/shard_map/ppermute | solution.py:377
  55.6 2.5 %collective-permute-done.15.g3 = bf16[2,48,256]{2,1,0:T(8,128)(2,1)S(1)} collective-permute-done((bf16[2,48,256]{2,1,0:T(8,128)(2,1)}, bf16[2,48,256]{2,1,0:T(8,128)(2,1)S(1)}, u32[]{:S(2)}, u32[]{:S(2)}) %collective-permute-start.15) | collective-permute-done | bytes 49184 | tf_op jit(solution)/shard_map/ppermute | solution.py:377
  58.2 0.6 copy-done.16
  58.8 1.6 %collect.1 = (bf16[8,48,256]{2,1,0:T(8,128)(2,1)}, bf16[4,48,128]{2,1,0:T(8,128)(2,1)}, bf16[4,48,128]{2,1,0:T(8,128)(2,1)}) custom-call(bf16[2,48,256]{2,1,0:T(8,128)(2,1)} %get-tuple-element.77.g0, bf16[2,48,256]{2,1,0:T(8,128)(2,1)} %copy-done.14, bf16[2,48,256]{2,1,0:T(8,128)(2,1)} %copy-done.15, bf16[2,48,256]{2,1,0:T(8,128)(2,1)} %copy-done.16), custom_call_target="tpu_custom_call" | custom-call | tf_op jit(solution)/shard_map/collect/pallas_call | solution.py:456
  60.4 0.6 copy-done.7
  61.2 4.9 %tap_sums.1 = bf16[64,1280]{1,0:T(8,128)(2,1)} custom-call(bf16[8,48,256]{2,1,0:T(8,128)(2,1)} %get-tuple-element.81.grad_ref, bf16[22,24,384]{2,1,0:T(8,128)(2,1)} %get-tuple-element.91.pad_ref, f32[384,128]{1,0:T(8,128)} %constant.68.clone.fold, bf16[384,192]{1,0:T(8,128)(2,1)} %get-tuple-element.92.v0, bf16[384,192]{1,0:T(8,128)(2,1)} %copy-done.7, ...), custom_call_target="tpu_custom_call" | custom-call | tf_op jit(solution)/shard_map/tap_sums/pallas_call | solution.py:482
  66.6 1.6 %reduce.4 = bf16[64,1280]{1,0:T(8,128)(2,1)S(1)} reduce(bf16[64,1,1280]{2,0,1:T(8,128)(2,1)} %bitcast.14, bf16[]{:T(256)} %broadcast.32), dimensions={1}, to_apply=%copy.25.reduce_sub_computation | reduce | bytes 327682 | tf_op jit(solution)/shard_map/all_to_all | solution.py:483
  68.2 23.8 %all_to_all.22 = bf16[64,2,640]{2,1,0:T(2,128)(2,1)S(1)} all-to-all(bf16[64,2,640]{2,1,0:T(2,128)(2,1)S(1)} %reshape.81), channel_id=1, replica_groups=mesh['tiles'=64,'chan'=4] {'tiles'}, dimensions={0} | all-to-all | bytes 327680 | tf_op jit(solution)/shard_map/all_to_all | solution.py:483
  92.2 0.7 copy.32
  92.9 1.6 %totals.1 = bf16[64,1280]{1,0:T(8,128)(2,1)} custom-call(bf16[64,1280]{1,0:T(8,128)(2,1)} %bitcast.13), custom_call_target="tpu_custom_call" | custom-call | tf_op jit(solution)/shard_map/totals/pallas_call | solution.py:485
  94.5 1.6 %reduce.5 = bf16[64,1280]{1,0:T(8,128)(2,1)S(1)} reduce(bf16[64,1,1280]{2,0,1:T(8,128)(2,1)} %bitcast.11, bf16[]{:T(256)} %broadcast.32), dimensions={1}, to_apply=%copy.26.reduce_sub_computation | reduce | bytes 327682 | tf_op jit(solution)/shard_map/all_to_all | solution.py:488
  96.1 0.7 reshape.83
  96.9 9.0 %all-to-all-start.1 = ((bf16[64,2,640]{2,1,0:T(2,128)(2,1)}), bf16[64,2,640]{2,1,0:T(2,128)(2,1)S(1)}, u32[]{:S(2)}, u32[]{:S(2)}) async-start(bf16[64,2,640]{2,1,0:T(2,128)(2,1)} %reshape.83), calls=%async_computation.1 | async-start | bytes 327680 | tf_op jit(solution)/shard_map/all_to_all | solution.py:488
  106.3 1.0 collective-permute-start.21
  107.2 2.8 %collective-permute-start.22 = (bf16[2,48,256]{2,1,0:T(8,128)(2,1)S(1)}, bf16[2,48,256]{2,1,0:T(8,128)(2,1)S(1)}, u32[]{:S(2)}, u32[]{:S(2)}) collective-permute-start(bf16[2,48,256]{2,1,0:T(8,128)(2,1)S(1)} %copy-done.36), channel_id=1, source_target_pairs={{0,2},{1,3},{2,0},{3,1},{4,6},{5,7},{6,4},{7,5},{8,10},{9,11},{10,... | collective-permute-start | bytes 147464 | tf_op jit(solution)/shard_map/ppermute | solution.py:377
  110.0 0.9 collective-permute-start.23
  111.0 4.3 %collective-permute-start.17 = (bf16[4,48,128]{2,1,0:T(8,128)(2,1)S(1)}, bf16[4,48,128]{2,1,0:T(8,128)(2,1)S(1)}, u32[]{:S(2)}, u32[]{:S(2)}) collective-permute-start(bf16[4,48,128]{2,1,0:T(8,128)(2,1)S(1)} %copy-done.41), channel_id=1, source_target_pairs={{0,8},{4,12},{8,16},{12,20},{16,24},{20,28},{24,32},{28,36},{32,40... | collective-permute-start | bytes 147464 | tf_op jit(solution)/shard_map/ppermute | solution.py:391
  115.3 4.3 %collective-permute-start.18 = (bf16[4,48,128]{2,1,0:T(8,128)(2,1)S(1)}, bf16[4,48,128]{2,1,0:T(8,128)(2,1)S(1)}, u32[]{:S(2)}, u32[]{:S(2)}) collective-permute-start(bf16[4,48,128]{2,1,0:T(8,128)(2,1)S(1)} %copy-done.41), channel_id=1, source_target_pairs={{0,12},{4,8},{8,20},{12,16},{16,28},{20,24},{24,36},{28,32},{32,44... | collective-permute-start | bytes 147464 | tf_op jit(solution)/shard_map/ppermute | solution.py:391
  119.6 2.2 %collective-permute-start.19 = (bf16[4,48,128]{2,1,0:T(8,128)(2,1)S(1)}, bf16[4,48,128]{2,1,0:T(8,128)(2,1)S(1)}, u32[]{:S(2)}, u32[]{:S(2)}) collective-permute-start(bf16[4,48,128]{2,1,0:T(8,128)(2,1)S(1)} %copy-done.40), channel_id=1, source_target_pairs={{8,0},{12,4},{16,8},{20,12},{24,16},{28,20},{32,24},{36,28},{40,32... | collective-permute-start | bytes 147464 | tf_op jit(solution)/shard_map/ppermute | solution.py:391
  121.8 1.9 %collective-permute-start.20 = (bf16[4,48,128]{2,1,0:T(8,128)(2,1)S(1)}, bf16[4,48,128]{2,1,0:T(8,128)(2,1)S(1)}, u32[]{:S(2)}, u32[]{:S(2)}) collective-permute-start(bf16[4,48,128]{2,1,0:T(8,128)(2,1)S(1)} %copy-done.40), channel_id=1, source_target_pairs={{8,4},{12,0},{16,12},{20,8},{24,20},{28,16},{32,28},{36,24},{40,36... | collective-permute-start | bytes 147464 | tf_op jit(solution)/shard_map/ppermute | solution.py:391
  123.8 4.2 %collective-permute-done.19.ds_ = bf16[4,48,128]{2,1,0:T(8,128)(2,1)S(1)} collective-permute-done((bf16[4,48,128]{2,1,0:T(8,128)(2,1)S(1)}, bf16[4,48,128]{2,1,0:T(8,128)(2,1)S(1)}, u32[]{:S(2)}, u32[]{:S(2)}) %collective-permute-start.19) | collective-permute-done | bytes 49184 | tf_op jit(solution)/shard_map/ppermute | solution.py:391
  128.0 2.6 %collective-permute-done.20.dc = bf16[4,48,128]{2,1,0:T(8,128)(2,1)S(1)} collective-permute-done((bf16[4,48,128]{2,1,0:T(8,128)(2,1)S(1)}, bf16[4,48,128]{2,1,0:T(8,128)(2,1)S(1)}, u32[]{:S(2)}, u32[]{:S(2)}) %collective-permute-start.20) | collective-permute-done | bytes 49184 | tf_op jit(solution)/shard_map/ppermute | solution.py:391
  131.3 6.7 %unmix.1 = (bf16[8,48,256]{2,1,0:T(8,128)(2,1)}, bf16[8,48,256]{2,1,0:T(8,128)(2,1)}) custom-call(s32[8,8]{1,0:T(8,128)} %adj.3, bf16[8,48,256]{2,1,0:T(8,128)(2,1)} %get-tuple-element.81.grad_ref, bf16[8,48,256]{2,1,0:T(8,128)(2,1)} %copy-done.6, bf16[4,48,128]{2,1,0:T(8,128)(2,1)} %copy-done.24, bf16[4,48,128]{2,1,0:T(8,128)(2,1)} %copy-done.27, ...), custom_call_target="tpu_custom_call" | custom-call | tf_op jit(solution)/shard_map/unmix/pallas_call | solution.py:498
  138.1 0.7 copy.31
  138.8 1.7 %finish.1 = (f32[48,49]{1,0:T(8,128)}, f32[192,192]{1,0:T(8,128)}, f32[192,192]{1,0:T(8,128)}) custom-call(bf16[64,1280]{1,0:T(8,128)(2,1)} %bitcast.12), custom_call_target="tpu_custom_call" | custom-call | tf_op jit(solution)/shard_map/finish/pallas_call | solution.py:502
  (122 shorter events, 3.4 us)
Async XLA Ops:
  0.6 20.7 %collective-permute-start.1 = (bf16[16,48,256]{2,1,0:T(8,128)(2,1)}, bf16[16,48,256]{2,1,0:T(8,128)(2,1)S(1)}, u32[]{:S(2)}, u32[]{:S(2)}) collective-permute-start(bf16[16,48,256]{2,1,0:T(8,128)(2,1)} %x_ref.3), channel_id=1, source_target_pairs={{0,4},{4,0},{8,12},{12,8},{16,20},{20,16},{24,28},{28,24},{32,36},... | collective-permute-start | bytes 1179656 | tf_op jit(solution)/shard_map/ppermute | solution.py:391
  1.4 7.2 %copy-start.12 = (bf16[192,192]{1,0:T(8,128)(2,1)S(1)}, bf16[192,192]{1,0:T(8,128)(2,1)}, u32[]{:S(2)}) copy-start(bf16[192,192]{1,0:T(8,128)(2,1)} %param.26) | copy-start | bytes 221188
  1.4 7.3 %copy-start.13 = (bf16[192,192]{1,0:T(8,128)(2,1)S(1)}, bf16[192,192]{1,0:T(8,128)(2,1)}, u32[]{:S(2)}) copy-start(bf16[192,192]{1,0:T(8,128)(2,1)} %param.24) | copy-start | bytes 221188
  3.4 10.5 %collective-permute-start.2 = (bf16[8,48,128]{2,1,0:T(8,128)(2,1)}, bf16[8,48,128]{2,1,0:T(8,128)(2,1)S(1)}, u32[]{:S(2)}, u32[]{:S(2)}) collective-permute-start(bf16[8,48,128]{2,1,0:T(8,128)(2,1)} %get-tuple-element.64), channel_id=1, source_target_pairs={{4,8},{8,4},{12,16},{16,12},{20,24},{24,20},{28,32},{32,28},{36,40... | collective-permute-start | bytes 294920 | tf_op jit(solution)/shard_map/ppermute | solution.py:391
  8.7 11.8 %copy-start.42 = (bf16[2,48,256]{2,1,0:T(8,128)(2,1)S(1)}, bf16[2,48,256]{2,1,0:T(8,128)(2,1)}, u32[]{:S(2)}) copy-start(bf16[2,48,256]{2,1,0:T(8,128)(2,1)} %get-tuple-element.70) | copy-start | bytes 147460
  8.7 11.8 %copy-start.30 = (f32[48,49]{1,0:T(8,128)S(1)}, f32[48,49]{1,0:T(8,128)}, u32[]{:S(2)}) copy-start(f32[48,49]{1,0:T(8,128)} %param.22) | copy-start | bytes 28228
  8.7 12.6 %copy-start = (bf16[400,192]{1,0:T(8,128)(2,1)}, bf16[400,192]{1,0:T(8,128)(2,1)S(1)}, u32[]{:S(2)}) copy-start(bf16[400,192]{1,0:T(8,128)(2,1)S(1)} %pad_maximum_fusion.w0) | copy-start | bytes 460804
  8.8 22.4 %collective-permute-start.10 = (bf16[400,192]{1,0:T(8,128)(2,1)S(1)}, bf16[400,192]{1,0:T(8,128)(2,1)S(1)}, u32[]{:S(2)}, u32[]{:S(2)}) collective-permute-start(bf16[400,192]{1,0:T(8,128)(2,1)S(1)} %pad_maximum_fusion.w0), channel_id=1, source_target_pairs={{0,1},{1,2},{2,3},{3,0},{4,5},{5,6},{6,7},{7,4},{8,9},{9,10},{10,1... | collective-permute-start | bytes 460808 | tf_op jit(solution)/shard_map/ppermute | solution.py:377
  10.0 22.6 %collective-permute-start.11 = (bf16[400,192]{1,0:T(8,128)(2,1)S(1)}, bf16[400,192]{1,0:T(8,128)(2,1)S(1)}, u32[]{:S(2)}, u32[]{:S(2)}) collective-permute-start(bf16[400,192]{1,0:T(8,128)(2,1)S(1)} %pad_maximum_fusion.w0), channel_id=1, source_target_pairs={{0,2},{1,3},{2,0},{3,1},{4,6},{5,7},{6,4},{7,5},{8,10},{9,11},{10,... | collective-permute-start | bytes 460808 | tf_op jit(solution)/shard_map/ppermute | solution.py:377
  10.9 1.1 collective-permute-start
  12.0 8.4 %copy-start.32 = (s32[16]{0:T(128)}, s32[16]{0:T(128)S(1)}, u32[]{:S(2)}) copy-start(s32[16]{0:T(128)S(1)} %collective-permute-done.par_slots) | copy-start | bytes 196
  12.0 22.5 %collective-permute-start.12 = (bf16[400,192]{1,0:T(8,128)(2,1)S(1)}, bf16[400,192]{1,0:T(8,128)(2,1)S(1)}, u32[]{:S(2)}, u32[]{:S(2)}) collective-permute-start(bf16[400,192]{1,0:T(8,128)(2,1)S(1)} %pad_maximum_fusion.w0), channel_id=1, source_target_pairs={{0,3},{1,0},{2,1},{3,2},{4,7},{5,4},{6,5},{7,6},{8,11},{9,8},{10,9... | collective-permute-start | bytes 460808 | tf_op jit(solution)/shard_map/ppermute | solution.py:377
  13.9 10.5 %copy-start.10 = (bf16[8,48,128]{2,1,0:T(8,128)(2,1)}, bf16[8,48,128]{2,1,0:T(8,128)(2,1)S(1)}, u32[]{:S(2)}) copy-start(bf16[8,48,128]{2,1,0:T(8,128)(2,1)S(1)} %collective-permute-done.2.sa_ref) | copy-start | bytes 294916
  13.9 6.5 %collective-permute-start.3 = (bf16[8,48,128]{2,1,0:T(8,128)(2,1)S(1)}, bf16[8,48,128]{2,1,0:T(8,128)(2,1)S(1)}, u32[]{:S(2)}, u32[]{:S(2)}) collective-permute-start(bf16[8,48,128]{2,1,0:T(8,128)(2,1)S(1)} %copy-done.34), channel_id=1, source_target_pairs={{4,12},{8,0},{12,20},{16,8},{20,28},{24,16},{28,36},{32,24},{36,44... | collective-permute-start | bytes 294920 | tf_op jit(solution)/shard_map/ppermute | solution.py:391
  20.4 10.6 %collective-permute-start.7 = (bf16[2,48,256]{2,1,0:T(8,128)(2,1)S(1)}, bf16[2,48,256]{2,1,0:T(8,128)(2,1)S(1)}, u32[]{:S(2)}, u32[]{:S(2)}) collective-permute-start(bf16[2,48,256]{2,1,0:T(8,128)(2,1)S(1)} %copy-done.42), channel_id=1, source_target_pairs={{0,1},{1,2},{2,3},{3,0},{4,5},{5,6},{6,7},{7,4},{8,9},{9,10},{10,1... | collective-permute-start | bytes 147464 | tf_op jit(solution)/shard_map/ppermute | solution.py:377
  21.4 9.7 %copy-start.38 = (bf16[2,48,256]{2,1,0:T(8,128)(2,1)S(1)}, bf16[2,48,256]{2,1,0:T(8,128)(2,1)}, u32[]{:S(2)}) copy-start(bf16[2,48,256]{2,1,0:T(8,128)(2,1)} %get-tuple-element.72) | copy-start | bytes 147460
  21.4 16.5 %collective-permute-start.8 = (bf16[2,48,256]{2,1,0:T(8,128)(2,1)S(1)}, bf16[2,48,256]{2,1,0:T(8,128)(2,1)S(1)}, u32[]{:S(2)}, u32[]{:S(2)}) collective-permute-start(bf16[2,48,256]{2,1,0:T(8,128)(2,1)S(1)} %copy-done.39), channel_id=1, source_target_pairs={{0,2},{1,3},{2,0},{3,1},{4,6},{5,7},{6,4},{7,5},{8,10},{9,11},{10,... | collective-permute-start | bytes 147464 | tf_op jit(solution)/shard_map/ppermute | solution.py:377
  31.0 6.8 %copy-start.17 = (bf16[2,48,256]{2,1,0:T(8,128)(2,1)}, bf16[2,48,256]{2,1,0:T(8,128)(2,1)S(1)}, u32[]{:S(2)}) copy-start(bf16[2,48,256]{2,1,0:T(8,128)(2,1)S(1)} %collective-permute-done.7.b1) | copy-start | bytes 147460
  31.1 6.8 %collective-permute-start.9 = (bf16[2,48,256]{2,1,0:T(8,128)(2,1)S(1)}, bf16[2,48,256]{2,1,0:T(8,128)(2,1)S(1)}, u32[]{:S(2)}, u32[]{:S(2)}) collective-permute-start(bf16[2,48,256]{2,1,0:T(8,128)(2,1)S(1)} %copy-done.38), channel_id=1, source_target_pairs={{0,3},{1,0},{2,1},{3,2},{4,7},{5,4},{6,5},{7,6},{8,11},{9,8},{10,9... | collective-permute-start | bytes 147464 | tf_op jit(solution)/shard_map/ppermute | solution.py:377
  31.2 6.7 %collective-permute-start.4 = (bf16[2,48,256]{2,1,0:T(8,128)(2,1)}, bf16[2,48,256]{2,1,0:T(8,128)(2,1)S(1)}, u32[]{:S(2)}, u32[]{:S(2)}) collective-permute-start(bf16[2,48,256]{2,1,0:T(8,128)(2,1)} %get-tuple-element.66), channel_id=1, source_target_pairs={{0,1},{1,2},{2,3},{3,0},{4,5},{5,6},{6,7},{7,4},{8,9},{9,10},{10,1... | collective-permute-start | bytes 147464 | tf_op jit(solution)/shard_map/ppermute | solution.py:377
  32.6 5.3 %collective-permute-start.5 = (bf16[2,48,256]{2,1,0:T(8,128)(2,1)}, bf16[2,48,256]{2,1,0:T(8,128)(2,1)S(1)}, u32[]{:S(2)}, u32[]{:S(2)}) collective-permute-start(bf16[2,48,256]{2,1,0:T(8,128)(2,1)} %get-tuple-element.67), channel_id=1, source_target_pairs={{0,2},{1,3},{2,0},{3,1},{4,6},{5,7},{6,4},{7,5},{8,10},{9,11},{10,... | collective-permute-start | bytes 147464 | tf_op jit(solution)/shard_map/ppermute | solution.py:377
  34.5 3.5 %collective-permute-start.6 = (bf16[2,48,256]{2,1,0:T(8,128)(2,1)}, bf16[2,48,256]{2,1,0:T(8,128)(2,1)S(1)}, u32[]{:S(2)}, u32[]{:S(2)}) collective-permute-start(bf16[2,48,256]{2,1,0:T(8,128)(2,1)} %get-tuple-element.68), channel_id=1, source_target_pairs={{0,3},{1,0},{2,1},{3,2},{4,7},{5,4},{6,5},{7,6},{8,11},{9,8},{10,9... | collective-permute-start | bytes 147464 | tf_op jit(solution)/shard_map/ppermute | solution.py:377
  43.7 16.7 %collective-permute-start.24 = (bf16[384,192]{1,0:T(8,128)(2,1)}, bf16[384,192]{1,0:T(8,128)(2,1)S(1)}, u32[]{:S(2)}, u32[]{:S(2)}) collective-permute-start(bf16[384,192]{1,0:T(8,128)(2,1)} %get-tuple-element.93), channel_id=1, source_target_pairs={{0,3},{1,0},{2,1},{3,2},{4,7},{5,4},{6,5},{7,6},{8,11},{9,8},{10,9... | collective-permute-start | bytes 442376 | tf_op jit(solution)/shard_map/ppermute | solution.py:467
  45.1 15.3 %collective-permute-start.25 = (bf16[384,192]{1,0:T(8,128)(2,1)}, bf16[384,192]{1,0:T(8,128)(2,1)S(1)}, u32[]{:S(2)}, u32[]{:S(2)}) collective-permute-start(bf16[384,192]{1,0:T(8,128)(2,1)} %get-tuple-element.94), channel_id=1, source_target_pairs={{0,2},{1,3},{2,0},{3,1},{4,6},{5,7},{6,4},{7,5},{8,10},{9,11},{10,... | collective-permute-start | bytes 442376 | tf_op jit(solution)/shard_map/ppermute | solution.py:467
  46.2 14.2 %collective-permute-start.26 = (bf16[384,192]{1,0:T(8,128)(2,1)}, bf16[384,192]{1,0:T(8,128)(2,1)S(1)}, u32[]{:S(2)}, u32[]{:S(2)}) collective-permute-start(bf16[384,192]{1,0:T(8,128)(2,1)} %get-tuple-element.95), channel_id=1, source_target_pairs={{0,1},{1,2},{2,3},{3,0},{4,5},{5,6},{6,7},{7,4},{8,9},{9,10},{10,1... | collective-permute-start | bytes 442376 | tf_op jit(solution)/shard_map/ppermute | solution.py:467
  48.2 5.0 %collective-permute-start.13 = (bf16[2,48,256]{2,1,0:T(8,128)(2,1)}, bf16[2,48,256]{2,1,0:T(8,128)(2,1)S(1)}, u32[]{:S(2)}, u32[]{:S(2)}) collective-permute-start(bf16[2,48,256]{2,1,0:T(8,128)(2,1)} %get-tuple-element.78), channel_id=1, source_target_pairs={{0,1},{1,2},{2,3},{3,0},{4,5},{5,6},{6,7},{7,4},{8,9},{9,10},{10,1... | collective-permute-start | bytes 147464 | tf_op jit(solution)/shard_map/ppermute | solution.py:377
  48.3 7.3 %collective-permute-start.14 = (bf16[2,48,256]{2,1,0:T(8,128)(2,1)}, bf16[2,48,256]{2,1,0:T(8,128)(2,1)S(1)}, u32[]{:S(2)}, u32[]{:S(2)}) collective-permute-start(bf16[2,48,256]{2,1,0:T(8,128)(2,1)} %get-tuple-element.79), channel_id=1, source_target_pairs={{0,2},{1,3},{2,0},{3,1},{4,6},{5,7},{6,4},{7,5},{8,10},{9,11},{10,... | collective-permute-start | bytes 147464 | tf_op jit(solution)/shard_map/ppermute | solution.py:377
  53.2 4.9 %collective-permute-start.15 = (bf16[2,48,256]{2,1,0:T(8,128)(2,1)}, bf16[2,48,256]{2,1,0:T(8,128)(2,1)S(1)}, u32[]{:S(2)}, u32[]{:S(2)}) collective-permute-start(bf16[2,48,256]{2,1,0:T(8,128)(2,1)} %get-tuple-element.80), channel_id=1, source_target_pairs={{0,3},{1,0},{2,1},{3,2},{4,7},{5,4},{6,5},{7,6},{8,11},{9,8},{10,9... | collective-permute-start | bytes 147464 | tf_op jit(solution)/shard_map/ppermute | solution.py:377
  96.1 10.2 %copy-start.37 = (bf16[2,48,256]{2,1,0:T(8,128)(2,1)S(1)}, bf16[2,48,256]{2,1,0:T(8,128)(2,1)}, u32[]{:S(2)}) copy-start(bf16[2,48,256]{2,1,0:T(8,128)(2,1)} %get-tuple-element.86) | copy-start | bytes 147460
  96.1 14.9 %copy-start.41 = (bf16[4,48,128]{2,1,0:T(8,128)(2,1)S(1)}, bf16[4,48,128]{2,1,0:T(8,128)(2,1)}, u32[]{:S(2)}) copy-start(bf16[4,48,128]{2,1,0:T(8,128)(2,1)} %get-tuple-element.82) | copy-start | bytes 147460
  96.1 23.5 %copy-start.40 = (bf16[4,48,128]{2,1,0:T(8,128)(2,1)S(1)}, bf16[4,48,128]{2,1,0:T(8,128)(2,1)}, u32[]{:S(2)}) copy-start(bf16[4,48,128]{2,1,0:T(8,128)(2,1)} %get-tuple-element.83) | copy-start | bytes 147460
  96.9 9.0 %copy-start.4 = (bf16[8,48,256]{2,1,0:T(8,128)(2,1)S(1)}, bf16[8,48,256]{2,1,0:T(8,128)(2,1)}, u32[]{:S(2)}) copy-start(bf16[8,48,256]{2,1,0:T(8,128)(2,1)} %get-tuple-element.81.grad_ref) | copy-start | bytes 589828
  96.9 10.4 %copy-start.36 = (bf16[2,48,256]{2,1,0:T(8,128)(2,1)S(1)}, bf16[2,48,256]{2,1,0:T(8,128)(2,1)}, u32[]{:S(2)}) copy-start(bf16[2,48,256]{2,1,0:T(8,128)(2,1)} %get-tuple-element.87) | copy-start | bytes 147460
  96.9 13.2 %copy-start.35 = (bf16[2,48,256]{2,1,0:T(8,128)(2,1)S(1)}, bf16[2,48,256]{2,1,0:T(8,128)(2,1)}, u32[]{:S(2)}) copy-start(bf16[2,48,256]{2,1,0:T(8,128)(2,1)} %get-tuple-element.88) | copy-start | bytes 147460
  96.9 41.1 %all-to-all-start.1 = ((bf16[64,2,640]{2,1,0:T(2,128)(2,1)}), bf16[64,2,640]{2,1,0:T(2,128)(2,1)S(1)}, u32[]{:S(2)}, u32[]{:S(2)}) async-start(bf16[64,2,640]{2,1,0:T(2,128)(2,1)} %reshape.83), calls=%async_computation.1 | async-start | bytes 327680 | tf_op jit(solution)/shard_map/all_to_all | solution.py:488
  105.8 24.7 %collective-permute-start.16 = (bf16[8,48,256]{2,1,0:T(8,128)(2,1)S(1)}, bf16[8,48,256]{2,1,0:T(8,128)(2,1)S(1)}, u32[]{:S(2)}, u32[]{:S(2)}) collective-permute-start(bf16[8,48,256]{2,1,0:T(8,128)(2,1)S(1)} %copy-done.4), channel_id=1, source_target_pairs={{0,4},{4,0},{8,12},{12,8},{16,20},{20,16},{24,28},{28,24},{32,36},... | collective-permute-start | bytes 589832 | tf_op jit(solution)/shard_map/ppermute | solution.py:391
  106.3 9.0 %collective-permute-start.21 = (bf16[2,48,256]{2,1,0:T(8,128)(2,1)S(1)}, bf16[2,48,256]{2,1,0:T(8,128)(2,1)S(1)}, u32[]{:S(2)}, u32[]{:S(2)}) collective-permute-start(bf16[2,48,256]{2,1,0:T(8,128)(2,1)S(1)} %copy-done.37), channel_id=1, source_target_pairs={{0,1},{1,2},{2,3},{3,0},{4,5},{5,6},{6,7},{7,4},{8,9},{9,10},{10,1... | collective-permute-start | bytes 147464 | tf_op jit(solution)/shard_map/ppermute | solution.py:377
  107.2 12.3 %collective-permute-start.22 = (bf16[2,48,256]{2,1,0:T(8,128)(2,1)S(1)}, bf16[2,48,256]{2,1,0:T(8,128)(2,1)S(1)}, u32[]{:S(2)}, u32[]{:S(2)}) collective-permute-start(bf16[2,48,256]{2,1,0:T(8,128)(2,1)S(1)} %copy-done.36), channel_id=1, source_target_pairs={{0,2},{1,3},{2,0},{3,1},{4,6},{5,7},{6,4},{7,5},{8,10},{9,11},{10,... | collective-permute-start | bytes 147464 | tf_op jit(solution)/shard_map/ppermute | solution.py:377
  110.0 11.8 %collective-permute-start.23 = (bf16[2,48,256]{2,1,0:T(8,128)(2,1)S(1)}, bf16[2,48,256]{2,1,0:T(8,128)(2,1)S(1)}, u32[]{:S(2)}, u32[]{:S(2)}) collective-permute-start(bf16[2,48,256]{2,1,0:T(8,128)(2,1)S(1)} %copy-done.35), channel_id=1, source_target_pairs={{0,3},{1,0},{2,1},{3,2},{4,7},{5,4},{6,5},{7,6},{8,11},{9,8},{10,9... | collective-permute-start | bytes 147464 | tf_op jit(solution)/shard_map/ppermute | solution.py:377
  111.0 12.8 %collective-permute-start.17 = (bf16[4,48,128]{2,1,0:T(8,128)(2,1)S(1)}, bf16[4,48,128]{2,1,0:T(8,128)(2,1)S(1)}, u32[]{:S(2)}, u32[]{:S(2)}) collective-permute-start(bf16[4,48,128]{2,1,0:T(8,128)(2,1)S(1)} %copy-done.41), channel_id=1, source_target_pairs={{0,8},{4,12},{8,16},{12,20},{16,24},{20,28},{24,32},{28,36},{32,40... | collective-permute-start | bytes 147464 | tf_op jit(solution)/shard_map/ppermute | solution.py:391
  115.3 15.3 %copy-start.20 = (bf16[2,48,256]{2,1,0:T(8,128)(2,1)}, bf16[2,48,256]{2,1,0:T(8,128)(2,1)S(1)}, u32[]{:S(2)}) copy-start(bf16[2,48,256]{2,1,0:T(8,128)(2,1)S(1)} %collective-permute-done.21.r1) | copy-start | bytes 147460
  115.3 8.5 %collective-permute-start.18 = (bf16[4,48,128]{2,1,0:T(8,128)(2,1)S(1)}, bf16[4,48,128]{2,1,0:T(8,128)(2,1)S(1)}, u32[]{:S(2)}, u32[]{:S(2)}) collective-permute-start(bf16[4,48,128]{2,1,0:T(8,128)(2,1)S(1)} %copy-done.41), channel_id=1, source_target_pairs={{0,12},{4,8},{8,20},{12,16},{16,28},{20,24},{24,36},{28,32},{32,44... | collective-permute-start | bytes 147464 | tf_op jit(solution)/shard_map/ppermute | solution.py:391
  119.6 11.0 %copy-start.21 = (bf16[2,48,256]{2,1,0:T(8,128)(2,1)}, bf16[2,48,256]{2,1,0:T(8,128)(2,1)S(1)}, u32[]{:S(2)}) copy-start(bf16[2,48,256]{2,1,0:T(8,128)(2,1)S(1)} %collective-permute-done.22.r2) | copy-start | bytes 147460
  119.6 8.4 %collective-permute-start.19 = (bf16[4,48,128]{2,1,0:T(8,128)(2,1)S(1)}, bf16[4,48,128]{2,1,0:T(8,128)(2,1)S(1)}, u32[]{:S(2)}, u32[]{:S(2)}) collective-permute-start(bf16[4,48,128]{2,1,0:T(8,128)(2,1)S(1)} %copy-done.40), channel_id=1, source_target_pairs={{8,0},{12,4},{16,8},{20,12},{24,16},{28,20},{32,24},{36,28},{40,32... | collective-permute-start | bytes 147464 | tf_op jit(solution)/shard_map/ppermute | solution.py:391
  121.8 8.8 %copy-start.23 = (bf16[2,48,256]{2,1,0:T(8,128)(2,1)}, bf16[2,48,256]{2,1,0:T(8,128)(2,1)S(1)}, u32[]{:S(2)}) copy-start(bf16[2,48,256]{2,1,0:T(8,128)(2,1)S(1)} %collective-permute-done.23.r3) | copy-start | bytes 147460
  121.8 8.7 %collective-permute-start.20 = (bf16[4,48,128]{2,1,0:T(8,128)(2,1)S(1)}, bf16[4,48,128]{2,1,0:T(8,128)(2,1)S(1)}, u32[]{:S(2)}, u32[]{:S(2)}) collective-permute-start(bf16[4,48,128]{2,1,0:T(8,128)(2,1)S(1)} %copy-done.40), channel_id=1, source_target_pairs={{8,4},{12,0},{16,12},{20,8},{24,20},{28,16},{32,28},{36,24},{40,36... | collective-permute-start | bytes 147464 | tf_op jit(solution)/shard_map/ppermute | solution.py:391
  123.8 6.8 %copy-start.24 = (bf16[4,48,128]{2,1,0:T(8,128)(2,1)}, bf16[4,48,128]{2,1,0:T(8,128)(2,1)S(1)}, u32[]{:S(2)}) copy-start(bf16[4,48,128]{2,1,0:T(8,128)(2,1)S(1)} %collective-permute-done.17.us) | copy-start | bytes 147460
  123.8 6.8 %copy-start.27 = (bf16[4,48,128]{2,1,0:T(8,128)(2,1)}, bf16[4,48,128]{2,1,0:T(8,128)(2,1)S(1)}, u32[]{:S(2)}) copy-start(bf16[4,48,128]{2,1,0:T(8,128)(2,1)S(1)} %collective-permute-done.18.uc) | copy-start | bytes 147460
  (24 other events, 43.6 us)

commit v2 on v1

--- a/solution.py
+++ b/solution.py
@@ -72,9 +72,8 @@
     return jnp.where(keep, natural.astype(F32), swap_halves(other)).astype(BF16)
 
 
-def prepare_kernel(x_ref, cot_ref, scale_ref, strips_ref, d0, d1, d2, d3):
+def strips_kernel(x_ref, strips_ref):
     odd = lax.axis_index("tiles") & 1
-    mine = lax.axis_index("chan")
 
     @pl.when(odd == 1)
     def _():
@@ -86,11 +85,27 @@
         for s in range(8):
             strips_ref[s] = pack_pair(x_ref[s, :, 0:128], x_ref[s + 8, :, 0:128], True)
 
+
+def sends_kernel(cot_ref, scale_ref, in_ref, w_out_ref, b_ref, gain_ref, *rest):
+    outs, small = rest[0:4], rest[4]
+    mine = lax.axis_index("chan")
     scale = column(scale_ref[...])
-    for j, out in enumerate((d0, d1, d2, d3)):
+    small[...] = jnp.zeros((16, 256), F32)
+    small[0:1, 0:192] = b_ref[...].astype(F32)
+    small[1:2, 0:48] = gain_ref[...].astype(F32)
+    tails = []
+    for ref in (in_ref, w_out_ref):
+        tail = ref[:, 128:192].astype(F32)
+        tails.append(jnp.concatenate([tail[0:96], tail[96:192]], axis=1).astype(BF16))
+    for j, out in enumerate(outs):
         first = 2 * ((mine + j) & 3)
         for i in range(2):
-            out[i] = (cot_ref[first + i].astype(F32) * scale).astype(BF16)
+            out[48 * i : 48 * i + 48] = (cot_ref[first + i].astype(F32) * scale).astype(BF16)
+        out[96:288, 0:128] = in_ref[:, 0:128]
+        out[96:288, 128:256] = w_out_ref[:, 0:128]
+        out[288:384, 0:128] = tails[0]
+        out[288:384, 128:256] = tails[1]
+        out[384:400] = small[...].astype(BF16)
 
 
 def gather_tile(table, up_g, mid_g, down_g, t, center, entries):
@@ -189,15 +204,27 @@
         out[1] = flat[first + 1]
 
 
-def weights_kernel(w0, w1, w2, w3, in_t, out_t, bias, gain):
+def turn_kernel(p0, p1, p2, p3, w_in, w_out, in_t, out_t, bias, gain, dbranch):
     mine = lax.axis_index("chan")
     unit = eye(192)
-    for j, ref in enumerate((w0, w1, w2, w3)):
-        in_t[j] = dot(unit, ref[0:192], NT).astype(BF16)
-        out_t[j] = dot(unit, ref[192:384], NT).astype(BF16)
-        cols = dot(unit, ref[384:400], NT)
+    for j, ref in enumerate((p0, p1, p2, p3)):
+        a = (mine + 4 - j) & 3
+        for i in range(2):
+            dbranch[a, :, 256 * i : 256 * i + 256] = ref[48 * i : 48 * i + 48]
+        for full, turned, lanes in ((w_in, in_t, 0), (w_out, out_t, 128)):
+            tail = ref[288:384, lanes : lanes + 128].astype(F32)
+            whole = jnp.concatenate(
+                [
+                    ref[96:288, lanes : lanes + 128].astype(F32),
+                    jnp.concatenate([tail[:, 0:64], tail[:, 64:128]], axis=0),
+                ],
+                axis=1,
+            ).astype(BF16)
+            full[j] = whole
+            turned[j] = dot(unit, whole, NT).astype(BF16)
+        cols = dot(unit, ref[384:400, 0:192], NT)
         bias[j] = jnp.broadcast_to(cols[:, 0:1], (192, 128))
-        gain[(mine + 4 - j) & 3] = jnp.broadcast_to(cols[0:48, 1:2], (48, 128))
+        gain[a] = jnp.broadcast_to(cols[0:48, 1:2], (48, 128))
 
 
 def across(col_block):
@@ -205,18 +232,17 @@
 
 
 def mlp_kernel(
-    m0, m1, m2, m3, b0, b1, b2, b3, w0, w1, w2, w3, in_t, out_t, bias, gain,
-    g0, g1, g2, g3, r0, r1, r2, r3, v0, v1, v2, v3,
-    mixed_s, dbranch_s, back_s, branch_s,
+    m0, m1, m2, m3, w_in, w_out, in_t, out_t, bias, gain, db_ref,
+    g0, g1, g2, g3, r0, r1, r2, r3, act_ref, pre_ref, normed_ref,
+    mixed_s, back_s, branch_s,
 ):
     mine = lax.axis_index("chan")
-    for j, (m_ref, b_ref) in enumerate(((m0, b0), (m1, b1), (m2, b2), (m3, b3))):
+    for j, m_ref in enumerate((m0, m1, m2, m3)):
         a = (mine + 4 - j) & 3
         for i in range(2):
             mixed_s[a, :, 256 * i : 256 * i + 256] = m_ref[i]
-            dbranch_s[a, :, 256 * i : 256 * i + 256] = b_ref[i]
     mixed = mixed_s[...].reshape(192, 512).astype(F32)
-    dbranch = dbranch_s[...].reshape(192, 512)
+    dbranch = db_ref[...].reshape(192, 512)
     mean = jnp.sum(mixed, axis=0, keepdims=True) / CHANNELS
     inv = lax.rsqrt(
         jnp.sum(mixed * mixed, axis=0, keepdims=True) / CHANNELS - mean * mean + EPSILON
@@ -224,9 +250,10 @@
     x_hat = (mixed - mean) * inv
     gain_full = across(gain[...].reshape(192, 128))
     normed = (x_hat * gain_full).astype(BF16)
+    normed_ref[...] = normed
     branch = jnp.zeros((192, 512), F32)
     dnormed = jnp.zeros((192, 512), F32)
-    for j, (w_ref, v_ref) in enumerate(((w0, v0), (w1, v1), (w2, v2), (w3, v3))):
+    for j in range(4):
         preact = dot(in_t[j], normed, NN) + across(bias[j])
         square = preact * preact
         tangent = jnp.tanh(GELU_SCALE * (preact + GELU_CUBIC * square * preact))
@@ -236,10 +263,10 @@
             GELU_SCALE * (1.0 + 3.0 * GELU_CUBIC * square)
         )
         branch = branch + dot(out_t[j], act, NN)
-        pre_grad = (dot(w_ref[192:384], dbranch, NN) * slope).astype(BF16)
-        dnormed = dnormed + dot(w_ref[0:192], pre_grad, NN)
-        v_ref[0:192] = dot(normed, pre_grad, NT).astype(BF16)
-        v_ref[192:384] = dot(act, dbranch, NT).astype(BF16)
+        pre_grad = (dot(w_out[j], dbranch, NN) * slope).astype(BF16)
+        dnormed = dnormed + dot(w_in[j], pre_grad, NN)
+        act_ref[j] = act
+        pre_ref[j] = pre_grad
     xhat_grad = dnormed * gain_full
     first = jnp.sum(xhat_grad, axis=0, keepdims=True) / CHANNELS
     second = jnp.sum(xhat_grad * x_hat, axis=0, keepdims=True) / CHANNELS
@@ -253,16 +280,23 @@
             r_ref[i] = branch_s[a, :, 256 * i : 256 * i + 256]
 
 
-def collect_kernel(g0, g1, g2, g3, grad_ref, top_ref, bottom_ref):
+def outer_kernel(act_ref, pre_ref, normed_ref, db_ref, v0, v1, v2, v3):
+    normed = normed_ref[...]
+    dbranch = db_ref[...].reshape(192, 512)
+    for j, v_ref in enumerate((v0, v1, v2, v3)):
+        v_ref[0:192] = dot(normed, pre_ref[j], NT).astype(BF16)
+        v_ref[192:384] = dot(act_ref[j], dbranch, NT).astype(BF16)
+
+
+def taps_kernel(
+    g0, g1, g2, g3, pad_ref, fold, grad_ref, top_ref, bottom_ref, out_ref, pad, grad_t, sums
+):
     mine = lax.axis_index("chan")
     for j, ref in enumerate((g0, g1, g2, g3)):
         grad_ref[pl.ds(2 * ((mine + 4 - j) & 3), 2)] = ref[...]
     for t in range(4):
         top_ref[t] = pack_pair(grad_ref[t, :, 0:128], grad_ref[t + 4, :, 0:128], True)
         bottom_ref[t] = pack_pair(grad_ref[t, :, 128:256], grad_ref[t + 4, :, 128:256], False)
-
-
-def taps_kernel(grad_ref, pad_ref, fold, v0, v1, v2, v3, out_ref, pad, grad_t, sums):
     pad[...] = pad_ref[...].astype(F32)
     grad_t[...] = grad_ref[...].reshape(384, 256).astype(F32).T
     sums[...] = jnp.zeros((64, 384), F32)
@@ -283,21 +317,25 @@
         return carry
 
     lax.fori_loop(0, 3, lane_block, 0)
-    total = jnp.zeros((384, 192), F32)
-    for ref in (v0, v1, v2, v3):
-        total = total + ref[...].astype(F32)
+    out_ref[...] = lax.dot_general(
+        sums[...], fold[...], NN, precision=lax.Precision.HIGHEST, preferred_element_type=F32
+    )
+
+
+def pieces_kernel(v0, v1, v2, v3, taps_ref, out_ref, total, rows):
+    total[...] = (
+        v0[...].astype(F32) + v1[...].astype(F32) + v2[...].astype(F32) + v3[...].astype(F32)
+    )
+    rows[...] = jnp.zeros((64, 16, 128), F32)
     for q in range(6):
-        out_ref[:, 128 * q : 128 * q + 128] = total[64 * q : 64 * q + 64, 0:128].astype(BF16)
+        rows[:, q, :] = total[64 * q : 64 * q + 64, 0:128]
     for q in range(3):
-        both = jnp.concatenate(
+        rows[:, 6 + q, :] = jnp.concatenate(
             [total[128 * q : 128 * q + 64, 128:192], total[128 * q + 64 : 128 * q + 128, 128:192]],
             axis=1,
         )
-        out_ref[:, 768 + 128 * q : 896 + 128 * q] = both.astype(BF16)
-    folded = lax.dot_general(
-        sums[...], fold[...], NN, precision=lax.Precision.HIGHEST, preferred_element_type=F32
-    )
-    out_ref[:, 1152:1280] = folded.astype(BF16)
+    rows[:, 9, :] = taps_ref[...]
+    out_ref[...] = rows[...].astype(BF16)
 
 
 def total_kernel(factor, in_ref, out_ref):
@@ -305,13 +343,18 @@
     out_ref[...] = jnp.broadcast_to(total, in_ref.shape).astype(out_ref.dtype)
 
 
-def finish_kernel(in_ref, dw_ref, w1_ref, w2_ref):
+def finish_kernel(in_ref, dw_ref, w1_ref, w2_ref, rows):
+    rows[...] = in_ref[...].astype(F32)
     for q in range(6):
         out, row = (w1_ref, 64 * q) if q < 3 else (w2_ref, 64 * q - 192)
-        out[row : row + 64, 0:128] = in_ref[:, 128 * q : 128 * q + 128].astype(F32)
-        lo = 768 + 128 * (q // 2) + 64 * (q % 2)
-        out[row : row + 64, 128:192] = in_ref[:, lo : lo + 64].astype(F32)
-    dw_ref[...] = in_ref[:, 1152:1280].astype(F32).T[0:48, 0:49]
+        out[row : row + 64, 0:128] = rows[:, q, :]
+    for q in range(3):
+        both = rows[:, 6 + q, :]
+        for half in range(2):
+            row = 128 * q + 64 * half
+            out, row = (w1_ref, row) if row < 192 else (w2_ref, row - 192)
+            out[row : row + 64, 128:192] = both[:, 64 * half : 64 * half + 64]
+    dw_ref[...] = rows[:, 9, :].T[0:48, 0:49]
 
 
 def unmix_kernel(
@@ -390,19 +433,28 @@
         pairs = [(i, target(i)) for i in range(devices)]
         return lax.ppermute(value, "tiles", [p for p in pairs if 0 <= p[1] < devices])
 
+    def after(value, *first):
+        return lax.optimization_barrier((value, first))[0]
+
     tile_chunk = shape(2, 48, 256)
-    prep = call(prepare_kernel, [shape(8, 48, 128)] + [tile_chunk] * 4, n_in=3, name="prepare")
-    strips, *dbranch = prep(x_scan, cotangent, scale_row)
     par_x = hop(x_scan, lambda i: i ^ 1)
     par_slots = hop(slot_owner, lambda i: i ^ 1)
+    strips = call(strips_kernel, shape(8, 48, 128), n_in=1, name="strips")(x_scan)
     near = hop(strips, lambda i: i + 1 if i & 1 else i - 1)
     far = hop(strips, lambda i: i + 2 if i & 1 else i - 2)
-    taps = jnp.tile(dw_weight.T, (1, 8))
-
-    small = jnp.zeros((16, 192), BF16).at[0].set(b_in).at[1, 0:48].set(ln_gain)
-    packed = jnp.concatenate([w_in, w_out, small], axis=0)
-    all_dbranch = along_chan(dbranch)
-    all_weights = along_chan([packed] * 4)
+    taps = jnp.tile(after(dw_weight, strips).T, (1, 8))
+
+    sends = call(
+        sends_kernel,
+        [shape(400, 256)] * 4,
+        scratch=[pltpu.VMEM((16, 256), F32)],
+        n_in=6,
+        name="sends",
+    )(
+        cotangent, after(scale_row, strips), w_in, w_out,
+        b_in.reshape(1, 192), ln_gain.reshape(1, 48),
+    )
+    all_sends = along_chan(sends)
 
     grid_scratch = lambda entries: [
         pltpu.VMEM((entries, 48, 256), BF16),
@@ -425,65 +477,64 @@
     )
     all_mixed = along_chan(mixed)
 
+    square = shape(4, 192, 192)
     turn = call(
-        weights_kernel,
-        [
-            shape(4, 192, 192),
-            shape(4, 192, 192),
-            shape(4, 192, 128, dtype=F32),
-            shape(4, 48, 128, dtype=F32),
-        ],
+        turn_kernel,
+        [square] * 4
+        + [shape(4, 192, 128, dtype=F32), shape(4, 48, 128, dtype=F32), shape(4, 48, 512)],
         n_in=4,
         name="turn",
     )
-    turned = turn(*all_weights)
-
-    mlp = call(
+    turned = turn(*after(all_sends, mixed[0]))
+
+    hidden = shape(4, 192, 512)
+    results = call(
         mlp_kernel,
-        [tile_chunk] * 8 + [shape(384, 192)] * 4,
-        scratch=[pltpu.VMEM((4, 48, 512), BF16)] * 4,
-        n_in=16,
+        [tile_chunk] * 8 + [hidden, hidden, shape(192, 512)],
+        scratch=[pltpu.VMEM((4, 48, 512), BF16)] * 3,
+        n_in=11,
         name="mlp",
-    )
-    results = mlp(*all_mixed, *all_dbranch, *all_weights, *turned)
+    )(*all_mixed, *turned)
     all_back = along_chan(results[0:4])
-    collect = call(
-        collect_kernel,
-        [shape(8, 48, 256), shape(4, 48, 128), shape(4, 48, 128)],
-        n_in=4,
-        name="collect",
-    )
-    grads, top, bottom = collect(*all_back)
+    partials = call(outer_kernel, [shape(384, 192)] * 4, n_in=4, name="outer")(
+        *results[8:11], turned[6]
+    )
+    all_partials = [partials[0]]
+    for j in range(1, 4):
+        all_partials.append(
+            lax.ppermute(partials[j], "chan", [(i, (i - j) % 4) for i in range(4)])
+        )
+    grads, top, bottom, tap_sums = call(
+        taps_kernel,
+        [shape(8, 48, 256), shape(4, 48, 128), shape(4, 48, 128), shape(64, 128, dtype=F32)],
+        scratch=[
+            pltpu.VMEM((22, WIDE, 384), F32),
+            pltpu.VMEM((256, 384), F32),
+            pltpu.VMEM((64, 384), F32),
+        ],
+        n_in=6,
+        name="tap_sums",
+    )(*all_back, padded, fold)
+    pieces = call(
+        pieces_kernel,
+        shape(64, 16, 128),
+        scratch=[pltpu.VMEM((384, 192), F32), pltpu.VMEM((64, 16, 128), F32)],
+        n_in=5,
+        name="pieces",
+    )(*all_partials, tap_sums)
+    arrived = lax.all_to_all(pieces, "tiles", 0, 0, tiled=True)
+
+    grads, top, bottom = after((grads, top, bottom), pieces)
     par_grads = hop(grads, lambda i: i ^ 1)
     from_up = hop(bottom, lambda i: i + 2)
     from_up_cross = hop(bottom, lambda i: (i ^ 1) + 2)
     from_down = hop(top, lambda i: i - 2)
     from_down_cross = hop(top, lambda i: (i ^ 1) - 2)
-
-    partials = results[8:12]
-    all_partials = [partials[0]]
-    for j in range(1, 4):
-        all_partials.append(
-            lax.ppermute(partials[j], "chan", [(i, (i - j) % 4) for i in range(4)])
-        )
-    all_branch = along_chan(results[4:8])
-
-    tap_sums = call(
-        taps_kernel,
-        shape(64, 1280),
-        scratch=[
-            pltpu.VMEM((22, WIDE, 384), F32),
-            pltpu.VMEM((256, 384), F32),
-            pltpu.VMEM((64, 384), F32),
-        ],
-        n_in=7,
-        name="tap_sums",
-    )
-    pieces = tap_sums(grads, padded, fold, *all_partials)
-    arrived = lax.all_to_all(pieces, "tiles", 0, 0, tiled=True)
+    all_branch = along_chan(after(results[4:8], pieces))
+
     factor = 1.0 / math.sqrt(adjacency.shape[0] * devices * PIX)
     totals = call(
-        functools.partial(total_kernel, factor), shape(64, 1280), n_in=1, name="totals"
+        functools.partial(total_kernel, factor), shape(64, 16, 128), n_in=1, name="totals"
     )(arrived)
     spread = lax.all_to_all(totals, "tiles", 0, 0, tiled=True)
 
@@ -497,11 +548,12 @@
     )
     output, grad_in = unmix(
         adjacency, grads, par_grads, from_up, from_up_cross, from_down, from_down_cross,
-        cotangent, taps, up_p, mid_p, down_p, owned, scale_row, *all_branch
+        cotangent, taps, up_p, mid_p, down_p, owned, after(scale_row, totals), *all_branch
     )
     grad_dw, grad_w1, grad_w2 = call(
         finish_kernel,
         [shape(48, 49, dtype=F32), shape(192, 192, dtype=F32), shape(192, 192, dtype=F32)],
+        scratch=[pltpu.VMEM((64, 16, 128), F32)],
         n_in=1,
         name="finish",
     )(spread)

time: 141 us -> 137 us (0.972)
  the two profiles are of different devices: /device:TPU:123 before, /device:TPU:32 now
where the time goes in v2:
time: 137 us
  starting transfers between devices  48 us (35%)
  Pallas kernels  38.7 us (28%)
  blocking collectives  24.4 us (18%)
  waiting for transfers between devices  17.1 us (12%)
  local copies, waits for them, and re-layouts  7.5 us (5%)
    all_to_all x1, blocking collectives, body(): arrived = lax.all_to_all(pieces, 'tiles', 0, 0, tiled=True)  24.4 us
    ppermute x9, starting transfers between devices, hop(): lax.ppermute(value, 'tiles', [p for p in pairs if 0 <= p[1] < devices])  20.6 us
    ppermute x12, starting transfers between devices, along_chan(): lax.ppermute(values[j], 'chan', [(i, (i + j) % 4) for i in range(4)])  17.3 us
    ppermute x12, waiting for transfers between devices, along_chan(): lax.ppermute(values[j], 'chan', [(i, (i + j) % 4) for i in range(4)])  12.4 us
    pallas_call x1, Pallas kernels, body(): unmix(adjacency, grads, par_grads, from_up, from_up_cross, from_down, fro...  6.72 us
    pallas_call x1, Pallas kernels, body(): mix(slot_owner, par_slots, adjacency, x_scan, par_x, near, far, taps, up_...  6.71 us
    unnamed x76, local copies, waits for them, and re-layouts  6.07 us
    all_to_all x1, starting transfers between devices, body(): spread = lax.all_to_all(totals, 'tiles', 0, 0, tiled=True)  5.87 us
  transfers between devices with their start and end apart: 25, of which 6 were waited for; matrix products, arithmetic and copies ran while one was open for 1% of the time, Pallas kernels for 18%

profile of v2, /device:TPU:32, one launch (start us, length us, event | category | flops | bytes accessed | tf_op | source)
XLA Modules:
  0.0 136.7 jit_solution(4473938255448724119)
XLA Ops:
  0.7 1.7 %strips.1 = bf16[8,48,128]{2,1,0:T(8,128)(2,1)} custom-call(bf16[16,48,256]{2,1,0:T(8,128)(2,1)} %x_ref.3), custom_call_target="tpu_custom_call" | custom-call | tf_op jit(solution)/shard_map/strips/pallas_call | solution.py:442
  2.5 0.6 reshape.24.b_ref
  3.0 2.1 %sends.1 = (bf16[400,256]{1,0:T(8,128)(2,1)}, bf16[400,256]{1,0:T(8,128)(2,1)}, bf16[400,256]{1,0:T(8,128)(2,1)}, bf16[400,256]{1,0:T(8,128)(2,1)}) custom-call(bf16[8,48,256]{2,1,0:T(8,128)(2,1)} %cot_ref.3, f32[1,48]{1,0:T(1,128)} %bitcast.4, bf16[192,192]{1,0:T(8,128)(2,1)} %in_ref.1, bf16[192,192]{1,0:T(8,128)(2,1)} %w_out_ref.1, ...), custom_call_target="tpu_custom_call" | custom-call | tf_op jit(solution)/shard_map/sends/pallas_call | solution.py:447
  5.2 1.5 %collective-permute-start.7 = (bf16[400,256]{1,0:T(8,128)(2,1)}, bf16[400,256]{1,0:T(8,128)(2,1)S(1)}, u32[]{:S(2)}, u32[]{:S(2)}) collective-permute-start(bf16[400,256]{1,0:T(8,128)(2,1)} %get-tuple-element.67), channel_id=1, source_target_pairs={{0,1},{1,2},{2,3},{3,0},{4,5},{5,6},{6,7},{7,4},{8,9},{9,10},{10,1... | collective-permute-start | bytes 614408 | tf_op jit(solution)/shard_map/ppermute | solution.py:420
  6.7 4.5 %collective-permute-start.3 = (bf16[8,48,128]{2,1,0:T(8,128)(2,1)S(1)}, bf16[8,48,128]{2,1,0:T(8,128)(2,1)S(1)}, u32[]{:S(2)}, u32[]{:S(2)}) collective-permute-start(bf16[8,48,128]{2,1,0:T(8,128)(2,1)S(1)} %copy-done.12), channel_id=1, source_target_pairs={{4,12},{8,0},{12,20},{16,8},{20,28},{24,16},{28,36},{32,24},{36,44... | collective-permute-start | bytes 294920 | tf_op jit(solution)/shard_map/ppermute | solution.py:434
  11.2 2.8 %collective-permute-start.8 = (bf16[400,256]{1,0:T(8,128)(2,1)}, bf16[400,256]{1,0:T(8,128)(2,1)S(1)}, u32[]{:S(2)}, u32[]{:S(2)}) collective-permute-start(bf16[400,256]{1,0:T(8,128)(2,1)} %get-tuple-element.68), channel_id=1, source_target_pairs={{0,2},{1,3},{2,0},{3,1},{4,6},{5,7},{6,4},{7,5},{8,10},{9,11},{10,... | collective-permute-start | bytes 614408 | tf_op jit(solution)/shard_map/ppermute | solution.py:420
  14.6 1.4 %collective-permute-start.9 = (bf16[400,256]{1,0:T(8,128)(2,1)}, bf16[400,256]{1,0:T(8,128)(2,1)S(1)}, u32[]{:S(2)}, u32[]{:S(2)}) collective-permute-start(bf16[400,256]{1,0:T(8,128)(2,1)} %get-tuple-element.69), channel_id=1, source_target_pairs={{0,3},{1,0},{2,1},{3,2},{4,7},{5,4},{6,5},{7,6},{8,11},{9,8},{10,9... | collective-permute-start | bytes 614408 | tf_op jit(solution)/shard_map/ppermute | solution.py:420
  16.0 2.5 %collective-permute-start.2 = (bf16[8,48,128]{2,1,0:T(8,128)(2,1)S(1)}, bf16[8,48,128]{2,1,0:T(8,128)(2,1)S(1)}, u32[]{:S(2)}, u32[]{:S(2)}) collective-permute-start(bf16[8,48,128]{2,1,0:T(8,128)(2,1)S(1)} %copy-done.12), channel_id=1, source_target_pairs={{4,8},{8,4},{12,16},{16,12},{20,24},{24,20},{28,32},{32,28},{36,40... | collective-permute-start | bytes 294920 | tf_op jit(solution)/shard_map/ppermute | solution.py:434
  18.6 0.8 tile.10.taps
  19.4 4.7 %collective-permute-done.2.sa_ref = bf16[8,48,128]{2,1,0:T(8,128)(2,1)S(1)} collective-permute-done((bf16[8,48,128]{2,1,0:T(8,128)(2,1)S(1)}, bf16[8,48,128]{2,1,0:T(8,128)(2,1)S(1)}, u32[]{:S(2)}, u32[]{:S(2)}) %collective-permute-start.2) | collective-permute-done | bytes 98336 | tf_op jit(solution)/shard_map/ppermute | solution.py:434
  24.0 0.6 copy-done.11
  24.7 0.8 copy-done.1
  25.5 6.7 %mix.1 = (bf16[8,48,256]{2,1,0:T(8,128)(2,1)}, bf16[22,24,384]{2,1,0:T(8,128)(2,1)}, bf16[2,48,256]{2,1,0:T(8,128)(2,1)}, bf16[2,48,256]{2,1,0:T(8,128)(2,1)}, b...) custom-call(s32[16]{0:T(128)} %own_slots.1, s32[16]{0:T(128)} %copy-done.28, s32[8,8]{1,0:T(8,128)} %adj.3, ...), custom_call_target="tpu_custom_call" | custom-call | tf_op jit(solution)/shard_map/mix/pallas_call | solution.py:475
  32.2 0.6 collective-permute-start.4
  32.8 1.0 collective-permute-start.5
  33.8 1.7 %collective-permute-start.6 = (bf16[2,48,256]{2,1,0:T(8,128)(2,1)}, bf16[2,48,256]{2,1,0:T(8,128)(2,1)S(1)}, u32[]{:S(2)}, u32[]{:S(2)}) collective-permute-start(bf16[2,48,256]{2,1,0:T(8,128)(2,1)} %get-tuple-element.64), channel_id=1, source_target_pairs={{0,3},{1,0},{2,1},{3,2},{4,7},{5,4},{6,5},{7,6},{8,11},{9,8},{10,9... | collective-permute-start | bytes 147464 | tf_op jit(solution)/shard_map/ppermute | solution.py:420
  35.6 0.6 copy-done.3
  36.3 2.9 %turn.1 = (bf16[4,192,192]{2,1,0:T(8,128)(2,1)}, bf16[4,192,192]{2,1,0:T(8,128)(2,1)}, bf16[4,192,192]{2,1,0:T(8,128)(2,1)}, bf16[4,192,192]{2,1,0:T(8,128)(2,1)...) custom-call(bf16[400,256]{1,0:T(8,128)(2,1)} %get-tuple-element.70.p0, ...), custom_call_target="tpu_custom_call" | custom-call | tf_op jit(solution)/shard_map/turn/pallas_call | solution.py:488
  39.2 0.6 copy-done.19
  39.8 5.1 %mlp.1 = (bf16[2,48,256]{2,1,0:T(8,128)(2,1)}, bf16[2,48,256]{2,1,0:T(8,128)(2,1)}, bf16[2,48,256]{2,1,0:T(8,128)(2,1)}, bf16[2,48,256]{2,1,0:T(8,128)(2,1)}, bf...) custom-call(bf16[2,48,256]{2,1,0:T(8,128)(2,1)} %get-tuple-element.6, ...), custom_call_target="tpu_custom_call" | custom-call | tf_op jit(solution)/shard_map/mlp/pallas_call | solution.py:491
  45.0 2.8 %outer.1 = (bf16[384,192]{1,0:T(8,128)(2,1)}, bf16[384,192]{1,0:T(8,128)(2,1)}, bf16[384,192]{1,0:T(8,128)(2,1)}, bf16[384,192]{1,0:T(8,128)(2,1)}) custom-call(bf16[4,192,512]{2,1,0:T(8,128)(2,1)} %get-tuple-element.89.act_ref, bf16[4,192,512]{2,1,0:T(8,128)(2,1)} %get-tuple-element.90.pre_ref, bf16[192,512]{1,0:T(8,128)(2,1)} %get-tuple-element.91.normed_ref, ...), custom_call_target="tpu_custom_call" | custom-call | tf_op jit(solution)/shard_map/outer/pallas_call | solution.py:499
  47.7 2.4 %collective-permute-start.13 = (bf16[384,192]{1,0:T(8,128)(2,1)}, bf16[384,192]{1,0:T(8,128)(2,1)S(1)}, u32[]{:S(2)}, u32[]{:S(2)}) collective-permute-start(bf16[384,192]{1,0:T(8,128)(2,1)} %get-tuple-element.93), channel_id=1, source_target_pairs={{0,3},{1,0},{2,1},{3,2},{4,7},{5,4},{6,5},{7,6},{8,11},{9,8},{10,9... | collective-permute-start | bytes 442376 | tf_op jit(solution)/shard_map/ppermute | solution.py:505
  50.1 1.1 collective-permute-start.14
  51.2 0.8 collective-permute-start.15
  52.0 1.6 %collective-permute-start.10 = (bf16[2,48,256]{2,1,0:T(8,128)(2,1)S(1)}, bf16[2,48,256]{2,1,0:T(8,128)(2,1)S(1)}, u32[]{:S(2)}, u32[]{:S(2)}) collective-permute-start(bf16[2,48,256]{2,1,0:T(8,128)(2,1)S(1)} %copy-done.36), channel_id=1, source_target_pairs={{0,1},{1,2},{2,3},{3,0},{4,5},{5,6},{6,7},{7,4},{8,9},{9,10},{10,1... | collective-permute-start | bytes 147464 | tf_op jit(solution)/shard_map/ppermute | solution.py:420
  53.6 2.3 %collective-permute-start.11 = (bf16[2,48,256]{2,1,0:T(8,128)(2,1)S(1)}, bf16[2,48,256]{2,1,0:T(8,128)(2,1)S(1)}, u32[]{:S(2)}, u32[]{:S(2)}) collective-permute-start(bf16[2,48,256]{2,1,0:T(8,128)(2,1)S(1)} %copy-done.35), channel_id=1, source_target_pairs={{0,2},{1,3},{2,0},{3,1},{4,6},{5,7},{6,4},{7,5},{8,10},{9,11},{10,... | collective-permute-start | bytes 147464 | tf_op jit(solution)/shard_map/ppermute | solution.py:420
  55.9 5.1 %collective-permute-done.10.g1 = bf16[2,48,256]{2,1,0:T(8,128)(2,1)S(1)} collective-permute-done((bf16[2,48,256]{2,1,0:T(8,128)(2,1)S(1)}, bf16[2,48,256]{2,1,0:T(8,128)(2,1)S(1)}, u32[]{:S(2)}, u32[]{:S(2)}) %collective-permute-start.10) | collective-permute-done | bytes 49184 | tf_op jit(solution)/shard_map/ppermute | solution.py:420
  60.9 0.6 collective-permute-start.12
  61.6 3.5 %collective-permute-done.12.g3 = bf16[2,48,256]{2,1,0:T(8,128)(2,1)S(1)} collective-permute-done((bf16[2,48,256]{2,1,0:T(8,128)(2,1)S(1)}, bf16[2,48,256]{2,1,0:T(8,128)(2,1)S(1)}, u32[]{:S(2)}, u32[]{:S(2)}) %collective-permute-start.12) | collective-permute-done | bytes 49184 | tf_op jit(solution)/shard_map/ppermute | solution.py:420
  65.0 0.6 copy-done.15
  65.6 4.6 %tap_sums.1 = (bf16[8,48,256]{2,1,0:T(8,128)(2,1)}, bf16[4,48,128]{2,1,0:T(8,128)(2,1)}, bf16[4,48,128]{2,1,0:T(8,128)(2,1)}, f32[64,128]{1,0:T(8,128)}) custom-call(bf16[2,48,256]{2,1,0:T(8,128)(2,1)} %get-tuple-element.81.g0, bf16[2,48,256]{2,1,0:T(8,128)(2,1)} %copy-done.13, bf16[2,48,256]{2,1,0:T(8,128)(2,1)} %copy-done.14, ...), custom_call_target="tpu_custom_call" | custom-call | tf_op jit(solution)/shard_map/tap_sums/pallas_call | solution.py:507
  70.3 0.6 copy-done.7
  71.1 2.3 %pieces.1 = bf16[64,16,128]{2,1,0:T(8,128)(2,1)} custom-call(bf16[384,192]{1,0:T(8,128)(2,1)} %get-tuple-element.92.v0, bf16[384,192]{1,0:T(8,128)(2,1)} %copy-done.7, bf16[384,192]{1,0:T(8,128)(2,1)} %copy-done.8, bf16[384,192]{1,0:T(8,128)(2,1)} %copy-done.9, f32[64,128]{1,0:T(8,128)} %get-tuple-element.96.taps_ref), custom_call_target="tpu_custom_call" | custom-call | tf_op jit(solution)/shard_map/pieces/pallas_call | solution.py:518
  73.4 24.4 %all_to_all.10.in_ref = bf16[64,16,128]{2,1,0:T(8,128)(2,1)} all-to-all(bf16[64,16,128]{2,1,0:T(8,128)(2,1)} %pieces.1), channel_id=1, replica_groups=mesh['tiles'=64,'chan'=4] {'tiles'}, dimensions={0} | all-to-all | bytes 524288 | tf_op jit(solution)/shard_map/all_to_all | solution.py:525
  97.8 1.7 %totals.1 = bf16[64,16,128]{2,1,0:T(8,128)(2,1)} custom-call(bf16[64,16,128]{2,1,0:T(8,128)(2,1)} %all_to_all.10.in_ref), custom_call_target="tpu_custom_call" | custom-call | tf_op jit(solution)/shard_map/totals/pallas_call | solution.py:536
  99.6 5.9 %all-to-all-start.1 = ((bf16[64,16,128]{2,1,0:T(8,128)(2,1)}), bf16[64,16,128]{2,1,0:T(8,128)(2,1)S(1)}, u32[]{:S(2)}, u32[]{:S(2)}) async-start(bf16[64,16,128]{2,1,0:T(8,128)(2,1)} %totals.1), calls=%async_computation.1 | async-start | bytes 524288 | tf_op jit(solution)/shard_map/all_to_all | solution.py:539
  105.7 3.3 %collective-permute-start.18 = (bf16[4,48,128]{2,1,0:T(8,128)(2,1)S(1)}, bf16[4,48,128]{2,1,0:T(8,128)(2,1)S(1)}, u32[]{:S(2)}, u32[]{:S(2)}) collective-permute-start(bf16[4,48,128]{2,1,0:T(8,128)(2,1)S(1)} %copy-done.33), channel_id=1, source_target_pairs={{0,12},{4,8},{8,20},{12,16},{16,28},{20,24},{24,36},{28,32},{32,44... | collective-permute-start | bytes 147464 | tf_op jit(solution)/shard_map/ppermute | solution.py:434
  109.0 3.4 %collective-permute-start.17 = (bf16[4,48,128]{2,1,0:T(8,128)(2,1)S(1)}, bf16[4,48,128]{2,1,0:T(8,128)(2,1)S(1)}, u32[]{:S(2)}, u32[]{:S(2)}) collective-permute-start(bf16[4,48,128]{2,1,0:T(8,128)(2,1)S(1)} %copy-done.33), channel_id=1, source_target_pairs={{0,8},{4,12},{8,16},{12,20},{16,24},{20,28},{24,32},{28,36},{32,40... | collective-permute-start | bytes 147464 | tf_op jit(solution)/shard_map/ppermute | solution.py:434
  112.4 4.1 %collective-permute-start.20 = (bf16[4,48,128]{2,1,0:T(8,128)(2,1)S(1)}, bf16[4,48,128]{2,1,0:T(8,128)(2,1)S(1)}, u32[]{:S(2)}, u32[]{:S(2)}) collective-permute-start(bf16[4,48,128]{2,1,0:T(8,128)(2,1)S(1)} %copy-done.32), channel_id=1, source_target_pairs={{8,4},{12,0},{16,12},{20,8},{24,20},{28,16},{32,28},{36,24},{40,36... | collective-permute-start | bytes 147464 | tf_op jit(solution)/shard_map/ppermute | solution.py:434
  116.5 2.5 %collective-permute-start.19 = (bf16[4,48,128]{2,1,0:T(8,128)(2,1)S(1)}, bf16[4,48,128]{2,1,0:T(8,128)(2,1)S(1)}, u32[]{:S(2)}, u32[]{:S(2)}) collective-permute-start(bf16[4,48,128]{2,1,0:T(8,128)(2,1)S(1)} %copy-done.32), channel_id=1, source_target_pairs={{8,0},{12,4},{16,8},{20,12},{24,16},{28,20},{32,24},{36,28},{40,32... | collective-permute-start | bytes 147464 | tf_op jit(solution)/shard_map/ppermute | solution.py:434
  119.1 3.3 %collective-permute-start.22 = (bf16[2,48,256]{2,1,0:T(8,128)(2,1)S(1)}, bf16[2,48,256]{2,1,0:T(8,128)(2,1)S(1)}, u32[]{:S(2)}, u32[]{:S(2)}) collective-permute-start(bf16[2,48,256]{2,1,0:T(8,128)(2,1)S(1)} %copy-done.30), channel_id=1, source_target_pairs={{0,2},{1,3},{2,0},{3,1},{4,6},{5,7},{6,4},{7,5},{8,10},{9,11},{10,... | collective-permute-start | bytes 147464 | tf_op jit(solution)/shard_map/ppermute | solution.py:420
  122.8 2.1 %collective-permute-done.21.r1 = bf16[2,48,256]{2,1,0:T(8,128)(2,1)S(1)} collective-permute-done((bf16[2,48,256]{2,1,0:T(8,128)(2,1)S(1)}, bf16[2,48,256]{2,1,0:T(8,128)(2,1)S(1)}, u32[]{:S(2)}, u32[]{:S(2)}) %collective-permute-start.21) | collective-permute-done | bytes 49184 | tf_op jit(solution)/shard_map/ppermute | solution.py:420
  124.9 0.5 collective-permute-done.22.r2
  125.4 1.2 collective-permute-done.23.r3
  126.7 0.6 copy-done.25
  127.3 6.7 %unmix.1 = (bf16[8,48,256]{2,1,0:T(8,128)(2,1)}, bf16[8,48,256]{2,1,0:T(8,128)(2,1)}) custom-call(s32[8,8]{1,0:T(8,128)} %adj.3, bf16[8,48,256]{2,1,0:T(8,128)(2,1)} %get-tuple-element.97.grad_ref, bf16[8,48,256]{2,1,0:T(8,128)(2,1)} %copy-done.6, bf16[4,48,128]{2,1,0:T(8,128)(2,1)} %copy-done.17, bf16[4,48,128]{2,1,0:T(8,128)(2,1)} %copy-done.16, ...), custom_call_target="tpu_custom_call" | custom-call | tf_op jit(solution)/shard_map/unmix/pallas_call | solution.py:549
  134.1 0.7 copy-done
  134.8 1.9 %finish.1 = (f32[48,49]{1,0:T(8,128)}, f32[192,192]{1,0:T(8,128)}, f32[192,192]{1,0:T(8,128)}) custom-call(bf16[64,16,128]{2,1,0:T(8,128)(2,1)} %copy-done), custom_call_target="tpu_custom_call" | custom-call | tf_op jit(solution)/shard_map/finish/pallas_call | solution.py:553
  (94 shorter events, 1.9 us)
Async XLA Ops:
  0.6 1.8 %copy-start.37 = (bf16[192]{0:T(256)(128)(2,1)S(1)}, bf16[192]{0:T(256)(128)(2,1)}, u32[]{:S(2)}) copy-start(bf16[192]{0:T(256)(128)(2,1)} %param.21) | copy-start | bytes 1156
  0.6 23.4 %collective-permute-start.1 = (bf16[16,48,256]{2,1,0:T(8,128)(2,1)}, bf16[16,48,256]{2,1,0:T(8,128)(2,1)S(1)}, u32[]{:S(2)}, u32[]{:S(2)}) collective-permute-start(bf16[16,48,256]{2,1,0:T(8,128)(2,1)} %x_ref.3), channel_id=1, source_target_pairs={{0,4},{4,0},{8,12},{12,8},{16,20},{20,16},{24,28},{28,24},{32,36},... | collective-permute-start | bytes 1179656 | tf_op jit(solution)/shard_map/ppermute | solution.py:434
  3.0 3.6 %copy-start.12 = (bf16[8,48,128]{2,1,0:T(8,128)(2,1)S(1)}, bf16[8,48,128]{2,1,0:T(8,128)(2,1)}, u32[]{:S(2)}) copy-start(bf16[8,48,128]{2,1,0:T(8,128)(2,1)} %strips.1) | copy-start | bytes 294916
  3.0 15.4 %copy-start.26 = (f32[48,49]{1,0:T(8,128)S(1)}, f32[48,49]{1,0:T(8,128)}, u32[]{:S(2)}) copy-start(f32[48,49]{1,0:T(8,128)} %param.18) | copy-start | bytes 28228
  5.2 6.0 %copy-start.27 = (s32[16]{0:T(128)S(1)}, s32[16]{0:T(128)}, u32[]{:S(2)}) copy-start(s32[16]{0:T(128)} %own_slots.1) | copy-start | bytes 196
  5.2 28.6 %collective-permute-start.7 = (bf16[400,256]{1,0:T(8,128)(2,1)}, bf16[400,256]{1,0:T(8,128)(2,1)S(1)}, u32[]{:S(2)}, u32[]{:S(2)}) collective-permute-start(bf16[400,256]{1,0:T(8,128)(2,1)} %get-tuple-element.67), channel_id=1, source_target_pairs={{0,1},{1,2},{2,3},{3,0},{4,5},{5,6},{6,7},{7,4},{8,9},{9,10},{10,1... | collective-permute-start | bytes 614408 | tf_op jit(solution)/shard_map/ppermute | solution.py:420
  6.7 9.3 %collective-permute-start.3 = (bf16[8,48,128]{2,1,0:T(8,128)(2,1)S(1)}, bf16[8,48,128]{2,1,0:T(8,128)(2,1)S(1)}, u32[]{:S(2)}, u32[]{:S(2)}) collective-permute-start(bf16[8,48,128]{2,1,0:T(8,128)(2,1)S(1)} %copy-done.12), channel_id=1, source_target_pairs={{4,12},{8,0},{12,20},{16,8},{20,28},{24,16},{28,36},{32,24},{36,44... | collective-permute-start | bytes 294920 | tf_op jit(solution)/shard_map/ppermute | solution.py:434
  11.1 2.9 %collective-permute-start = (s32[16]{0:T(128)S(1)}, s32[16]{0:T(128)S(1)}, u32[]{:S(2)}, u32[]{:S(2)}) collective-permute-start(s32[16]{0:T(128)S(1)} %copy-done.27), channel_id=1, source_target_pairs={{0,4},{4,0},{8,12},{12,8},{16,20},{20,16},{24,28},{28,24},{32,36},... | collective-permute-start | bytes 200 | tf_op jit(solution)/shard_map/ppermute | solution.py:434
  11.2 24.3 %collective-permute-start.8 = (bf16[400,256]{1,0:T(8,128)(2,1)}, bf16[400,256]{1,0:T(8,128)(2,1)S(1)}, u32[]{:S(2)}, u32[]{:S(2)}) collective-permute-start(bf16[400,256]{1,0:T(8,128)(2,1)} %get-tuple-element.68), channel_id=1, source_target_pairs={{0,2},{1,3},{2,0},{3,1},{4,6},{5,7},{6,4},{7,5},{8,10},{9,11},{10,... | collective-permute-start | bytes 614408 | tf_op jit(solution)/shard_map/ppermute | solution.py:420
  14.6 21.0 %collective-permute-start.9 = (bf16[400,256]{1,0:T(8,128)(2,1)}, bf16[400,256]{1,0:T(8,128)(2,1)S(1)}, u32[]{:S(2)}, u32[]{:S(2)}) collective-permute-start(bf16[400,256]{1,0:T(8,128)(2,1)} %get-tuple-element.69), channel_id=1, source_target_pairs={{0,3},{1,0},{2,1},{3,2},{4,7},{5,4},{6,5},{7,6},{8,11},{9,8},{10,9... | collective-permute-start | bytes 614408 | tf_op jit(solution)/shard_map/ppermute | solution.py:420
  16.0 2.6 %copy-start.10 = (bf16[8,48,128]{2,1,0:T(8,128)(2,1)}, bf16[8,48,128]{2,1,0:T(8,128)(2,1)S(1)}, u32[]{:S(2)}) copy-start(bf16[8,48,128]{2,1,0:T(8,128)(2,1)S(1)} %collective-permute-done.3.sb_ref) | copy-start | bytes 294916
  16.0 8.0 %collective-permute-start.2 = (bf16[8,48,128]{2,1,0:T(8,128)(2,1)S(1)}, bf16[8,48,128]{2,1,0:T(8,128)(2,1)S(1)}, u32[]{:S(2)}, u32[]{:S(2)}) collective-permute-start(bf16[8,48,128]{2,1,0:T(8,128)(2,1)S(1)} %copy-done.12), channel_id=1, source_target_pairs={{4,8},{8,4},{12,16},{16,12},{20,24},{24,20},{28,32},{32,28},{36,40... | collective-permute-start | bytes 294920 | tf_op jit(solution)/shard_map/ppermute | solution.py:434
  32.2 7.0 %collective-permute-start.4 = (bf16[2,48,256]{2,1,0:T(8,128)(2,1)}, bf16[2,48,256]{2,1,0:T(8,128)(2,1)S(1)}, u32[]{:S(2)}, u32[]{:S(2)}) collective-permute-start(bf16[2,48,256]{2,1,0:T(8,128)(2,1)} %get-tuple-element.62), channel_id=1, source_target_pairs={{0,1},{1,2},{2,3},{3,0},{4,5},{5,6},{6,7},{7,4},{8,9},{9,10},{10,1... | collective-permute-start | bytes 147464 | tf_op jit(solution)/shard_map/ppermute | solution.py:420
  32.8 6.4 %collective-permute-start.5 = (bf16[2,48,256]{2,1,0:T(8,128)(2,1)}, bf16[2,48,256]{2,1,0:T(8,128)(2,1)S(1)}, u32[]{:S(2)}, u32[]{:S(2)}) collective-permute-start(bf16[2,48,256]{2,1,0:T(8,128)(2,1)} %get-tuple-element.63), channel_id=1, source_target_pairs={{0,2},{1,3},{2,0},{3,1},{4,6},{5,7},{6,4},{7,5},{8,10},{9,11},{10,... | collective-permute-start | bytes 147464 | tf_op jit(solution)/shard_map/ppermute | solution.py:420
  33.8 1.8 %copy-start.2 = (bf16[400,256]{1,0:T(8,128)(2,1)}, bf16[400,256]{1,0:T(8,128)(2,1)S(1)}, u32[]{:S(2)}) copy-start(bf16[400,256]{1,0:T(8,128)(2,1)S(1)} %collective-permute-done.7.p1) | copy-start | bytes 614404
  33.8 5.4 %collective-permute-start.6 = (bf16[2,48,256]{2,1,0:T(8,128)(2,1)}, bf16[2,48,256]{2,1,0:T(8,128)(2,1)S(1)}, u32[]{:S(2)}, u32[]{:S(2)}) collective-permute-start(bf16[2,48,256]{2,1,0:T(8,128)(2,1)} %get-tuple-element.64), channel_id=1, source_target_pairs={{0,3},{1,0},{2,1},{3,2},{4,7},{5,4},{6,5},{7,6},{8,11},{9,8},{10,9... | collective-permute-start | bytes 147464 | tf_op jit(solution)/shard_map/ppermute | solution.py:420
  44.9 7.1 %copy-start.36 = (bf16[2,48,256]{2,1,0:T(8,128)(2,1)S(1)}, bf16[2,48,256]{2,1,0:T(8,128)(2,1)}, u32[]{:S(2)}) copy-start(bf16[2,48,256]{2,1,0:T(8,128)(2,1)} %get-tuple-element.82) | copy-start | bytes 147460
  44.9 8.7 %copy-start.35 = (bf16[2,48,256]{2,1,0:T(8,128)(2,1)S(1)}, bf16[2,48,256]{2,1,0:T(8,128)(2,1)}, u32[]{:S(2)}) copy-start(bf16[2,48,256]{2,1,0:T(8,128)(2,1)} %get-tuple-element.83) | copy-start | bytes 147460
  44.9 16.0 %copy-start.34 = (bf16[2,48,256]{2,1,0:T(8,128)(2,1)S(1)}, bf16[2,48,256]{2,1,0:T(8,128)(2,1)}, u32[]{:S(2)}) copy-start(bf16[2,48,256]{2,1,0:T(8,128)(2,1)} %get-tuple-element.84) | copy-start | bytes 147460
  47.7 22.6 %collective-permute-start.13 = (bf16[384,192]{1,0:T(8,128)(2,1)}, bf16[384,192]{1,0:T(8,128)(2,1)S(1)}, u32[]{:S(2)}, u32[]{:S(2)}) collective-permute-start(bf16[384,192]{1,0:T(8,128)(2,1)} %get-tuple-element.93), channel_id=1, source_target_pairs={{0,3},{1,0},{2,1},{3,2},{4,7},{5,4},{6,5},{7,6},{8,11},{9,8},{10,9... | collective-permute-start | bytes 442376 | tf_op jit(solution)/shard_map/ppermute | solution.py:505
  50.1 20.2 %collective-permute-start.14 = (bf16[384,192]{1,0:T(8,128)(2,1)}, bf16[384,192]{1,0:T(8,128)(2,1)S(1)}, u32[]{:S(2)}, u32[]{:S(2)}) collective-permute-start(bf16[384,192]{1,0:T(8,128)(2,1)} %get-tuple-element.94), channel_id=1, source_target_pairs={{0,2},{1,3},{2,0},{3,1},{4,6},{5,7},{6,4},{7,5},{8,10},{9,11},{10,... | collective-permute-start | bytes 442376 | tf_op jit(solution)/shard_map/ppermute | solution.py:505
  51.2 19.2 %collective-permute-start.15 = (bf16[384,192]{1,0:T(8,128)(2,1)}, bf16[384,192]{1,0:T(8,128)(2,1)S(1)}, u32[]{:S(2)}, u32[]{:S(2)}) collective-permute-start(bf16[384,192]{1,0:T(8,128)(2,1)} %get-tuple-element.95), channel_id=1, source_target_pairs={{0,1},{1,2},{2,3},{3,0},{4,5},{5,6},{6,7},{7,4},{8,9},{9,10},{10,1... | collective-permute-start | bytes 442376 | tf_op jit(solution)/shard_map/ppermute | solution.py:505
  52.0 9.0 %collective-permute-start.10 = (bf16[2,48,256]{2,1,0:T(8,128)(2,1)S(1)}, bf16[2,48,256]{2,1,0:T(8,128)(2,1)S(1)}, u32[]{:S(2)}, u32[]{:S(2)}) collective-permute-start(bf16[2,48,256]{2,1,0:T(8,128)(2,1)S(1)} %copy-done.36), channel_id=1, source_target_pairs={{0,1},{1,2},{2,3},{3,0},{4,5},{5,6},{6,7},{7,4},{8,9},{9,10},{10,1... | collective-permute-start | bytes 147464 | tf_op jit(solution)/shard_map/ppermute | solution.py:420
  53.6 7.9 %collective-permute-start.11 = (bf16[2,48,256]{2,1,0:T(8,128)(2,1)S(1)}, bf16[2,48,256]{2,1,0:T(8,128)(2,1)S(1)}, u32[]{:S(2)}, u32[]{:S(2)}) collective-permute-start(bf16[2,48,256]{2,1,0:T(8,128)(2,1)S(1)} %copy-done.35), channel_id=1, source_target_pairs={{0,2},{1,3},{2,0},{3,1},{4,6},{5,7},{6,4},{7,5},{8,10},{9,11},{10,... | collective-permute-start | bytes 147464 | tf_op jit(solution)/shard_map/ppermute | solution.py:420
  60.9 4.1 %copy-start.13 = (bf16[2,48,256]{2,1,0:T(8,128)(2,1)}, bf16[2,48,256]{2,1,0:T(8,128)(2,1)S(1)}, u32[]{:S(2)}) copy-start(bf16[2,48,256]{2,1,0:T(8,128)(2,1)S(1)} %collective-permute-done.10.g1) | copy-start | bytes 147460
  60.9 4.1 %collective-permute-start.12 = (bf16[2,48,256]{2,1,0:T(8,128)(2,1)S(1)}, bf16[2,48,256]{2,1,0:T(8,128)(2,1)S(1)}, u32[]{:S(2)}, u32[]{:S(2)}) collective-permute-start(bf16[2,48,256]{2,1,0:T(8,128)(2,1)S(1)} %copy-done.34), channel_id=1, source_target_pairs={{0,3},{1,0},{2,1},{3,2},{4,7},{5,4},{6,5},{7,6},{8,11},{9,8},{10,9... | collective-permute-start | bytes 147464 | tf_op jit(solution)/shard_map/ppermute | solution.py:420
  61.6 3.5 %copy-start.14 = (bf16[2,48,256]{2,1,0:T(8,128)(2,1)}, bf16[2,48,256]{2,1,0:T(8,128)(2,1)S(1)}, u32[]{:S(2)}) copy-start(bf16[2,48,256]{2,1,0:T(8,128)(2,1)S(1)} %collective-permute-done.11.g2) | copy-start | bytes 147460
  99.5 5.9 %copy-start.5 = (bf16[8,48,256]{2,1,0:T(8,128)(2,1)S(1)}, bf16[8,48,256]{2,1,0:T(8,128)(2,1)}, u32[]{:S(2)}) copy-start(bf16[8,48,256]{2,1,0:T(8,128)(2,1)} %get-tuple-element.97.grad_ref) | copy-start | bytes 589828
  99.5 6.2 %copy-start.33 = (bf16[4,48,128]{2,1,0:T(8,128)(2,1)S(1)}, bf16[4,48,128]{2,1,0:T(8,128)(2,1)}, u32[]{:S(2)}) copy-start(bf16[4,48,128]{2,1,0:T(8,128)(2,1)} %get-tuple-element.98) | copy-start | bytes 147460
  99.5 12.9 %copy-start.32 = (bf16[4,48,128]{2,1,0:T(8,128)(2,1)S(1)}, bf16[4,48,128]{2,1,0:T(8,128)(2,1)}, u32[]{:S(2)}) copy-start(bf16[4,48,128]{2,1,0:T(8,128)(2,1)} %get-tuple-element.99) | copy-start | bytes 147460
  99.5 19.4 %copy-start.31 = (bf16[2,48,256]{2,1,0:T(8,128)(2,1)S(1)}, bf16[2,48,256]{2,1,0:T(8,128)(2,1)}, u32[]{:S(2)}) copy-start(bf16[2,48,256]{2,1,0:T(8,128)(2,1)} %get-tuple-element.107) | copy-start | bytes 147460
  99.6 19.6 %copy-start.30 = (bf16[2,48,256]{2,1,0:T(8,128)(2,1)S(1)}, bf16[2,48,256]{2,1,0:T(8,128)(2,1)}, u32[]{:S(2)}) copy-start(bf16[2,48,256]{2,1,0:T(8,128)(2,1)} %get-tuple-element.108) | copy-start | bytes 147460
  99.6 22.9 %copy-start.29 = (bf16[2,48,256]{2,1,0:T(8,128)(2,1)S(1)}, bf16[2,48,256]{2,1,0:T(8,128)(2,1)}, u32[]{:S(2)}) copy-start(bf16[2,48,256]{2,1,0:T(8,128)(2,1)} %get-tuple-element.109) | copy-start | bytes 147460
  99.6 34.5 %all-to-all-start.1 = ((bf16[64,16,128]{2,1,0:T(8,128)(2,1)}), bf16[64,16,128]{2,1,0:T(8,128)(2,1)S(1)}, u32[]{:S(2)}, u32[]{:S(2)}) async-start(bf16[64,16,128]{2,1,0:T(8,128)(2,1)} %totals.1), calls=%async_computation.1 | async-start | bytes 524288 | tf_op jit(solution)/shard_map/all_to_all | solution.py:539
  105.5 21.2 %collective-permute-start.16 = (bf16[8,48,256]{2,1,0:T(8,128)(2,1)S(1)}, bf16[8,48,256]{2,1,0:T(8,128)(2,1)S(1)}, u32[]{:S(2)}, u32[]{:S(2)}) collective-permute-start(bf16[8,48,256]{2,1,0:T(8,128)(2,1)S(1)} %copy-done.5), channel_id=1, source_target_pairs={{0,4},{4,0},{8,12},{12,8},{16,20},{20,16},{24,28},{28,24},{32,36},... | collective-permute-start | bytes 589832 | tf_op jit(solution)/shard_map/ppermute | solution.py:434
  105.7 13.3 %collective-permute-start.18 = (bf16[4,48,128]{2,1,0:T(8,128)(2,1)S(1)}, bf16[4,48,128]{2,1,0:T(8,128)(2,1)S(1)}, u32[]{:S(2)}, u32[]{:S(2)}) collective-permute-start(bf16[4,48,128]{2,1,0:T(8,128)(2,1)S(1)} %copy-done.33), channel_id=1, source_target_pairs={{0,12},{4,8},{8,20},{12,16},{16,28},{20,24},{24,36},{28,32},{32,44... | collective-permute-start | bytes 147464 | tf_op jit(solution)/shard_map/ppermute | solution.py:434
  109.0 10.1 %collective-permute-start.17 = (bf16[4,48,128]{2,1,0:T(8,128)(2,1)S(1)}, bf16[4,48,128]{2,1,0:T(8,128)(2,1)S(1)}, u32[]{:S(2)}, u32[]{:S(2)}) collective-permute-start(bf16[4,48,128]{2,1,0:T(8,128)(2,1)S(1)} %copy-done.33), channel_id=1, source_target_pairs={{0,8},{4,12},{8,16},{12,20},{16,24},{20,28},{24,32},{28,36},{32,40... | collective-permute-start | bytes 147464 | tf_op jit(solution)/shard_map/ppermute | solution.py:434
  112.4 10.0 %collective-permute-start.20 = (bf16[4,48,128]{2,1,0:T(8,128)(2,1)S(1)}, bf16[4,48,128]{2,1,0:T(8,128)(2,1)S(1)}, u32[]{:S(2)}, u32[]{:S(2)}) collective-permute-start(bf16[4,48,128]{2,1,0:T(8,128)(2,1)S(1)} %copy-done.32), channel_id=1, source_target_pairs={{8,4},{12,0},{16,12},{20,8},{24,20},{28,16},{32,28},{36,24},{40,36... | collective-permute-start | bytes 147464 | tf_op jit(solution)/shard_map/ppermute | solution.py:434
  116.5 6.3 %collective-permute-start.19 = (bf16[4,48,128]{2,1,0:T(8,128)(2,1)S(1)}, bf16[4,48,128]{2,1,0:T(8,128)(2,1)S(1)}, u32[]{:S(2)}, u32[]{:S(2)}) collective-permute-start(bf16[4,48,128]{2,1,0:T(8,128)(2,1)S(1)} %copy-done.32), channel_id=1, source_target_pairs={{8,0},{12,4},{16,8},{20,12},{24,16},{28,20},{32,24},{36,28},{40,32... | collective-permute-start | bytes 147464 | tf_op jit(solution)/shard_map/ppermute | solution.py:434
  119.0 7.6 %copy-start.16 = (bf16[4,48,128]{2,1,0:T(8,128)(2,1)}, bf16[4,48,128]{2,1,0:T(8,128)(2,1)S(1)}, u32[]{:S(2)}) copy-start(bf16[4,48,128]{2,1,0:T(8,128)(2,1)S(1)} %collective-permute-done.18.uc) | copy-start | bytes 147460
  119.0 5.9 %collective-permute-start.21 = (bf16[2,48,256]{2,1,0:T(8,128)(2,1)S(1)}, bf16[2,48,256]{2,1,0:T(8,128)(2,1)S(1)}, u32[]{:S(2)}, u32[]{:S(2)}) collective-permute-start(bf16[2,48,256]{2,1,0:T(8,128)(2,1)S(1)} %copy-done.31), channel_id=1, source_target_pairs={{0,1},{1,2},{2,3},{3,0},{4,5},{5,6},{6,7},{7,4},{8,9},{9,10},{10,1... | collective-permute-start | bytes 147464 | tf_op jit(solution)/shard_map/ppermute | solution.py:420
  119.1 7.5 %copy-start.17 = (bf16[4,48,128]{2,1,0:T(8,128)(2,1)}, bf16[4,48,128]{2,1,0:T(8,128)(2,1)S(1)}, u32[]{:S(2)}) copy-start(bf16[4,48,128]{2,1,0:T(8,128)(2,1)S(1)} %collective-permute-done.17.us) | copy-start | bytes 147460
  119.1 6.3 %collective-permute-start.22 = (bf16[2,48,256]{2,1,0:T(8,128)(2,1)S(1)}, bf16[2,48,256]{2,1,0:T(8,128)(2,1)S(1)}, u32[]{:S(2)}, u32[]{:S(2)}) collective-permute-start(bf16[2,48,256]{2,1,0:T(8,128)(2,1)S(1)} %copy-done.30), channel_id=1, source_target_pairs={{0,2},{1,3},{2,0},{3,1},{4,6},{5,7},{6,4},{7,5},{8,10},{9,11},{10,... | collective-permute-start | bytes 147464 | tf_op jit(solution)/shard_map/ppermute | solution.py:420
  122.5 4.2 %copy-start.18 = (bf16[4,48,128]{2,1,0:T(8,128)(2,1)}, bf16[4,48,128]{2,1,0:T(8,128)(2,1)S(1)}, u32[]{:S(2)}) copy-start(bf16[4,48,128]{2,1,0:T(8,128)(2,1)S(1)} %collective-permute-done.20.dc) | copy-start | bytes 147460
  122.5 4.2 %collective-permute-start.23 = (bf16[2,48,256]{2,1,0:T(8,128)(2,1)S(1)}, bf16[2,48,256]{2,1,0:T(8,128)(2,1)S(1)}, u32[]{:S(2)}, u32[]{:S(2)}) collective-permute-start(bf16[2,48,256]{2,1,0:T(8,128)(2,1)S(1)} %copy-done.29), channel_id=1, source_target_pairs={{0,3},{1,0},{2,1},{3,2},{4,7},{5,4},{6,5},{7,6},{8,11},{9,8},{10,9... | collective-permute-start | bytes 147464 | tf_op jit(solution)/shard_map/ppermute | solution.py:420
  122.8 3.9 %copy-start.20 = (bf16[4,48,128]{2,1,0:T(8,128)(2,1)}, bf16[4,48,128]{2,1,0:T(8,128)(2,1)S(1)}, u32[]{:S(2)}) copy-start(bf16[4,48,128]{2,1,0:T(8,128)(2,1)S(1)} %collective-permute-done.19.ds_) | copy-start | bytes 147460
  124.9 1.8 %copy-start.22 = (bf16[2,48,256]{2,1,0:T(8,128)(2,1)}, bf16[2,48,256]{2,1,0:T(8,128)(2,1)S(1)}, u32[]{:S(2)}) copy-start(bf16[2,48,256]{2,1,0:T(8,128)(2,1)S(1)} %collective-permute-done.21.r1) | copy-start | bytes 147460
  125.4 1.3 copy-start.24
  (15 other events, 10.0 us)

commit v3 on v2

v3 whole, which is shorter than its diff:
```python
import functools
import math

import jax
import jax.numpy as jnp
import numpy as np
from jax import lax
from jax.experimental import pallas as pl
from jax.experimental.pallas import tpu as pltpu
from jax.sharding import Mesh
from jax.sharding import PartitionSpec as P

CHANNELS = 192
SIDE = 16
PIX = 256
WIDE = 24
EPSILON = 1e-06
GELU_SCALE = 0.7978845608
GELU_CUBIC = 0.044715

F32 = jnp.float32
BF16 = jnp.bfloat16
NT = (((1,), (1,)), ((), ()))
NN = (((1,), (0,)), ((), ()))


def dot(a, b, dims):
    return lax.dot_general(a, b, dims, preferred_element_type=F32)


def placement_tables():
    up = np.zeros((72, 384), np.float32)
    mid = np.zeros((384, 768), np.float32)
    down = np.zeros((72, 384), np.float32)
    for j in range(22):
        if j < 3:
            side, col = 0, 13 + j
        elif j < 19:
            side, col = 1, j - 3
        else:
            side, col = 2, j - 19
        for i in range(3):
            up[i * WIDE + j, 128 * side + 16 * (13 + i) + col - 128] = 1
            down[i * WIDE + j, 128 * side + 16 * i + col] = 1
        for i in range(16):
            block = (1, 0, 2)[side]
            mid[i * WIDE + j, 256 * block + 16 * i + col] = 1
    return up.astype(jnp.bfloat16), mid.astype(jnp.bfloat16), down.astype(jnp.bfloat16)


def column(row):
    n = row.shape[1]
    same = lax.broadcasted_iota(jnp.int32, (n, n), 0) == lax.broadcasted_iota(jnp.int32, (n, n), 1)
    return jnp.sum(jnp.where(same, jnp.broadcast_to(row, (n, n)), 0.0), axis=1, keepdims=True)


def eye(n):
    same = lax.broadcasted_iota(jnp.int32, (n, n), 0) == lax.broadcasted_iota(jnp.int32, (n, n), 1)
    return same.astype(F32).astype(BF16)


def swap_halves(value):
    return pltpu.roll(value.astype(F32), 64, 1)


def low_lanes(shape):
    return lax.broadcasted_iota(jnp.int32, shape, 1) < 64


def pack_pair(natural, other, natural_low):
    shape = natural.shape
    keep = low_lanes(shape) if natural_low else jnp.logical_not(low_lanes(shape))
    return jnp.where(keep, natural.astype(F32), swap_halves(other)).astype(BF16)


def my_owner():
    return 2 * lax.axis_index("chip") + lax.axis_index("core")


def strips_kernel(x_ref, strips_ref):
    odd = lax.axis_index("core")

    @pl.when(odd == 1)
    def _():
        for s in range(8):
            strips_ref[s] = pack_pair(x_ref[s, :, 128:256], x_ref[s + 8, :, 128:256], False)

    @pl.when(odd == 0)
    def _():
        for s in range(8):
            strips_ref[s] = pack_pair(x_ref[s, :, 0:128], x_ref[s + 8, :, 0:128], True)


def pack_tail(value):
    return jnp.concatenate([value[0:96], value[96:192]], axis=1)


def unpack_tail(value):
    return jnp.concatenate([value[:, 0:64], value[:, 64:128]], axis=0)


def sends_kernel(cot_ref, scale_ref, in_ref, w_out_ref, b_ref, gain_ref, dw_ref, spread, *rest):
    outs, taps_ref, small, turned = rest[0:4], rest[4], rest[5], rest[6]
    turned[...] = jnp.zeros((128, 128), F32)
    turned[0:48, 0:49] = dw_ref[...]
    taps_ref[...] = lax.dot_general(
        turned[...].T[0:56], spread[...], NN,
        precision=lax.Precision.HIGHEST, preferred_element_type=F32,
    )
    mine = lax.axis_index("chan")
    scale = column(scale_ref[...])
    small[...] = jnp.zeros((16, 256), F32)
    small[0:1, 0:192] = b_ref[...].astype(F32)
    small[1:2, 0:48] = gain_ref[...].astype(F32)
    tails = []
    for ref in (in_ref, w_out_ref):
        tails.append(pack_tail(ref[:, 128:192].astype(F32)).astype(BF16))
    for j, out in enumerate(outs):
        first = 2 * ((mine + j) & 3)
        for i in range(2):
            out[48 * i : 48 * i + 48] = (cot_ref[first + i].astype(F32) * scale).astype(BF16)
        out[96:288, 0:128] = in_ref[:, 0:128]
        out[96:288, 128:256] = w_out_ref[:, 0:128]
        out[288:384, 0:128] = tails[0]
        out[288:384, 128:256] = tails[1]
        out[384:400] = small[...].astype(BF16)


def gather_tile(table, up_g, mid_g, down_g, t, center, entries):
    rows = pl.ds(48 * t, 48)
    mid_g[rows, 0:256] = table[center]
    mid_g[rows, 256:512] = table[entries[3]]
    mid_g[rows, 512:768] = table[entries[4]]
    for k in range(3):
        up_g[rows, 128 * k : 128 * k + 128] = table[entries[k], :, 128:256]
        down_g[rows, 128 * k : 128 * k + 128] = table[entries[5 + k], :, 0:128]


def build_padded(pad, up_g, mid_g, down_g, up_p, mid_p, down_p):
    pad[0:3] = dot(up_p[...], up_g[...], NT).reshape(3, WIDE, 384)
    pad[3:19] = dot(mid_p[...], mid_g[...], NT).reshape(16, WIDE, 384)
    pad[19:22] = dot(down_p[...], down_g[...], NT).reshape(3, WIDE, 384)


def convolve(pad, taps, result, flip):
    def lane_block(block, carry):
        lanes = pl.ds(pl.multiple_of(block * 128, 128), 128)
        acc = [jnp.zeros((16, 128), F32) for _ in range(16)]
        for b in range(7):
            weights = []
            for a in range(7):
                tap = 7 * a + b
                weights.append(taps[pl.ds(48 - tap if flip else tap, 1), lanes])
            for r in range(22):
                line = pad[r, pl.ds(b, 16), lanes]
                for a in range(7):
                    i = r - a
                    if 0 <= i < 16:
                        acc[i] = acc[i] + line * weights[a]
        for i in range(16):
            result[pl.ds(16 * i, 16), lanes] = acc[i]
        return carry

    lax.fori_loop(0, 3, lane_block, 0)


def fill_edges(table, near_ref, far_ref, below):
    odd = lax.axis_index("core")

    def fill(upper, lower):
        for s in range(8):
            up = upper[s]
            table[s, :, 128:256] = up
            table[s + 8, :, 128:256] = swap_halves(up).astype(BF16)
            down = lower[s]
            table[below + s, :, 0:128] = down
            table[below + 8 + s, :, 0:128] = swap_halves(down).astype(BF16)

    @pl.when(odd == 0)
    def _():
        fill(near_ref, far_ref)

    @pl.when(odd == 1)
    def _():
        fill(far_ref, near_ref)


OFFSETS = (-17, -16, -15, -1, 1, 15, 16, 17)


def mix_kernel(
    own_slots, par_slots, adj, x_ref, par_ref, near_ref, far_ref, taps, up_p, mid_p, down_p,
    owned_ref, pad_out, m0, m1, m2, m3,
    place, table, up_g, mid_g, down_g, pad, result, flat,
):
    me = my_owner()
    odd = lax.axis_index("core")
    mine = lax.axis_index("chan")
    base = 8 * me
    for t in range(8):
        place[t] = 0
    for s in range(16):
        for slots, row in ((own_slots, odd), (par_slots, 1 - odd)):
            t = slots[s] - base

            @pl.when((t >= 0) & (t < 8))
            def _():
                place[t] = 16 + 16 * row + s

    table[pl.ds(16 + 16 * odd, 16)] = x_ref[...]
    table[pl.ds(32 - 16 * odd, 16)] = par_ref[...]
    table[64] = jnp.zeros((48, 256), BF16)

    fill_edges(table, near_ref, far_ref, 48)
    for t in range(8):
        center = place[t]
        entries = [jnp.where(adj[t, k] < 512, center + OFFSETS[k], 64) for k in range(8)]
        gather_tile(table, up_g, mid_g, down_g, t, center, entries)
    owned_ref[...] = mid_g[:, 0:256].reshape(8, 48, 256)
    build_padded(pad, up_g, mid_g, down_g, up_p, mid_p, down_p)
    pad_out[...] = pad[...].astype(BF16)
    convolve(pad, taps, result, False)
    flat[...] = result[...].T.astype(BF16).reshape(8, 48, 256)
    for j, out in enumerate((m0, m1, m2, m3)):
        first = 2 * ((mine + j) & 3)
        out[0] = flat[first]
        out[1] = flat[first + 1]


def turn_kernel(p0, p1, p2, p3, w_in, w_out, in_t, out_t, bias, gain, dbranch):
    mine = lax.axis_index("chan")
    unit = eye(192)
    for j, ref in enumerate((p0, p1, p2, p3)):
        a = (mine + 4 - j) & 3
        for i in range(2):
            dbranch[a, :, 256 * i : 256 * i + 256] = ref[48 * i : 48 * i + 48]
        for full, turned, lanes in ((w_in, in_t, 0), (w_out, out_t, 128)):
            tail = ref[288:384, lanes : lanes + 128].astype(F32)
            whole = jnp.concatenate(
                [
                    ref[96:288, lanes : lanes + 128].astype(F32),
                    unpack_tail(tail),
                ],
                axis=1,
            ).astype(BF16)
            full[j] = whole
            turned[j] = dot(unit, whole, NT).astype(BF16)
        cols = dot(unit, ref[384:400, 0:192], NT)
        bias[j] = jnp.broadcast_to(cols[:, 0:1], (192, 128))
        gain[a] = jnp.broadcast_to(cols[0:48, 1:2], (48, 128))


def across(col_block):
    return jnp.concatenate([col_block] * 4, axis=1)


def mlp_kernel(
    m0, m1, m2, m3, w_in, w_out, in_t, out_t, bias, gain, db_ref,
    g0, g1, g2, g3, mixed_s, back_s, branch_s,
):
    mine = lax.axis_index("chan")
    for j, m_ref in enumerate((m0, m1, m2, m3)):
        a = (mine + 4 - j) & 3
        for i in range(2):
            mixed_s[a, :, 256 * i : 256 * i + 256] = m_ref[i]
    mixed = mixed_s[...].reshape(192, 512).astype(F32)
    dbranch = db_ref[...].reshape(192, 512)
    mean = jnp.sum(mixed, axis=0, keepdims=True) / CHANNELS
    inv = lax.rsqrt(
        jnp.sum(mixed * mixed, axis=0, keepdims=True) / CHANNELS - mean * mean + EPSILON
    )
    x_hat = (mixed - mean) * inv
    gain_full = across(gain[...].reshape(192, 128))
    normed = (x_hat * gain_full).astype(BF16)
    branch = jnp.zeros((192, 512), F32)
    dnormed = jnp.zeros((192, 512), F32)
    for j in range(4):
        preact = dot(in_t[j], normed, NN) + across(bias[j])
        square = preact * preact
        tangent = jnp.tanh(GELU_SCALE * (preact + GELU_CUBIC * square * preact))
        half = 0.5 * (1.0 + tangent)
        act = (preact * half).astype(BF16)
        slope = half + 0.5 * preact * (1.0 - tangent * tangent) * (
            GELU_SCALE * (1.0 + 3.0 * GELU_CUBIC * square)
        )
        branch = branch + dot(out_t[j], act, NN)
        pre_grad = (dot(w_out[j], dbranch, NN) * slope).astype(BF16)
        dnormed = dnormed + dot(w_in[j], pre_grad, NN)
        packet = (g0, g3, g2, g1)[j]
        for grad, lanes in (
            (dot(normed, pre_grad, NT), slice(0, 128)),
            (dot(act, dbranch, NT), slice(128, 256)),
        ):
            packet[96:288, lanes] = grad[:, 0:128].astype(BF16)
            packet[288:384, lanes] = pack_tail(grad[:, 128:192]).astype(BF16)
    xhat_grad = dnormed * gain_full
    first = jnp.sum(xhat_grad, axis=0, keepdims=True) / CHANNELS
    second = jnp.sum(xhat_grad * x_hat, axis=0, keepdims=True) / CHANNELS
    dmixed = (inv * (xhat_grad - first - x_hat * second)).astype(BF16)
    back_s[...] = dmixed.reshape(4, 48, 512)
    branch_s[...] = branch.astype(BF16).reshape(4, 48, 512)
    for j, g_ref in enumerate((g0, g1, g2, g3)):
        a = (mine + j) & 3
        for i in range(2):
            g_ref[48 * i : 48 * i + 48] = back_s[a, :, 256 * i : 256 * i + 256]
            g_ref[384 + 48 * i : 432 + 48 * i] = branch_s[a, :, 256 * i : 256 * i + 256]


def land_kernel(g0, g1, g2, g3, grad_ref):
    mine = lax.axis_index("chan")
    for j, ref in enumerate((g0, g1, g2, g3)):
        first = 2 * ((mine + 4 - j) & 3)
        for i in range(2):
            grad_ref[first + i] = ref[48 * i : 48 * i + 48]


BLOCKS = tuple(
    (64 * q + 32 * h, 64 * q + 32 * h + 32, q, 32 * h) for q in range(9) for h in range(2)
)


def pieces_kernel(
    g0, g1, g2, g3, grad_ref, pad_ref, fold, out_ref, pad, grad_t, sums, total, rows
):
    pad[...] = pad_ref[...].astype(F32)
    grad_t[...] = grad_ref[...].reshape(384, 256).astype(F32).T
    sums[...] = jnp.zeros((64, 384), F32)

    def lane_block(block, carry):
        lanes = pl.ds(pl.multiple_of(block * 128, 128), 128)
        lines = [grad_t[pl.ds(16 * i, 16), lanes] for i in range(16)]
        for b in range(7):
            acc = [jnp.zeros((16, 128), F32) for _ in range(7)]
            for r in range(22):
                line = pad[r, pl.ds(b, 16), lanes]
                for a in range(7):
                    i = r - a
                    if 0 <= i < 16:
                        acc[a] = acc[a] + line * lines[i]
            for a in range(7):
                sums[pl.ds(7 * a + b, 1), lanes] = jnp.sum(acc[a], axis=0, keepdims=True)
        return carry

    lax.fori_loop(0, 3, lane_block, 0)
    total[...] = sum(ref[96:384].astype(F32) for ref in (g0, g1, g2, g3))
    rows[...] = jnp.zeros((64, 16, 128), F32)
    for lo, hi, q, d in BLOCKS:
        rows[d : d + hi - lo, q, :] = total[lo % 288 : lo % 288 + hi - lo, pl.ds(128 * (lo // 288), 128)]
    rows[:, 9, :] = lax.dot_general(
        sums[...], fold[...], NN, precision=lax.Precision.HIGHEST, preferred_element_type=F32
    )
    out_ref[...] = rows[...].astype(BF16)


def edges_kernel(own_ref, par_ref, edge_ref):
    odd = lax.axis_index("core")

    @pl.when(odd == 1)
    def _():
        for t in range(8):
            edge_ref[t] = pack_pair(par_ref[t, :, 128:256], own_ref[t, :, 128:256], False)

    @pl.when(odd == 0)
    def _():
        for t in range(8):
            edge_ref[t] = pack_pair(own_ref[t, :, 0:128], par_ref[t, :, 0:128], True)


def total_kernel(factor, in_ref, out_ref):
    total = jnp.sum(in_ref[...].astype(F32), axis=0, keepdims=True) * factor
    out_ref[...] = jnp.broadcast_to(total, in_ref.shape).astype(out_ref.dtype)


def finish_kernel(in_ref, dw_ref, w1_ref, w2_ref, rows, flat):
    rows[...] = in_ref[...].astype(F32)
    for q in range(9):
        flat[64 * q : 64 * q + 64] = rows[:, q, :]
    for out, row in ((w1_ref, 0), (w2_ref, 288)):
        out[:, 0:128] = flat[row : row + 192]
        out[:, 128:192] = unpack_tail(flat[row + 192 : row + 288])
    dw_ref[...] = rows[:, 9, :].T[0:48, 0:49]


def unmix_kernel(
    adj, grad_ref, par_ref, near_ref, far_ref, cot_ref, taps, up_p, mid_p, down_p,
    owned_ref, scale_ref, r0, r1, r2, r3,
    out_ref, gin_ref,
    table, up_g, mid_g, down_g, pad, result,
):
    me = my_owner()
    odd = lax.axis_index("core")
    mine = lax.axis_index("chan")
    start = 16 * (me // 2) - 16
    table[pl.ds(16 + 8 * odd, 8)] = grad_ref[...]
    table[pl.ds(24 - 8 * odd, 8)] = par_ref[...]
    table[48] = jnp.zeros((48, 256), BF16)
    fill_edges(table, near_ref, far_ref, 32)
    for t in range(8):
        center = 16 + 8 * odd + t
        entries = [jnp.where(adj[t, k] < 512, adj[t, k] - start, 48) for k in range(8)]
        gather_tile(table, up_g, mid_g, down_g, t, center, entries)
    build_padded(pad, up_g, mid_g, down_g, up_p, mid_p, down_p)
    convolve(pad, taps, result, True)
    back = result[...].T.reshape(8, 48, 256)
    gin_ref[...] = (cot_ref[...].astype(F32) + back).astype(BF16)
    scale = column(scale_ref[...])
    for j, ref in enumerate((r0, r1, r2, r3)):
        first = 2 * ((mine + 4 - j) & 3)
        for i in range(2):
            out_ref[first + i] = (
                owned_ref[first + i].astype(F32) + scale * ref[384 + 48 * i : 432 + 48 * i].astype(F32)
            ).astype(BF16)


def call(kernel, shapes, scratch=(), smem=0, n_in=0, name=None, near=()):
    vmem = pl.BlockSpec(memory_space=pltpu.VMEM)
    scalar = pl.BlockSpec(memory_space=pltpu.SMEM)
    many = isinstance(shapes, (list, tuple))
    inner = pl.pallas_call(
        kernel,
        out_shape=shapes,
        in_specs=[scalar] * smem + [vmem] * (n_in - smem),
        out_specs=[vmem] * len(shapes) if many else vmem,
        scratch_shapes=list(scratch),
        compiler_params=pltpu.CompilerParams(vmem_limit_bytes=24 << 20),
        name=name,
    )

    def run(*args):
        held = [
            pltpu.with_memory_space_constraint(a, pltpu.VMEM) if i in near else a
            for i, a in enumerate(args)
        ]
        return inner(*held)

    return run


def shape(*dims, dtype=BF16):
    return jax.ShapeDtypeStruct(dims, dtype)


def held(*dims, dtype=BF16):
    return pltpu.VMEM(dims, dtype)


def along_chan(values):
    got = [values[0]]
    for j in range(1, 4):
        got.append(lax.ppermute(values[j], "chan", [(i, (i + j) % 4) for i in range(4)]))
    return got


def body(
    x_scan, slot_owner, adjacency, cotangent, dw_weight, ln_gain, w_in, b_in, w_out, layer_scale
):
    devices = lax.axis_size("chip") * 2
    up_p, mid_p, down_p = (jnp.asarray(v) for v in placement_tables())
    fold_map = (np.arange(384)[:, None] % 48 == np.arange(128)[None, :]).astype(np.float32)
    fold = jnp.asarray(fold_map)
    spread_map = jnp.asarray(np.ascontiguousarray(fold_map.T))
    scale_row = layer_scale.reshape(1, 48)
    owners = ("chip", "core")

    def after(value, *first):
        return lax.optimization_barrier((value, first))[0]

    def partner(value):
        return lax.ppermute(value, "core", [(0, 1), (1, 0)])

    def next_chip(value):
        pairs = [(i, i + 1 if i & 1 else i - 1) for i in range(devices)]
        return lax.ppermute(value, owners, [p for p in pairs if 0 <= p[1] < devices])

    tile_chunk = held(2, 48, 256)
    par_x = partner(x_scan)
    par_slots = partner(slot_owner)
    strips = call(strips_kernel, held(8, 48, 128), n_in=1, name="strips")(x_scan)
    near = next_chip(strips)
    far = partner(near)
    *sends, taps = call(
        sends_kernel,
        [held(400, 256)] * 4 + [held(56, 384, dtype=F32)],
        scratch=[pltpu.VMEM((16, 256), F32), pltpu.VMEM((128, 128), F32)],
        n_in=8,
        name="sends",
    )(
        cotangent, after(scale_row, strips, par_x, par_slots), w_in, w_out,
        b_in.reshape(1, 192), ln_gain.reshape(1, 48), dw_weight, spread_map,
    )
    all_sends = along_chan(after(sends, near))

    grid_scratch = lambda entries: [
        pltpu.VMEM((entries, 48, 256), BF16),
        pltpu.VMEM((384, 384), BF16),
        pltpu.VMEM((384, 768), BF16),
        pltpu.VMEM((384, 384), BF16),
        pltpu.VMEM((22, WIDE, 384), F32),
        pltpu.VMEM((256, 384), F32),
    ]
    mix = call(
        mix_kernel,
        [shape(8, 48, 256), shape(22, WIDE, 384)] + [tile_chunk] * 4,
        scratch=[pltpu.SMEM((8,), jnp.int32)] + grid_scratch(65) + [pltpu.VMEM((8, 48, 256), BF16)],
        smem=3,
        n_in=11,
        name="mix",
        near=(4, 5, 6, 7),
    )
    owned, padded, *mixed = mix(
        slot_owner, par_slots, adjacency, x_scan, par_x, near, far, taps, up_p, mid_p, down_p
    )
    all_mixed = along_chan(mixed)

    square = held(4, 192, 192)
    turn = call(
        turn_kernel,
        [square] * 4
        + [held(4, 192, 128, dtype=F32), held(4, 48, 128, dtype=F32), held(4, 48, 512)],
        n_in=4,
        name="turn",
        near=(0, 1, 2, 3),
    )
    turned = turn(*after(all_sends, mixed[0]))

    results = call(
        mlp_kernel,
        [held(480, 256)] * 4,
        scratch=[pltpu.VMEM((4, 48, 512), BF16)] * 3,
        n_in=11,
        name="mlp",
        near=range(11),
    )(*all_mixed, *turned)
    all_back = along_chan(results)
    grads = call(land_kernel, held(8, 48, 256), n_in=4, name="land", near=range(4))(*all_back)
    par_grads = partner(grads)
    pieces = call(
        pieces_kernel,
        held(64, 16, 128),
        scratch=[
            pltpu.VMEM((22, WIDE, 384), F32),
            pltpu.VMEM((256, 384), F32),
            pltpu.VMEM((64, 384), F32),
            pltpu.VMEM((288, 256), F32),
            pltpu.VMEM((64, 16, 128), F32),
        ],
        n_in=7,
        name="pieces",
        near=range(5),
    )(*all_back, grads, padded, fold)

    edges = call(edges_kernel, held(8, 48, 128), n_in=2, name="edges", near=(0, 1))(
        after(grads, pieces), par_grads
    )
    near_grads = next_chip(edges)
    arrived = lax.all_to_all(after(pieces, edges), owners, 0, 0, tiled=True)

    factor = 1.0 / math.sqrt(adjacency.shape[0] * devices * PIX)
    arrived, near_grads = lax.optimization_barrier((arrived, near_grads))
    far_grads = partner(near_grads)
    totals = call(
        functools.partial(total_kernel, factor), held(64, 16, 128), n_in=1, name="totals", near=(0,)
    )(arrived)
    spread = lax.all_to_all(totals, owners, 0, 0, tiled=True)

    unmix = call(
        unmix_kernel,
        [shape(8, 48, 256), shape(8, 48, 256)],
        scratch=grid_scratch(49),
        smem=1,
        n_in=16,
        name="unmix",
        near=(1, 2, 3, 4, 12, 13, 14, 15),
    )
    output, grad_in = unmix(
        adjacency, grads, par_grads, near_grads, far_grads,
        cotangent, taps, up_p, mid_p, down_p, owned, after(scale_row, totals), *all_back
    )
    grad_dw, grad_w1, grad_w2 = call(
        finish_kernel,
        [shape(48, 49, dtype=F32), shape(192, 192, dtype=F32), shape(192, 192, dtype=F32)],
        scratch=[pltpu.VMEM((64, 16, 128), F32), pltpu.VMEM((576, 128), F32)],
        n_in=1,
        name="finish",
        near=(0,),
    )(spread)
    return (output, grad_in, grad_dw, grad_w1, grad_w2)


def solution(mesh):
    chips, chan = mesh.devices.shape[0] // 2, mesh.devices.shape[1]
    parts = Mesh(mesh.devices.reshape(chips, 2, chan), ("chip", "core", "chan"))
    tiles = ("chip", "core")
    in_specs = (
        P(tiles, "chan", None),
        P(tiles),
        P(tiles, None),
        P(tiles, "chan", None),
        P("chan", None),
        P("chan"),
        P(None, "chan"),
        P("chan"),
        P("chan", None),
        P("chan"),
    )
    out_specs = (
        P(tiles, "chan", None),
        P(tiles, "chan", None),
        P("chan", None),
        P(None, "chan"),
        P("chan", None),
    )
    return jax.shard_map(body, mesh=parts, in_specs=in_specs, out_specs=out_specs, check_vma=False)
```

time: 137 us -> 100 us (0.73)
  the two profiles are of different devices: /device:TPU:32 before, /device:TPU:1 now
where the time goes in v3:
time: 100 us; the launch traced here: 99.5 us
  starting transfers between devices  40.6 us (41%)
  waiting for transfers between devices  30.4 us (30%)
  Pallas kernels  20.4 us (20%)
  local copies, waits for them, and re-layouts  7.39 us (7%)
    pallas_call x11, Pallas kernels, run(): return inner(*held)  20.4 us
    ppermute x9, waiting for transfers between devices, along_chan(): lax.ppermute(values[j], 'chan', [(i, (i + j) % 4) for i in range(4)])  12.5 us
    all_to_all x1, starting transfers between devices, body(): arrived = lax.all_to_all(after(pieces, edges), owners, 0, 0, tiled=True)  12.2 us
    ppermute x9, starting transfers between devices, along_chan(): lax.ppermute(values[j], 'chan', [(i, (i + j) % 4) for i in range(4)])  11.1 us
    unnamed x34, local copies, waits for them, and re-layouts  6.73 us
    ppermute x5, starting transfers between devices, partner(): return lax.ppermute(value, 'core', [(0, 1), (1, 0)])  6.65 us
    all_to_all x1, waiting for transfers between devices, body(): arrived = lax.all_to_all(after(pieces, edges), owners, 0, 0, tiled=True)  6.25 us
    all_to_all x1, waiting for transfers between devices, body(): spread = lax.all_to_all(totals, owners, 0, 0, tiled=True)  5.83 us
  transfers between devices with their start and end apart: 18, of which 12 were waited for; matrix products, arithmetic and copies ran while one was open for 1% of the time, Pallas kernels for 16%

profile of v3, /device:TPU:1, one launch (start us, length us, event | category | flops | bytes accessed | tf_op | source)
XLA Modules:
  0.0 99.5 jit_solution(4594096890085067372)
XLA Ops:
  0.6 3.3 %collective-permute-start.1 = (bf16[16,48,256]{2,1,0:T(8,128)(2,1)}, bf16[16,48,256]{2,1,0:T(8,128)(2,1)S(1)}, u32[]{:S(2)}, u32[]{:S(2)}) collective-permute-start(bf16[16,48,256]{2,1,0:T(8,128)(2,1)} %x_ref.3), channel_id=1, source_target_pairs={{0,4},{4,0},{1,5},{5,1},{2,6},{6,2},{3,7},{7,3},{8,12},{12,8},{9,1... | collective-permute-start | bytes 1179656 | tf_op jit(solution)/shard_map/ppermute | solution.py:469
  4.0 1.0 copy-done.1
  5.0 0.1 strips.1
  5.1 2.1 %collective-permute-start.2 = (bf16[8,48,128]{2,1,0:T(8,128)(2,1)S(1)}, bf16[8,48,128]{2,1,0:T(8,128)(2,1)S(1)}, u32[]{:S(2)}, u32[]{:S(2)}) collective-permute-start(bf16[8,48,128]{2,1,0:T(8,128)(2,1)S(1)} %strips.1), channel_id=1, source_target_pairs={{4,8},{8,4},{12,16},{16,12},{20,24},{24,20},{28,32},{32,28},{36,40... | collective-permute-start | bytes 294920 | tf_op jit(solution)/shard_map/ppermute | solution.py:473
  7.2 0.7 reshape.20.b_ref
  7.9 0.6 collective-permute-done.par_slots
  8.5 0.9 copy-done.3
  9.4 0.9 copy-done.7
  10.3 0.9 copy-done.9
  11.2 0.9 copy-done.10
  12.1 0.7 copy-done.11
  12.9 0.7 copy-done.13
  13.5 0.7 copy-done.15
  14.2 0.3 sends.1
  14.6 0.8 collective-permute-start.7
  15.4 2.5 %collective-permute-start.8 = (bf16[400,256]{1,0:T(8,128)(2,1)S(1)}, bf16[400,256]{1,0:T(8,128)(2,1)S(1)}, u32[]{:S(2)}, u32[]{:S(2)}) collective-permute-start(bf16[400,256]{1,0:T(8,128)(2,1)S(1)} %get-tuple-element.58), channel_id=1, source_target_pairs={{0,2},{1,3},{2,0},{3,1},{4,6},{5,7},{6,4},{7,5},{8,10},{9,11},{10,... | collective-permute-start | bytes 614408 | tf_op jit(solution)/shard_map/ppermute | solution.py:450
  17.8 1.2 %collective-permute-start.9 = (bf16[400,256]{1,0:T(8,128)(2,1)S(1)}, bf16[400,256]{1,0:T(8,128)(2,1)S(1)}, u32[]{:S(2)}, u32[]{:S(2)}) collective-permute-start(bf16[400,256]{1,0:T(8,128)(2,1)S(1)} %get-tuple-element.59), channel_id=1, source_target_pairs={{0,3},{1,0},{2,1},{3,2},{4,7},{5,4},{6,5},{7,6},{8,11},{9,8},{10,9... | collective-permute-start | bytes 614408 | tf_op jit(solution)/shard_map/ppermute | solution.py:450
  19.0 1.0 %collective-permute-start.3 = (bf16[8,48,128]{2,1,0:T(8,128)(2,1)S(1)}, bf16[8,48,128]{2,1,0:T(8,128)(2,1)S(1)}, u32[]{:S(2)}, u32[]{:S(2)}) collective-permute-start(bf16[8,48,128]{2,1,0:T(8,128)(2,1)S(1)} %collective-permute-done.2.near_ref), channel_id=1, source_target_pairs={{0,4},{4,0},{1,5},{5,1},{2,6},{6,2},{3,7},{7,3},{8,12},{12,8},{9,1... | collective-permute-start | bytes 294920 | tf_op jit(solution)/shard_map/ppermute | solution.py:469
  20.0 0.9 collective-permute-done.3.far_ref
  21.0 5.2 %mix.1 = (bf16[8,48,256]{2,1,0:T(8,128)(2,1)S(1)}, bf16[22,24,384]{2,1,0:T(8,128)(2,1)S(1)}, bf16[2,48,256]{2,1,0:T(8,128)(2,1)S(1)}, bf16[2,48,256]{2,1,0:T(8,1...) custom-call(s32[16]{0:T(128)S(1)} %copy-done.16, s32[16]{0:T(128)S(1)} %collective-permute-done.par_slots, ...), custom_call_target="tpu_custom_call" | custom-call | tf_op jit(solution)/shard_map/mix/pallas_call | solution.py:434
  26.2 0.4 collective-permute-start.4
  26.6 0.6 collective-permute-start.5
  27.2 1.9 %collective-permute-start.6 = (bf16[2,48,256]{2,1,0:T(8,128)(2,1)S(1)}, bf16[2,48,256]{2,1,0:T(8,128)(2,1)S(1)}, u32[]{:S(2)}, u32[]{:S(2)}) collective-permute-start(bf16[2,48,256]{2,1,0:T(8,128)(2,1)S(1)} %get-tuple-element.51), channel_id=1, source_target_pairs={{0,3},{1,0},{2,1},{3,2},{4,7},{5,4},{6,5},{7,6},{8,11},{9,8},{10,9... | collective-permute-start | bytes 147464 | tf_op jit(solution)/shard_map/ppermute | solution.py:450
  29.1 0.6 turn.1
  29.7 0.7 collective-permute-done.4.m1
  30.4 0.6 collective-permute-done.5.m2
  31.0 0.8 collective-permute-done.6.m3
  31.8 2.7 %mlp.1 = (bf16[480,256]{1,0:T(8,128)(2,1)S(1)}, bf16[480,256]{1,0:T(8,128)(2,1)S(1)}, bf16[480,256]{1,0:T(8,128)(2,1)S(1)}, bf16[480,256]{1,0:T(8,128)(2,1)S(1)}) custom-call(bf16[2,48,256]{2,1,0:T(8,128)(2,1)S(1)} %get-tuple-element.48.m0, bf16[2,48,256]{2,1,0:T(8,128)(2,1)S(1)} %collective-permute-done.4.m1, ...), custom_call_target="tpu_custom_call" | custom-call | tf_op jit(solution)/shard_map/mlp/pallas_call | solution.py:434
  34.5 1.3 %collective-permute-start.10 = (bf16[480,256]{1,0:T(8,128)(2,1)S(1)}, bf16[480,256]{1,0:T(8,128)(2,1)S(1)}, u32[]{:S(2)}, u32[]{:S(2)}) collective-permute-start(bf16[480,256]{1,0:T(8,128)(2,1)S(1)} %get-tuple-element.72), channel_id=1, source_target_pairs={{0,1},{1,2},{2,3},{3,0},{4,5},{5,6},{6,7},{7,4},{8,9},{9,10},{10,1... | collective-permute-start | bytes 737288 | tf_op jit(solution)/shard_map/ppermute | solution.py:450
  35.8 2.1 %collective-permute-start.11 = (bf16[480,256]{1,0:T(8,128)(2,1)S(1)}, bf16[480,256]{1,0:T(8,128)(2,1)S(1)}, u32[]{:S(2)}, u32[]{:S(2)}) collective-permute-start(bf16[480,256]{1,0:T(8,128)(2,1)S(1)} %get-tuple-element.73), channel_id=1, source_target_pairs={{0,2},{1,3},{2,0},{3,1},{4,6},{5,7},{6,4},{7,5},{8,10},{9,11},{10,... | collective-permute-start | bytes 737288 | tf_op jit(solution)/shard_map/ppermute | solution.py:450
  37.9 0.4 collective-permute-start.12
  38.3 3.6 %collective-permute-done.10.g1.r1 = bf16[480,256]{1,0:T(8,128)(2,1)S(1)} collective-permute-done((bf16[480,256]{1,0:T(8,128)(2,1)S(1)}, bf16[480,256]{1,0:T(8,128)(2,1)S(1)}, u32[]{:S(2)}, u32[]{:S(2)}) %collective-permute-start.10) | collective-permute-done | bytes 245792 | tf_op jit(solution)/shard_map/ppermute | solution.py:450
  41.9 5.3 %collective-permute-done.11.g2.r2 = bf16[480,256]{1,0:T(8,128)(2,1)S(1)} collective-permute-done((bf16[480,256]{1,0:T(8,128)(2,1)S(1)}, bf16[480,256]{1,0:T(8,128)(2,1)S(1)}, u32[]{:S(2)}, u32[]{:S(2)}) %collective-permute-start.11) | collective-permute-done | bytes 245792 | tf_op jit(solution)/shard_map/ppermute | solution.py:450
  47.2 1.5 %collective-permute-done.12.g3.r3 = bf16[480,256]{1,0:T(8,128)(2,1)S(1)} collective-permute-done((bf16[480,256]{1,0:T(8,128)(2,1)S(1)}, bf16[480,256]{1,0:T(8,128)(2,1)S(1)}, u32[]{:S(2)}, u32[]{:S(2)}) %collective-permute-start.12) | collective-permute-done | bytes 245792 | tf_op jit(solution)/shard_map/ppermute | solution.py:450
  48.7 1.6 %collective-permute-start.13 = (bf16[8,48,256]{2,1,0:T(8,128)(2,1)S(1)}, bf16[8,48,256]{2,1,0:T(8,128)(2,1)S(1)}, u32[]{:S(2)}, u32[]{:S(2)}) collective-permute-start(bf16[8,48,256]{2,1,0:T(8,128)(2,1)S(1)} %land.1.grad_ref.own_ref), channel_id=1, source_target_pairs={{0,4},{4,0},{1,5},{5,1},{2,6},{6,2},{3,7},{7,3},{8,12},{12,8},{9,1... | collective-permute-start | bytes 589832 | tf_op jit(solution)/shard_map/ppermute | solution.py:469
  50.3 3.7 %pieces.1 = bf16[64,16,128]{2,1,0:T(8,128)(2,1)} custom-call(bf16[480,256]{1,0:T(8,128)(2,1)S(1)} %get-tuple-element.71.g0.r0, bf16[480,256]{1,0:T(8,128)(2,1)S(1)} %collective-permute-done.10.g1.r1, bf16[480,256]{1,0:T(8,128)(2,1)S(1)} %collective-permute-done.11.g2.r2, bf16[480,256]{1,0:T(8,128)(2,1)S(1)} %collective-permute-done.12.g3.r3, ...), custom_call_target="tpu_custom_call" | custom-call | tf_op jit(solution)/shard_map/pieces/pallas_call | solution.py:434
  54.1 0.1 edges.1
  54.2 12.2 %all-to-all-start = ((bf16[64,16,128]{2,1,0:T(8,128)(2,1)}), bf16[64,16,128]{2,1,0:T(8,128)(2,1)S(1)}, u32[]{:S(2)}, u32[]{:S(2)}) async-start(bf16[64,16,128]{2,1,0:T(8,128)(2,1)} %pieces.1), calls=%async_computation | async-start | bytes 524288 | tf_op jit(solution)/shard_map/all_to_all | solution.py:556
  66.4 3.5 %collective-permute-start.14 = (bf16[8,48,128]{2,1,0:T(8,128)(2,1)S(1)}, bf16[8,48,128]{2,1,0:T(8,128)(2,1)S(1)}, u32[]{:S(2)}, u32[]{:S(2)}) collective-permute-start(bf16[8,48,128]{2,1,0:T(8,128)(2,1)S(1)} %edges.1), channel_id=1, source_target_pairs={{4,8},{8,4},{12,16},{16,12},{20,24},{24,20},{28,32},{32,28},{36,40... | collective-permute-start | bytes 294920 | tf_op jit(solution)/shard_map/ppermute | solution.py:473
  69.9 3.4 %collective-permute-done.14.near_ref = bf16[8,48,128]{2,1,0:T(8,128)(2,1)S(1)} collective-permute-done((bf16[8,48,128]{2,1,0:T(8,128)(2,1)S(1)}, bf16[8,48,128]{2,1,0:T(8,128)(2,1)S(1)}, u32[]{:S(2)}, u32[]{:S(2)}) %collective-permute-start.14) | collective-permute-done | bytes 98336 | tf_op jit(solution)/shard_map/ppermute | solution.py:473
  73.3 6.3 %all-to-all-done.in_ref = bf16[64,16,128]{2,1,0:T(8,128)(2,1)S(1)} async-done(((bf16[64,16,128]{2,1,0:T(8,128)(2,1)}), bf16[64,16,128]{2,1,0:T(8,128)(2,1)S(1)}, u32[]{:S(2)}, u32[]{:S(2)}) %all-to-all-start) | async-done | bytes 262176 | tf_op jit(solution)/shard_map/all_to_all | solution.py:556
  79.5 0.8 totals.1
  80.3 5.1 %all-to-all-start.1 = ((bf16[64,16,128]{2,1,0:T(8,128)(2,1)}), bf16[64,16,128]{2,1,0:T(8,128)(2,1)S(1)}, u32[]{:S(2)}, u32[]{:S(2)}) async-start(bf16[64,16,128]{2,1,0:T(8,128)(2,1)} %totals.1), calls=%async_computation.1 | async-start | bytes 524288 | tf_op jit(solution)/shard_map/all_to_all | solution.py:564
  85.4 0.5 collective-permute-start.15
  85.9 0.9 collective-permute-done.15.far_ref
  86.9 5.8 %unmix.1 = (bf16[8,48,256]{2,1,0:T(8,128)(2,1)}, bf16[8,48,256]{2,1,0:T(8,128)(2,1)}) custom-call(s32[8,8]{1,0:T(8,128)S(1)} %copy-done.12, bf16[8,48,256]{2,1,0:T(8,128)(2,1)S(1)} %land.1.grad_ref.own_ref, bf16[8,48,256]{2,1,0:T(8,128)(2,1)S(1)} %collective-permute-done.13.par_ref, bf16[8,48,128]{2,1,0:T(8,128)(2,1)S(1)} %collective-permute-done.14.near_ref, ...), custom_call_target="tpu_custom_call" | custom-call | tf_op jit(solution)/shard_map/unmix/pallas_call | solution.py:434
  92.7 5.8 %all-to-all-done.1.in_ref = bf16[64,16,128]{2,1,0:T(8,128)(2,1)S(1)} async-done(((bf16[64,16,128]{2,1,0:T(8,128)(2,1)}), bf16[64,16,128]{2,1,0:T(8,128)(2,1)S(1)}, u32[]{:S(2)}, u32[]{:S(2)}) %all-to-all-start.1) | async-done | bytes 262176 | tf_op jit(solution)/shard_map/all_to_all | solution.py:564
  98.5 1.0 finish.1
  (34 shorter events, 0.2 us)
Async XLA Ops:
  0.6 20.3 %copy-start = (bf16[384,768]{1,0:T(8,128)(2,1)S(1)}, bf16[384,768]{1,0:T(8,128)(2,1)}, u32[]{:S(2)}) copy-start(bf16[384,768]{1,0:T(8,128)(2,1)} %constant.11.clone.mid_p) | copy-start | bytes 1769476
  0.6 7.8 %collective-permute-start.1 = (bf16[16,48,256]{2,1,0:T(8,128)(2,1)}, bf16[16,48,256]{2,1,0:T(8,128)(2,1)S(1)}, u32[]{:S(2)}, u32[]{:S(2)}) collective-permute-start(bf16[16,48,256]{2,1,0:T(8,128)(2,1)} %x_ref.3), channel_id=1, source_target_pairs={{0,4},{4,0},{1,5},{5,1},{2,6},{6,2},{3,7},{7,3},{8,12},{12,8},{9,1... | collective-permute-start | bytes 1179656 | tf_op jit(solution)/shard_map/ppermute | solution.py:469
  4.0 1.0 %copy-start.1 = (bf16[16,48,256]{2,1,0:T(8,128)(2,1)S(1)}, bf16[16,48,256]{2,1,0:T(8,128)(2,1)}, u32[]{:S(2)}) copy-start(bf16[16,48,256]{2,1,0:T(8,128)(2,1)} %x_ref.3) | copy-start | bytes 1179652
  5.1 15.9 %copy-start.2 = (bf16[16,48,256]{2,1,0:T(8,128)(2,1)S(1)}, bf16[16,48,256]{2,1,0:T(8,128)(2,1)}, u32[]{:S(2)}) copy-start(bf16[16,48,256]{2,1,0:T(8,128)(2,1)} %x_ref.3) | copy-start | bytes 1179652
  5.1 9.5 %collective-permute-start.2 = (bf16[8,48,128]{2,1,0:T(8,128)(2,1)S(1)}, bf16[8,48,128]{2,1,0:T(8,128)(2,1)S(1)}, u32[]{:S(2)}, u32[]{:S(2)}) collective-permute-start(bf16[8,48,128]{2,1,0:T(8,128)(2,1)S(1)} %strips.1), channel_id=1, source_target_pairs={{4,8},{8,4},{12,16},{16,12},{20,24},{24,20},{28,32},{32,28},{36,40... | collective-permute-start | bytes 294920 | tf_op jit(solution)/shard_map/ppermute | solution.py:473
  7.1 1.3 %collective-permute-start = (s32[16]{0:T(128)}, s32[16]{0:T(128)S(1)}, u32[]{:S(2)}, u32[]{:S(2)}) collective-permute-start(s32[16]{0:T(128)} %own_slots.1), channel_id=1, source_target_pairs={{0,4},{4,0},{1,5},{5,1},{2,6},{6,2},{3,7},{7,3},{8,12},{12,8},{9,1... | collective-permute-start | bytes 200 | tf_op jit(solution)/shard_map/ppermute | solution.py:469
  8.5 0.9 copy-start.3
  9.4 0.9 copy-start.7
  10.3 0.9 copy-start.9
  11.2 0.9 copy-start.10
  12.1 0.7 copy-start.11
  12.9 0.7 copy-start.13
  13.5 0.7 copy-start.15
  14.2 6.8 %copy-start.5 = (bf16[72,384]{1,0:T(8,128)(2,1)S(1)}, bf16[72,384]{1,0:T(8,128)(2,1)}, u32[]{:S(2)}) copy-start(bf16[72,384]{1,0:T(8,128)(2,1)} %constant.12.clone.down_p) | copy-start | bytes 165892
  14.2 6.8 %copy-start.6 = (bf16[72,384]{1,0:T(8,128)(2,1)S(1)}, bf16[72,384]{1,0:T(8,128)(2,1)}, u32[]{:S(2)}) copy-start(bf16[72,384]{1,0:T(8,128)(2,1)} %constant.10.clone.up_p) | copy-start | bytes 165892
  14.6 6.4 %copy-start.12 = (s32[8,8]{1,0:T(8,128)S(1)}, s32[8,8]{1,0:T(8,128)}, u32[]{:S(2)}) copy-start(s32[8,8]{1,0:T(8,128)} %adj.3) | copy-start | bytes 772
  14.6 6.4 %copy-start.16 = (s32[16]{0:T(128)S(1)}, s32[16]{0:T(128)}, u32[]{:S(2)}) copy-start(s32[16]{0:T(128)} %own_slots.1) | copy-start | bytes 196
  14.6 12.6 %collective-permute-start.7 = (bf16[400,256]{1,0:T(8,128)(2,1)S(1)}, bf16[400,256]{1,0:T(8,128)(2,1)S(1)}, u32[]{:S(2)}, u32[]{:S(2)}) collective-permute-start(bf16[400,256]{1,0:T(8,128)(2,1)S(1)} %get-tuple-element.57), channel_id=1, source_target_pairs={{0,1},{1,2},{2,3},{3,0},{4,5},{5,6},{6,7},{7,4},{8,9},{9,10},{10,1... | collective-permute-start | bytes 614408 | tf_op jit(solution)/shard_map/ppermute | solution.py:450
  15.4 13.7 %collective-permute-start.8 = (bf16[400,256]{1,0:T(8,128)(2,1)S(1)}, bf16[400,256]{1,0:T(8,128)(2,1)S(1)}, u32[]{:S(2)}, u32[]{:S(2)}) collective-permute-start(bf16[400,256]{1,0:T(8,128)(2,1)S(1)} %get-tuple-element.58), channel_id=1, source_target_pairs={{0,2},{1,3},{2,0},{3,1},{4,6},{5,7},{6,4},{7,5},{8,10},{9,11},{10,... | collective-permute-start | bytes 614408 | tf_op jit(solution)/shard_map/ppermute | solution.py:450
  17.8 11.3 %collective-permute-start.9 = (bf16[400,256]{1,0:T(8,128)(2,1)S(1)}, bf16[400,256]{1,0:T(8,128)(2,1)S(1)}, u32[]{:S(2)}, u32[]{:S(2)}) collective-permute-start(bf16[400,256]{1,0:T(8,128)(2,1)S(1)} %get-tuple-element.59), channel_id=1, source_target_pairs={{0,3},{1,0},{2,1},{3,2},{4,7},{5,4},{6,5},{7,6},{8,11},{9,8},{10,9... | collective-permute-start | bytes 614408 | tf_op jit(solution)/shard_map/ppermute | solution.py:450
  19.0 2.0 %collective-permute-start.3 = (bf16[8,48,128]{2,1,0:T(8,128)(2,1)S(1)}, bf16[8,48,128]{2,1,0:T(8,128)(2,1)S(1)}, u32[]{:S(2)}, u32[]{:S(2)}) collective-permute-start(bf16[8,48,128]{2,1,0:T(8,128)(2,1)S(1)} %collective-permute-done.2.near_ref), channel_id=1, source_target_pairs={{0,4},{4,0},{1,5},{5,1},{2,6},{6,2},{3,7},{7,3},{8,12},{12,8},{9,1... | collective-permute-start | bytes 294920 | tf_op jit(solution)/shard_map/ppermute | solution.py:469
  26.2 4.2 %collective-permute-start.4 = (bf16[2,48,256]{2,1,0:T(8,128)(2,1)S(1)}, bf16[2,48,256]{2,1,0:T(8,128)(2,1)S(1)}, u32[]{:S(2)}, u32[]{:S(2)}) collective-permute-start(bf16[2,48,256]{2,1,0:T(8,128)(2,1)S(1)} %get-tuple-element.49), channel_id=1, source_target_pairs={{0,1},{1,2},{2,3},{3,0},{4,5},{5,6},{6,7},{7,4},{8,9},{9,10},{10,1... | collective-permute-start | bytes 147464 | tf_op jit(solution)/shard_map/ppermute | solution.py:450
  26.6 4.5 %collective-permute-start.5 = (bf16[2,48,256]{2,1,0:T(8,128)(2,1)S(1)}, bf16[2,48,256]{2,1,0:T(8,128)(2,1)S(1)}, u32[]{:S(2)}, u32[]{:S(2)}) collective-permute-start(bf16[2,48,256]{2,1,0:T(8,128)(2,1)S(1)} %get-tuple-element.50), channel_id=1, source_target_pairs={{0,2},{1,3},{2,0},{3,1},{4,6},{5,7},{6,4},{7,5},{8,10},{9,11},{10,... | collective-permute-start | bytes 147464 | tf_op jit(solution)/shard_map/ppermute | solution.py:450
  27.2 4.6 %collective-permute-start.6 = (bf16[2,48,256]{2,1,0:T(8,128)(2,1)S(1)}, bf16[2,48,256]{2,1,0:T(8,128)(2,1)S(1)}, u32[]{:S(2)}, u32[]{:S(2)}) collective-permute-start(bf16[2,48,256]{2,1,0:T(8,128)(2,1)S(1)} %get-tuple-element.51), channel_id=1, source_target_pairs={{0,3},{1,0},{2,1},{3,2},{4,7},{5,4},{6,5},{7,6},{8,11},{9,8},{10,9... | collective-permute-start | bytes 147464 | tf_op jit(solution)/shard_map/ppermute | solution.py:450
  34.5 7.4 %collective-permute-start.10 = (bf16[480,256]{1,0:T(8,128)(2,1)S(1)}, bf16[480,256]{1,0:T(8,128)(2,1)S(1)}, u32[]{:S(2)}, u32[]{:S(2)}) collective-permute-start(bf16[480,256]{1,0:T(8,128)(2,1)S(1)} %get-tuple-element.72), channel_id=1, source_target_pairs={{0,1},{1,2},{2,3},{3,0},{4,5},{5,6},{6,7},{7,4},{8,9},{9,10},{10,1... | collective-permute-start | bytes 737288 | tf_op jit(solution)/shard_map/ppermute | solution.py:450
  35.8 11.4 %collective-permute-start.11 = (bf16[480,256]{1,0:T(8,128)(2,1)S(1)}, bf16[480,256]{1,0:T(8,128)(2,1)S(1)}, u32[]{:S(2)}, u32[]{:S(2)}) collective-permute-start(bf16[480,256]{1,0:T(8,128)(2,1)S(1)} %get-tuple-element.73), channel_id=1, source_target_pairs={{0,2},{1,3},{2,0},{3,1},{4,6},{5,7},{6,4},{7,5},{8,10},{9,11},{10,... | collective-permute-start | bytes 737288 | tf_op jit(solution)/shard_map/ppermute | solution.py:450
  37.9 10.8 %collective-permute-start.12 = (bf16[480,256]{1,0:T(8,128)(2,1)S(1)}, bf16[480,256]{1,0:T(8,128)(2,1)S(1)}, u32[]{:S(2)}, u32[]{:S(2)}) collective-permute-start(bf16[480,256]{1,0:T(8,128)(2,1)S(1)} %get-tuple-element.74), channel_id=1, source_target_pairs={{0,3},{1,0},{2,1},{3,2},{4,7},{5,4},{6,5},{7,6},{8,11},{9,8},{10,9... | collective-permute-start | bytes 737288 | tf_op jit(solution)/shard_map/ppermute | solution.py:450
  48.7 1.7 %copy-start.8 = (f32[384,128]{1,0:T(8,128)S(1)}, f32[384,128]{1,0:T(8,128)}, u32[]{:S(2)}) copy-start(f32[384,128]{1,0:T(8,128)} %constant.13.clone.fold) | copy-start | bytes 589828
  48.7 5.4 %collective-permute-start.13 = (bf16[8,48,256]{2,1,0:T(8,128)(2,1)S(1)}, bf16[8,48,256]{2,1,0:T(8,128)(2,1)S(1)}, u32[]{:S(2)}, u32[]{:S(2)}) collective-permute-start(bf16[8,48,256]{2,1,0:T(8,128)(2,1)S(1)} %land.1.grad_ref.own_ref), channel_id=1, source_target_pairs={{0,4},{4,0},{1,5},{5,1},{2,6},{6,2},{3,7},{7,3},{8,12},{12,8},{9,1... | collective-permute-start | bytes 589832 | tf_op jit(solution)/shard_map/ppermute | solution.py:469
  54.2 25.3 %all-to-all-start = ((bf16[64,16,128]{2,1,0:T(8,128)(2,1)}), bf16[64,16,128]{2,1,0:T(8,128)(2,1)S(1)}, u32[]{:S(2)}, u32[]{:S(2)}) async-start(bf16[64,16,128]{2,1,0:T(8,128)(2,1)} %pieces.1), calls=%async_computation | async-start | bytes 524288 | tf_op jit(solution)/shard_map/all_to_all | solution.py:556
  66.4 6.9 %collective-permute-start.14 = (bf16[8,48,128]{2,1,0:T(8,128)(2,1)S(1)}, bf16[8,48,128]{2,1,0:T(8,128)(2,1)S(1)}, u32[]{:S(2)}, u32[]{:S(2)}) collective-permute-start(bf16[8,48,128]{2,1,0:T(8,128)(2,1)S(1)} %edges.1), channel_id=1, source_target_pairs={{4,8},{8,4},{12,16},{16,12},{20,24},{24,20},{28,32},{32,28},{36,40... | collective-permute-start | bytes 294920 | tf_op jit(solution)/shard_map/ppermute | solution.py:473
  80.3 6.6 %copy-start.4 = (bf16[8,48,256]{2,1,0:T(8,128)(2,1)S(1)}, bf16[8,48,256]{2,1,0:T(8,128)(2,1)}, u32[]{:S(2)}) copy-start(bf16[8,48,256]{2,1,0:T(8,128)(2,1)} %cot_ref.3) | copy-start | bytes 589828
  80.3 18.2 %all-to-all-start.1 = ((bf16[64,16,128]{2,1,0:T(8,128)(2,1)}), bf16[64,16,128]{2,1,0:T(8,128)(2,1)S(1)}, u32[]{:S(2)}, u32[]{:S(2)}) async-start(bf16[64,16,128]{2,1,0:T(8,128)(2,1)} %totals.1), calls=%async_computation.1 | async-start | bytes 524288 | tf_op jit(solution)/shard_map/all_to_all | solution.py:564
  85.4 1.5 %copy-start.14 = (f32[48]{0:T(128)S(1)}, f32[48]{0:T(128)}, u32[]{:S(2)}) copy-start(f32[48]{0:T(128)} %param.24) | copy-start | bytes 580
  85.4 1.5 %collective-permute-start.15 = (bf16[8,48,128]{2,1,0:T(8,128)(2,1)S(1)}, bf16[8,48,128]{2,1,0:T(8,128)(2,1)S(1)}, u32[]{:S(2)}, u32[]{:S(2)}) collective-permute-start(bf16[8,48,128]{2,1,0:T(8,128)(2,1)S(1)} %collective-permute-done.14.near_ref), channel_id=1, source_target_pairs={{0,4},{4,0},{1,5},{5,1},{2,6},{6,2},{3,7},{7,3},{8,12},{12,8},{9,1... | collective-permute-start | bytes 294920 | tf_op jit(solution)/shard_map/ppermute | solution.py:469

commit v4 on v3

--- a/solution.py
+++ b/solution.py
@@ -77,18 +77,23 @@
     return 2 * lax.axis_index("chip") + lax.axis_index("core")
 
 
-def strips_kernel(x_ref, strips_ref):
+def strips_kernel(x_ref, strips_ref, half, sem):
     odd = lax.axis_index("core")
+    copy = pltpu.make_async_copy(
+        x_ref.at[:, :, pl.ds(pl.multiple_of(128 * odd, 128), 128)], half, sem
+    )
+    copy.start()
+    copy.wait()
 
     @pl.when(odd == 1)
     def _():
         for s in range(8):
-            strips_ref[s] = pack_pair(x_ref[s, :, 128:256], x_ref[s + 8, :, 128:256], False)
+            strips_ref[s] = pack_pair(half[s], half[s + 8], False)
 
     @pl.when(odd == 0)
     def _():
         for s in range(8):
-            strips_ref[s] = pack_pair(x_ref[s, :, 0:128], x_ref[s + 8, :, 0:128], True)
+            strips_ref[s] = pack_pair(half[s], half[s + 8], True)
 
 
 def pack_tail(value):
@@ -256,7 +261,7 @@
 
 def mlp_kernel(
     m0, m1, m2, m3, w_in, w_out, in_t, out_t, bias, gain, db_ref,
-    g0, g1, g2, g3, mixed_s, back_s, branch_s,
+    g0, g1, g2, g3, keep_ref, give_ref, mixed_s, back_s, branch_s, halves,
 ):
     mine = lax.axis_index("chan")
     for j, m_ref in enumerate((m0, m1, m2, m3)):
@@ -286,13 +291,12 @@
         branch = branch + dot(out_t[j], act, NN)
         pre_grad = (dot(w_out[j], dbranch, NN) * slope).astype(BF16)
         dnormed = dnormed + dot(w_in[j], pre_grad, NN)
-        packet = (g0, g3, g2, g1)[j]
-        for grad, lanes in (
-            (dot(normed, pre_grad, NT), slice(0, 128)),
-            (dot(act, dbranch, NT), slice(128, 256)),
-        ):
-            packet[96:288, lanes] = grad[:, 0:128].astype(BF16)
-            packet[288:384, lanes] = pack_tail(grad[:, 128:192]).astype(BF16)
+        for side, grad in enumerate((dot(normed, pre_grad, NT), dot(act, dbranch, NT))):
+            halves[side, j, 0:192] = grad[:, 0:128].astype(BF16)
+            halves[side, j, 192:288] = pack_tail(grad[:, 128:192]).astype(BF16)
+    core = lax.axis_index("core")
+    keep_ref[...] = halves[core]
+    give_ref[...] = halves[1 - core]
     xhat_grad = dnormed * gain_full
     first = jnp.sum(xhat_grad, axis=0, keepdims=True) / CHANNELS
     second = jnp.sum(xhat_grad * x_hat, axis=0, keepdims=True) / CHANNELS
@@ -303,7 +307,7 @@
         a = (mine + j) & 3
         for i in range(2):
             g_ref[48 * i : 48 * i + 48] = back_s[a, :, 256 * i : 256 * i + 256]
-            g_ref[384 + 48 * i : 432 + 48 * i] = branch_s[a, :, 256 * i : 256 * i + 256]
+            g_ref[96 + 48 * i : 144 + 48 * i] = branch_s[a, :, 256 * i : 256 * i + 256]
 
 
 def land_kernel(g0, g1, g2, g3, grad_ref):
@@ -314,14 +318,16 @@
             grad_ref[first + i] = ref[48 * i : 48 * i + 48]
 
 
-BLOCKS = tuple(
-    (64 * q + 32 * h, 64 * q + 32 * h + 32, q, 32 * h) for q in range(9) for h in range(2)
-)
-
-
-def pieces_kernel(
-    g0, g1, g2, g3, grad_ref, pad_ref, fold, out_ref, pad, grad_t, sums, total, rows
-):
+def merge_kernel(t0, t1, t2, t3, keep_ref, got_ref, g0, g1, g2, g3):
+    for j, (tiles, out) in enumerate(zip((t0, t1, t2, t3), (g0, g1, g2, g3))):
+        below = (4 - j) & 3
+        both = (keep_ref[below].astype(F32) + got_ref[below].astype(F32)).astype(BF16)
+        out[0:192] = tiles[...]
+        out[192:336, 0:128] = both[0:144]
+        out[192:336, 128:256] = both[144:288]
+
+
+def taps_kernel(grad_ref, pad_ref, fold, out_ref, pad, grad_t, sums):
     pad[...] = pad_ref[...].astype(F32)
     grad_t[...] = grad_ref[...].reshape(384, 256).astype(F32).T
     sums[...] = jnp.zeros((64, 384), F32)
@@ -342,13 +348,21 @@
         return carry
 
     lax.fori_loop(0, 3, lane_block, 0)
-    total[...] = sum(ref[96:384].astype(F32) for ref in (g0, g1, g2, g3))
-    rows[...] = jnp.zeros((64, 16, 128), F32)
-    for lo, hi, q, d in BLOCKS:
-        rows[d : d + hi - lo, q, :] = total[lo % 288 : lo % 288 + hi - lo, pl.ds(128 * (lo // 288), 128)]
-    rows[:, 9, :] = lax.dot_general(
+    out_ref[...] = lax.dot_general(
         sums[...], fold[...], NN, precision=lax.Precision.HIGHEST, preferred_element_type=F32
     )
+
+
+def pieces_kernel(g0, g1, g2, g3, taps_ref, out_ref, total, rows):
+    for half in range(2):
+        lanes = slice(128 * half, 128 * half + 128)
+        total[144 * half : 144 * half + 144] = sum(
+            ref[192:336, lanes].astype(F32) for ref in (g0, g1, g2, g3)
+        )
+    total[288:352] = taps_ref[...]
+    rows[...] = jnp.zeros((32, 16, 128), F32)
+    for q in range(11):
+        rows[:, q, :] = total[32 * q : 32 * q + 32]
     out_ref[...] = rows[...].astype(BF16)
 
 
@@ -371,14 +385,17 @@
     out_ref[...] = jnp.broadcast_to(total, in_ref.shape).astype(out_ref.dtype)
 
 
-def finish_kernel(in_ref, dw_ref, w1_ref, w2_ref, rows, flat):
-    rows[...] = in_ref[...].astype(F32)
-    for q in range(9):
-        flat[64 * q : 64 * q + 64] = rows[:, q, :]
-    for out, row in ((w1_ref, 0), (w2_ref, 288)):
-        out[:, 0:128] = flat[row : row + 192]
-        out[:, 128:192] = unpack_tail(flat[row + 192 : row + 288])
-    dw_ref[...] = rows[:, 9, :].T[0:48, 0:49]
+def finish_kernel(in_ref, other_ref, dw_ref, w1_ref, w2_ref, rows, flat):
+    core = lax.axis_index("core")
+    for ref, side in ((in_ref, core), (other_ref, 1 - core)):
+        rows[...] = ref[...].astype(F32)
+        for q in range(11):
+            flat[side, 32 * q : 32 * q + 32] = rows[:, q, :]
+    for out, side in ((w1_ref, 0), (w2_ref, 1)):
+        out[:, 0:128] = flat[side, 0:192]
+        out[:, 128:192] = unpack_tail(flat[side, 192:288])
+    dw = flat[0, 288:352] + flat[1, 288:352]
+    dw_ref[...] = dw.T[0:48, 0:49]
 
 
 def unmix_kernel(
@@ -408,30 +425,59 @@
         first = 2 * ((mine + 4 - j) & 3)
         for i in range(2):
             out_ref[first + i] = (
-                owned_ref[first + i].astype(F32) + scale * ref[384 + 48 * i : 432 + 48 * i].astype(F32)
+                owned_ref[first + i].astype(F32) + scale * ref[96 + 48 * i : 144 + 48 * i].astype(F32)
             ).astype(BF16)
 
 
-def call(kernel, shapes, scratch=(), smem=0, n_in=0, name=None, near=()):
+def fetching(kernel, fetch, n_in):
+    def outer(*refs):
+        inputs, rest = list(refs[:n_in]), refs[n_in:]
+        rest, local, sems = rest[: -len(fetch) - 1], rest[-len(fetch) - 1 : -1], rest[-1]
+        copies = [
+            pltpu.make_async_copy(inputs[i], buf, sems.at[n])
+            for n, (i, buf) in enumerate(zip(fetch, local))
+        ]
+        for copy in copies:
+            copy.start()
+        for copy in copies:
+            copy.wait()
+        for i, buf in zip(fetch, local):
+            inputs[i] = buf
+        kernel(*inputs, *rest)
+
+    return outer
+
+
+def call(kernel, shapes, scratch=(), smem=0, n_in=0, name=None, near=(), fetch=()):
     vmem = pl.BlockSpec(memory_space=pltpu.VMEM)
     scalar = pl.BlockSpec(memory_space=pltpu.SMEM)
     many = isinstance(shapes, (list, tuple))
-    inner = pl.pallas_call(
-        kernel,
-        out_shape=shapes,
-        in_specs=[scalar] * smem + [vmem] * (n_in - smem),
-        out_specs=[vmem] * len(shapes) if many else vmem,
-        scratch_shapes=list(scratch),
-        compiler_params=pltpu.CompilerParams(vmem_limit_bytes=24 << 20),
-        name=name,
-    )
 
     def run(*args):
-        held = [
-            pltpu.with_memory_space_constraint(a, pltpu.VMEM) if i in near else a
-            for i, a in enumerate(args)
+        specs = [
+            pl.BlockSpec(memory_space=pltpu.HBM) if i in fetch else scalar if i < smem else vmem
+            for i in range(n_in)
         ]
-        return inner(*held)
+        scratches = list(scratch)
+        if fetch:
+            scratches += [pltpu.VMEM(args[i].shape, args[i].dtype) for i in fetch]
+            scratches.append(pltpu.SemaphoreType.DMA((len(fetch),)))
+        inner = pl.pallas_call(
+            fetching(kernel, fetch, n_in) if fetch else kernel,
+            out_shape=shapes,
+            in_specs=specs,
+            out_specs=[vmem] * len(shapes) if many else vmem,
+            scratch_shapes=scratches,
+            compiler_params=pltpu.CompilerParams(vmem_limit_bytes=24 << 20),
+            name=name,
+        )
+        spaces = {**{i: pltpu.VMEM for i in near}, **{i: pltpu.HBM for i in fetch}}
+        return inner(
+            *(
+                pltpu.with_memory_space_constraint(a, spaces[i]) if i in spaces else a
+                for i, a in enumerate(args)
+            )
+        )
 
     return run
 
@@ -475,7 +521,14 @@
     tile_chunk = held(2, 48, 256)
     par_x = partner(x_scan)
     par_slots = partner(slot_owner)
-    strips = call(strips_kernel, held(8, 48, 128), n_in=1, name="strips")(x_scan)
+    strips = pl.pallas_call(
+        strips_kernel,
+        out_shape=held(8, 48, 128),
+        in_specs=[pl.BlockSpec(memory_space=pltpu.HBM)],
+        out_specs=pl.BlockSpec(memory_space=pltpu.VMEM),
+        scratch_shapes=[pltpu.VMEM((16, 48, 128), BF16), pltpu.SemaphoreType.DMA(())],
+        name="strips",
+    )(pltpu.with_memory_space_constraint(x_scan, pltpu.HBM))
     near = next_chip(strips)
     far = partner(near)
     *sends, taps = call(
@@ -484,6 +537,7 @@
         scratch=[pltpu.VMEM((16, 256), F32), pltpu.VMEM((128, 128), F32)],
         n_in=8,
         name="sends",
+        fetch=range(8),
     )(
         cotangent, after(scale_row, strips, par_x, par_slots), w_in, w_out,
         b_in.reshape(1, 192), ln_gain.reshape(1, 48), dw_weight, spread_map,
@@ -523,45 +577,53 @@
     )
     turned = turn(*after(all_sends, mixed[0]))
 
-    results = call(
+    *packets, keep, give = call(
         mlp_kernel,
-        [held(480, 256)] * 4,
-        scratch=[pltpu.VMEM((4, 48, 512), BF16)] * 3,
+        [held(192, 256)] * 4 + [held(4, 288, 128)] * 2,
+        scratch=[pltpu.VMEM((4, 48, 512), BF16)] * 3 + [pltpu.VMEM((2, 4, 288, 128), BF16)],
         n_in=11,
         name="mlp",
         near=range(11),
     )(*all_mixed, *turned)
-    all_back = along_chan(results)
+    packets = call(
+        merge_kernel, [held(336, 256)] * 4, n_in=6, name="merge", near=range(6)
+    )(*packets, keep, partner(give))
+    all_back = along_chan(packets)
     grads = call(land_kernel, held(8, 48, 256), n_in=4, name="land", near=range(4))(*all_back)
     par_grads = partner(grads)
-    pieces = call(
-        pieces_kernel,
-        held(64, 16, 128),
+    tap_sums = call(
+        taps_kernel,
+        held(64, 128, dtype=F32),
         scratch=[
             pltpu.VMEM((22, WIDE, 384), F32),
             pltpu.VMEM((256, 384), F32),
             pltpu.VMEM((64, 384), F32),
-            pltpu.VMEM((288, 256), F32),
-            pltpu.VMEM((64, 16, 128), F32),
         ],
-        n_in=7,
+        n_in=3,
+        name="tap_sums",
+        near=(0,),
+    )(grads, padded, fold)
+    edges = call(edges_kernel, held(8, 48, 128), n_in=2, name="edges", near=(0, 1))(
+        after(grads, tap_sums), par_grads
+    )
+    near_grads = next_chip(edges)
+    pieces = call(
+        pieces_kernel,
+        held(32, 16, 128),
+        scratch=[pltpu.VMEM((352, 128), F32), pltpu.VMEM((32, 16, 128), F32)],
+        n_in=5,
         name="pieces",
         near=range(5),
-    )(*all_back, grads, padded, fold)
-
-    edges = call(edges_kernel, held(8, 48, 128), n_in=2, name="edges", near=(0, 1))(
-        after(grads, pieces), par_grads
-    )
-    near_grads = next_chip(edges)
-    arrived = lax.all_to_all(after(pieces, edges), owners, 0, 0, tiled=True)
+    )(*all_back, tap_sums)
+    arrived = lax.all_to_all(after(pieces, edges), "chip", 0, 0, tiled=True)
+    arrived, near_grads = lax.optimization_barrier((arrived, near_grads))
 
     factor = 1.0 / math.sqrt(adjacency.shape[0] * devices * PIX)
-    arrived, near_grads = lax.optimization_barrier((arrived, near_grads))
     far_grads = partner(near_grads)
     totals = call(
-        functools.partial(total_kernel, factor), held(64, 16, 128), n_in=1, name="totals", near=(0,)
+        functools.partial(total_kernel, factor), held(32, 16, 128), n_in=1, name="totals", near=(0,)
     )(arrived)
-    spread = lax.all_to_all(totals, owners, 0, 0, tiled=True)
+    spread = lax.all_to_all(totals, "chip", 0, 0, tiled=True)
 
     unmix = call(
         unmix_kernel,
@@ -576,14 +638,15 @@
         adjacency, grads, par_grads, near_grads, far_grads,
         cotangent, taps, up_p, mid_p, down_p, owned, after(scale_row, totals), *all_back
     )
+    spread = after(spread, output)
     grad_dw, grad_w1, grad_w2 = call(
         finish_kernel,
         [shape(48, 49, dtype=F32), shape(192, 192, dtype=F32), shape(192, 192, dtype=F32)],
-        scratch=[pltpu.VMEM((64, 16, 128), F32), pltpu.VMEM((576, 128), F32)],
-        n_in=1,
+        scratch=[pltpu.VMEM((32, 16, 128), F32), pltpu.VMEM((2, 352, 128), F32)],
+        n_in=2,
         name="finish",
-        near=(0,),
-    )(spread)
+        near=(0, 1),
+    )(spread, partner(spread))
     return (output, grad_in, grad_dw, grad_w1, grad_w2)
 
 

time: 100 us -> 93.3 us (0.933)
  waiting for transfers between devices: 30.4 us -> 22.3 us
  local copies, waits for them, and re-layouts: 7.39 us -> 1.26 us
  starting transfers between devices: 40.6 us -> 45.9 us
  Pallas kernels: 20.4 us -> 22.7 us
    all_to_all x2, waiting for transfers between devices: 12.1 us -> 3.67 us  [the longest x1 1.95 us: body(): arrived = lax.all_to_all(after(pieces, edges), 'chip', 0, 0, tiled=True)]
    unnamed x34 -> x18, local copies, waits for them, and re-layouts: 6.73 us -> 0.04 us
    ppermute x5 -> x7, starting transfers between devices: 6.65 us -> 10.8 us  [partner(): return lax.ppermute(value, 'core', [(0, 1), (1, 0)])]
    pallas_call x11 -> x13, Pallas kernels: 20.4 us -> 22.7 us  [the longest x12 21.6 us: run(): inner(*(pltpu.with_memory_space_constraint(a, spaces[i]) if i in spaces e...]
    all_to_all x2, starting transfers between devices: 17.2 us -> 19.4 us  [the longest x1 11.6 us: body(): arrived = lax.all_to_all(after(pieces, edges), 'chip', 0, 0, tiled=True)]
    ppermute x9, waiting for transfers between devices: 12.5 us -> 10.5 us  [along_chan(): lax.ppermute(values[j], 'chan', [(i, (i + j) % 4) for i in range(4)])]
    ppermute x9, starting transfers between devices: 11.1 us -> 9.36 us  [along_chan(): lax.ppermute(values[j], 'chan', [(i, (i + j) % 4) for i in range(4)])]
    ppermute x5 -> x7, waiting for transfers between devices: 2.47 us -> 4.11 us  [partner(): return lax.ppermute(value, 'core', [(0, 1), (1, 0)])]
  transfers between devices with their start and end apart: 18 -> 20, of which waited for: 12 -> 14; matrix products, arithmetic and copies ran while one was open for 1% -> 1% of each run, Pallas kernels for 16% -> 19%
where the time goes in v4:
time: 93.3 us; the launch traced here: 93 us
  starting transfers between devices  45.9 us (49%)
  Pallas kernels  22.7 us (24%)
  waiting for transfers between devices  22.3 us (24%)
  local copies, waits for them, and re-layouts  1.26 us (1%)
    pallas_call x12, Pallas kernels, run(): inner(*(pltpu.with_memory_space_constraint(a, spaces[i]) if i in spaces e...  21.6 us
    all_to_all x1, starting transfers between devices, body(): arrived = lax.all_to_all(after(pieces, edges), 'chip', 0, 0, tiled=True)  11.6 us
    ppermute x7, starting transfers between devices, partner(): return lax.ppermute(value, 'core', [(0, 1), (1, 0)])  10.8 us
    ppermute x9, waiting for transfers between devices, along_chan(): lax.ppermute(values[j], 'chan', [(i, (i + j) % 4) for i in range(4)])  10.5 us
    ppermute x9, starting transfers between devices, along_chan(): lax.ppermute(values[j], 'chan', [(i, (i + j) % 4) for i in range(4)])  9.36 us
    all_to_all x1, starting transfers between devices, body(): spread = lax.all_to_all(totals, 'chip', 0, 0, tiled=True)  7.74 us
    ppermute x2, starting transfers between devices, next_chip(): lax.ppermute(value, owners, [p for p in pairs if 0 <= p[1] < devices])  6.44 us
    ppermute x7, waiting for transfers between devices, partner(): return lax.ppermute(value, 'core', [(0, 1), (1, 0)])  4.11 us
  transfers between devices with their start and end apart: 20, of which 14 were waited for; matrix products, arithmetic and copies ran while one was open for 1% of the time, Pallas kernels for 19%

profile of v4, /device:TPU:1, one launch (start us, length us, event | category | flops | bytes accessed | tf_op | source)
XLA Modules:
  0.0 93.0 jit_solution(13952339625001619414)
XLA Ops:
  0.6 0.0 copy-start
  0.6 3.3 %collective-permute-start.1 = (bf16[16,48,256]{2,1,0:T(8,128)(2,1)}, bf16[16,48,256]{2,1,0:T(8,128)(2,1)S(1)}, u32[]{:S(2)}, u32[]{:S(2)}) collective-permute-start(bf16[16,48,256]{2,1,0:T(8,128)(2,1)} %x_ref.3), channel_id=1, source_target_pairs={{0,4},{4,0},{1,5},{5,1},{2,6},{6,2},{3,7},{7,3},{8,12},{12,8},{9,1... | collective-permute-start | bytes 1179656 | tf_op jit(solution)/shard_map/ppermute | solution.py:515
  4.0 1.0 %strips.1 = bf16[8,48,128]{2,1,0:T(8,128)(2,1)S(1)} custom-call(bf16[16,48,256]{2,1,0:T(8,128)(2,1)} %x_ref.3), custom_call_target="tpu_custom_call" | custom-call | tf_op jit(solution)/shard_map/strips/pallas_call | solution.py:524
  5.0 2.1 %collective-permute-start.2 = (bf16[8,48,128]{2,1,0:T(8,128)(2,1)S(1)}, bf16[8,48,128]{2,1,0:T(8,128)(2,1)S(1)}, u32[]{:S(2)}, u32[]{:S(2)}) collective-permute-start(bf16[8,48,128]{2,1,0:T(8,128)(2,1)S(1)} %strips.1), channel_id=1, source_target_pairs={{4,8},{8,4},{12,16},{16,12},{20,24},{24,20},{28,32},{32,28},{36,40... | collective-permute-start | bytes 294920 | tf_op jit(solution)/shard_map/ppermute | solution.py:519
  7.1 0.1 collective-permute-start
  7.2 1.2 %reshape.20.refs_4_ = bf16[1,192]{1,0:T(2,128)(2,1)} reshape(bf16[192]{0:T(256)(128)(2,1)} %param.22) | data formatting | bytes 768 | tf_op jit(solution)/shard_map/reshape | solution.py:543
  8.4 0.0 collective-permute-done.par_slots
  8.4 1.6 %sends.1 = (bf16[400,256]{1,0:T(8,128)(2,1)S(1)}, bf16[400,256]{1,0:T(8,128)(2,1)S(1)}, bf16[400,256]{1,0:T(8,128)(2,1)S(1)}, bf16[400,256]{1,0:T(8,128)(2,1)S(1)}, f32[56,384]{1,0:T(8,128)S(1)}) custom-call(bf16[8,48,256]{2,1,0:T(8,128)(2,1)} %cot_ref.1, f32[1,48]{1,0:T(1,128)} %bitcast.2, bf16[192,192]{1,0:T(8,128)(2,1)} %refs_2_.1, ...), custom_call_target="tpu_custom_call" | custom-call | tf_op jit(solution)/shard_map/sends/pallas_call | solution.py:475
  10.1 1.0 %collective-permute-done.2.near_ref = bf16[8,48,128]{2,1,0:T(8,128)(2,1)S(1)} collective-permute-done((bf16[8,48,128]{2,1,0:T(8,128)(2,1)S(1)}, bf16[8,48,128]{2,1,0:T(8,128)(2,1)S(1)}, u32[]{:S(2)}, u32[]{:S(2)}) %collective-permute-start.2) | collective-permute-done | bytes 98336 | tf_op jit(solution)/shard_map/ppermute | solution.py:519
  11.1 2.3 %collective-permute-start.8 = (bf16[400,256]{1,0:T(8,128)(2,1)S(1)}, bf16[400,256]{1,0:T(8,128)(2,1)S(1)}, u32[]{:S(2)}, u32[]{:S(2)}) collective-permute-start(bf16[400,256]{1,0:T(8,128)(2,1)S(1)} %get-tuple-element.65), channel_id=1, source_target_pairs={{0,2},{1,3},{2,0},{3,1},{4,6},{5,7},{6,4},{7,5},{8,10},{9,11},{10,... | collective-permute-start | bytes 614408 | tf_op jit(solution)/shard_map/ppermute | solution.py:496
  13.4 1.2 %collective-permute-start.9 = (bf16[400,256]{1,0:T(8,128)(2,1)S(1)}, bf16[400,256]{1,0:T(8,128)(2,1)S(1)}, u32[]{:S(2)}, u32[]{:S(2)}) collective-permute-start(bf16[400,256]{1,0:T(8,128)(2,1)S(1)} %get-tuple-element.66), channel_id=1, source_target_pairs={{0,3},{1,0},{2,1},{3,2},{4,7},{5,4},{6,5},{7,6},{8,11},{9,8},{10,9... | collective-permute-start | bytes 614408 | tf_op jit(solution)/shard_map/ppermute | solution.py:496
  14.5 1.4 %collective-permute-start.3 = (bf16[8,48,128]{2,1,0:T(8,128)(2,1)S(1)}, bf16[8,48,128]{2,1,0:T(8,128)(2,1)S(1)}, u32[]{:S(2)}, u32[]{:S(2)}) collective-permute-start(bf16[8,48,128]{2,1,0:T(8,128)(2,1)S(1)} %collective-permute-done.2.near_ref), channel_id=1, source_target_pairs={{0,4},{4,0},{1,5},{5,1},{2,6},{6,2},{3,7},{7,3},{8,12},{12,8},{9,1... | collective-permute-start | bytes 294920 | tf_op jit(solution)/shard_map/ppermute | solution.py:515
  15.9 0.9 %collective-permute-done.3.far_ref = bf16[8,48,128]{2,1,0:T(8,128)(2,1)S(1)} collective-permute-done((bf16[8,48,128]{2,1,0:T(8,128)(2,1)S(1)}, bf16[8,48,128]{2,1,0:T(8,128)(2,1)S(1)}, u32[]{:S(2)}, u32[]{:S(2)}) %collective-permute-start.3) | collective-permute-done | bytes 98336 | tf_op jit(solution)/shard_map/ppermute | solution.py:515
  16.8 5.2 %mix.1 = (bf16[8,48,256]{2,1,0:T(8,128)(2,1)S(1)}, bf16[22,24,384]{2,1,0:T(8,128)(2,1)S(1)}, bf16[2,48,256]{2,1,0:T(8,128)(2,1)S(1)}, bf16[2,48,256]{2,1,0:T(8,1...) custom-call(s32[16]{0:T(128)S(1)} %copy-done.8, s32[16]{0:T(128)S(1)} %collective-permute-done.par_slots, ...), custom_call_target="tpu_custom_call" | custom-call | tf_op jit(solution)/shard_map/mix/pallas_call | solution.py:475
  22.0 0.4 collective-permute-start.4
  22.4 0.6 collective-permute-start.5
  23.0 0.7 collective-permute-done.7.p1
  23.7 1.2 %collective-permute-start.6 = (bf16[2,48,256]{2,1,0:T(8,128)(2,1)S(1)}, bf16[2,48,256]{2,1,0:T(8,128)(2,1)S(1)}, u32[]{:S(2)}, u32[]{:S(2)}) collective-permute-start(bf16[2,48,256]{2,1,0:T(8,128)(2,1)S(1)} %get-tuple-element.58), channel_id=1, source_target_pairs={{0,3},{1,0},{2,1},{3,2},{4,7},{5,4},{6,5},{7,6},{8,11},{9,8},{10,9... | collective-permute-start | bytes 147464 | tf_op jit(solution)/shard_map/ppermute | solution.py:496
  24.9 0.6 turn.1
  25.5 0.7 collective-permute-done.4.m1
  26.3 0.6 collective-permute-done.5.m2
  26.9 0.8 collective-permute-done.6.m3
  27.7 2.8 %mlp.1 = (bf16[192,256]{1,0:T(8,128)(2,1)S(1)}, bf16[192,256]{1,0:T(8,128)(2,1)S(1)}, bf16[192,256]{1,0:T(8,128)(2,1)S(1)}, bf16[192,256]{1,0:T(8,128)(2,1)S(1)}...) custom-call(bf16[2,48,256]{2,1,0:T(8,128)(2,1)S(1)} %get-tuple-element.55.m0, ...), custom_call_target="tpu_custom_call" | custom-call | tf_op jit(solution)/shard_map/mlp/pallas_call | solution.py:475
  30.4 1.8 %collective-permute-start.10 = (bf16[4,288,128]{2,1,0:T(8,128)(2,1)S(1)}, bf16[4,288,128]{2,1,0:T(8,128)(2,1)S(1)}, u32[]{:S(2)}, u32[]{:S(2)}) collective-permute-start(bf16[4,288,128]{2,1,0:T(8,128)(2,1)S(1)} %get-tuple-element.83), channel_id=1, source_target_pairs={{0,4},{4,0},{1,5},{5,1},{2,6},{6,2},{3,7},{7,3},{8,12},{12,8},{9,1... | collective-permute-start | bytes 884744 | tf_op jit(solution)/shard_map/ppermute | solution.py:515
  32.2 1.2 %collective-permute-done.10.got_ref = bf16[4,288,128]{2,1,0:T(8,128)(2,1)S(1)} collective-permute-done((bf16[4,288,128]{2,1,0:T(8,128)(2,1)S(1)}, bf16[4,288,128]{2,1,0:T(8,128)(2,1)S(1)}, u32[]{:S(2)}, u32[]{:S(2)}) %collective-permute-start.10) | collective-permute-done | bytes 294944 | tf_op jit(solution)/shard_map/ppermute | solution.py:515
  33.4 0.1 merge.1
  33.5 1.3 %collective-permute-start.11 = (bf16[336,256]{1,0:T(8,128)(2,1)S(1)}, bf16[336,256]{1,0:T(8,128)(2,1)S(1)}, u32[]{:S(2)}, u32[]{:S(2)}) collective-permute-start(bf16[336,256]{1,0:T(8,128)(2,1)S(1)} %get-tuple-element.85), channel_id=1, source_target_pairs={{0,1},{1,2},{2,3},{3,0},{4,5},{5,6},{6,7},{7,4},{8,9},{9,10},{10,1... | collective-permute-start | bytes 516104 | tf_op jit(solution)/shard_map/ppermute | solution.py:496
  34.8 2.4 %collective-permute-start.12 = (bf16[336,256]{1,0:T(8,128)(2,1)S(1)}, bf16[336,256]{1,0:T(8,128)(2,1)S(1)}, u32[]{:S(2)}, u32[]{:S(2)}) collective-permute-start(bf16[336,256]{1,0:T(8,128)(2,1)S(1)} %get-tuple-element.86), channel_id=1, source_target_pairs={{0,2},{1,3},{2,0},{3,1},{4,6},{5,7},{6,4},{7,5},{8,10},{9,11},{10,... | collective-permute-start | bytes 516104 | tf_op jit(solution)/shard_map/ppermute | solution.py:496
  37.2 0.1 collective-permute-start.13
  37.3 3.1 %collective-permute-done.11.g1.r1 = bf16[336,256]{1,0:T(8,128)(2,1)S(1)} collective-permute-done((bf16[336,256]{1,0:T(8,128)(2,1)S(1)}, bf16[336,256]{1,0:T(8,128)(2,1)S(1)}, u32[]{:S(2)}, u32[]{:S(2)}) %collective-permute-start.11) | collective-permute-done | bytes 172064 | tf_op jit(solution)/shard_map/ppermute | solution.py:496
  40.4 4.6 %collective-permute-done.12.g2.r2 = bf16[336,256]{1,0:T(8,128)(2,1)S(1)} collective-permute-done((bf16[336,256]{1,0:T(8,128)(2,1)S(1)}, bf16[336,256]{1,0:T(8,128)(2,1)S(1)}, u32[]{:S(2)}, u32[]{:S(2)}) %collective-permute-start.12) | collective-permute-done | bytes 172064 | tf_op jit(solution)/shard_map/ppermute | solution.py:496
  45.0 1.3 %collective-permute-start.14 = (bf16[8,48,256]{2,1,0:T(8,128)(2,1)S(1)}, bf16[8,48,256]{2,1,0:T(8,128)(2,1)S(1)}, u32[]{:S(2)}, u32[]{:S(2)}) collective-permute-start(bf16[8,48,256]{2,1,0:T(8,128)(2,1)S(1)} %land.1.grad_ref.own_ref), channel_id=1, source_target_pairs={{0,4},{4,0},{1,5},{5,1},{2,6},{6,2},{3,7},{7,3},{8,12},{12,8},{9,1... | collective-permute-start | bytes 589832 | tf_op jit(solution)/shard_map/ppermute | solution.py:515
  46.3 2.8 %tap_sums.1.taps_ref = f32[64,128]{1,0:T(8,128)S(1)} custom-call(bf16[8,48,256]{2,1,0:T(8,128)(2,1)S(1)} %land.1.grad_ref.own_ref, bf16[22,24,384]{2,1,0:T(8,128)(2,1)S(1)} %get-tuple-element.88.pad_ref, f32[384,128]{1,0:T(8,128)S(1)} %copy-done.5), custom_call_target="tpu_custom_call" | custom-call | tf_op jit(solution)/shard_map/tap_sums/pallas_call | solution.py:475
  49.1 0.8 pieces.1
  49.9 0.1 edges.1
  50.0 11.6 %all-to-all-start = ((bf16[32,16,128]{2,1,0:T(8,128)(2,1)}), bf16[32,16,128]{2,1,0:T(8,128)(2,1)S(1)}, u32[]{:S(2)}, u32[]{:S(2)}) async-start(bf16[32,16,128]{2,1,0:T(8,128)(2,1)} %pieces.1), calls=%async_computation | async-start | bytes 262144 | tf_op jit(solution)/shard_map/all_to_all | solution.py:618
  61.7 4.4 %collective-permute-start.15 = (bf16[8,48,128]{2,1,0:T(8,128)(2,1)S(1)}, bf16[8,48,128]{2,1,0:T(8,128)(2,1)S(1)}, u32[]{:S(2)}, u32[]{:S(2)}) collective-permute-start(bf16[8,48,128]{2,1,0:T(8,128)(2,1)S(1)} %edges.1), channel_id=1, source_target_pairs={{4,8},{8,4},{12,16},{16,12},{20,24},{24,20},{28,32},{32,28},{36,40... | collective-permute-start | bytes 294920 | tf_op jit(solution)/shard_map/ppermute | solution.py:519
  66.1 3.0 %collective-permute-done.15.near_ref = bf16[8,48,128]{2,1,0:T(8,128)(2,1)S(1)} collective-permute-done((bf16[8,48,128]{2,1,0:T(8,128)(2,1)S(1)}, bf16[8,48,128]{2,1,0:T(8,128)(2,1)S(1)}, u32[]{:S(2)}, u32[]{:S(2)}) %collective-permute-start.15) | collective-permute-done | bytes 98336 | tf_op jit(solution)/shard_map/ppermute | solution.py:519
  69.1 1.9 %all-to-all-done.in_ref = bf16[32,16,128]{2,1,0:T(8,128)(2,1)S(1)} async-done(((bf16[32,16,128]{2,1,0:T(8,128)(2,1)}), bf16[32,16,128]{2,1,0:T(8,128)(2,1)S(1)}, u32[]{:S(2)}, u32[]{:S(2)}) %all-to-all-start) | async-done | bytes 131104 | tf_op jit(solution)/shard_map/all_to_all | solution.py:618
  71.0 0.7 totals.1
  71.7 7.7 %all-to-all-start.1 = ((bf16[32,16,128]{2,1,0:T(8,128)(2,1)}), bf16[32,16,128]{2,1,0:T(8,128)(2,1)S(1)}, u32[]{:S(2)}, u32[]{:S(2)}) async-start(bf16[32,16,128]{2,1,0:T(8,128)(2,1)} %totals.1), calls=%async_computation.1 | async-start | bytes 262144 | tf_op jit(solution)/shard_map/all_to_all | solution.py:626
  79.5 0.8 collective-permute-start.16
  80.3 0.9 %collective-permute-done.16.far_ref = bf16[8,48,128]{2,1,0:T(8,128)(2,1)S(1)} collective-permute-done((bf16[8,48,128]{2,1,0:T(8,128)(2,1)S(1)}, bf16[8,48,128]{2,1,0:T(8,128)(2,1)S(1)}, u32[]{:S(2)}, u32[]{:S(2)}) %collective-permute-start.16) | collective-permute-done | bytes 98336 | tf_op jit(solution)/shard_map/ppermute | solution.py:515
  81.3 5.8 %unmix.1 = (bf16[8,48,256]{2,1,0:T(8,128)(2,1)}, bf16[8,48,256]{2,1,0:T(8,128)(2,1)}) custom-call(s32[8,8]{1,0:T(8,128)S(1)} %copy-done.6, bf16[8,48,256]{2,1,0:T(8,128)(2,1)S(1)} %land.1.grad_ref.own_ref, bf16[8,48,256]{2,1,0:T(8,128)(2,1)S(1)} %collective-permute-done.14.par_ref, bf16[8,48,128]{2,1,0:T(8,128)(2,1)S(1)} %collective-permute-done.15.near_ref, ...), custom_call_target="tpu_custom_call" | custom-call | tf_op jit(solution)/shard_map/unmix/pallas_call | solution.py:475
  87.1 1.7 %all-to-all-done.1.in_ref = bf16[32,16,128]{2,1,0:T(8,128)(2,1)S(1)} async-done(((bf16[32,16,128]{2,1,0:T(8,128)(2,1)}), bf16[32,16,128]{2,1,0:T(8,128)(2,1)S(1)}, u32[]{:S(2)}, u32[]{:S(2)}) %all-to-all-start.1) | async-done | bytes 131104 | tf_op jit(solution)/shard_map/all_to_all | solution.py:626
  88.8 2.1 %collective-permute-start.17 = (bf16[32,16,128]{2,1,0:T(8,128)(2,1)S(1)}, bf16[32,16,128]{2,1,0:T(8,128)(2,1)S(1)}, u32[]{:S(2)}, u32[]{:S(2)}) collective-permute-start(bf16[32,16,128]{2,1,0:T(8,128)(2,1)S(1)} %all-to-all-done.1.in_ref), channel_id=1, source_target_pairs={{0,4},{4,0},{1,5},{5,1},{2,6},{6,2},{3,7},{7,3},{8,12},{12,8},{9,1... | collective-permute-start | bytes 393224 | tf_op jit(solution)/shard_map/ppermute | solution.py:515
  90.9 1.0 %collective-permute-done.17.other_ref = bf16[32,16,128]{2,1,0:T(8,128)(2,1)S(1)} collective-permute-done((bf16[32,16,128]{2,1,0:T(8,128)(2,1)S(1)}, bf16[32,16,128]{2,1,0:T(8,128)(2,1)S(1)}, u32[]{:S(2)}, u32[]{:S(2)}) %collective-permute-start.17) | collective-permute-done | bytes 131104 | tf_op jit(solution)/shard_map/ppermute | solution.py:515
  91.9 1.1 %finish.1 = (f32[48,49]{1,0:T(8,128)}, f32[192,192]{1,0:T(8,128)}, f32[192,192]{1,0:T(8,128)}) custom-call(bf16[32,16,128]{2,1,0:T(8,128)(2,1)S(1)} %all-to-all-done.1.in_ref, bf16[32,16,128]{2,1,0:T(8,128)(2,1)S(1)} %collective-permute-done.17.other_ref), custom_call_target="tpu_custom_call" | custom-call | tf_op jit(solution)/shard_map/finish/pallas_call | solution.py:475
  (24 shorter events, 0.1 us)
Async XLA Ops:
  0.6 16.2 %copy-start = (bf16[384,768]{1,0:T(8,128)(2,1)S(1)}, bf16[384,768]{1,0:T(8,128)(2,1)}, u32[]{:S(2)}) copy-start(bf16[384,768]{1,0:T(8,128)(2,1)} %constant.11.clone.mid_p) | copy-start | bytes 1769476
  0.6 7.8 %collective-permute-start.1 = (bf16[16,48,256]{2,1,0:T(8,128)(2,1)}, bf16[16,48,256]{2,1,0:T(8,128)(2,1)S(1)}, u32[]{:S(2)}, u32[]{:S(2)}) collective-permute-start(bf16[16,48,256]{2,1,0:T(8,128)(2,1)} %x_ref.3), channel_id=1, source_target_pairs={{0,4},{4,0},{1,5},{5,1},{2,6},{6,2},{3,7},{7,3},{8,12},{12,8},{9,1... | collective-permute-start | bytes 1179656 | tf_op jit(solution)/shard_map/ppermute | solution.py:515
  5.0 11.8 %copy-start.1 = (bf16[16,48,256]{2,1,0:T(8,128)(2,1)S(1)}, bf16[16,48,256]{2,1,0:T(8,128)(2,1)}, u32[]{:S(2)}) copy-start(bf16[16,48,256]{2,1,0:T(8,128)(2,1)} %x_ref.3) | copy-start | bytes 1179652
  5.0 6.1 %collective-permute-start.2 = (bf16[8,48,128]{2,1,0:T(8,128)(2,1)S(1)}, bf16[8,48,128]{2,1,0:T(8,128)(2,1)S(1)}, u32[]{:S(2)}, u32[]{:S(2)}) collective-permute-start(bf16[8,48,128]{2,1,0:T(8,128)(2,1)S(1)} %strips.1), channel_id=1, source_target_pairs={{4,8},{8,4},{12,16},{16,12},{20,24},{24,20},{28,32},{32,28},{36,40... | collective-permute-start | bytes 294920 | tf_op jit(solution)/shard_map/ppermute | solution.py:519
  7.1 1.3 %collective-permute-start = (s32[16]{0:T(128)}, s32[16]{0:T(128)S(1)}, u32[]{:S(2)}, u32[]{:S(2)}) collective-permute-start(s32[16]{0:T(128)} %own_slots.1), channel_id=1, source_target_pairs={{0,4},{4,0},{1,5},{5,1},{2,6},{6,2},{3,7},{7,3},{8,12},{12,8},{9,1... | collective-permute-start | bytes 200 | tf_op jit(solution)/shard_map/ppermute | solution.py:515
  8.4 8.4 %copy-start.3 = (bf16[72,384]{1,0:T(8,128)(2,1)S(1)}, bf16[72,384]{1,0:T(8,128)(2,1)}, u32[]{:S(2)}) copy-start(bf16[72,384]{1,0:T(8,128)(2,1)} %constant.12.clone.down_p) | copy-start | bytes 165892
  8.4 8.4 %copy-start.4 = (bf16[72,384]{1,0:T(8,128)(2,1)S(1)}, bf16[72,384]{1,0:T(8,128)(2,1)}, u32[]{:S(2)}) copy-start(bf16[72,384]{1,0:T(8,128)(2,1)} %constant.10.clone.up_p) | copy-start | bytes 165892
  11.1 5.7 %copy-start.6 = (s32[8,8]{1,0:T(8,128)S(1)}, s32[8,8]{1,0:T(8,128)}, u32[]{:S(2)}) copy-start(s32[8,8]{1,0:T(8,128)} %adj.3) | copy-start | bytes 772
  11.1 5.7 %copy-start.8 = (s32[16]{0:T(128)S(1)}, s32[16]{0:T(128)}, u32[]{:S(2)}) copy-start(s32[16]{0:T(128)} %own_slots.1) | copy-start | bytes 196
  11.1 12.6 %collective-permute-start.7 = (bf16[400,256]{1,0:T(8,128)(2,1)S(1)}, bf16[400,256]{1,0:T(8,128)(2,1)S(1)}, u32[]{:S(2)}, u32[]{:S(2)}) collective-permute-start(bf16[400,256]{1,0:T(8,128)(2,1)S(1)} %get-tuple-element.64), channel_id=1, source_target_pairs={{0,1},{1,2},{2,3},{3,0},{4,5},{5,6},{6,7},{7,4},{8,9},{9,10},{10,1... | collective-permute-start | bytes 614408 | tf_op jit(solution)/shard_map/ppermute | solution.py:496
  11.1 13.8 %collective-permute-start.8 = (bf16[400,256]{1,0:T(8,128)(2,1)S(1)}, bf16[400,256]{1,0:T(8,128)(2,1)S(1)}, u32[]{:S(2)}, u32[]{:S(2)}) collective-permute-start(bf16[400,256]{1,0:T(8,128)(2,1)S(1)} %get-tuple-element.65), channel_id=1, source_target_pairs={{0,2},{1,3},{2,0},{3,1},{4,6},{5,7},{6,4},{7,5},{8,10},{9,11},{10,... | collective-permute-start | bytes 614408 | tf_op jit(solution)/shard_map/ppermute | solution.py:496
  13.4 11.6 %collective-permute-start.9 = (bf16[400,256]{1,0:T(8,128)(2,1)S(1)}, bf16[400,256]{1,0:T(8,128)(2,1)S(1)}, u32[]{:S(2)}, u32[]{:S(2)}) collective-permute-start(bf16[400,256]{1,0:T(8,128)(2,1)S(1)} %get-tuple-element.66), channel_id=1, source_target_pairs={{0,3},{1,0},{2,1},{3,2},{4,7},{5,4},{6,5},{7,6},{8,11},{9,8},{10,9... | collective-permute-start | bytes 614408 | tf_op jit(solution)/shard_map/ppermute | solution.py:496
  14.5 2.3 %collective-permute-start.3 = (bf16[8,48,128]{2,1,0:T(8,128)(2,1)S(1)}, bf16[8,48,128]{2,1,0:T(8,128)(2,1)S(1)}, u32[]{:S(2)}, u32[]{:S(2)}) collective-permute-start(bf16[8,48,128]{2,1,0:T(8,128)(2,1)S(1)} %collective-permute-done.2.near_ref), channel_id=1, source_target_pairs={{0,4},{4,0},{1,5},{5,1},{2,6},{6,2},{3,7},{7,3},{8,12},{12,8},{9,1... | collective-permute-start | bytes 294920 | tf_op jit(solution)/shard_map/ppermute | solution.py:515
  22.0 4.2 %collective-permute-start.4 = (bf16[2,48,256]{2,1,0:T(8,128)(2,1)S(1)}, bf16[2,48,256]{2,1,0:T(8,128)(2,1)S(1)}, u32[]{:S(2)}, u32[]{:S(2)}) collective-permute-start(bf16[2,48,256]{2,1,0:T(8,128)(2,1)S(1)} %get-tuple-element.56), channel_id=1, source_target_pairs={{0,1},{1,2},{2,3},{3,0},{4,5},{5,6},{6,7},{7,4},{8,9},{9,10},{10,1... | collective-permute-start | bytes 147464 | tf_op jit(solution)/shard_map/ppermute | solution.py:496
  22.4 4.5 %collective-permute-start.5 = (bf16[2,48,256]{2,1,0:T(8,128)(2,1)S(1)}, bf16[2,48,256]{2,1,0:T(8,128)(2,1)S(1)}, u32[]{:S(2)}, u32[]{:S(2)}) collective-permute-start(bf16[2,48,256]{2,1,0:T(8,128)(2,1)S(1)} %get-tuple-element.57), channel_id=1, source_target_pairs={{0,2},{1,3},{2,0},{3,1},{4,6},{5,7},{6,4},{7,5},{8,10},{9,11},{10,... | collective-permute-start | bytes 147464 | tf_op jit(solution)/shard_map/ppermute | solution.py:496
  23.7 3.9 %collective-permute-start.6 = (bf16[2,48,256]{2,1,0:T(8,128)(2,1)S(1)}, bf16[2,48,256]{2,1,0:T(8,128)(2,1)S(1)}, u32[]{:S(2)}, u32[]{:S(2)}) collective-permute-start(bf16[2,48,256]{2,1,0:T(8,128)(2,1)S(1)} %get-tuple-element.58), channel_id=1, source_target_pairs={{0,3},{1,0},{2,1},{3,2},{4,7},{5,4},{6,5},{7,6},{8,11},{9,8},{10,9... | collective-permute-start | bytes 147464 | tf_op jit(solution)/shard_map/ppermute | solution.py:496
  30.4 3.0 %collective-permute-start.10 = (bf16[4,288,128]{2,1,0:T(8,128)(2,1)S(1)}, bf16[4,288,128]{2,1,0:T(8,128)(2,1)S(1)}, u32[]{:S(2)}, u32[]{:S(2)}) collective-permute-start(bf16[4,288,128]{2,1,0:T(8,128)(2,1)S(1)} %get-tuple-element.83), channel_id=1, source_target_pairs={{0,4},{4,0},{1,5},{5,1},{2,6},{6,2},{3,7},{7,3},{8,12},{12,8},{9,1... | collective-permute-start | bytes 884744 | tf_op jit(solution)/shard_map/ppermute | solution.py:515
  33.5 6.9 %collective-permute-start.11 = (bf16[336,256]{1,0:T(8,128)(2,1)S(1)}, bf16[336,256]{1,0:T(8,128)(2,1)S(1)}, u32[]{:S(2)}, u32[]{:S(2)}) collective-permute-start(bf16[336,256]{1,0:T(8,128)(2,1)S(1)} %get-tuple-element.85), channel_id=1, source_target_pairs={{0,1},{1,2},{2,3},{3,0},{4,5},{5,6},{6,7},{7,4},{8,9},{9,10},{10,1... | collective-permute-start | bytes 516104 | tf_op jit(solution)/shard_map/ppermute | solution.py:496
  34.8 10.2 %collective-permute-start.12 = (bf16[336,256]{1,0:T(8,128)(2,1)S(1)}, bf16[336,256]{1,0:T(8,128)(2,1)S(1)}, u32[]{:S(2)}, u32[]{:S(2)}) collective-permute-start(bf16[336,256]{1,0:T(8,128)(2,1)S(1)} %get-tuple-element.86), channel_id=1, source_target_pairs={{0,2},{1,3},{2,0},{3,1},{4,6},{5,7},{6,4},{7,5},{8,10},{9,11},{10,... | collective-permute-start | bytes 516104 | tf_op jit(solution)/shard_map/ppermute | solution.py:496
  37.2 7.8 %collective-permute-start.13 = (bf16[336,256]{1,0:T(8,128)(2,1)S(1)}, bf16[336,256]{1,0:T(8,128)(2,1)S(1)}, u32[]{:S(2)}, u32[]{:S(2)}) collective-permute-start(bf16[336,256]{1,0:T(8,128)(2,1)S(1)} %get-tuple-element.87), channel_id=1, source_target_pairs={{0,3},{1,0},{2,1},{3,2},{4,7},{5,4},{6,5},{7,6},{8,11},{9,8},{10,9... | collective-permute-start | bytes 516104 | tf_op jit(solution)/shard_map/ppermute | solution.py:496
  45.0 1.3 %copy-start.5 = (f32[384,128]{1,0:T(8,128)S(1)}, f32[384,128]{1,0:T(8,128)}, u32[]{:S(2)}) copy-start(f32[384,128]{1,0:T(8,128)} %constant.13.clone.fold) | copy-start | bytes 589828
  45.0 4.9 %collective-permute-start.14 = (bf16[8,48,256]{2,1,0:T(8,128)(2,1)S(1)}, bf16[8,48,256]{2,1,0:T(8,128)(2,1)S(1)}, u32[]{:S(2)}, u32[]{:S(2)}) collective-permute-start(bf16[8,48,256]{2,1,0:T(8,128)(2,1)S(1)} %land.1.grad_ref.own_ref), channel_id=1, source_target_pairs={{0,4},{4,0},{1,5},{5,1},{2,6},{6,2},{3,7},{7,3},{8,12},{12,8},{9,1... | collective-permute-start | bytes 589832 | tf_op jit(solution)/shard_map/ppermute | solution.py:515
  50.0 21.0 %all-to-all-start = ((bf16[32,16,128]{2,1,0:T(8,128)(2,1)}), bf16[32,16,128]{2,1,0:T(8,128)(2,1)S(1)}, u32[]{:S(2)}, u32[]{:S(2)}) async-start(bf16[32,16,128]{2,1,0:T(8,128)(2,1)} %pieces.1), calls=%async_computation | async-start | bytes 262144 | tf_op jit(solution)/shard_map/all_to_all | solution.py:618
  61.7 7.4 %collective-permute-start.15 = (bf16[8,48,128]{2,1,0:T(8,128)(2,1)S(1)}, bf16[8,48,128]{2,1,0:T(8,128)(2,1)S(1)}, u32[]{:S(2)}, u32[]{:S(2)}) collective-permute-start(bf16[8,48,128]{2,1,0:T(8,128)(2,1)S(1)} %edges.1), channel_id=1, source_target_pairs={{4,8},{8,4},{12,16},{16,12},{20,24},{24,20},{28,32},{32,28},{36,40... | collective-permute-start | bytes 294920 | tf_op jit(solution)/shard_map/ppermute | solution.py:519
  71.7 9.5 %copy-start.2 = (bf16[8,48,256]{2,1,0:T(8,128)(2,1)S(1)}, bf16[8,48,256]{2,1,0:T(8,128)(2,1)}, u32[]{:S(2)}) copy-start(bf16[8,48,256]{2,1,0:T(8,128)(2,1)} %cot_ref.1) | copy-start | bytes 589828
  71.7 17.1 %all-to-all-start.1 = ((bf16[32,16,128]{2,1,0:T(8,128)(2,1)}), bf16[32,16,128]{2,1,0:T(8,128)(2,1)S(1)}, u32[]{:S(2)}, u32[]{:S(2)}) async-start(bf16[32,16,128]{2,1,0:T(8,128)(2,1)} %totals.1), calls=%async_computation.1 | async-start | bytes 262144 | tf_op jit(solution)/shard_map/all_to_all | solution.py:626
  79.5 1.8 %copy-start.7 = (f32[48]{0:T(128)S(1)}, f32[48]{0:T(128)}, u32[]{:S(2)}) copy-start(f32[48]{0:T(128)} %param.24) | copy-start | bytes 580
  79.5 1.8 %collective-permute-start.16 = (bf16[8,48,128]{2,1,0:T(8,128)(2,1)S(1)}, bf16[8,48,128]{2,1,0:T(8,128)(2,1)S(1)}, u32[]{:S(2)}, u32[]{:S(2)}) collective-permute-start(bf16[8,48,128]{2,1,0:T(8,128)(2,1)S(1)} %collective-permute-done.15.near_ref), channel_id=1, source_target_pairs={{0,4},{4,0},{1,5},{5,1},{2,6},{6,2},{3,7},{7,3},{8,12},{12,8},{9,1... | collective-permute-start | bytes 294920 | tf_op jit(solution)/shard_map/ppermute | solution.py:515
  88.8 3.1 %collective-permute-start.17 = (bf16[32,16,128]{2,1,0:T(8,128)(2,1)S(1)}, bf16[32,16,128]{2,1,0:T(8,128)(2,1)S(1)}, u32[]{:S(2)}, u32[]{:S(2)}) collective-permute-start(bf16[32,16,128]{2,1,0:T(8,128)(2,1)S(1)} %all-to-all-done.1.in_ref), channel_id=1, source_target_pairs={{0,4},{4,0},{1,5},{5,1},{2,6},{6,2},{3,7},{7,3},{8,12},{12,8},{9,1... | collective-permute-start | bytes 393224 | tf_op jit(solution)/shard_map/ppermute | solution.py:515

commit v5 on v4

--- a/solution.py
+++ b/solution.py
@@ -142,9 +142,10 @@
 
 
 def build_padded(pad, up_g, mid_g, down_g, up_p, mid_p, down_p):
-    pad[0:3] = dot(up_p[...], up_g[...], NT).reshape(3, WIDE, 384)
-    pad[3:19] = dot(mid_p[...], mid_g[...], NT).reshape(16, WIDE, 384)
-    pad[19:22] = dot(down_p[...], down_g[...], NT).reshape(3, WIDE, 384)
+    for maps, cells, lo, hi in ((up_p, up_g, 0, 72), (mid_p, mid_g, 72, 456), (down_p, down_g, 456, 528)):
+        rows = dot(maps[...], cells[...], NT)
+        for block in range(3):
+            pad[block, lo:hi] = rows[:, 128 * block : 128 * block + 128]
 
 
 def convolve(pad, taps, result, flip):
@@ -157,7 +158,7 @@
                 tap = 7 * a + b
                 weights.append(taps[pl.ds(48 - tap if flip else tap, 1), lanes])
             for r in range(22):
-                line = pad[r, pl.ds(b, 16), lanes]
+                line = pad[block, pl.ds(WIDE * r + b, 16)]
                 for a in range(7):
                     i = r - a
                     if 0 <= i < 16:
@@ -318,13 +319,11 @@
             grad_ref[first + i] = ref[48 * i : 48 * i + 48]
 
 
-def merge_kernel(t0, t1, t2, t3, keep_ref, got_ref, g0, g1, g2, g3):
-    for j, (tiles, out) in enumerate(zip((t0, t1, t2, t3), (g0, g1, g2, g3))):
-        below = (4 - j) & 3
-        both = (keep_ref[below].astype(F32) + got_ref[below].astype(F32)).astype(BF16)
-        out[0:192] = tiles[...]
-        out[192:336, 0:128] = both[0:144]
-        out[192:336, 128:256] = both[144:288]
+def merge_kernel(keep_ref, got_ref, out_ref):
+    mine = lax.axis_index("chan")
+    for j in range(4):
+        both = keep_ref[j].astype(F32) + got_ref[j].astype(F32)
+        out_ref[(mine + 4 - j) & 3] = both.astype(BF16)
 
 
 def taps_kernel(grad_ref, pad_ref, fold, out_ref, pad, grad_t, sums):
@@ -338,7 +337,7 @@
         for b in range(7):
             acc = [jnp.zeros((16, 128), F32) for _ in range(7)]
             for r in range(22):
-                line = pad[r, pl.ds(b, 16), lanes]
+                line = pad[block, pl.ds(WIDE * r + b, 16)]
                 for a in range(7):
                     i = r - a
                     if 0 <= i < 16:
@@ -353,12 +352,8 @@
     )
 
 
-def pieces_kernel(g0, g1, g2, g3, taps_ref, out_ref, total, rows):
-    for half in range(2):
-        lanes = slice(128 * half, 128 * half + 128)
-        total[144 * half : 144 * half + 144] = sum(
-            ref[192:336, lanes].astype(F32) for ref in (g0, g1, g2, g3)
-        )
+def pieces_kernel(parts_ref, taps_ref, out_ref, total, rows):
+    total[0:288] = jnp.sum(parts_ref[...].astype(F32), axis=0)
     total[288:352] = taps_ref[...]
     rows[...] = jnp.zeros((32, 16, 128), F32)
     for q in range(11):
@@ -549,12 +544,12 @@
         pltpu.VMEM((384, 384), BF16),
         pltpu.VMEM((384, 768), BF16),
         pltpu.VMEM((384, 384), BF16),
-        pltpu.VMEM((22, WIDE, 384), F32),
+        pltpu.VMEM((3, 22 * WIDE, 128), F32),
         pltpu.VMEM((256, 384), F32),
     ]
     mix = call(
         mix_kernel,
-        [shape(8, 48, 256), shape(22, WIDE, 384)] + [tile_chunk] * 4,
+        [shape(8, 48, 256), shape(3, 22 * WIDE, 128)] + [tile_chunk] * 4,
         scratch=[pltpu.SMEM((8,), jnp.int32)] + grid_scratch(65) + [pltpu.VMEM((8, 48, 256), BF16)],
         smem=3,
         n_in=11,
@@ -585,17 +580,18 @@
         name="mlp",
         near=range(11),
     )(*all_mixed, *turned)
-    packets = call(
-        merge_kernel, [held(336, 256)] * 4, n_in=6, name="merge", near=range(6)
-    )(*packets, keep, partner(give))
     all_back = along_chan(packets)
+    merged = call(merge_kernel, held(4, 288, 128), n_in=2, name="merge", near=range(2))(
+        keep, partner(give)
+    )
+    partials = lax.all_to_all(merged, "chan", 0, 0, tiled=True)
     grads = call(land_kernel, held(8, 48, 256), n_in=4, name="land", near=range(4))(*all_back)
     par_grads = partner(grads)
     tap_sums = call(
         taps_kernel,
         held(64, 128, dtype=F32),
         scratch=[
-            pltpu.VMEM((22, WIDE, 384), F32),
+            pltpu.VMEM((3, 22 * WIDE, 128), F32),
             pltpu.VMEM((256, 384), F32),
             pltpu.VMEM((64, 384), F32),
         ],
@@ -611,10 +607,10 @@
         pieces_kernel,
         held(32, 16, 128),
         scratch=[pltpu.VMEM((352, 128), F32), pltpu.VMEM((32, 16, 128), F32)],
-        n_in=5,
+        n_in=2,
         name="pieces",
-        near=range(5),
-    )(*all_back, tap_sums)
+        near=range(2),
+    )(partials, tap_sums)
     arrived = lax.all_to_all(after(pieces, edges), "chip", 0, 0, tiled=True)
     arrived, near_grads = lax.optimization_barrier((arrived, near_grads))
 

time: 93.3 us -> 89.5 us (0.959)
  waiting for transfers between devices: 22.3 us -> 16.9 us
  starting transfers between devices: 45.9 us -> 50.9 us
  Pallas kernels: 22.7 us -> 19.3 us
    ppermute x9, waiting for transfers between devices: 10.5 us -> 5.26 us  [along_chan(): lax.ppermute(values[j], 'chan', [(i, (i + j) % 4) for i in range(4)])]
    all_to_all x0 -> x1, starting transfers between devices: none -> 3.45 us  [body(): partials = lax.all_to_all(merged, 'chan', 0, 0, tiled=True)]
    pallas_call x12, Pallas kernels: 21.6 us -> 18.3 us  [run(): inner(*(pltpu.with_memory_space_constraint(a, spaces[i]) if i in spaces e...]
    all_to_all x0 -> x1, waiting for transfers between devices: none -> 1.85 us  [body(): partials = lax.all_to_all(merged, 'chan', 0, 0, tiled=True)]
    ppermute x9, starting transfers between devices: 9.36 us -> 7.57 us  [along_chan(): lax.ppermute(values[j], 'chan', [(i, (i + j) % 4) for i in range(4)])]
    ppermute x7, starting transfers between devices: 10.8 us -> 12.4 us  [partner(): return lax.ppermute(value, 'core', [(0, 1), (1, 0)])]
    ppermute x2, starting transfers between devices: 6.44 us -> 7.77 us  [next_chip(): lax.ppermute(value, owners, [p for p in pairs if 0 <= p[1] < devices])]
    all_to_all x1, waiting for transfers between devices: 1.95 us -> 0.69 us  [body(): arrived = lax.all_to_all(after(pieces, edges), 'chip', 0, 0, tiled=True)]
  transfers between devices with their start and end apart: 20 -> 21, of which waited for: 14 -> 14; matrix products, arithmetic and copies ran while one was open for 1% -> 1% of each run, Pallas kernels for 19% -> 16%
where the time goes in v5:
time: 89.5 us; the launch traced here: 89.1 us
  starting transfers between devices  50.9 us (57%)
  Pallas kernels  19.3 us (22%)
  waiting for transfers between devices  16.9 us (19%)
  local copies, waits for them, and re-layouts  1.26 us (1%)
    pallas_call x12, Pallas kernels, run(): inner(*(pltpu.with_memory_space_constraint(a, spaces[i]) if i in spaces e...  18.3 us
    ppermute x7, starting transfers between devices, partner(): return lax.ppermute(value, 'core', [(0, 1), (1, 0)])  12.4 us
    all_to_all x1, starting transfers between devices, body(): arrived = lax.all_to_all(after(pieces, edges), 'chip', 0, 0, tiled=True)  11.7 us
    all_to_all x1, starting transfers between devices, body(): spread = lax.all_to_all(totals, 'chip', 0, 0, tiled=True)  7.98 us
    ppermute x2, starting transfers between devices, next_chip(): lax.ppermute(value, owners, [p for p in pairs if 0 <= p[1] < devices])  7.77 us
    ppermute x9, starting transfers between devices, along_chan(): lax.ppermute(values[j], 'chan', [(i, (i + j) % 4) for i in range(4)])  7.57 us
    ppermute x9, waiting for transfers between devices, along_chan(): lax.ppermute(values[j], 'chan', [(i, (i + j) % 4) for i in range(4)])  5.26 us
    ppermute x2, waiting for transfers between devices, next_chip(): lax.ppermute(value, owners, [p for p in pairs if 0 <= p[1] < devices])  3.96 us
  transfers between devices with their start and end apart: 21, of which 14 were waited for; matrix products, arithmetic and copies ran while one was open for 1% of the time, Pallas kernels for 16%

profile of v5, /device:TPU:1, one launch (start us, length us, event | category | flops | bytes accessed | tf_op | source)
XLA Modules:
  0.0 89.1 jit_solution(14636576976245902735)
XLA Ops:
  0.6 0.0 copy-start
  0.6 3.3 %collective-permute-start.1 = (bf16[16,48,256]{2,1,0:T(8,128)(2,1)}, bf16[16,48,256]{2,1,0:T(8,128)(2,1)S(1)}, u32[]{:S(2)}, u32[]{:S(2)}) collective-permute-start(bf16[16,48,256]{2,1,0:T(8,128)(2,1)} %x_ref.3), channel_id=1, source_target_pairs={{0,4},{4,0},{1,5},{5,1},{2,6},{6,2},{3,7},{7,3},{8,12},{12,8},{9,1... | collective-permute-start | bytes 1179656 | tf_op jit(solution)/shard_map/ppermute | solution.py:510
  4.0 1.0 %strips.1 = bf16[8,48,128]{2,1,0:T(8,128)(2,1)S(1)} custom-call(bf16[16,48,256]{2,1,0:T(8,128)(2,1)} %x_ref.3), custom_call_target="tpu_custom_call" | custom-call | tf_op jit(solution)/shard_map/strips/pallas_call | solution.py:519
  5.0 0.0 copy-start.1
  5.0 2.1 %collective-permute-start.2 = (bf16[8,48,128]{2,1,0:T(8,128)(2,1)S(1)}, bf16[8,48,128]{2,1,0:T(8,128)(2,1)S(1)}, u32[]{:S(2)}, u32[]{:S(2)}) collective-permute-start(bf16[8,48,128]{2,1,0:T(8,128)(2,1)S(1)} %strips.1), channel_id=1, source_target_pairs={{4,8},{8,4},{12,16},{16,12},{20,24},{24,20},{28,32},{32,28},{36,40... | collective-permute-start | bytes 294920 | tf_op jit(solution)/shard_map/ppermute | solution.py:514
  7.1 0.1 collective-permute-start
  7.2 1.2 %reshape.20.refs_4_ = bf16[1,192]{1,0:T(2,128)(2,1)} reshape(bf16[192]{0:T(256)(128)(2,1)} %param.22) | data formatting | bytes 768 | tf_op jit(solution)/shard_map/reshape | solution.py:538
  8.4 0.0 collective-permute-done.par_slots
  8.4 1.6 %sends.1 = (bf16[400,256]{1,0:T(8,128)(2,1)S(1)}, bf16[400,256]{1,0:T(8,128)(2,1)S(1)}, bf16[400,256]{1,0:T(8,128)(2,1)S(1)}, bf16[400,256]{1,0:T(8,128)(2,1)S(1)}, f32[56,384]{1,0:T(8,128)S(1)}) custom-call(bf16[8,48,256]{2,1,0:T(8,128)(2,1)} %cot_ref.1, f32[1,48]{1,0:T(1,128)} %bitcast.2, bf16[192,192]{1,0:T(8,128)(2,1)} %refs_2_.1, ...), custom_call_target="tpu_custom_call" | custom-call | tf_op jit(solution)/shard_map/sends/pallas_call | solution.py:470
  10.1 1.0 %collective-permute-done.2.near_ref = bf16[8,48,128]{2,1,0:T(8,128)(2,1)S(1)} collective-permute-done((bf16[8,48,128]{2,1,0:T(8,128)(2,1)S(1)}, bf16[8,48,128]{2,1,0:T(8,128)(2,1)S(1)}, u32[]{:S(2)}, u32[]{:S(2)}) %collective-permute-start.2) | collective-permute-done | bytes 98336 | tf_op jit(solution)/shard_map/ppermute | solution.py:514
  11.1 2.3 %collective-permute-start.8 = (bf16[400,256]{1,0:T(8,128)(2,1)S(1)}, bf16[400,256]{1,0:T(8,128)(2,1)S(1)}, u32[]{:S(2)}, u32[]{:S(2)}) collective-permute-start(bf16[400,256]{1,0:T(8,128)(2,1)S(1)} %get-tuple-element.61), channel_id=1, source_target_pairs={{0,2},{1,3},{2,0},{3,1},{4,6},{5,7},{6,4},{7,5},{8,10},{9,11},{10,... | collective-permute-start | bytes 614408 | tf_op jit(solution)/shard_map/ppermute | solution.py:491
  13.4 1.2 %collective-permute-start.9 = (bf16[400,256]{1,0:T(8,128)(2,1)S(1)}, bf16[400,256]{1,0:T(8,128)(2,1)S(1)}, u32[]{:S(2)}, u32[]{:S(2)}) collective-permute-start(bf16[400,256]{1,0:T(8,128)(2,1)S(1)} %get-tuple-element.62), channel_id=1, source_target_pairs={{0,3},{1,0},{2,1},{3,2},{4,7},{5,4},{6,5},{7,6},{8,11},{9,8},{10,9... | collective-permute-start | bytes 614408 | tf_op jit(solution)/shard_map/ppermute | solution.py:491
  14.5 1.4 %collective-permute-start.3 = (bf16[8,48,128]{2,1,0:T(8,128)(2,1)S(1)}, bf16[8,48,128]{2,1,0:T(8,128)(2,1)S(1)}, u32[]{:S(2)}, u32[]{:S(2)}) collective-permute-start(bf16[8,48,128]{2,1,0:T(8,128)(2,1)S(1)} %collective-permute-done.2.near_ref), channel_id=1, source_target_pairs={{0,4},{4,0},{1,5},{5,1},{2,6},{6,2},{3,7},{7,3},{8,12},{12,8},{9,1... | collective-permute-start | bytes 294920 | tf_op jit(solution)/shard_map/ppermute | solution.py:510
  15.9 0.9 %collective-permute-done.3.far_ref = bf16[8,48,128]{2,1,0:T(8,128)(2,1)S(1)} collective-permute-done((bf16[8,48,128]{2,1,0:T(8,128)(2,1)S(1)}, bf16[8,48,128]{2,1,0:T(8,128)(2,1)S(1)}, u32[]{:S(2)}, u32[]{:S(2)}) %collective-permute-start.3) | collective-permute-done | bytes 98336 | tf_op jit(solution)/shard_map/ppermute | solution.py:510
  16.8 3.6 %mix.1 = (bf16[8,48,256]{2,1,0:T(8,128)(2,1)S(1)}, bf16[3,528,128]{2,1,0:T(8,128)(2,1)S(1)}, bf16[2,48,256]{2,1,0:T(8,128)(2,1)S(1)}, bf16[2,48,256]{2,1,0:T(8,1...) custom-call(s32[16]{0:T(128)S(1)} %copy-done.8, s32[16]{0:T(128)S(1)} %collective-permute-done.par_slots, ...), custom_call_target="tpu_custom_call" | custom-call | tf_op jit(solution)/shard_map/mix/pallas_call | solution.py:470
  20.4 0.4 collective-permute-start.4
  20.8 0.6 collective-permute-start.5
  21.4 1.9 %collective-permute-done.7.p1 = bf16[400,256]{1,0:T(8,128)(2,1)S(1)} collective-permute-done((bf16[400,256]{1,0:T(8,128)(2,1)S(1)}, bf16[400,256]{1,0:T(8,128)(2,1)S(1)}, u32[]{:S(2)}, u32[]{:S(2)}) %collective-permute-start.7) | collective-permute-done | bytes 204832 | tf_op jit(solution)/shard_map/ppermute | solution.py:491
  23.3 0.7 collective-permute-done.9.p3
  24.1 0.6 turn.1
  24.7 0.6 collective-permute-done.5.m2
  25.3 1.5 %collective-permute-done.6.m3 = bf16[2,48,256]{2,1,0:T(8,128)(2,1)S(1)} collective-permute-done((bf16[2,48,256]{2,1,0:T(8,128)(2,1)S(1)}, bf16[2,48,256]{2,1,0:T(8,128)(2,1)S(1)}, u32[]{:S(2)}, u32[]{:S(2)}) %collective-permute-start.6) | collective-permute-done | bytes 49184 | tf_op jit(solution)/shard_map/ppermute | solution.py:491
  26.7 2.8 %mlp.1 = (bf16[192,256]{1,0:T(8,128)(2,1)S(1)}, bf16[192,256]{1,0:T(8,128)(2,1)S(1)}, bf16[192,256]{1,0:T(8,128)(2,1)S(1)}, bf16[192,256]{1,0:T(8,128)(2,1)S(1)}...) custom-call(bf16[2,48,256]{2,1,0:T(8,128)(2,1)S(1)} %get-tuple-element.51.m0, ...), custom_call_target="tpu_custom_call" | custom-call | tf_op jit(solution)/shard_map/mlp/pallas_call | solution.py:470
  29.5 1.4 %collective-permute-start.14 = (bf16[4,288,128]{2,1,0:T(8,128)(2,1)S(1)}, bf16[4,288,128]{2,1,0:T(8,128)(2,1)S(1)}, u32[]{:S(2)}, u32[]{:S(2)}) collective-permute-start(bf16[4,288,128]{2,1,0:T(8,128)(2,1)S(1)} %get-tuple-element.79), channel_id=1, source_target_pairs={{0,4},{4,0},{1,5},{5,1},{2,6},{6,2},{3,7},{7,3},{8,12},{12,8},{9,1... | collective-permute-start | bytes 884744 | tf_op jit(solution)/shard_map/ppermute | solution.py:510
  30.9 0.8 collective-permute-start.10
  31.7 2.4 %collective-permute-start.11 = (bf16[192,256]{1,0:T(8,128)(2,1)S(1)}, bf16[192,256]{1,0:T(8,128)(2,1)S(1)}, u32[]{:S(2)}, u32[]{:S(2)}) collective-permute-start(bf16[192,256]{1,0:T(8,128)(2,1)S(1)} %get-tuple-element.76), channel_id=1, source_target_pairs={{0,2},{1,3},{2,0},{3,1},{4,6},{5,7},{6,4},{7,5},{8,10},{9,11},{10,... | collective-permute-start | bytes 294920 | tf_op jit(solution)/shard_map/ppermute | solution.py:491
  34.1 0.8 merge.1
  34.9 3.5 %all-to-all-start = ((bf16[4,288,128]{2,1,0:T(8,128)(2,1)}), bf16[4,288,128]{2,1,0:T(8,128)(2,1)S(1)}, u32[]{:S(2)}, u32[]{:S(2)}) async-start(bf16[4,288,128]{2,1,0:T(8,128)(2,1)} %merge.1), calls=%async_computation | async-start | bytes 589824 | tf_op jit(solution)/shard_map/all_to_all | solution.py:587
  38.3 0.5 collective-permute-done.11.g2.r2
  38.8 0.1 collective-permute-done.12.g3.r3
  38.9 1.2 %collective-permute-start.13 = (bf16[8,48,256]{2,1,0:T(8,128)(2,1)S(1)}, bf16[8,48,256]{2,1,0:T(8,128)(2,1)S(1)}, u32[]{:S(2)}, u32[]{:S(2)}) collective-permute-start(bf16[8,48,256]{2,1,0:T(8,128)(2,1)S(1)} %land.1.grad_ref.own_ref), channel_id=1, source_target_pairs={{0,4},{4,0},{1,5},{5,1},{2,6},{6,2},{3,7},{7,3},{8,12},{12,8},{9,1... | collective-permute-start | bytes 589832 | tf_op jit(solution)/shard_map/ppermute | solution.py:510
  40.1 1.9 %tap_sums.1.taps_ref = f32[64,128]{1,0:T(8,128)S(1)} custom-call(bf16[8,48,256]{2,1,0:T(8,128)(2,1)S(1)} %land.1.grad_ref.own_ref, bf16[3,528,128]{2,1,0:T(8,128)(2,1)S(1)} %get-tuple-element.80.pad_ref, f32[384,128]{1,0:T(8,128)S(1)} %copy-done.5), custom_call_target="tpu_custom_call" | custom-call | tf_op jit(solution)/shard_map/tap_sums/pallas_call | solution.py:470
  42.1 0.1 edges.1
  42.2 1.9 %all-to-all-done.parts_ref = bf16[4,288,128]{2,1,0:T(8,128)(2,1)S(1)} async-done(((bf16[4,288,128]{2,1,0:T(8,128)(2,1)}), bf16[4,288,128]{2,1,0:T(8,128)(2,1)S(1)}, u32[]{:S(2)}, u32[]{:S(2)}) %all-to-all-start) | async-done | bytes 294944 | tf_op jit(solution)/shard_map/all_to_all | solution.py:587
  44.0 0.8 pieces.1
  44.9 11.7 %all-to-all-start.1 = ((bf16[32,16,128]{2,1,0:T(8,128)(2,1)}), bf16[32,16,128]{2,1,0:T(8,128)(2,1)S(1)}, u32[]{:S(2)}, u32[]{:S(2)}) async-start(bf16[32,16,128]{2,1,0:T(8,128)(2,1)} %pieces.1), calls=%async_computation.1 | async-start | bytes 262144 | tf_op jit(solution)/shard_map/all_to_all | solution.py:614
  56.6 5.7 %collective-permute-start.15 = (bf16[8,48,128]{2,1,0:T(8,128)(2,1)S(1)}, bf16[8,48,128]{2,1,0:T(8,128)(2,1)S(1)}, u32[]{:S(2)}, u32[]{:S(2)}) collective-permute-start(bf16[8,48,128]{2,1,0:T(8,128)(2,1)S(1)} %edges.1), channel_id=1, source_target_pairs={{4,8},{8,4},{12,16},{16,12},{20,24},{24,20},{28,32},{32,28},{36,40... | collective-permute-start | bytes 294920 | tf_op jit(solution)/shard_map/ppermute | solution.py:514
  62.3 2.9 %collective-permute-done.15.near_ref = bf16[8,48,128]{2,1,0:T(8,128)(2,1)S(1)} collective-permute-done((bf16[8,48,128]{2,1,0:T(8,128)(2,1)S(1)}, bf16[8,48,128]{2,1,0:T(8,128)(2,1)S(1)}, u32[]{:S(2)}, u32[]{:S(2)}) %collective-permute-start.15) | collective-permute-done | bytes 98336 | tf_op jit(solution)/shard_map/ppermute | solution.py:514
  65.2 0.7 all-to-all-done.1.in_ref
  65.9 0.7 totals.1
  66.6 8.0 %all-to-all-start.2 = ((bf16[32,16,128]{2,1,0:T(8,128)(2,1)}), bf16[32,16,128]{2,1,0:T(8,128)(2,1)S(1)}, u32[]{:S(2)}, u32[]{:S(2)}) async-start(bf16[32,16,128]{2,1,0:T(8,128)(2,1)} %totals.1), calls=%async_computation.2 | async-start | bytes 262144 | tf_op jit(solution)/shard_map/all_to_all | solution.py:622
  74.6 1.9 %collective-permute-start.16 = (bf16[8,48,128]{2,1,0:T(8,128)(2,1)S(1)}, bf16[8,48,128]{2,1,0:T(8,128)(2,1)S(1)}, u32[]{:S(2)}, u32[]{:S(2)}) collective-permute-start(bf16[8,48,128]{2,1,0:T(8,128)(2,1)S(1)} %collective-permute-done.15.near_ref), channel_id=1, source_target_pairs={{0,4},{4,0},{1,5},{5,1},{2,6},{6,2},{3,7},{7,3},{8,12},{12,8},{9,1... | collective-permute-start | bytes 294920 | tf_op jit(solution)/shard_map/ppermute | solution.py:510
  76.6 0.9 %collective-permute-done.16.far_ref = bf16[8,48,128]{2,1,0:T(8,128)(2,1)S(1)} collective-permute-done((bf16[8,48,128]{2,1,0:T(8,128)(2,1)S(1)}, bf16[8,48,128]{2,1,0:T(8,128)(2,1)S(1)}, u32[]{:S(2)}, u32[]{:S(2)}) %collective-permute-start.16) | collective-permute-done | bytes 98336 | tf_op jit(solution)/shard_map/ppermute | solution.py:510
  77.5 4.2 %unmix.1 = (bf16[8,48,256]{2,1,0:T(8,128)(2,1)}, bf16[8,48,256]{2,1,0:T(8,128)(2,1)}) custom-call(s32[8,8]{1,0:T(8,128)S(1)} %copy-done.6, bf16[8,48,256]{2,1,0:T(8,128)(2,1)S(1)} %land.1.grad_ref.own_ref, bf16[8,48,256]{2,1,0:T(8,128)(2,1)S(1)} %collective-permute-done.13.par_ref, bf16[8,48,128]{2,1,0:T(8,128)(2,1)S(1)} %collective-permute-done.15.near_ref, ...), custom_call_target="tpu_custom_call" | custom-call | tf_op jit(solution)/shard_map/unmix/pallas_call | solution.py:470
  81.7 2.2 %all-to-all-done.2.in_ref = bf16[32,16,128]{2,1,0:T(8,128)(2,1)S(1)} async-done(((bf16[32,16,128]{2,1,0:T(8,128)(2,1)}), bf16[32,16,128]{2,1,0:T(8,128)(2,1)S(1)}, u32[]{:S(2)}, u32[]{:S(2)}) %all-to-all-start.2) | async-done | bytes 131104 | tf_op jit(solution)/shard_map/all_to_all | solution.py:622
  84.0 3.1 %collective-permute-start.17 = (bf16[32,16,128]{2,1,0:T(8,128)(2,1)S(1)}, bf16[32,16,128]{2,1,0:T(8,128)(2,1)S(1)}, u32[]{:S(2)}, u32[]{:S(2)}) collective-permute-start(bf16[32,16,128]{2,1,0:T(8,128)(2,1)S(1)} %all-to-all-done.2.in_ref), channel_id=1, source_target_pairs={{0,4},{4,0},{1,5},{5,1},{2,6},{6,2},{3,7},{7,3},{8,12},{12,8},{9,1... | collective-permute-start | bytes 393224 | tf_op jit(solution)/shard_map/ppermute | solution.py:510
  87.0 1.0 %collective-permute-done.17.other_ref = bf16[32,16,128]{2,1,0:T(8,128)(2,1)S(1)} collective-permute-done((bf16[32,16,128]{2,1,0:T(8,128)(2,1)S(1)}, bf16[32,16,128]{2,1,0:T(8,128)(2,1)S(1)}, u32[]{:S(2)}, u32[]{:S(2)}) %collective-permute-start.17) | collective-permute-done | bytes 131104 | tf_op jit(solution)/shard_map/ppermute | solution.py:510
  88.0 1.1 %finish.1 = (f32[48,49]{1,0:T(8,128)}, f32[192,192]{1,0:T(8,128)}, f32[192,192]{1,0:T(8,128)}) custom-call(bf16[32,16,128]{2,1,0:T(8,128)(2,1)S(1)} %all-to-all-done.2.in_ref, bf16[32,16,128]{2,1,0:T(8,128)(2,1)S(1)} %collective-permute-done.17.other_ref), custom_call_target="tpu_custom_call" | custom-call | tf_op jit(solution)/shard_map/finish/pallas_call | solution.py:470
  (26 shorter events, 0.1 us)
Async XLA Ops:
  0.6 16.2 %copy-start = (bf16[384,768]{1,0:T(8,128)(2,1)S(1)}, bf16[384,768]{1,0:T(8,128)(2,1)}, u32[]{:S(2)}) copy-start(bf16[384,768]{1,0:T(8,128)(2,1)} %constant.11.clone.mid_p) | copy-start | bytes 1769476
  0.6 7.8 %collective-permute-start.1 = (bf16[16,48,256]{2,1,0:T(8,128)(2,1)}, bf16[16,48,256]{2,1,0:T(8,128)(2,1)S(1)}, u32[]{:S(2)}, u32[]{:S(2)}) collective-permute-start(bf16[16,48,256]{2,1,0:T(8,128)(2,1)} %x_ref.3), channel_id=1, source_target_pairs={{0,4},{4,0},{1,5},{5,1},{2,6},{6,2},{3,7},{7,3},{8,12},{12,8},{9,1... | collective-permute-start | bytes 1179656 | tf_op jit(solution)/shard_map/ppermute | solution.py:510
  5.0 11.8 %copy-start.1 = (bf16[16,48,256]{2,1,0:T(8,128)(2,1)S(1)}, bf16[16,48,256]{2,1,0:T(8,128)(2,1)}, u32[]{:S(2)}) copy-start(bf16[16,48,256]{2,1,0:T(8,128)(2,1)} %x_ref.3) | copy-start | bytes 1179652
  5.0 6.1 %collective-permute-start.2 = (bf16[8,48,128]{2,1,0:T(8,128)(2,1)S(1)}, bf16[8,48,128]{2,1,0:T(8,128)(2,1)S(1)}, u32[]{:S(2)}, u32[]{:S(2)}) collective-permute-start(bf16[8,48,128]{2,1,0:T(8,128)(2,1)S(1)} %strips.1), channel_id=1, source_target_pairs={{4,8},{8,4},{12,16},{16,12},{20,24},{24,20},{28,32},{32,28},{36,40... | collective-permute-start | bytes 294920 | tf_op jit(solution)/shard_map/ppermute | solution.py:514
  7.1 1.3 %collective-permute-start = (s32[16]{0:T(128)}, s32[16]{0:T(128)S(1)}, u32[]{:S(2)}, u32[]{:S(2)}) collective-permute-start(s32[16]{0:T(128)} %own_slots.1), channel_id=1, source_target_pairs={{0,4},{4,0},{1,5},{5,1},{2,6},{6,2},{3,7},{7,3},{8,12},{12,8},{9,1... | collective-permute-start | bytes 200 | tf_op jit(solution)/shard_map/ppermute | solution.py:510
  8.4 8.4 %copy-start.3 = (bf16[72,384]{1,0:T(8,128)(2,1)S(1)}, bf16[72,384]{1,0:T(8,128)(2,1)}, u32[]{:S(2)}) copy-start(bf16[72,384]{1,0:T(8,128)(2,1)} %constant.12.clone.down_p) | copy-start | bytes 165892
  8.4 8.4 %copy-start.4 = (bf16[72,384]{1,0:T(8,128)(2,1)S(1)}, bf16[72,384]{1,0:T(8,128)(2,1)}, u32[]{:S(2)}) copy-start(bf16[72,384]{1,0:T(8,128)(2,1)} %constant.10.clone.up_p) | copy-start | bytes 165892
  11.1 5.7 %copy-start.6 = (s32[8,8]{1,0:T(8,128)S(1)}, s32[8,8]{1,0:T(8,128)}, u32[]{:S(2)}) copy-start(s32[8,8]{1,0:T(8,128)} %adj.3) | copy-start | bytes 772
  11.1 5.7 %copy-start.8 = (s32[16]{0:T(128)S(1)}, s32[16]{0:T(128)}, u32[]{:S(2)}) copy-start(s32[16]{0:T(128)} %own_slots.1) | copy-start | bytes 196
  11.1 12.2 %collective-permute-start.7 = (bf16[400,256]{1,0:T(8,128)(2,1)S(1)}, bf16[400,256]{1,0:T(8,128)(2,1)S(1)}, u32[]{:S(2)}, u32[]{:S(2)}) collective-permute-start(bf16[400,256]{1,0:T(8,128)(2,1)S(1)} %get-tuple-element.60), channel_id=1, source_target_pairs={{0,1},{1,2},{2,3},{3,0},{4,5},{5,6},{6,7},{7,4},{8,9},{9,10},{10,1... | collective-permute-start | bytes 614408 | tf_op jit(solution)/shard_map/ppermute | solution.py:491
  11.1 12.2 %collective-permute-start.8 = (bf16[400,256]{1,0:T(8,128)(2,1)S(1)}, bf16[400,256]{1,0:T(8,128)(2,1)S(1)}, u32[]{:S(2)}, u32[]{:S(2)}) collective-permute-start(bf16[400,256]{1,0:T(8,128)(2,1)S(1)} %get-tuple-element.61), channel_id=1, source_target_pairs={{0,2},{1,3},{2,0},{3,1},{4,6},{5,7},{6,4},{7,5},{8,10},{9,11},{10,... | collective-permute-start | bytes 614408 | tf_op jit(solution)/shard_map/ppermute | solution.py:491
  13.4 10.7 %collective-permute-start.9 = (bf16[400,256]{1,0:T(8,128)(2,1)S(1)}, bf16[400,256]{1,0:T(8,128)(2,1)S(1)}, u32[]{:S(2)}, u32[]{:S(2)}) collective-permute-start(bf16[400,256]{1,0:T(8,128)(2,1)S(1)} %get-tuple-element.62), channel_id=1, source_target_pairs={{0,3},{1,0},{2,1},{3,2},{4,7},{5,4},{6,5},{7,6},{8,11},{9,8},{10,9... | collective-permute-start | bytes 614408 | tf_op jit(solution)/shard_map/ppermute | solution.py:491
  14.5 2.3 %collective-permute-start.3 = (bf16[8,48,128]{2,1,0:T(8,128)(2,1)S(1)}, bf16[8,48,128]{2,1,0:T(8,128)(2,1)S(1)}, u32[]{:S(2)}, u32[]{:S(2)}) collective-permute-start(bf16[8,48,128]{2,1,0:T(8,128)(2,1)S(1)} %collective-permute-done.2.near_ref), channel_id=1, source_target_pairs={{0,4},{4,0},{1,5},{5,1},{2,6},{6,2},{3,7},{7,3},{8,12},{12,8},{9,1... | collective-permute-start | bytes 294920 | tf_op jit(solution)/shard_map/ppermute | solution.py:510
  20.4 4.3 %collective-permute-start.4 = (bf16[2,48,256]{2,1,0:T(8,128)(2,1)S(1)}, bf16[2,48,256]{2,1,0:T(8,128)(2,1)S(1)}, u32[]{:S(2)}, u32[]{:S(2)}) collective-permute-start(bf16[2,48,256]{2,1,0:T(8,128)(2,1)S(1)} %get-tuple-element.52), channel_id=1, source_target_pairs={{0,1},{1,2},{2,3},{3,0},{4,5},{5,6},{6,7},{7,4},{8,9},{9,10},{10,1... | collective-permute-start | bytes 147464 | tf_op jit(solution)/shard_map/ppermute | solution.py:491
  20.8 4.5 %collective-permute-start.5 = (bf16[2,48,256]{2,1,0:T(8,128)(2,1)S(1)}, bf16[2,48,256]{2,1,0:T(8,128)(2,1)S(1)}, u32[]{:S(2)}, u32[]{:S(2)}) collective-permute-start(bf16[2,48,256]{2,1,0:T(8,128)(2,1)S(1)} %get-tuple-element.53), channel_id=1, source_target_pairs={{0,2},{1,3},{2,0},{3,1},{4,6},{5,7},{6,4},{7,5},{8,10},{9,11},{10,... | collective-permute-start | bytes 147464 | tf_op jit(solution)/shard_map/ppermute | solution.py:491
  23.3 3.4 %collective-permute-start.6 = (bf16[2,48,256]{2,1,0:T(8,128)(2,1)S(1)}, bf16[2,48,256]{2,1,0:T(8,128)(2,1)S(1)}, u32[]{:S(2)}, u32[]{:S(2)}) collective-permute-start(bf16[2,48,256]{2,1,0:T(8,128)(2,1)S(1)} %get-tuple-element.54), channel_id=1, source_target_pairs={{0,3},{1,0},{2,1},{3,2},{4,7},{5,4},{6,5},{7,6},{8,11},{9,8},{10,9... | collective-permute-start | bytes 147464 | tf_op jit(solution)/shard_map/ppermute | solution.py:491
  29.5 4.5 %collective-permute-start.14 = (bf16[4,288,128]{2,1,0:T(8,128)(2,1)S(1)}, bf16[4,288,128]{2,1,0:T(8,128)(2,1)S(1)}, u32[]{:S(2)}, u32[]{:S(2)}) collective-permute-start(bf16[4,288,128]{2,1,0:T(8,128)(2,1)S(1)} %get-tuple-element.79), channel_id=1, source_target_pairs={{0,4},{4,0},{1,5},{5,1},{2,6},{6,2},{3,7},{7,3},{8,12},{12,8},{9,1... | collective-permute-start | bytes 884744 | tf_op jit(solution)/shard_map/ppermute | solution.py:510
  30.9 7.4 %collective-permute-start.10 = (bf16[192,256]{1,0:T(8,128)(2,1)S(1)}, bf16[192,256]{1,0:T(8,128)(2,1)S(1)}, u32[]{:S(2)}, u32[]{:S(2)}) collective-permute-start(bf16[192,256]{1,0:T(8,128)(2,1)S(1)} %get-tuple-element.75), channel_id=1, source_target_pairs={{0,1},{1,2},{2,3},{3,0},{4,5},{5,6},{6,7},{7,4},{8,9},{9,10},{10,1... | collective-permute-start | bytes 294920 | tf_op jit(solution)/shard_map/ppermute | solution.py:491
  31.7 7.2 %collective-permute-start.11 = (bf16[192,256]{1,0:T(8,128)(2,1)S(1)}, bf16[192,256]{1,0:T(8,128)(2,1)S(1)}, u32[]{:S(2)}, u32[]{:S(2)}) collective-permute-start(bf16[192,256]{1,0:T(8,128)(2,1)S(1)} %get-tuple-element.76), channel_id=1, source_target_pairs={{0,2},{1,3},{2,0},{3,1},{4,6},{5,7},{6,4},{7,5},{8,10},{9,11},{10,... | collective-permute-start | bytes 294920 | tf_op jit(solution)/shard_map/ppermute | solution.py:491
  34.1 4.8 %collective-permute-start.12 = (bf16[192,256]{1,0:T(8,128)(2,1)S(1)}, bf16[192,256]{1,0:T(8,128)(2,1)S(1)}, u32[]{:S(2)}, u32[]{:S(2)}) collective-permute-start(bf16[192,256]{1,0:T(8,128)(2,1)S(1)} %get-tuple-element.77), channel_id=1, source_target_pairs={{0,3},{1,0},{2,1},{3,2},{4,7},{5,4},{6,5},{7,6},{8,11},{9,8},{10,9... | collective-permute-start | bytes 294920 | tf_op jit(solution)/shard_map/ppermute | solution.py:491
  34.9 9.2 %all-to-all-start = ((bf16[4,288,128]{2,1,0:T(8,128)(2,1)}), bf16[4,288,128]{2,1,0:T(8,128)(2,1)S(1)}, u32[]{:S(2)}, u32[]{:S(2)}) async-start(bf16[4,288,128]{2,1,0:T(8,128)(2,1)} %merge.1), calls=%async_computation | async-start | bytes 589824 | tf_op jit(solution)/shard_map/all_to_all | solution.py:587
  38.9 1.2 %copy-start.5 = (f32[384,128]{1,0:T(8,128)S(1)}, f32[384,128]{1,0:T(8,128)}, u32[]{:S(2)}) copy-start(f32[384,128]{1,0:T(8,128)} %constant.13.clone.fold) | copy-start | bytes 589828
  38.9 3.1 %collective-permute-start.13 = (bf16[8,48,256]{2,1,0:T(8,128)(2,1)S(1)}, bf16[8,48,256]{2,1,0:T(8,128)(2,1)S(1)}, u32[]{:S(2)}, u32[]{:S(2)}) collective-permute-start(bf16[8,48,256]{2,1,0:T(8,128)(2,1)S(1)} %land.1.grad_ref.own_ref), channel_id=1, source_target_pairs={{0,4},{4,0},{1,5},{5,1},{2,6},{6,2},{3,7},{7,3},{8,12},{12,8},{9,1... | collective-permute-start | bytes 589832 | tf_op jit(solution)/shard_map/ppermute | solution.py:510
  44.9 21.0 %all-to-all-start.1 = ((bf16[32,16,128]{2,1,0:T(8,128)(2,1)}), bf16[32,16,128]{2,1,0:T(8,128)(2,1)S(1)}, u32[]{:S(2)}, u32[]{:S(2)}) async-start(bf16[32,16,128]{2,1,0:T(8,128)(2,1)} %pieces.1), calls=%async_computation.1 | async-start | bytes 262144 | tf_op jit(solution)/shard_map/all_to_all | solution.py:614
  56.6 8.7 %collective-permute-start.15 = (bf16[8,48,128]{2,1,0:T(8,128)(2,1)S(1)}, bf16[8,48,128]{2,1,0:T(8,128)(2,1)S(1)}, u32[]{:S(2)}, u32[]{:S(2)}) collective-permute-start(bf16[8,48,128]{2,1,0:T(8,128)(2,1)S(1)} %edges.1), channel_id=1, source_target_pairs={{4,8},{8,4},{12,16},{16,12},{20,24},{24,20},{28,32},{32,28},{36,40... | collective-permute-start | bytes 294920 | tf_op jit(solution)/shard_map/ppermute | solution.py:514
  66.6 10.9 %copy-start.2 = (bf16[8,48,256]{2,1,0:T(8,128)(2,1)S(1)}, bf16[8,48,256]{2,1,0:T(8,128)(2,1)}, u32[]{:S(2)}) copy-start(bf16[8,48,256]{2,1,0:T(8,128)(2,1)} %cot_ref.1) | copy-start | bytes 589828
  66.6 17.3 %all-to-all-start.2 = ((bf16[32,16,128]{2,1,0:T(8,128)(2,1)}), bf16[32,16,128]{2,1,0:T(8,128)(2,1)S(1)}, u32[]{:S(2)}, u32[]{:S(2)}) async-start(bf16[32,16,128]{2,1,0:T(8,128)(2,1)} %totals.1), calls=%async_computation.2 | async-start | bytes 262144 | tf_op jit(solution)/shard_map/all_to_all | solution.py:622
  74.6 2.9 %copy-start.7 = (f32[48]{0:T(128)S(1)}, f32[48]{0:T(128)}, u32[]{:S(2)}) copy-start(f32[48]{0:T(128)} %param.24) | copy-start | bytes 580
  74.6 2.9 %collective-permute-start.16 = (bf16[8,48,128]{2,1,0:T(8,128)(2,1)S(1)}, bf16[8,48,128]{2,1,0:T(8,128)(2,1)S(1)}, u32[]{:S(2)}, u32[]{:S(2)}) collective-permute-start(bf16[8,48,128]{2,1,0:T(8,128)(2,1)S(1)} %collective-permute-done.15.near_ref), channel_id=1, source_target_pairs={{0,4},{4,0},{1,5},{5,1},{2,6},{6,2},{3,7},{7,3},{8,12},{12,8},{9,1... | collective-permute-start | bytes 294920 | tf_op jit(solution)/shard_map/ppermute | solution.py:510
  84.0 4.1 %collective-permute-start.17 = (bf16[32,16,128]{2,1,0:T(8,128)(2,1)S(1)}, bf16[32,16,128]{2,1,0:T(8,128)(2,1)S(1)}, u32[]{:S(2)}, u32[]{:S(2)}) collective-permute-start(bf16[32,16,128]{2,1,0:T(8,128)(2,1)S(1)} %all-to-all-done.2.in_ref), channel_id=1, source_target_pairs={{0,4},{4,0},{1,5},{5,1},{2,6},{6,2},{3,7},{7,3},{8,12},{12,8},{9,1... | collective-permute-start | bytes 393224 | tf_op jit(solution)/shard_map/ppermute | solution.py:510

commit v6 on v5

--- a/solution.py
+++ b/solution.py
@@ -29,9 +29,8 @@
 
 
 def placement_tables():
-    up = np.zeros((72, 384), np.float32)
-    mid = np.zeros((384, 768), np.float32)
-    down = np.zeros((72, 384), np.float32)
+    maps = np.zeros((22 * WIDE, 768), np.float32)
+    up, mid, down = maps[0:72], maps[72:456], maps[456:528]
     for j in range(22):
         if j < 3:
             side, col = 0, 13 + j
@@ -45,7 +44,7 @@
         for i in range(16):
             block = (1, 0, 2)[side]
             mid[i * WIDE + j, 256 * block + 16 * i + col] = 1
-    return up.astype(jnp.bfloat16), mid.astype(jnp.bfloat16), down.astype(jnp.bfloat16)
+    return maps.astype(jnp.bfloat16)
 
 
 def column(row):
@@ -77,45 +76,53 @@
     return 2 * lax.axis_index("chip") + lax.axis_index("core")
 
 
-def strips_kernel(x_ref, strips_ref, half, sem):
+def pack_tail(value):
+    return jnp.concatenate([value[0:96], value[96:192]], axis=1)
+
+
+def unpack_tail(value):
+    return jnp.concatenate([value[:, 0:64], value[:, 64:128]], axis=0)
+
+
+def open_kernel(
+    x_hbm, cot_hbm, scale_hbm, in_hbm, w_out_hbm, b_hbm, gain_hbm, dw_hbm, spread_hbm,
+    strips_ref, s0, s1, s2, s3, taps_ref, spread, x_ref,
+    cot_ref, scale_ref, in_ref, w_out_ref, b_ref, gain_ref, dw_ref, small, turned, sems,
+):
+    outs = (s0, s1, s2, s3)
+    mine = lax.axis_index("chan")
     odd = lax.axis_index("core")
-    copy = pltpu.make_async_copy(
-        x_ref.at[:, :, pl.ds(pl.multiple_of(128 * odd, 128), 128)], half, sem
-    )
-    copy.start()
-    copy.wait()
+    sources = (x_hbm, cot_hbm, scale_hbm, in_hbm, w_out_hbm, b_hbm, gain_hbm, dw_hbm, spread_hbm)
+    targets = (x_ref, cot_ref, scale_ref, in_ref, w_out_ref, b_ref, gain_ref, dw_ref, spread)
+    copies = [
+        pltpu.make_async_copy(source, target, sems.at[n])
+        for n, (source, target) in enumerate(zip(sources, targets))
+    ]
+    for copy in copies:
+        copy.start()
+    copies[0].wait()
 
     @pl.when(odd == 1)
     def _():
         for s in range(8):
-            strips_ref[s] = pack_pair(half[s], half[s + 8], False)
+            strips_ref[s] = pack_pair(x_ref[s, :, 128:256], x_ref[s + 8, :, 128:256], False)
 
     @pl.when(odd == 0)
     def _():
         for s in range(8):
-            strips_ref[s] = pack_pair(half[s], half[s + 8], True)
-
-
-def pack_tail(value):
-    return jnp.concatenate([value[0:96], value[96:192]], axis=1)
-
-
-def unpack_tail(value):
-    return jnp.concatenate([value[:, 0:64], value[:, 64:128]], axis=0)
-
-
-def sends_kernel(cot_ref, scale_ref, in_ref, w_out_ref, b_ref, gain_ref, dw_ref, spread, *rest):
-    outs, taps_ref, small, turned = rest[0:4], rest[4], rest[5], rest[6]
+            strips_ref[s] = pack_pair(x_ref[s, :, 0:128], x_ref[s + 8, :, 0:128], True)
+
+    for copy in copies[1:]:
+        copy.wait()
     turned[...] = jnp.zeros((128, 128), F32)
     turned[0:48, 0:49] = dw_ref[...]
     taps_ref[...] = lax.dot_general(
         turned[...].T[0:56], spread[...], NN,
         precision=lax.Precision.HIGHEST, preferred_element_type=F32,
     )
-    mine = lax.axis_index("chan")
     scale = column(scale_ref[...])
     small[...] = jnp.zeros((16, 256), F32)
-    small[0:1, 0:192] = b_ref[...].astype(F32)
+    small[0:1, 0:192] = b_ref[...].astype(F32).reshape(1, 192)
     small[1:2, 0:48] = gain_ref[...].astype(F32)
     tails = []
     for ref in (in_ref, w_out_ref):
@@ -141,9 +148,9 @@
         down_g[rows, 128 * k : 128 * k + 128] = table[entries[5 + k], :, 0:128]
 
 
-def build_padded(pad, up_g, mid_g, down_g, up_p, mid_p, down_p):
-    for maps, cells, lo, hi in ((up_p, up_g, 0, 72), (mid_p, mid_g, 72, 456), (down_p, down_g, 456, 528)):
-        rows = dot(maps[...], cells[...], NT)
+def build_padded(pad, up_g, mid_g, down_g, maps):
+    for cells, lo, hi in ((up_g, 0, 72), (mid_g, 72, 456), (down_g, 456, 528)):
+        rows = dot(maps[lo:hi, 0 : cells.shape[1]], cells[...], NT)
         for block in range(3):
             pad[block, lo:hi] = rows[:, 128 * block : 128 * block + 128]
 
@@ -195,7 +202,7 @@
 
 
 def mix_kernel(
-    own_slots, par_slots, adj, x_ref, par_ref, near_ref, far_ref, taps, up_p, mid_p, down_p,
+    own_slots, par_slots, adj, x_ref, par_ref, near_ref, far_ref, taps, maps,
     owned_ref, pad_out, m0, m1, m2, m3,
     place, table, up_g, mid_g, down_g, pad, result, flat,
 ):
@@ -223,7 +230,7 @@
         entries = [jnp.where(adj[t, k] < 512, center + OFFSETS[k], 64) for k in range(8)]
         gather_tile(table, up_g, mid_g, down_g, t, center, entries)
     owned_ref[...] = mid_g[:, 0:256].reshape(8, 48, 256)
-    build_padded(pad, up_g, mid_g, down_g, up_p, mid_p, down_p)
+    build_padded(pad, up_g, mid_g, down_g, maps)
     pad_out[...] = pad[...].astype(BF16)
     convolve(pad, taps, result, False)
     flat[...] = result[...].T.astype(BF16).reshape(8, 48, 256)
@@ -348,7 +355,7 @@
 
     lax.fori_loop(0, 3, lane_block, 0)
     out_ref[...] = lax.dot_general(
-        sums[...], fold[...], NN, precision=lax.Precision.HIGHEST, preferred_element_type=F32
+        sums[...], fold[...], NT, precision=lax.Precision.HIGHEST, preferred_element_type=F32
     )
 
 
@@ -394,7 +401,7 @@
 
 
 def unmix_kernel(
-    adj, grad_ref, par_ref, near_ref, far_ref, cot_ref, taps, up_p, mid_p, down_p,
+    adj, grad_ref, par_ref, near_ref, far_ref, cot_ref, taps, maps,
     owned_ref, scale_ref, r0, r1, r2, r3,
     out_ref, gin_ref,
     table, up_g, mid_g, down_g, pad, result,
@@ -411,7 +418,7 @@
         center = 16 + 8 * odd + t
         entries = [jnp.where(adj[t, k] < 512, adj[t, k] - start, 48) for k in range(8)]
         gather_tile(table, up_g, mid_g, down_g, t, center, entries)
-    build_padded(pad, up_g, mid_g, down_g, up_p, mid_p, down_p)
+    build_padded(pad, up_g, mid_g, down_g, maps)
     convolve(pad, taps, result, True)
     back = result[...].T.reshape(8, 48, 256)
     gin_ref[...] = (cot_ref[...].astype(F32) + back).astype(BF16)
@@ -424,52 +431,25 @@
             ).astype(BF16)
 
 
-def fetching(kernel, fetch, n_in):
-    def outer(*refs):
-        inputs, rest = list(refs[:n_in]), refs[n_in:]
-        rest, local, sems = rest[: -len(fetch) - 1], rest[-len(fetch) - 1 : -1], rest[-1]
-        copies = [
-            pltpu.make_async_copy(inputs[i], buf, sems.at[n])
-            for n, (i, buf) in enumerate(zip(fetch, local))
-        ]
-        for copy in copies:
-            copy.start()
-        for copy in copies:
-            copy.wait()
-        for i, buf in zip(fetch, local):
-            inputs[i] = buf
-        kernel(*inputs, *rest)
-
-    return outer
-
-
-def call(kernel, shapes, scratch=(), smem=0, n_in=0, name=None, near=(), fetch=()):
+def call(kernel, shapes, scratch=(), smem=0, n_in=0, name=None, near=()):
     vmem = pl.BlockSpec(memory_space=pltpu.VMEM)
     scalar = pl.BlockSpec(memory_space=pltpu.SMEM)
     many = isinstance(shapes, (list, tuple))
 
+    inner = pl.pallas_call(
+        kernel,
+        out_shape=shapes,
+        in_specs=[scalar] * smem + [vmem] * (n_in - smem),
+        out_specs=[vmem] * len(shapes) if many else vmem,
+        scratch_shapes=list(scratch),
+        compiler_params=pltpu.CompilerParams(vmem_limit_bytes=24 << 20),
+        name=name,
+    )
+
     def run(*args):
-        specs = [
-            pl.BlockSpec(memory_space=pltpu.HBM) if i in fetch else scalar if i < smem else vmem
-            for i in range(n_in)
-        ]
-        scratches = list(scratch)
-        if fetch:
-            scratches += [pltpu.VMEM(args[i].shape, args[i].dtype) for i in fetch]
-            scratches.append(pltpu.SemaphoreType.DMA((len(fetch),)))
-        inner = pl.pallas_call(
-            fetching(kernel, fetch, n_in) if fetch else kernel,
-            out_shape=shapes,
-            in_specs=specs,
-            out_specs=[vmem] * len(shapes) if many else vmem,
-            scratch_shapes=scratches,
-            compiler_params=pltpu.CompilerParams(vmem_limit_bytes=24 << 20),
-            name=name,
-        )
-        spaces = {**{i: pltpu.VMEM for i in near}, **{i: pltpu.HBM for i in fetch}}
         return inner(
             *(
-                pltpu.with_memory_space_constraint(a, spaces[i]) if i in spaces else a
+                pltpu.with_memory_space_constraint(a, pltpu.VMEM) if i in near else a
                 for i, a in enumerate(args)
             )
         )
@@ -496,9 +476,8 @@
     x_scan, slot_owner, adjacency, cotangent, dw_weight, ln_gain, w_in, b_in, w_out, layer_scale
 ):
     devices = lax.axis_size("chip") * 2
-    up_p, mid_p, down_p = (jnp.asarray(v) for v in placement_tables())
+    maps = jnp.asarray(placement_tables())
     fold_map = (np.arange(384)[:, None] % 48 == np.arange(128)[None, :]).astype(np.float32)
-    fold = jnp.asarray(fold_map)
     spread_map = jnp.asarray(np.ascontiguousarray(fold_map.T))
     scale_row = layer_scale.reshape(1, 48)
     owners = ("chip", "core")
@@ -516,28 +495,28 @@
     tile_chunk = held(2, 48, 256)
     par_x = partner(x_scan)
     par_slots = partner(slot_owner)
-    strips = pl.pallas_call(
-        strips_kernel,
-        out_shape=held(8, 48, 128),
-        in_specs=[pl.BlockSpec(memory_space=pltpu.HBM)],
-        out_specs=pl.BlockSpec(memory_space=pltpu.VMEM),
-        scratch_shapes=[pltpu.VMEM((16, 48, 128), BF16), pltpu.SemaphoreType.DMA(())],
-        name="strips",
-    )(pltpu.with_memory_space_constraint(x_scan, pltpu.HBM))
+    opening = (
+        x_scan, cotangent, scale_row, w_in, w_out, b_in, ln_gain.reshape(1, 48), dw_weight, spread_map
+    )
+    strips, *sends, taps, fold, own_x = pl.pallas_call(
+        open_kernel,
+        out_shape=[held(8, 48, 128)] + [held(400, 256)] * 4
+        + [held(56, 384, dtype=F32), held(128, 384, dtype=F32), held(16, 48, 256)],
+        in_specs=[pl.BlockSpec(memory_space=pltpu.HBM)] * 9,
+        out_specs=[pl.BlockSpec(memory_space=pltpu.VMEM)] * 8,
+        scratch_shapes=[pltpu.VMEM(v.shape, v.dtype) for v in opening[1:-1]]
+        + [
+            pltpu.VMEM((16, 256), F32),
+            pltpu.VMEM((128, 128), F32),
+            pltpu.SemaphoreType.DMA((9,)),
+        ],
+        compiler_params=pltpu.CompilerParams(vmem_limit_bytes=24 << 20),
+        name="open",
+    )(*(pltpu.with_memory_space_constraint(v, pltpu.HBM) for v in opening))
     near = next_chip(strips)
     far = partner(near)
-    *sends, taps = call(
-        sends_kernel,
-        [held(400, 256)] * 4 + [held(56, 384, dtype=F32)],
-        scratch=[pltpu.VMEM((16, 256), F32), pltpu.VMEM((128, 128), F32)],
-        n_in=8,
-        name="sends",
-        fetch=range(8),
-    )(
-        cotangent, after(scale_row, strips, par_x, par_slots), w_in, w_out,
-        b_in.reshape(1, 192), ln_gain.reshape(1, 48), dw_weight, spread_map,
-    )
-    all_sends = along_chan(after(sends, near))
+    sends[1] = after(sends[1], near, par_slots)
+    all_sends = along_chan(sends)
 
     grid_scratch = lambda entries: [
         pltpu.VMEM((entries, 48, 256), BF16),
@@ -552,12 +531,12 @@
         [shape(8, 48, 256), shape(3, 22 * WIDE, 128)] + [tile_chunk] * 4,
         scratch=[pltpu.SMEM((8,), jnp.int32)] + grid_scratch(65) + [pltpu.VMEM((8, 48, 256), BF16)],
         smem=3,
-        n_in=11,
+        n_in=9,
         name="mix",
-        near=(4, 5, 6, 7),
+        near=(3, 4, 5, 6, 7),
     )
     owned, padded, *mixed = mix(
-        slot_owner, par_slots, adjacency, x_scan, par_x, near, far, taps, up_p, mid_p, down_p
+        slot_owner, par_slots, adjacency, own_x, par_x, near, far, taps, maps
     )
     all_mixed = along_chan(mixed)
 
@@ -597,7 +576,7 @@
         ],
         n_in=3,
         name="tap_sums",
-        near=(0,),
+        near=(0, 2),
     )(grads, padded, fold)
     edges = call(edges_kernel, held(8, 48, 128), n_in=2, name="edges", near=(0, 1))(
         after(grads, tap_sums), par_grads
@@ -626,13 +605,13 @@
         [shape(8, 48, 256), shape(8, 48, 256)],
         scratch=grid_scratch(49),
         smem=1,
-        n_in=16,
+        n_in=14,
         name="unmix",
-        near=(1, 2, 3, 4, 12, 13, 14, 15),
+        near=(1, 2, 3, 4, 10, 11, 12, 13),
     )
     output, grad_in = unmix(
         adjacency, grads, par_grads, near_grads, far_grads,
-        cotangent, taps, up_p, mid_p, down_p, owned, after(scale_row, totals), *all_back
+        cotangent, taps, maps, owned, after(scale_row, totals), *all_back
     )
     spread = after(spread, output)
     grad_dw, grad_w1, grad_w2 = call(

time: 89.5 us -> 88 us (0.983)
  starting transfers between devices: 50.9 us -> 54 us
  waiting for transfers between devices: 16.9 us -> 14.2 us
  local copies, waits for them, and re-layouts: 1.26 us -> 0.03 us
    ppermute x9, starting transfers between devices: 7.57 us -> 10.3 us  [along_chan(): lax.ppermute(values[j], 'chan', [(i, (i + j) % 4) for i in range(4)])]
    ppermute x9, waiting for transfers between devices: 5.26 us -> 2.62 us  [along_chan(): lax.ppermute(values[j], 'chan', [(i, (i + j) % 4) for i in range(4)])]
    reshape x1 -> x0, local copies, waits for them, and re-layouts: 1.22 us -> none  [body(): b_in.reshape(1, 192)]
    pallas_call x13 -> x12, Pallas kernels: 19.3 us -> 18.6 us  [the longest x11 16.9 us: run(): inner(*(pltpu.with_memory_space_constraint(a, pltpu.VMEM) if i in near el...]
  transfers between devices with their start and end apart: 21 -> 21, of which waited for: 14 -> 12; matrix products, arithmetic and copies ran while one was open for 1% -> 0% of each run, Pallas kernels for 16% -> 15%
where the time goes in v6:
time: 88 us; the launch traced here: 87.6 us
  starting transfers between devices  54 us (61%)
  Pallas kernels  18.6 us (21%)
  waiting for transfers between devices  14.2 us (16%)
    pallas_call x11, Pallas kernels, run(): inner(*(pltpu.with_memory_space_constraint(a, pltpu.VMEM) if i in near el...  16.9 us
    all_to_all x1, starting transfers between devices, body(): arrived = lax.all_to_all(after(pieces, edges), 'chip', 0, 0, tiled=True)  12.5 us
    ppermute x7, starting transfers between devices, partner(): return lax.ppermute(value, 'core', [(0, 1), (1, 0)])  12.1 us
    ppermute x9, starting transfers between devices, along_chan(): lax.ppermute(values[j], 'chan', [(i, (i + j) % 4) for i in range(4)])  10.3 us
    all_to_all x1, starting transfers between devices, body(): spread = lax.all_to_all(totals, 'chip', 0, 0, tiled=True)  7.94 us
    ppermute x2, starting transfers between devices, next_chip(): lax.ppermute(value, owners, [p for p in pairs if 0 <= p[1] < devices])  7.6 us
    ppermute x2, waiting for transfers between devices, next_chip(): lax.ppermute(value, owners, [p for p in pairs if 0 <= p[1] < devices])  3.76 us
    all_to_all x1, starting transfers between devices, body(): partials = lax.all_to_all(merged, 'chan', 0, 0, tiled=True)  3.45 us
  transfers between devices with their start and end apart: 21, of which 12 were waited for; matrix products, arithmetic and copies ran while one was open for 0% of the time, Pallas kernels for 15%

profile of v6, /device:TPU:1, one launch (start us, length us, event | category | flops | bytes accessed | tf_op | source)
XLA Modules:
  0.0 87.6 jit_solution(12207092973592101663)
XLA Ops:
  0.6 0.0 copy-start
  0.6 3.3 %collective-permute-start.1 = (bf16[16,48,256]{2,1,0:T(8,128)(2,1)}, bf16[16,48,256]{2,1,0:T(8,128)(2,1)S(1)}, u32[]{:S(2)}, u32[]{:S(2)}) collective-permute-start(bf16[16,48,256]{2,1,0:T(8,128)(2,1)} %x_hbm.1), channel_id=1, source_target_pairs={{0,4},{4,0},{1,5},{5,1},{2,6},{6,2},{3,7},{7,3},{8,12},{12,8},{9,1... | collective-permute-start | bytes 1179656 | tf_op jit(solution)/shard_map/ppermute | solution.py:489
  4.0 1.7 %open.1 = (bf16[8,48,128]{2,1,0:T(8,128)(2,1)S(1)}, bf16[400,256]{1,0:T(8,128)(2,1)S(1)}, bf16[400,256]{1,0:T(8,128)(2,1)S(1)}, bf16[400,256]{1,0:T(8,128)(2,1)S...) custom-call(bf16[16,48,256]{2,1,0:T(8,128)(2,1)} %x_hbm.1, ...), custom_call_target="tpu_custom_call" | custom-call | tf_op jit(solution)/shard_map/open/pallas_call | solution.py:501
  5.7 0.0 copy-start.4
  5.7 1.9 %collective-permute-start.2 = (bf16[8,48,128]{2,1,0:T(8,128)(2,1)S(1)}, bf16[8,48,128]{2,1,0:T(8,128)(2,1)S(1)}, u32[]{:S(2)}, u32[]{:S(2)}) collective-permute-start(bf16[8,48,128]{2,1,0:T(8,128)(2,1)S(1)} %get-tuple-element.49), channel_id=1, source_target_pairs={{4,8},{8,4},{12,16},{16,12},{20,24},{24,20},{28,32},{32,28},{36,40... | collective-permute-start | bytes 294920 | tf_op jit(solution)/shard_map/ppermute | solution.py:493
  7.6 0.0 copy-start.2
  7.6 2.3 %collective-permute-start.8 = (bf16[400,256]{1,0:T(8,128)(2,1)S(1)}, bf16[400,256]{1,0:T(8,128)(2,1)S(1)}, u32[]{:S(2)}, u32[]{:S(2)}) collective-permute-start(bf16[400,256]{1,0:T(8,128)(2,1)S(1)} %get-tuple-element.58), channel_id=1, source_target_pairs={{0,2},{1,3},{2,0},{3,1},{4,6},{5,7},{6,4},{7,5},{8,10},{9,11},{10,... | collective-permute-start | bytes 614408 | tf_op jit(solution)/shard_map/ppermute | solution.py:471
  10.0 0.9 collective-permute-start.9
  10.8 0.3 collective-permute-done.par_slots
  11.1 0.8 collective-permute-done.2.near_ref
  11.9 0.0 collective-permute-start.7
  11.9 0.6 collective-permute-start.3
  12.5 0.9 %collective-permute-done.3.far_ref = bf16[8,48,128]{2,1,0:T(8,128)(2,1)S(1)} collective-permute-done((bf16[8,48,128]{2,1,0:T(8,128)(2,1)S(1)}, bf16[8,48,128]{2,1,0:T(8,128)(2,1)S(1)}, u32[]{:S(2)}, u32[]{:S(2)}) %collective-permute-start.3) | collective-permute-done | bytes 98336 | tf_op jit(solution)/shard_map/ppermute | solution.py:489
  13.5 0.0 collective-permute-done.1.par_ref
  13.5 3.6 %mix.1 = (bf16[8,48,256]{2,1,0:T(8,128)(2,1)S(1)}, bf16[3,528,128]{2,1,0:T(8,128)(2,1)S(1)}, bf16[2,48,256]{2,1,0:T(8,128)(2,1)S(1)}, bf16[2,48,256]{2,1,0:T(8,1...) custom-call(s32[16]{0:T(128)S(1)} %copy-done.4, s32[16]{0:T(128)S(1)} %collective-permute-done.par_slots, ...), custom_call_target="tpu_custom_call" | custom-call | tf_op jit(solution)/shard_map/mix/pallas_call | solution.py:450
  17.1 0.5 collective-permute-start.4
  17.7 3.2 %collective-permute-start.5 = (bf16[2,48,256]{2,1,0:T(8,128)(2,1)S(1)}, bf16[2,48,256]{2,1,0:T(8,128)(2,1)S(1)}, u32[]{:S(2)}, u32[]{:S(2)}) collective-permute-start(bf16[2,48,256]{2,1,0:T(8,128)(2,1)S(1)} %get-tuple-element.53), channel_id=1, source_target_pairs={{0,2},{1,3},{2,0},{3,1},{4,6},{5,7},{6,4},{7,5},{8,10},{9,11},{10,... | collective-permute-start | bytes 147464 | tf_op jit(solution)/shard_map/ppermute | solution.py:471
  20.8 0.1 collective-permute-start.6
  21.0 0.6 turn.1
  21.6 1.7 %collective-permute-done.5.m2 = bf16[2,48,256]{2,1,0:T(8,128)(2,1)S(1)} collective-permute-done((bf16[2,48,256]{2,1,0:T(8,128)(2,1)S(1)}, bf16[2,48,256]{2,1,0:T(8,128)(2,1)S(1)}, u32[]{:S(2)}, u32[]{:S(2)}) %collective-permute-start.5) | collective-permute-done | bytes 49184 | tf_op jit(solution)/shard_map/ppermute | solution.py:471
  23.3 0.8 collective-permute-done.6.m3
  24.1 2.8 %mlp.1 = (bf16[192,256]{1,0:T(8,128)(2,1)S(1)}, bf16[192,256]{1,0:T(8,128)(2,1)S(1)}, bf16[192,256]{1,0:T(8,128)(2,1)S(1)}, bf16[192,256]{1,0:T(8,128)(2,1)S(1)}...) custom-call(bf16[2,48,256]{2,1,0:T(8,128)(2,1)S(1)} %get-tuple-element.51.m0, ...), custom_call_target="tpu_custom_call" | custom-call | tf_op jit(solution)/shard_map/mlp/pallas_call | solution.py:450
  26.9 1.7 %collective-permute-start.14 = (bf16[4,288,128]{2,1,0:T(8,128)(2,1)S(1)}, bf16[4,288,128]{2,1,0:T(8,128)(2,1)S(1)}, u32[]{:S(2)}, u32[]{:S(2)}) collective-permute-start(bf16[4,288,128]{2,1,0:T(8,128)(2,1)S(1)} %get-tuple-element.76), channel_id=1, source_target_pairs={{0,4},{4,0},{1,5},{5,1},{2,6},{6,2},{3,7},{7,3},{8,12},{12,8},{9,1... | collective-permute-start | bytes 884744 | tf_op jit(solution)/shard_map/ppermute | solution.py:489
  28.5 0.0 collective-permute-start.10
  28.5 2.5 %collective-permute-start.11 = (bf16[192,256]{1,0:T(8,128)(2,1)S(1)}, bf16[192,256]{1,0:T(8,128)(2,1)S(1)}, u32[]{:S(2)}, u32[]{:S(2)}) collective-permute-start(bf16[192,256]{1,0:T(8,128)(2,1)S(1)} %get-tuple-element.73), channel_id=1, source_target_pairs={{0,2},{1,3},{2,0},{3,1},{4,6},{5,7},{6,4},{7,5},{8,10},{9,11},{10,... | collective-permute-start | bytes 294920 | tf_op jit(solution)/shard_map/ppermute | solution.py:471
  31.1 0.8 collective-permute-start.12
  31.8 0.8 merge.1
  32.6 3.5 %all-to-all-start = ((bf16[4,288,128]{2,1,0:T(8,128)(2,1)}), bf16[4,288,128]{2,1,0:T(8,128)(2,1)S(1)}, u32[]{:S(2)}, u32[]{:S(2)}) async-start(bf16[4,288,128]{2,1,0:T(8,128)(2,1)} %merge.1), calls=%async_computation | async-start | bytes 589824 | tf_op jit(solution)/shard_map/all_to_all | solution.py:566
  36.1 0.1 collective-permute-done.12.g3.r3
  36.3 1.5 %collective-permute-start.13 = (bf16[8,48,256]{2,1,0:T(8,128)(2,1)S(1)}, bf16[8,48,256]{2,1,0:T(8,128)(2,1)S(1)}, u32[]{:S(2)}, u32[]{:S(2)}) collective-permute-start(bf16[8,48,256]{2,1,0:T(8,128)(2,1)S(1)} %land.1.grad_ref.own_ref), channel_id=1, source_target_pairs={{0,4},{4,0},{1,5},{5,1},{2,6},{6,2},{3,7},{7,3},{8,12},{12,8},{9,1... | collective-permute-start | bytes 589832 | tf_op jit(solution)/shard_map/ppermute | solution.py:489
  37.8 2.0 %tap_sums.1.taps_ref = f32[64,128]{1,0:T(8,128)S(1)} custom-call(bf16[8,48,256]{2,1,0:T(8,128)(2,1)S(1)} %land.1.grad_ref.own_ref, bf16[3,528,128]{2,1,0:T(8,128)(2,1)S(1)} %get-tuple-element.77.pad_ref, f32[128,384]{1,0:T(8,128)S(1)} %get-tuple-element.78.fold), custom_call_target="tpu_custom_call" | custom-call | tf_op jit(solution)/shard_map/tap_sums/pallas_call | solution.py:450
  39.8 0.1 edges.1
  39.9 1.8 %all-to-all-done.parts_ref = bf16[4,288,128]{2,1,0:T(8,128)(2,1)S(1)} async-done(((bf16[4,288,128]{2,1,0:T(8,128)(2,1)}), bf16[4,288,128]{2,1,0:T(8,128)(2,1)S(1)}, u32[]{:S(2)}, u32[]{:S(2)}) %all-to-all-start) | async-done | bytes 294944 | tf_op jit(solution)/shard_map/all_to_all | solution.py:566
  41.8 0.8 pieces.1
  42.6 12.5 %all-to-all-start.1 = ((bf16[32,16,128]{2,1,0:T(8,128)(2,1)}), bf16[32,16,128]{2,1,0:T(8,128)(2,1)S(1)}, u32[]{:S(2)}, u32[]{:S(2)}) async-start(bf16[32,16,128]{2,1,0:T(8,128)(2,1)} %pieces.1), calls=%async_computation.1 | async-start | bytes 262144 | tf_op jit(solution)/shard_map/all_to_all | solution.py:593
  55.1 5.7 %collective-permute-start.15 = (bf16[8,48,128]{2,1,0:T(8,128)(2,1)S(1)}, bf16[8,48,128]{2,1,0:T(8,128)(2,1)S(1)}, u32[]{:S(2)}, u32[]{:S(2)}) collective-permute-start(bf16[8,48,128]{2,1,0:T(8,128)(2,1)S(1)} %edges.1), channel_id=1, source_target_pairs={{4,8},{8,4},{12,16},{16,12},{20,24},{24,20},{28,32},{32,28},{36,40... | collective-permute-start | bytes 294920 | tf_op jit(solution)/shard_map/ppermute | solution.py:493
  60.8 2.9 %collective-permute-done.15.near_ref = bf16[8,48,128]{2,1,0:T(8,128)(2,1)S(1)} collective-permute-done((bf16[8,48,128]{2,1,0:T(8,128)(2,1)S(1)}, bf16[8,48,128]{2,1,0:T(8,128)(2,1)S(1)}, u32[]{:S(2)}, u32[]{:S(2)}) %collective-permute-start.15) | collective-permute-done | bytes 98336 | tf_op jit(solution)/shard_map/ppermute | solution.py:493
  63.8 0.7 all-to-all-done.1.in_ref
  64.5 0.7 totals.1
  65.2 7.9 %all-to-all-start.2 = ((bf16[32,16,128]{2,1,0:T(8,128)(2,1)}), bf16[32,16,128]{2,1,0:T(8,128)(2,1)S(1)}, u32[]{:S(2)}, u32[]{:S(2)}) async-start(bf16[32,16,128]{2,1,0:T(8,128)(2,1)} %totals.1), calls=%async_computation.2 | async-start | bytes 262144 | tf_op jit(solution)/shard_map/all_to_all | solution.py:601
  73.1 0.0 copy-start.3
  73.1 1.9 %collective-permute-start.16 = (bf16[8,48,128]{2,1,0:T(8,128)(2,1)S(1)}, bf16[8,48,128]{2,1,0:T(8,128)(2,1)S(1)}, u32[]{:S(2)}, u32[]{:S(2)}) collective-permute-start(bf16[8,48,128]{2,1,0:T(8,128)(2,1)S(1)} %collective-permute-done.15.near_ref), channel_id=1, source_target_pairs={{0,4},{4,0},{1,5},{5,1},{2,6},{6,2},{3,7},{7,3},{8,12},{12,8},{9,1... | collective-permute-start | bytes 294920 | tf_op jit(solution)/shard_map/ppermute | solution.py:489
  75.1 0.9 %collective-permute-done.16.far_ref = bf16[8,48,128]{2,1,0:T(8,128)(2,1)S(1)} collective-permute-done((bf16[8,48,128]{2,1,0:T(8,128)(2,1)S(1)}, bf16[8,48,128]{2,1,0:T(8,128)(2,1)S(1)}, u32[]{:S(2)}, u32[]{:S(2)}) %collective-permute-start.16) | collective-permute-done | bytes 98336 | tf_op jit(solution)/shard_map/ppermute | solution.py:489
  76.0 4.3 %unmix.1 = (bf16[8,48,256]{2,1,0:T(8,128)(2,1)}, bf16[8,48,256]{2,1,0:T(8,128)(2,1)}) custom-call(s32[8,8]{1,0:T(8,128)S(1)} %copy-done.2, bf16[8,48,256]{2,1,0:T(8,128)(2,1)S(1)} %land.1.grad_ref.own_ref, bf16[8,48,256]{2,1,0:T(8,128)(2,1)S(1)} %collective-permute-done.13.par_ref, bf16[8,48,128]{2,1,0:T(8,128)(2,1)S(1)} %collective-permute-done.15.near_ref, ...), custom_call_target="tpu_custom_call" | custom-call | tf_op jit(solution)/shard_map/unmix/pallas_call | solution.py:450
  80.3 2.1 %all-to-all-done.2.in_ref = bf16[32,16,128]{2,1,0:T(8,128)(2,1)S(1)} async-done(((bf16[32,16,128]{2,1,0:T(8,128)(2,1)}), bf16[32,16,128]{2,1,0:T(8,128)(2,1)S(1)}, u32[]{:S(2)}, u32[]{:S(2)}) %all-to-all-start.2) | async-done | bytes 131104 | tf_op jit(solution)/shard_map/all_to_all | solution.py:601
  82.5 3.1 %collective-permute-start.17 = (bf16[32,16,128]{2,1,0:T(8,128)(2,1)S(1)}, bf16[32,16,128]{2,1,0:T(8,128)(2,1)S(1)}, u32[]{:S(2)}, u32[]{:S(2)}) collective-permute-start(bf16[32,16,128]{2,1,0:T(8,128)(2,1)S(1)} %all-to-all-done.2.in_ref), channel_id=1, source_target_pairs={{0,4},{4,0},{1,5},{5,1},{2,6},{6,2},{3,7},{7,3},{8,12},{12,8},{9,1... | collective-permute-start | bytes 393224 | tf_op jit(solution)/shard_map/ppermute | solution.py:489
  85.6 1.0 %collective-permute-done.17.other_ref = bf16[32,16,128]{2,1,0:T(8,128)(2,1)S(1)} collective-permute-done((bf16[32,16,128]{2,1,0:T(8,128)(2,1)S(1)}, bf16[32,16,128]{2,1,0:T(8,128)(2,1)S(1)}, u32[]{:S(2)}, u32[]{:S(2)}) %collective-permute-start.17) | collective-permute-done | bytes 131104 | tf_op jit(solution)/shard_map/ppermute | solution.py:489
  86.6 1.1 %finish.1 = (f32[48,49]{1,0:T(8,128)}, f32[192,192]{1,0:T(8,128)}, f32[192,192]{1,0:T(8,128)}) custom-call(bf16[32,16,128]{2,1,0:T(8,128)(2,1)S(1)} %all-to-all-done.2.in_ref, bf16[32,16,128]{2,1,0:T(8,128)(2,1)S(1)} %collective-permute-done.17.other_ref), custom_call_target="tpu_custom_call" | custom-call | tf_op jit(solution)/shard_map/finish/pallas_call | solution.py:450
  (16 shorter events, 0.1 us)
Async XLA Ops:
  0.6 12.8 %copy-start = (bf16[528,768]{1,0:T(8,128)(2,1)S(1)}, bf16[528,768]{1,0:T(8,128)(2,1)}, u32[]{:S(2)}) copy-start(bf16[528,768]{1,0:T(8,128)(2,1)} %constant.4.clone.maps) | copy-start | bytes 2433028
  0.6 12.8 %collective-permute-start.1 = (bf16[16,48,256]{2,1,0:T(8,128)(2,1)}, bf16[16,48,256]{2,1,0:T(8,128)(2,1)S(1)}, u32[]{:S(2)}, u32[]{:S(2)}) collective-permute-start(bf16[16,48,256]{2,1,0:T(8,128)(2,1)} %x_hbm.1), channel_id=1, source_target_pairs={{0,4},{4,0},{1,5},{5,1},{2,6},{6,2},{3,7},{7,3},{8,12},{12,8},{9,1... | collective-permute-start | bytes 1179656 | tf_op jit(solution)/shard_map/ppermute | solution.py:489
  5.7 4.3 %copy-start.4 = (s32[16]{0:T(128)S(1)}, s32[16]{0:T(128)}, u32[]{:S(2)}) copy-start(s32[16]{0:T(128)} %own_slots.1) | copy-start | bytes 196
  5.7 6.2 %collective-permute-start.2 = (bf16[8,48,128]{2,1,0:T(8,128)(2,1)S(1)}, bf16[8,48,128]{2,1,0:T(8,128)(2,1)S(1)}, u32[]{:S(2)}, u32[]{:S(2)}) collective-permute-start(bf16[8,48,128]{2,1,0:T(8,128)(2,1)S(1)} %get-tuple-element.49), channel_id=1, source_target_pairs={{4,8},{8,4},{12,16},{16,12},{20,24},{24,20},{28,32},{32,28},{36,40... | collective-permute-start | bytes 294920 | tf_op jit(solution)/shard_map/ppermute | solution.py:493
  7.6 5.9 %copy-start.2 = (s32[8,8]{1,0:T(8,128)S(1)}, s32[8,8]{1,0:T(8,128)}, u32[]{:S(2)}) copy-start(s32[8,8]{1,0:T(8,128)} %adj.3) | copy-start | bytes 772
  7.6 13.2 %collective-permute-start.8 = (bf16[400,256]{1,0:T(8,128)(2,1)S(1)}, bf16[400,256]{1,0:T(8,128)(2,1)S(1)}, u32[]{:S(2)}, u32[]{:S(2)}) collective-permute-start(bf16[400,256]{1,0:T(8,128)(2,1)S(1)} %get-tuple-element.58), channel_id=1, source_target_pairs={{0,2},{1,3},{2,0},{3,1},{4,6},{5,7},{6,4},{7,5},{8,10},{9,11},{10,... | collective-permute-start | bytes 614408 | tf_op jit(solution)/shard_map/ppermute | solution.py:471
  10.0 1.1 %collective-permute-start = (s32[16]{0:T(128)S(1)}, s32[16]{0:T(128)S(1)}, u32[]{:S(2)}, u32[]{:S(2)}) collective-permute-start(s32[16]{0:T(128)S(1)} %copy-done.4), channel_id=1, source_target_pairs={{0,4},{4,0},{1,5},{5,1},{2,6},{6,2},{3,7},{7,3},{8,12},{12,8},{9,1... | collective-permute-start | bytes 200 | tf_op jit(solution)/shard_map/ppermute | solution.py:489
  10.0 11.0 %collective-permute-start.9 = (bf16[400,256]{1,0:T(8,128)(2,1)S(1)}, bf16[400,256]{1,0:T(8,128)(2,1)S(1)}, u32[]{:S(2)}, u32[]{:S(2)}) collective-permute-start(bf16[400,256]{1,0:T(8,128)(2,1)S(1)} %get-tuple-element.59), channel_id=1, source_target_pairs={{0,3},{1,0},{2,1},{3,2},{4,7},{5,4},{6,5},{7,6},{8,11},{9,8},{10,9... | collective-permute-start | bytes 614408 | tf_op jit(solution)/shard_map/ppermute | solution.py:471
  11.9 9.1 %collective-permute-start.7 = (bf16[400,256]{1,0:T(8,128)(2,1)S(1)}, bf16[400,256]{1,0:T(8,128)(2,1)S(1)}, u32[]{:S(2)}, u32[]{:S(2)}) collective-permute-start(bf16[400,256]{1,0:T(8,128)(2,1)S(1)} %get-tuple-element.57), channel_id=1, source_target_pairs={{0,1},{1,2},{2,3},{3,0},{4,5},{5,6},{6,7},{7,4},{8,9},{9,10},{10,1... | collective-permute-start | bytes 614408 | tf_op jit(solution)/shard_map/ppermute | solution.py:471
  11.9 1.5 %collective-permute-start.3 = (bf16[8,48,128]{2,1,0:T(8,128)(2,1)S(1)}, bf16[8,48,128]{2,1,0:T(8,128)(2,1)S(1)}, u32[]{:S(2)}, u32[]{:S(2)}) collective-permute-start(bf16[8,48,128]{2,1,0:T(8,128)(2,1)S(1)} %collective-permute-done.2.near_ref), channel_id=1, source_target_pairs={{0,4},{4,0},{1,5},{5,1},{2,6},{6,2},{3,7},{7,3},{8,12},{12,8},{9,1... | collective-permute-start | bytes 294920 | tf_op jit(solution)/shard_map/ppermute | solution.py:489
  17.1 4.5 %collective-permute-start.4 = (bf16[2,48,256]{2,1,0:T(8,128)(2,1)S(1)}, bf16[2,48,256]{2,1,0:T(8,128)(2,1)S(1)}, u32[]{:S(2)}, u32[]{:S(2)}) collective-permute-start(bf16[2,48,256]{2,1,0:T(8,128)(2,1)S(1)} %get-tuple-element.52), channel_id=1, source_target_pairs={{0,1},{1,2},{2,3},{3,0},{4,5},{5,6},{6,7},{7,4},{8,9},{9,10},{10,1... | collective-permute-start | bytes 147464 | tf_op jit(solution)/shard_map/ppermute | solution.py:471
  17.7 5.7 %collective-permute-start.5 = (bf16[2,48,256]{2,1,0:T(8,128)(2,1)S(1)}, bf16[2,48,256]{2,1,0:T(8,128)(2,1)S(1)}, u32[]{:S(2)}, u32[]{:S(2)}) collective-permute-start(bf16[2,48,256]{2,1,0:T(8,128)(2,1)S(1)} %get-tuple-element.53), channel_id=1, source_target_pairs={{0,2},{1,3},{2,0},{3,1},{4,6},{5,7},{6,4},{7,5},{8,10},{9,11},{10,... | collective-permute-start | bytes 147464 | tf_op jit(solution)/shard_map/ppermute | solution.py:471
  20.8 3.2 %collective-permute-start.6 = (bf16[2,48,256]{2,1,0:T(8,128)(2,1)S(1)}, bf16[2,48,256]{2,1,0:T(8,128)(2,1)S(1)}, u32[]{:S(2)}, u32[]{:S(2)}) collective-permute-start(bf16[2,48,256]{2,1,0:T(8,128)(2,1)S(1)} %get-tuple-element.54), channel_id=1, source_target_pairs={{0,3},{1,0},{2,1},{3,2},{4,7},{5,4},{6,5},{7,6},{8,11},{9,8},{10,9... | collective-permute-start | bytes 147464 | tf_op jit(solution)/shard_map/ppermute | solution.py:471
  26.9 5.0 %collective-permute-start.14 = (bf16[4,288,128]{2,1,0:T(8,128)(2,1)S(1)}, bf16[4,288,128]{2,1,0:T(8,128)(2,1)S(1)}, u32[]{:S(2)}, u32[]{:S(2)}) collective-permute-start(bf16[4,288,128]{2,1,0:T(8,128)(2,1)S(1)} %get-tuple-element.76), channel_id=1, source_target_pairs={{0,4},{4,0},{1,5},{5,1},{2,6},{6,2},{3,7},{7,3},{8,12},{12,8},{9,1... | collective-permute-start | bytes 884744 | tf_op jit(solution)/shard_map/ppermute | solution.py:489
  28.5 7.5 %collective-permute-start.10 = (bf16[192,256]{1,0:T(8,128)(2,1)S(1)}, bf16[192,256]{1,0:T(8,128)(2,1)S(1)}, u32[]{:S(2)}, u32[]{:S(2)}) collective-permute-start(bf16[192,256]{1,0:T(8,128)(2,1)S(1)} %get-tuple-element.72), channel_id=1, source_target_pairs={{0,1},{1,2},{2,3},{3,0},{4,5},{5,6},{6,7},{7,4},{8,9},{9,10},{10,1... | collective-permute-start | bytes 294920 | tf_op jit(solution)/shard_map/ppermute | solution.py:471
  28.5 7.5 %collective-permute-start.11 = (bf16[192,256]{1,0:T(8,128)(2,1)S(1)}, bf16[192,256]{1,0:T(8,128)(2,1)S(1)}, u32[]{:S(2)}, u32[]{:S(2)}) collective-permute-start(bf16[192,256]{1,0:T(8,128)(2,1)S(1)} %get-tuple-element.73), channel_id=1, source_target_pairs={{0,2},{1,3},{2,0},{3,1},{4,6},{5,7},{6,4},{7,5},{8,10},{9,11},{10,... | collective-permute-start | bytes 294920 | tf_op jit(solution)/shard_map/ppermute | solution.py:471
  31.1 5.2 %collective-permute-start.12 = (bf16[192,256]{1,0:T(8,128)(2,1)S(1)}, bf16[192,256]{1,0:T(8,128)(2,1)S(1)}, u32[]{:S(2)}, u32[]{:S(2)}) collective-permute-start(bf16[192,256]{1,0:T(8,128)(2,1)S(1)} %get-tuple-element.74), channel_id=1, source_target_pairs={{0,3},{1,0},{2,1},{3,2},{4,7},{5,4},{6,5},{7,6},{8,11},{9,8},{10,9... | collective-permute-start | bytes 294920 | tf_op jit(solution)/shard_map/ppermute | solution.py:471
  32.6 9.2 %all-to-all-start = ((bf16[4,288,128]{2,1,0:T(8,128)(2,1)}), bf16[4,288,128]{2,1,0:T(8,128)(2,1)S(1)}, u32[]{:S(2)}, u32[]{:S(2)}) async-start(bf16[4,288,128]{2,1,0:T(8,128)(2,1)} %merge.1), calls=%async_computation | async-start | bytes 589824 | tf_op jit(solution)/shard_map/all_to_all | solution.py:566
  36.3 3.5 %collective-permute-start.13 = (bf16[8,48,256]{2,1,0:T(8,128)(2,1)S(1)}, bf16[8,48,256]{2,1,0:T(8,128)(2,1)S(1)}, u32[]{:S(2)}, u32[]{:S(2)}) collective-permute-start(bf16[8,48,256]{2,1,0:T(8,128)(2,1)S(1)} %land.1.grad_ref.own_ref), channel_id=1, source_target_pairs={{0,4},{4,0},{1,5},{5,1},{2,6},{6,2},{3,7},{7,3},{8,12},{12,8},{9,1... | collective-permute-start | bytes 589832 | tf_op jit(solution)/shard_map/ppermute | solution.py:489
  42.6 21.9 %all-to-all-start.1 = ((bf16[32,16,128]{2,1,0:T(8,128)(2,1)}), bf16[32,16,128]{2,1,0:T(8,128)(2,1)S(1)}, u32[]{:S(2)}, u32[]{:S(2)}) async-start(bf16[32,16,128]{2,1,0:T(8,128)(2,1)} %pieces.1), calls=%async_computation.1 | async-start | bytes 262144 | tf_op jit(solution)/shard_map/all_to_all | solution.py:593
  55.1 8.6 %collective-permute-start.15 = (bf16[8,48,128]{2,1,0:T(8,128)(2,1)S(1)}, bf16[8,48,128]{2,1,0:T(8,128)(2,1)S(1)}, u32[]{:S(2)}, u32[]{:S(2)}) collective-permute-start(bf16[8,48,128]{2,1,0:T(8,128)(2,1)S(1)} %edges.1), channel_id=1, source_target_pairs={{4,8},{8,4},{12,16},{16,12},{20,24},{24,20},{28,32},{32,28},{36,40... | collective-permute-start | bytes 294920 | tf_op jit(solution)/shard_map/ppermute | solution.py:493
  65.2 10.9 %copy-start.1 = (bf16[8,48,256]{2,1,0:T(8,128)(2,1)S(1)}, bf16[8,48,256]{2,1,0:T(8,128)(2,1)}, u32[]{:S(2)}) copy-start(bf16[8,48,256]{2,1,0:T(8,128)(2,1)} %cot_ref.1) | copy-start | bytes 589828
  65.2 17.3 %all-to-all-start.2 = ((bf16[32,16,128]{2,1,0:T(8,128)(2,1)}), bf16[32,16,128]{2,1,0:T(8,128)(2,1)S(1)}, u32[]{:S(2)}, u32[]{:S(2)}) async-start(bf16[32,16,128]{2,1,0:T(8,128)(2,1)} %totals.1), calls=%async_computation.2 | async-start | bytes 262144 | tf_op jit(solution)/shard_map/all_to_all | solution.py:601
  73.1 2.9 %copy-start.3 = (f32[48]{0:T(128)S(1)}, f32[48]{0:T(128)}, u32[]{:S(2)}) copy-start(f32[48]{0:T(128)} %param.21) | copy-start | bytes 580
  73.1 2.9 %collective-permute-start.16 = (bf16[8,48,128]{2,1,0:T(8,128)(2,1)S(1)}, bf16[8,48,128]{2,1,0:T(8,128)(2,1)S(1)}, u32[]{:S(2)}, u32[]{:S(2)}) collective-permute-start(bf16[8,48,128]{2,1,0:T(8,128)(2,1)S(1)} %collective-permute-done.15.near_ref), channel_id=1, source_target_pairs={{0,4},{4,0},{1,5},{5,1},{2,6},{6,2},{3,7},{7,3},{8,12},{12,8},{9,1... | collective-permute-start | bytes 294920 | tf_op jit(solution)/shard_map/ppermute | solution.py:489
  82.5 4.1 %collective-permute-start.17 = (bf16[32,16,128]{2,1,0:T(8,128)(2,1)S(1)}, bf16[32,16,128]{2,1,0:T(8,128)(2,1)S(1)}, u32[]{:S(2)}, u32[]{:S(2)}) collective-permute-start(bf16[32,16,128]{2,1,0:T(8,128)(2,1)S(1)} %all-to-all-done.2.in_ref), channel_id=1, source_target_pairs={{0,4},{4,0},{1,5},{5,1},{2,6},{6,2},{3,7},{7,3},{8,12},{12,8},{9,1... | collective-permute-start | bytes 393224 | tf_op jit(solution)/shard_map/ppermute | solution.py:489

commit v7 on v6

--- a/solution.py
+++ b/solution.py
@@ -400,15 +400,11 @@
     dw_ref[...] = dw.T[0:48, 0:49]
 
 
-def unmix_kernel(
-    adj, grad_ref, par_ref, near_ref, far_ref, cot_ref, taps, maps,
-    owned_ref, scale_ref, r0, r1, r2, r3,
-    out_ref, gin_ref,
-    table, up_g, mid_g, down_g, pad, result,
+def surround_kernel(
+    adj, grad_ref, par_ref, near_ref, far_ref, maps, pad, table, up_g, mid_g, down_g
 ):
     me = my_owner()
     odd = lax.axis_index("core")
-    mine = lax.axis_index("chan")
     start = 16 * (me // 2) - 16
     table[pl.ds(16 + 8 * odd, 8)] = grad_ref[...]
     table[pl.ds(24 - 8 * odd, 8)] = par_ref[...]
@@ -419,6 +415,12 @@
         entries = [jnp.where(adj[t, k] < 512, adj[t, k] - start, 48) for k in range(8)]
         gather_tile(table, up_g, mid_g, down_g, t, center, entries)
     build_padded(pad, up_g, mid_g, down_g, maps)
+
+
+def unmix_kernel(
+    pad, cot_ref, taps, owned_ref, scale_ref, r0, r1, r2, r3, out_ref, gin_ref, result
+):
+    mine = lax.axis_index("chan")
     convolve(pad, taps, result, True)
     back = result[...].T.reshape(8, 48, 256)
     gin_ref[...] = (cot_ref[...].astype(F32) + back).astype(BF16)
@@ -427,11 +429,12 @@
         first = 2 * ((mine + 4 - j) & 3)
         for i in range(2):
             out_ref[first + i] = (
-                owned_ref[first + i].astype(F32) + scale * ref[96 + 48 * i : 144 + 48 * i].astype(F32)
+                owned_ref[first + i].astype(F32)
+                + scale * ref[96 + 48 * i : 144 + 48 * i].astype(F32)
             ).astype(BF16)
 
 
-def call(kernel, shapes, scratch=(), smem=0, n_in=0, name=None, near=()):
+def call(kernel, shapes, scratch=(), smem=0, n_in=0, name=None, near=(), micros=None):
     vmem = pl.BlockSpec(memory_space=pltpu.VMEM)
     scalar = pl.BlockSpec(memory_space=pltpu.SMEM)
     many = isinstance(shapes, (list, tuple))
@@ -443,6 +446,9 @@
         out_specs=[vmem] * len(shapes) if many else vmem,
         scratch_shapes=list(scratch),
         compiler_params=pltpu.CompilerParams(vmem_limit_bytes=24 << 20),
+        cost_estimate=None if micros is None else pl.CostEstimate(
+            flops=int(micros * 1e9), transcendentals=0, bytes_accessed=int(micros * 3.69e6)
+        ),
         name=name,
     )
 
@@ -591,28 +597,33 @@
         near=range(2),
     )(partials, tap_sums)
     arrived = lax.all_to_all(after(pieces, edges), "chip", 0, 0, tiled=True)
-    arrived, near_grads = lax.optimization_barrier((arrived, near_grads))
 
     factor = 1.0 / math.sqrt(adjacency.shape[0] * devices * PIX)
     far_grads = partner(near_grads)
+    surrounded = call(
+        surround_kernel,
+        held(3, 22 * WIDE, 128, dtype=F32),
+        scratch=grid_scratch(49)[0:4],
+        smem=1,
+        n_in=6,
+        name="surround",
+        near=(1, 2, 3, 4),
+        micros=0.7,
+    )(adjacency, grads, par_grads, near_grads, far_grads, maps)
+    arrived, surrounded = lax.optimization_barrier((arrived, surrounded))
     totals = call(
         functools.partial(total_kernel, factor), held(32, 16, 128), n_in=1, name="totals", near=(0,)
     )(arrived)
     spread = lax.all_to_all(totals, "chip", 0, 0, tiled=True)
 
-    unmix = call(
+    output, grad_in = call(
         unmix_kernel,
         [shape(8, 48, 256), shape(8, 48, 256)],
-        scratch=grid_scratch(49),
-        smem=1,
-        n_in=14,
+        scratch=[pltpu.VMEM((256, 384), F32)],
+        n_in=9,
         name="unmix",
-        near=(1, 2, 3, 4, 10, 11, 12, 13),
-    )
-    output, grad_in = unmix(
-        adjacency, grads, par_grads, near_grads, far_grads,
-        cotangent, taps, maps, owned, after(scale_row, totals), *all_back
-    )
+        near=(0, 5, 6, 7, 8),
+    )(surrounded, cotangent, taps, owned, after(scale_row, totals), *all_back)
     spread = after(spread, output)
     grad_dw, grad_w1, grad_w2 = call(
         finish_kernel,

time: 88 us -> 85.7 us (0.974)
  starting transfers between devices: 54 us -> 47.3 us
  waiting for transfers between devices: 14.2 us -> 18.1 us
    all_to_all x1, waiting for transfers between devices: 0.72 us -> 5.55 us  [body(): arrived = lax.all_to_all(after(pieces, edges), 'chip', 0, 0, tiled=True)]
    all_to_all x1, starting transfers between devices: 7.94 us -> 4.09 us  [body(): spread = lax.all_to_all(totals, 'chip', 0, 0, tiled=True)]
    all_to_all x1, waiting for transfers between devices: 2.15 us -> 5.92 us  [body(): spread = lax.all_to_all(totals, 'chip', 0, 0, tiled=True)]
    ppermute x2, waiting for transfers between devices: 3.76 us -> 0.83 us  [next_chip(): lax.ppermute(value, owners, [p for p in pairs if 0 <= p[1] < devices])]
    ppermute x2, starting transfers between devices: 7.6 us -> 4.86 us  [next_chip(): lax.ppermute(value, owners, [p for p in pairs if 0 <= p[1] < devices])]
    all_to_all x1, waiting for transfers between devices: 1.84 us -> 0.01 us  [body(): partials = lax.all_to_all(merged, 'chan', 0, 0, tiled=True)]
    pallas_call x11 -> x12, Pallas kernels: 16.9 us -> 16.7 us  [run(): inner(*(pltpu.with_memory_space_constraint(a, pltpu.VMEM) if i in near el...]
  transfers between devices with their start and end apart: 21 -> 21, of which waited for: 12 -> 10; matrix products, arithmetic and copies ran while one was open for 0% -> 0% of each run, Pallas kernels for 15% -> 16%
where the time goes in v7:
time: 85.7 us; the launch traced here: 85.3 us
  starting transfers between devices  47.3 us (55%)
  Pallas kernels  18.4 us (21%)
  waiting for transfers between devices  18.1 us (21%)
    pallas_call x12, Pallas kernels, run(): inner(*(pltpu.with_memory_space_constraint(a, pltpu.VMEM) if i in near el...  16.7 us
    all_to_all x1, starting transfers between devices, body(): arrived = lax.all_to_all(after(pieces, edges), 'chip', 0, 0, tiled=True)  12.5 us
    ppermute x7, starting transfers between devices, partner(): return lax.ppermute(value, 'core', [(0, 1), (1, 0)])  12.1 us
    ppermute x9, starting transfers between devices, along_chan(): lax.ppermute(values[j], 'chan', [(i, (i + j) % 4) for i in range(4)])  10.3 us
    all_to_all x1, waiting for transfers between devices, body(): spread = lax.all_to_all(totals, 'chip', 0, 0, tiled=True)  5.92 us
    all_to_all x1, waiting for transfers between devices, body(): arrived = lax.all_to_all(after(pieces, edges), 'chip', 0, 0, tiled=True)  5.55 us
    ppermute x2, starting transfers between devices, next_chip(): lax.ppermute(value, owners, [p for p in pairs if 0 <= p[1] < devices])  4.86 us
    all_to_all x1, starting transfers between devices, body(): spread = lax.all_to_all(totals, 'chip', 0, 0, tiled=True)  4.09 us
  transfers between devices with their start and end apart: 21, of which 10 were waited for; matrix products, arithmetic and copies ran while one was open for 0% of the time, Pallas kernels for 16%

profile of v7, /device:TPU:1, one launch (start us, length us, event | category | flops | bytes accessed | tf_op | source)
XLA Modules:
  0.0 85.3 jit_solution(2112554669579033941)
XLA Ops:
  0.6 0.0 copy-start
  0.6 3.3 %collective-permute-start.1 = (bf16[16,48,256]{2,1,0:T(8,128)(2,1)}, bf16[16,48,256]{2,1,0:T(8,128)(2,1)S(1)}, u32[]{:S(2)}, u32[]{:S(2)}) collective-permute-start(bf16[16,48,256]{2,1,0:T(8,128)(2,1)} %x_hbm.1), channel_id=1, source_target_pairs={{0,4},{4,0},{1,5},{5,1},{2,6},{6,2},{3,7},{7,3},{8,12},{12,8},{9,1... | collective-permute-start | bytes 1179656 | tf_op jit(solution)/shard_map/ppermute | solution.py:495
  4.0 1.7 %open.1 = (bf16[8,48,128]{2,1,0:T(8,128)(2,1)S(1)}, bf16[400,256]{1,0:T(8,128)(2,1)S(1)}, bf16[400,256]{1,0:T(8,128)(2,1)S(1)}, bf16[400,256]{1,0:T(8,128)(2,1)S...) custom-call(bf16[16,48,256]{2,1,0:T(8,128)(2,1)} %x_hbm.1, ...), custom_call_target="tpu_custom_call" | custom-call | tf_op jit(solution)/shard_map/open/pallas_call | solution.py:507
  5.7 0.0 copy-start.4
  5.7 1.9 %collective-permute-start.2 = (bf16[8,48,128]{2,1,0:T(8,128)(2,1)S(1)}, bf16[8,48,128]{2,1,0:T(8,128)(2,1)S(1)}, u32[]{:S(2)}, u32[]{:S(2)}) collective-permute-start(bf16[8,48,128]{2,1,0:T(8,128)(2,1)S(1)} %get-tuple-element.49), channel_id=1, source_target_pairs={{4,8},{8,4},{12,16},{16,12},{20,24},{24,20},{28,32},{32,28},{36,40... | collective-permute-start | bytes 294920 | tf_op jit(solution)/shard_map/ppermute | solution.py:499
  7.6 0.0 copy-start.2
  7.6 2.3 %collective-permute-start.8 = (bf16[400,256]{1,0:T(8,128)(2,1)S(1)}, bf16[400,256]{1,0:T(8,128)(2,1)S(1)}, u32[]{:S(2)}, u32[]{:S(2)}) collective-permute-start(bf16[400,256]{1,0:T(8,128)(2,1)S(1)} %get-tuple-element.58), channel_id=1, source_target_pairs={{0,2},{1,3},{2,0},{3,1},{4,6},{5,7},{6,4},{7,5},{8,10},{9,11},{10,... | collective-permute-start | bytes 614408 | tf_op jit(solution)/shard_map/ppermute | solution.py:477
  10.0 0.9 %collective-permute-start.9 = (bf16[400,256]{1,0:T(8,128)(2,1)S(1)}, bf16[400,256]{1,0:T(8,128)(2,1)S(1)}, u32[]{:S(2)}, u32[]{:S(2)}) collective-permute-start(bf16[400,256]{1,0:T(8,128)(2,1)S(1)} %get-tuple-element.59), channel_id=1, source_target_pairs={{0,3},{1,0},{2,1},{3,2},{4,7},{5,4},{6,5},{7,6},{8,11},{9,8},{10,9... | collective-permute-start | bytes 614408 | tf_op jit(solution)/shard_map/ppermute | solution.py:477
  10.8 0.3 collective-permute-done.par_slots
  11.1 0.8 collective-permute-done.2.near_ref
  11.9 0.0 collective-permute-start.7
  11.9 0.6 collective-permute-start.3
  12.5 0.9 %collective-permute-done.3.far_ref = bf16[8,48,128]{2,1,0:T(8,128)(2,1)S(1)} collective-permute-done((bf16[8,48,128]{2,1,0:T(8,128)(2,1)S(1)}, bf16[8,48,128]{2,1,0:T(8,128)(2,1)S(1)}, u32[]{:S(2)}, u32[]{:S(2)}) %collective-permute-start.3) | collective-permute-done | bytes 98336 | tf_op jit(solution)/shard_map/ppermute | solution.py:495
  13.5 0.0 collective-permute-done.1.par_ref
  13.5 3.6 %mix.1 = (bf16[8,48,256]{2,1,0:T(8,128)(2,1)S(1)}, bf16[3,528,128]{2,1,0:T(8,128)(2,1)S(1)}, bf16[2,48,256]{2,1,0:T(8,128)(2,1)S(1)}, bf16[2,48,256]{2,1,0:T(8,1...) custom-call(s32[16]{0:T(128)S(1)} %copy-done.4, s32[16]{0:T(128)S(1)} %collective-permute-done.par_slots, ...), custom_call_target="tpu_custom_call" | custom-call | tf_op jit(solution)/shard_map/mix/pallas_call | solution.py:456
  17.1 0.5 collective-permute-start.4
  17.6 3.2 %collective-permute-start.5 = (bf16[2,48,256]{2,1,0:T(8,128)(2,1)S(1)}, bf16[2,48,256]{2,1,0:T(8,128)(2,1)S(1)}, u32[]{:S(2)}, u32[]{:S(2)}) collective-permute-start(bf16[2,48,256]{2,1,0:T(8,128)(2,1)S(1)} %get-tuple-element.53), channel_id=1, source_target_pairs={{0,2},{1,3},{2,0},{3,1},{4,6},{5,7},{6,4},{7,5},{8,10},{9,11},{10,... | collective-permute-start | bytes 147464 | tf_op jit(solution)/shard_map/ppermute | solution.py:477
  20.8 0.1 collective-permute-start.6
  20.9 0.6 turn.1
  21.5 1.7 %collective-permute-done.5.m2 = bf16[2,48,256]{2,1,0:T(8,128)(2,1)S(1)} collective-permute-done((bf16[2,48,256]{2,1,0:T(8,128)(2,1)S(1)}, bf16[2,48,256]{2,1,0:T(8,128)(2,1)S(1)}, u32[]{:S(2)}, u32[]{:S(2)}) %collective-permute-start.5) | collective-permute-done | bytes 49184 | tf_op jit(solution)/shard_map/ppermute | solution.py:477
  23.3 0.8 collective-permute-done.6.m3
  24.0 2.8 %mlp.1 = (bf16[192,256]{1,0:T(8,128)(2,1)S(1)}, bf16[192,256]{1,0:T(8,128)(2,1)S(1)}, bf16[192,256]{1,0:T(8,128)(2,1)S(1)}, bf16[192,256]{1,0:T(8,128)(2,1)S(1)}...) custom-call(bf16[2,48,256]{2,1,0:T(8,128)(2,1)S(1)} %get-tuple-element.51.m0, ...), custom_call_target="tpu_custom_call" | custom-call | tf_op jit(solution)/shard_map/mlp/pallas_call | solution.py:456
  26.8 1.7 %collective-permute-start.10 = (bf16[4,288,128]{2,1,0:T(8,128)(2,1)S(1)}, bf16[4,288,128]{2,1,0:T(8,128)(2,1)S(1)}, u32[]{:S(2)}, u32[]{:S(2)}) collective-permute-start(bf16[4,288,128]{2,1,0:T(8,128)(2,1)S(1)} %get-tuple-element.72), channel_id=1, source_target_pairs={{0,4},{4,0},{1,5},{5,1},{2,6},{6,2},{3,7},{7,3},{8,12},{12,8},{9,1... | collective-permute-start | bytes 884744 | tf_op jit(solution)/shard_map/ppermute | solution.py:495
  28.4 0.0 collective-permute-start.11
  28.4 2.5 %collective-permute-start.12 = (bf16[192,256]{1,0:T(8,128)(2,1)S(1)}, bf16[192,256]{1,0:T(8,128)(2,1)S(1)}, u32[]{:S(2)}, u32[]{:S(2)}) collective-permute-start(bf16[192,256]{1,0:T(8,128)(2,1)S(1)} %get-tuple-element.75), channel_id=1, source_target_pairs={{0,2},{1,3},{2,0},{3,1},{4,6},{5,7},{6,4},{7,5},{8,10},{9,11},{10,... | collective-permute-start | bytes 294920 | tf_op jit(solution)/shard_map/ppermute | solution.py:477
  31.0 0.8 collective-permute-start.13
  31.7 0.8 merge.1
  32.5 3.5 %all-to-all-start = ((bf16[4,288,128]{2,1,0:T(8,128)(2,1)}), bf16[4,288,128]{2,1,0:T(8,128)(2,1)S(1)}, u32[]{:S(2)}, u32[]{:S(2)}) async-start(bf16[4,288,128]{2,1,0:T(8,128)(2,1)} %merge.1), calls=%async_computation | async-start | bytes 589824 | tf_op jit(solution)/shard_map/all_to_all | solution.py:572
  36.0 0.1 collective-permute-done.13.g3.r3
  36.2 1.5 %collective-permute-start.14 = (bf16[8,48,256]{2,1,0:T(8,128)(2,1)S(1)}, bf16[8,48,256]{2,1,0:T(8,128)(2,1)S(1)}, u32[]{:S(2)}, u32[]{:S(2)}) collective-permute-start(bf16[8,48,256]{2,1,0:T(8,128)(2,1)S(1)} %land.1.grad_ref.own_ref), channel_id=1, source_target_pairs={{0,4},{4,0},{1,5},{5,1},{2,6},{6,2},{3,7},{7,3},{8,12},{12,8},{9,1... | collective-permute-start | bytes 589832 | tf_op jit(solution)/shard_map/ppermute | solution.py:495
  37.7 2.0 %tap_sums.1.taps_ref = f32[64,128]{1,0:T(8,128)S(1)} custom-call(bf16[8,48,256]{2,1,0:T(8,128)(2,1)S(1)} %land.1.grad_ref.own_ref, bf16[3,528,128]{2,1,0:T(8,128)(2,1)S(1)} %get-tuple-element.77.pad_ref, f32[128,384]{1,0:T(8,128)S(1)} %get-tuple-element.78.fold), custom_call_target="tpu_custom_call" | custom-call | tf_op jit(solution)/shard_map/tap_sums/pallas_call | solution.py:456
  39.7 0.1 edges.1
  39.8 2.9 %collective-permute-start.15 = (bf16[8,48,128]{2,1,0:T(8,128)(2,1)S(1)}, bf16[8,48,128]{2,1,0:T(8,128)(2,1)S(1)}, u32[]{:S(2)}, u32[]{:S(2)}) collective-permute-start(bf16[8,48,128]{2,1,0:T(8,128)(2,1)S(1)} %edges.1), channel_id=1, source_target_pairs={{4,8},{8,4},{12,16},{16,12},{20,24},{24,20},{28,32},{32,28},{36,40... | collective-permute-start | bytes 294920 | tf_op jit(solution)/shard_map/ppermute | solution.py:499
  42.8 0.8 pieces.1
  43.6 12.5 %all-to-all-start.1 = ((bf16[32,16,128]{2,1,0:T(8,128)(2,1)}), bf16[32,16,128]{2,1,0:T(8,128)(2,1)S(1)}, u32[]{:S(2)}, u32[]{:S(2)}) async-start(bf16[32,16,128]{2,1,0:T(8,128)(2,1)} %pieces.1), calls=%async_computation.1 | async-start | bytes 262144 | tf_op jit(solution)/shard_map/all_to_all | solution.py:599
  56.1 1.4 %collective-permute-start.16 = (bf16[8,48,128]{2,1,0:T(8,128)(2,1)S(1)}, bf16[8,48,128]{2,1,0:T(8,128)(2,1)S(1)}, u32[]{:S(2)}, u32[]{:S(2)}) collective-permute-start(bf16[8,48,128]{2,1,0:T(8,128)(2,1)S(1)} %collective-permute-done.15.near_ref), channel_id=1, source_target_pairs={{0,4},{4,0},{1,5},{5,1},{2,6},{6,2},{3,7},{7,3},{8,12},{12,8},{9,1... | collective-permute-start | bytes 294920 | tf_op jit(solution)/shard_map/ppermute | solution.py:495
  57.5 0.9 %collective-permute-done.16.far_ref = bf16[8,48,128]{2,1,0:T(8,128)(2,1)S(1)} collective-permute-done((bf16[8,48,128]{2,1,0:T(8,128)(2,1)S(1)}, bf16[8,48,128]{2,1,0:T(8,128)(2,1)S(1)}, u32[]{:S(2)}, u32[]{:S(2)}) %collective-permute-start.16) | collective-permute-done | bytes 98336 | tf_op jit(solution)/shard_map/ppermute | solution.py:495
  58.5 1.4 %surround.1.pad = f32[3,528,128]{2,1,0:T(8,128)S(1)} custom-call(s32[8,8]{1,0:T(8,128)S(1)} %copy-done.2, bf16[8,48,256]{2,1,0:T(8,128)(2,1)S(1)} %land.1.grad_ref.own_ref, bf16[8,48,256]{2,1,0:T(8,128)(2,1)S(1)} %collective-permute-done.14.par_ref, bf16[8,48,128]{2,1,0:T(8,128)(2,1)S(1)} %collective-permute-done.15.near_ref, ...), custom_call_target="tpu_custom_call" | custom-call | flops 700000000 | bytes 2583000 | tf_op jit(solution)/shard_map/surround/pallas_call | solution.py:456
  59.9 5.6 %all-to-all-done.1.in_ref = bf16[32,16,128]{2,1,0:T(8,128)(2,1)S(1)} async-done(((bf16[32,16,128]{2,1,0:T(8,128)(2,1)}), bf16[32,16,128]{2,1,0:T(8,128)(2,1)S(1)}, u32[]{:S(2)}, u32[]{:S(2)}) %all-to-all-start.1) | async-done | bytes 131104 | tf_op jit(solution)/shard_map/all_to_all | solution.py:599
  65.4 0.7 totals.1
  66.1 4.1 %all-to-all-start.2 = ((bf16[32,16,128]{2,1,0:T(8,128)(2,1)}), bf16[32,16,128]{2,1,0:T(8,128)(2,1)S(1)}, u32[]{:S(2)}, u32[]{:S(2)}) async-start(bf16[32,16,128]{2,1,0:T(8,128)(2,1)} %totals.1), calls=%async_computation.2 | async-start | bytes 262144 | tf_op jit(solution)/shard_map/all_to_all | solution.py:617
  70.2 0.0 copy-start.3
  70.3 0.6 copy-done.3
  70.9 2.8 %unmix.1 = (bf16[8,48,256]{2,1,0:T(8,128)(2,1)}, bf16[8,48,256]{2,1,0:T(8,128)(2,1)}) custom-call(f32[3,528,128]{2,1,0:T(8,128)S(1)} %surround.1.pad, bf16[8,48,256]{2,1,0:T(8,128)(2,1)S(1)} %copy-done.1, f32[56,384]{1,0:T(8,128)S(1)} %get-tuple-element.50.taps, bf16[8,48,256]{2,1,0:T(8,128)(2,1)S(1)} %get-tuple-element.82.owned_ref, f32[1,48]{1,0:T(1,128)S(1)} %bitcast.3, ...), custom_call_target="tpu_custom_call" | custom-call | tf_op jit(solution)/shard_map/unmix/pallas_call | solution.py:456
  73.7 5.9 %all-to-all-done.2.in_ref = bf16[32,16,128]{2,1,0:T(8,128)(2,1)S(1)} async-done(((bf16[32,16,128]{2,1,0:T(8,128)(2,1)}), bf16[32,16,128]{2,1,0:T(8,128)(2,1)S(1)}, u32[]{:S(2)}, u32[]{:S(2)}) %all-to-all-start.2) | async-done | bytes 131104 | tf_op jit(solution)/shard_map/all_to_all | solution.py:617
  79.6 3.6 %collective-permute-start.17 = (bf16[32,16,128]{2,1,0:T(8,128)(2,1)S(1)}, bf16[32,16,128]{2,1,0:T(8,128)(2,1)S(1)}, u32[]{:S(2)}, u32[]{:S(2)}) collective-permute-start(bf16[32,16,128]{2,1,0:T(8,128)(2,1)S(1)} %all-to-all-done.2.in_ref), channel_id=1, source_target_pairs={{0,4},{4,0},{1,5},{5,1},{2,6},{6,2},{3,7},{7,3},{8,12},{12,8},{9,1... | collective-permute-start | bytes 393224 | tf_op jit(solution)/shard_map/ppermute | solution.py:495
  83.2 1.0 %collective-permute-done.17.other_ref = bf16[32,16,128]{2,1,0:T(8,128)(2,1)S(1)} collective-permute-done((bf16[32,16,128]{2,1,0:T(8,128)(2,1)S(1)}, bf16[32,16,128]{2,1,0:T(8,128)(2,1)S(1)}, u32[]{:S(2)}, u32[]{:S(2)}) %collective-permute-start.17) | collective-permute-done | bytes 131104 | tf_op jit(solution)/shard_map/ppermute | solution.py:495
  84.2 1.1 %finish.1 = (f32[48,49]{1,0:T(8,128)}, f32[192,192]{1,0:T(8,128)}, f32[192,192]{1,0:T(8,128)}) custom-call(bf16[32,16,128]{2,1,0:T(8,128)(2,1)S(1)} %all-to-all-done.2.in_ref, bf16[32,16,128]{2,1,0:T(8,128)(2,1)S(1)} %collective-permute-done.17.other_ref), custom_call_target="tpu_custom_call" | custom-call | tf_op jit(solution)/shard_map/finish/pallas_call | solution.py:456
  (17 shorter events, 0.1 us)
Async XLA Ops:
  0.6 12.8 %copy-start = (bf16[528,768]{1,0:T(8,128)(2,1)S(1)}, bf16[528,768]{1,0:T(8,128)(2,1)}, u32[]{:S(2)}) copy-start(bf16[528,768]{1,0:T(8,128)(2,1)} %constant.4.clone.maps) | copy-start | bytes 2433028
  0.6 12.8 %collective-permute-start.1 = (bf16[16,48,256]{2,1,0:T(8,128)(2,1)}, bf16[16,48,256]{2,1,0:T(8,128)(2,1)S(1)}, u32[]{:S(2)}, u32[]{:S(2)}) collective-permute-start(bf16[16,48,256]{2,1,0:T(8,128)(2,1)} %x_hbm.1), channel_id=1, source_target_pairs={{0,4},{4,0},{1,5},{5,1},{2,6},{6,2},{3,7},{7,3},{8,12},{12,8},{9,1... | collective-permute-start | bytes 1179656 | tf_op jit(solution)/shard_map/ppermute | solution.py:495
  5.7 4.3 %copy-start.4 = (s32[16]{0:T(128)S(1)}, s32[16]{0:T(128)}, u32[]{:S(2)}) copy-start(s32[16]{0:T(128)} %own_slots.1) | copy-start | bytes 196
  5.7 6.2 %collective-permute-start.2 = (bf16[8,48,128]{2,1,0:T(8,128)(2,1)S(1)}, bf16[8,48,128]{2,1,0:T(8,128)(2,1)S(1)}, u32[]{:S(2)}, u32[]{:S(2)}) collective-permute-start(bf16[8,48,128]{2,1,0:T(8,128)(2,1)S(1)} %get-tuple-element.49), channel_id=1, source_target_pairs={{4,8},{8,4},{12,16},{16,12},{20,24},{24,20},{28,32},{32,28},{36,40... | collective-permute-start | bytes 294920 | tf_op jit(solution)/shard_map/ppermute | solution.py:499
  7.6 5.9 %copy-start.2 = (s32[8,8]{1,0:T(8,128)S(1)}, s32[8,8]{1,0:T(8,128)}, u32[]{:S(2)}) copy-start(s32[8,8]{1,0:T(8,128)} %adj.3) | copy-start | bytes 772
  7.6 13.1 %collective-permute-start.8 = (bf16[400,256]{1,0:T(8,128)(2,1)S(1)}, bf16[400,256]{1,0:T(8,128)(2,1)S(1)}, u32[]{:S(2)}, u32[]{:S(2)}) collective-permute-start(bf16[400,256]{1,0:T(8,128)(2,1)S(1)} %get-tuple-element.58), channel_id=1, source_target_pairs={{0,2},{1,3},{2,0},{3,1},{4,6},{5,7},{6,4},{7,5},{8,10},{9,11},{10,... | collective-permute-start | bytes 614408 | tf_op jit(solution)/shard_map/ppermute | solution.py:477
  10.0 1.1 %collective-permute-start = (s32[16]{0:T(128)S(1)}, s32[16]{0:T(128)S(1)}, u32[]{:S(2)}, u32[]{:S(2)}) collective-permute-start(s32[16]{0:T(128)S(1)} %copy-done.4), channel_id=1, source_target_pairs={{0,4},{4,0},{1,5},{5,1},{2,6},{6,2},{3,7},{7,3},{8,12},{12,8},{9,1... | collective-permute-start | bytes 200 | tf_op jit(solution)/shard_map/ppermute | solution.py:495
  10.0 10.9 %collective-permute-start.9 = (bf16[400,256]{1,0:T(8,128)(2,1)S(1)}, bf16[400,256]{1,0:T(8,128)(2,1)S(1)}, u32[]{:S(2)}, u32[]{:S(2)}) collective-permute-start(bf16[400,256]{1,0:T(8,128)(2,1)S(1)} %get-tuple-element.59), channel_id=1, source_target_pairs={{0,3},{1,0},{2,1},{3,2},{4,7},{5,4},{6,5},{7,6},{8,11},{9,8},{10,9... | collective-permute-start | bytes 614408 | tf_op jit(solution)/shard_map/ppermute | solution.py:477
  11.9 9.0 %collective-permute-start.7 = (bf16[400,256]{1,0:T(8,128)(2,1)S(1)}, bf16[400,256]{1,0:T(8,128)(2,1)S(1)}, u32[]{:S(2)}, u32[]{:S(2)}) collective-permute-start(bf16[400,256]{1,0:T(8,128)(2,1)S(1)} %get-tuple-element.57), channel_id=1, source_target_pairs={{0,1},{1,2},{2,3},{3,0},{4,5},{5,6},{6,7},{7,4},{8,9},{9,10},{10,1... | collective-permute-start | bytes 614408 | tf_op jit(solution)/shard_map/ppermute | solution.py:477
  11.9 1.5 %collective-permute-start.3 = (bf16[8,48,128]{2,1,0:T(8,128)(2,1)S(1)}, bf16[8,48,128]{2,1,0:T(8,128)(2,1)S(1)}, u32[]{:S(2)}, u32[]{:S(2)}) collective-permute-start(bf16[8,48,128]{2,1,0:T(8,128)(2,1)S(1)} %collective-permute-done.2.near_ref), channel_id=1, source_target_pairs={{0,4},{4,0},{1,5},{5,1},{2,6},{6,2},{3,7},{7,3},{8,12},{12,8},{9,1... | collective-permute-start | bytes 294920 | tf_op jit(solution)/shard_map/ppermute | solution.py:495
  17.1 4.5 %collective-permute-start.4 = (bf16[2,48,256]{2,1,0:T(8,128)(2,1)S(1)}, bf16[2,48,256]{2,1,0:T(8,128)(2,1)S(1)}, u32[]{:S(2)}, u32[]{:S(2)}) collective-permute-start(bf16[2,48,256]{2,1,0:T(8,128)(2,1)S(1)} %get-tuple-element.52), channel_id=1, source_target_pairs={{0,1},{1,2},{2,3},{3,0},{4,5},{5,6},{6,7},{7,4},{8,9},{9,10},{10,1... | collective-permute-start | bytes 147464 | tf_op jit(solution)/shard_map/ppermute | solution.py:477
  17.6 5.7 %collective-permute-start.5 = (bf16[2,48,256]{2,1,0:T(8,128)(2,1)S(1)}, bf16[2,48,256]{2,1,0:T(8,128)(2,1)S(1)}, u32[]{:S(2)}, u32[]{:S(2)}) collective-permute-start(bf16[2,48,256]{2,1,0:T(8,128)(2,1)S(1)} %get-tuple-element.53), channel_id=1, source_target_pairs={{0,2},{1,3},{2,0},{3,1},{4,6},{5,7},{6,4},{7,5},{8,10},{9,11},{10,... | collective-permute-start | bytes 147464 | tf_op jit(solution)/shard_map/ppermute | solution.py:477
  20.8 3.2 %collective-permute-start.6 = (bf16[2,48,256]{2,1,0:T(8,128)(2,1)S(1)}, bf16[2,48,256]{2,1,0:T(8,128)(2,1)S(1)}, u32[]{:S(2)}, u32[]{:S(2)}) collective-permute-start(bf16[2,48,256]{2,1,0:T(8,128)(2,1)S(1)} %get-tuple-element.54), channel_id=1, source_target_pairs={{0,3},{1,0},{2,1},{3,2},{4,7},{5,4},{6,5},{7,6},{8,11},{9,8},{10,9... | collective-permute-start | bytes 147464 | tf_op jit(solution)/shard_map/ppermute | solution.py:477
  26.8 5.0 %collective-permute-start.10 = (bf16[4,288,128]{2,1,0:T(8,128)(2,1)S(1)}, bf16[4,288,128]{2,1,0:T(8,128)(2,1)S(1)}, u32[]{:S(2)}, u32[]{:S(2)}) collective-permute-start(bf16[4,288,128]{2,1,0:T(8,128)(2,1)S(1)} %get-tuple-element.72), channel_id=1, source_target_pairs={{0,4},{4,0},{1,5},{5,1},{2,6},{6,2},{3,7},{7,3},{8,12},{12,8},{9,1... | collective-permute-start | bytes 884744 | tf_op jit(solution)/shard_map/ppermute | solution.py:495
  28.4 7.5 %collective-permute-start.11 = (bf16[192,256]{1,0:T(8,128)(2,1)S(1)}, bf16[192,256]{1,0:T(8,128)(2,1)S(1)}, u32[]{:S(2)}, u32[]{:S(2)}) collective-permute-start(bf16[192,256]{1,0:T(8,128)(2,1)S(1)} %get-tuple-element.74), channel_id=1, source_target_pairs={{0,1},{1,2},{2,3},{3,0},{4,5},{5,6},{6,7},{7,4},{8,9},{9,10},{10,1... | collective-permute-start | bytes 294920 | tf_op jit(solution)/shard_map/ppermute | solution.py:477
  28.4 7.5 %collective-permute-start.12 = (bf16[192,256]{1,0:T(8,128)(2,1)S(1)}, bf16[192,256]{1,0:T(8,128)(2,1)S(1)}, u32[]{:S(2)}, u32[]{:S(2)}) collective-permute-start(bf16[192,256]{1,0:T(8,128)(2,1)S(1)} %get-tuple-element.75), channel_id=1, source_target_pairs={{0,2},{1,3},{2,0},{3,1},{4,6},{5,7},{6,4},{7,5},{8,10},{9,11},{10,... | collective-permute-start | bytes 294920 | tf_op jit(solution)/shard_map/ppermute | solution.py:477
  31.0 5.2 %collective-permute-start.13 = (bf16[192,256]{1,0:T(8,128)(2,1)S(1)}, bf16[192,256]{1,0:T(8,128)(2,1)S(1)}, u32[]{:S(2)}, u32[]{:S(2)}) collective-permute-start(bf16[192,256]{1,0:T(8,128)(2,1)S(1)} %get-tuple-element.76), channel_id=1, source_target_pairs={{0,3},{1,0},{2,1},{3,2},{4,7},{5,4},{6,5},{7,6},{8,11},{9,8},{10,9... | collective-permute-start | bytes 294920 | tf_op jit(solution)/shard_map/ppermute | solution.py:477
  32.5 10.3 %all-to-all-start = ((bf16[4,288,128]{2,1,0:T(8,128)(2,1)}), bf16[4,288,128]{2,1,0:T(8,128)(2,1)S(1)}, u32[]{:S(2)}, u32[]{:S(2)}) async-start(bf16[4,288,128]{2,1,0:T(8,128)(2,1)} %merge.1), calls=%async_computation | async-start | bytes 589824 | tf_op jit(solution)/shard_map/all_to_all | solution.py:572
  36.2 3.5 %collective-permute-start.14 = (bf16[8,48,256]{2,1,0:T(8,128)(2,1)S(1)}, bf16[8,48,256]{2,1,0:T(8,128)(2,1)S(1)}, u32[]{:S(2)}, u32[]{:S(2)}) collective-permute-start(bf16[8,48,256]{2,1,0:T(8,128)(2,1)S(1)} %land.1.grad_ref.own_ref), channel_id=1, source_target_pairs={{0,4},{4,0},{1,5},{5,1},{2,6},{6,2},{3,7},{7,3},{8,12},{12,8},{9,1... | collective-permute-start | bytes 589832 | tf_op jit(solution)/shard_map/ppermute | solution.py:495
  39.8 16.3 %collective-permute-start.15 = (bf16[8,48,128]{2,1,0:T(8,128)(2,1)S(1)}, bf16[8,48,128]{2,1,0:T(8,128)(2,1)S(1)}, u32[]{:S(2)}, u32[]{:S(2)}) collective-permute-start(bf16[8,48,128]{2,1,0:T(8,128)(2,1)S(1)} %edges.1), channel_id=1, source_target_pairs={{4,8},{8,4},{12,16},{16,12},{20,24},{24,20},{28,32},{32,28},{36,40... | collective-permute-start | bytes 294920 | tf_op jit(solution)/shard_map/ppermute | solution.py:499
  43.6 21.8 %all-to-all-start.1 = ((bf16[32,16,128]{2,1,0:T(8,128)(2,1)}), bf16[32,16,128]{2,1,0:T(8,128)(2,1)S(1)}, u32[]{:S(2)}, u32[]{:S(2)}) async-start(bf16[32,16,128]{2,1,0:T(8,128)(2,1)} %pieces.1), calls=%async_computation.1 | async-start | bytes 262144 | tf_op jit(solution)/shard_map/all_to_all | solution.py:599
  56.1 2.3 %collective-permute-start.16 = (bf16[8,48,128]{2,1,0:T(8,128)(2,1)S(1)}, bf16[8,48,128]{2,1,0:T(8,128)(2,1)S(1)}, u32[]{:S(2)}, u32[]{:S(2)}) collective-permute-start(bf16[8,48,128]{2,1,0:T(8,128)(2,1)S(1)} %collective-permute-done.15.near_ref), channel_id=1, source_target_pairs={{0,4},{4,0},{1,5},{5,1},{2,6},{6,2},{3,7},{7,3},{8,12},{12,8},{9,1... | collective-permute-start | bytes 294920 | tf_op jit(solution)/shard_map/ppermute | solution.py:495
  66.1 4.1 %copy-start.1 = (bf16[8,48,256]{2,1,0:T(8,128)(2,1)S(1)}, bf16[8,48,256]{2,1,0:T(8,128)(2,1)}, u32[]{:S(2)}) copy-start(bf16[8,48,256]{2,1,0:T(8,128)(2,1)} %cot_ref.1) | copy-start | bytes 589828
  66.1 13.4 %all-to-all-start.2 = ((bf16[32,16,128]{2,1,0:T(8,128)(2,1)}), bf16[32,16,128]{2,1,0:T(8,128)(2,1)S(1)}, u32[]{:S(2)}, u32[]{:S(2)}) async-start(bf16[32,16,128]{2,1,0:T(8,128)(2,1)} %totals.1), calls=%async_computation.2 | async-start | bytes 262144 | tf_op jit(solution)/shard_map/all_to_all | solution.py:617
  70.2 0.7 copy-start.3
  79.6 4.6 %collective-permute-start.17 = (bf16[32,16,128]{2,1,0:T(8,128)(2,1)S(1)}, bf16[32,16,128]{2,1,0:T(8,128)(2,1)S(1)}, u32[]{:S(2)}, u32[]{:S(2)}) collective-permute-start(bf16[32,16,128]{2,1,0:T(8,128)(2,1)S(1)} %all-to-all-done.2.in_ref), channel_id=1, source_target_pairs={{0,4},{4,0},{1,5},{5,1},{2,6},{6,2},{3,7},{7,3},{8,12},{12,8},{9,1... | collective-permute-start | bytes 393224 | tf_op jit(solution)/shard_map/ppermute | solution.py:495

commit v8 on v7

--- a/solution.py
+++ b/solution.py
@@ -269,7 +269,7 @@
 
 def mlp_kernel(
     m0, m1, m2, m3, w_in, w_out, in_t, out_t, bias, gain, db_ref,
-    g0, g1, g2, g3, keep_ref, give_ref, mixed_s, back_s, branch_s, halves,
+    g0, g1, g2, g3, r0, r1, r2, r3, keep_ref, give_ref, mixed_s, back_s, branch_s, halves,
 ):
     mine = lax.axis_index("chan")
     for j, m_ref in enumerate((m0, m1, m2, m3)):
@@ -311,11 +311,11 @@
     dmixed = (inv * (xhat_grad - first - x_hat * second)).astype(BF16)
     back_s[...] = dmixed.reshape(4, 48, 512)
     branch_s[...] = branch.astype(BF16).reshape(4, 48, 512)
-    for j, g_ref in enumerate((g0, g1, g2, g3)):
+    for j, (g_ref, r_ref) in enumerate(((g0, r0), (g1, r1), (g2, r2), (g3, r3))):
         a = (mine + j) & 3
         for i in range(2):
             g_ref[48 * i : 48 * i + 48] = back_s[a, :, 256 * i : 256 * i + 256]
-            g_ref[96 + 48 * i : 144 + 48 * i] = branch_s[a, :, 256 * i : 256 * i + 256]
+            r_ref[48 * i : 48 * i + 48] = branch_s[a, :, 256 * i : 256 * i + 256]
 
 
 def land_kernel(g0, g1, g2, g3, grad_ref):
@@ -430,7 +430,7 @@
         for i in range(2):
             out_ref[first + i] = (
                 owned_ref[first + i].astype(F32)
-                + scale * ref[96 + 48 * i : 144 + 48 * i].astype(F32)
+                + scale * ref[48 * i : 48 * i + 48].astype(F32)
             ).astype(BF16)
 
 
@@ -557,15 +557,15 @@
     )
     turned = turn(*after(all_sends, mixed[0]))
 
-    *packets, keep, give = call(
+    *tiles, keep, give = call(
         mlp_kernel,
-        [held(192, 256)] * 4 + [held(4, 288, 128)] * 2,
+        [held(96, 256)] * 8 + [held(4, 288, 128)] * 2,
         scratch=[pltpu.VMEM((4, 48, 512), BF16)] * 3 + [pltpu.VMEM((2, 4, 288, 128), BF16)],
         n_in=11,
         name="mlp",
         near=range(11),
     )(*all_mixed, *turned)
-    all_back = along_chan(packets)
+    all_back = along_chan(tiles[0:4])
     merged = call(merge_kernel, held(4, 288, 128), n_in=2, name="merge", near=range(2))(
         keep, partner(give)
     )
@@ -600,6 +600,7 @@
 
     factor = 1.0 / math.sqrt(adjacency.shape[0] * devices * PIX)
     far_grads = partner(near_grads)
+    all_branch = along_chan(after(tiles[4:8], pieces))
     surrounded = call(
         surround_kernel,
         held(3, 22 * WIDE, 128, dtype=F32),
@@ -623,7 +624,7 @@
         n_in=9,
         name="unmix",
         near=(0, 5, 6, 7, 8),
-    )(surrounded, cotangent, taps, owned, after(scale_row, totals), *all_back)
+    )(surrounded, cotangent, taps, owned, after(scale_row, totals), *all_branch)
     spread = after(spread, output)
     grad_dw, grad_w1, grad_w2 = call(
         finish_kernel,

time: 85.7 us -> 85.7 us (level)
  starting transfers between devices: 47.3 us -> 52.7 us
  waiting for transfers between devices: 18.1 us -> 13.4 us
    all_to_all x1, waiting for transfers between devices: 5.92 us -> 0.01 us  [body(): spread = lax.all_to_all(totals, 'chip', 0, 0, tiled=True)]
    ppermute x9 -> x12, starting transfers between devices: 10.3 us -> 15.5 us  [along_chan(): lax.ppermute(values[j], 'chan', [(i, (i + j) % 4) for i in range(4)])]
    ppermute x9 -> x12, waiting for transfers between devices: 2.62 us -> 4.53 us  [along_chan(): lax.ppermute(values[j], 'chan', [(i, (i + j) % 4) for i in range(4)])]
  transfers between devices with their start and end apart: 21 -> 24, of which waited for: 10 -> 10; matrix products, arithmetic and copies ran while one was open for 0% -> 0% of each run, Pallas kernels for 16% -> 16%
where the time goes in v8:
time: 85.7 us; the launch traced here: 85.4 us
  starting transfers between devices  52.7 us (61%)
  Pallas kernels  18.4 us (21%)
  waiting for transfers between devices  13.4 us (16%)
    pallas_call x12, Pallas kernels, run(): inner(*(pltpu.with_memory_space_constraint(a, pltpu.VMEM) if i in near el...  16.7 us
    ppermute x12, starting transfers between devices, along_chan(): lax.ppermute(values[j], 'chan', [(i, (i + j) % 4) for i in range(4)])  15.5 us
    all_to_all x1, starting transfers between devices, body(): arrived = lax.all_to_all(after(pieces, edges), 'chip', 0, 0, tiled=True)  12.2 us
    ppermute x7, starting transfers between devices, partner(): return lax.ppermute(value, 'core', [(0, 1), (1, 0)])  11.9 us
    all_to_all x1, waiting for transfers between devices, body(): arrived = lax.all_to_all(after(pieces, edges), 'chip', 0, 0, tiled=True)  4.88 us
    ppermute x2, starting transfers between devices, next_chip(): lax.ppermute(value, owners, [p for p in pairs if 0 <= p[1] < devices])  4.86 us
    all_to_all x1, starting transfers between devices, body(): spread = lax.all_to_all(totals, 'chip', 0, 0, tiled=True)  4.77 us
    ppermute x12, waiting for transfers between devices, along_chan(): lax.ppermute(values[j], 'chan', [(i, (i + j) % 4) for i in range(4)])  4.53 us
  transfers between devices with their start and end apart: 24, of which 10 were waited for; matrix products, arithmetic and copies ran while one was open for 0% of the time, Pallas kernels for 16%

profile of v8, /device:TPU:1, one launch (start us, length us, event | category | flops | bytes accessed | tf_op | source)
XLA Modules:
  0.0 85.4 jit_solution(331482875435606640)
XLA Ops:
  0.6 0.0 copy-start
  0.6 3.3 %collective-permute-start.1 = (bf16[16,48,256]{2,1,0:T(8,128)(2,1)}, bf16[16,48,256]{2,1,0:T(8,128)(2,1)S(1)}, u32[]{:S(2)}, u32[]{:S(2)}) collective-permute-start(bf16[16,48,256]{2,1,0:T(8,128)(2,1)} %x_hbm.1), channel_id=1, source_target_pairs={{0,4},{4,0},{1,5},{5,1},{2,6},{6,2},{3,7},{7,3},{8,12},{12,8},{9,1... | collective-permute-start | bytes 1179656 | tf_op jit(solution)/shard_map/ppermute | solution.py:495
  4.0 1.7 %open.1 = (bf16[8,48,128]{2,1,0:T(8,128)(2,1)S(1)}, bf16[400,256]{1,0:T(8,128)(2,1)S(1)}, bf16[400,256]{1,0:T(8,128)(2,1)S(1)}, bf16[400,256]{1,0:T(8,128)(2,1)S...) custom-call(bf16[16,48,256]{2,1,0:T(8,128)(2,1)} %x_hbm.1, ...), custom_call_target="tpu_custom_call" | custom-call | tf_op jit(solution)/shard_map/open/pallas_call | solution.py:507
  5.7 0.0 copy-start.4
  5.7 1.9 %collective-permute-start.2 = (bf16[8,48,128]{2,1,0:T(8,128)(2,1)S(1)}, bf16[8,48,128]{2,1,0:T(8,128)(2,1)S(1)}, u32[]{:S(2)}, u32[]{:S(2)}) collective-permute-start(bf16[8,48,128]{2,1,0:T(8,128)(2,1)S(1)} %get-tuple-element.57), channel_id=1, source_target_pairs={{4,8},{8,4},{12,16},{16,12},{20,24},{24,20},{28,32},{32,28},{36,40... | collective-permute-start | bytes 294920 | tf_op jit(solution)/shard_map/ppermute | solution.py:499
  7.6 0.0 copy-start.2
  7.6 2.3 %collective-permute-start.8 = (bf16[400,256]{1,0:T(8,128)(2,1)S(1)}, bf16[400,256]{1,0:T(8,128)(2,1)S(1)}, u32[]{:S(2)}, u32[]{:S(2)}) collective-permute-start(bf16[400,256]{1,0:T(8,128)(2,1)S(1)} %get-tuple-element.66), channel_id=1, source_target_pairs={{0,2},{1,3},{2,0},{3,1},{4,6},{5,7},{6,4},{7,5},{8,10},{9,11},{10,... | collective-permute-start | bytes 614408 | tf_op jit(solution)/shard_map/ppermute | solution.py:477
  10.0 0.9 %collective-permute-start.9 = (bf16[400,256]{1,0:T(8,128)(2,1)S(1)}, bf16[400,256]{1,0:T(8,128)(2,1)S(1)}, u32[]{:S(2)}, u32[]{:S(2)}) collective-permute-start(bf16[400,256]{1,0:T(8,128)(2,1)S(1)} %get-tuple-element.67), channel_id=1, source_target_pairs={{0,3},{1,0},{2,1},{3,2},{4,7},{5,4},{6,5},{7,6},{8,11},{9,8},{10,9... | collective-permute-start | bytes 614408 | tf_op jit(solution)/shard_map/ppermute | solution.py:477
  10.8 0.3 collective-permute-done.par_slots
  11.1 0.8 collective-permute-done.2.near_ref
  11.9 0.6 collective-permute-start.3
  12.5 0.9 %collective-permute-done.3.far_ref = bf16[8,48,128]{2,1,0:T(8,128)(2,1)S(1)} collective-permute-done((bf16[8,48,128]{2,1,0:T(8,128)(2,1)S(1)}, bf16[8,48,128]{2,1,0:T(8,128)(2,1)S(1)}, u32[]{:S(2)}, u32[]{:S(2)}) %collective-permute-start.3) | collective-permute-done | bytes 98336 | tf_op jit(solution)/shard_map/ppermute | solution.py:495
  13.5 3.6 %mix.1 = (bf16[8,48,256]{2,1,0:T(8,128)(2,1)S(1)}, bf16[3,528,128]{2,1,0:T(8,128)(2,1)S(1)}, bf16[2,48,256]{2,1,0:T(8,128)(2,1)S(1)}, bf16[2,48,256]{2,1,0:T(8,1...) custom-call(s32[16]{0:T(128)S(1)} %copy-done.4, s32[16]{0:T(128)S(1)} %collective-permute-done.par_slots, ...), custom_call_target="tpu_custom_call" | custom-call | tf_op jit(solution)/shard_map/mix/pallas_call | solution.py:456
  17.1 0.5 collective-permute-start.4
  17.6 3.2 %collective-permute-start.5 = (bf16[2,48,256]{2,1,0:T(8,128)(2,1)S(1)}, bf16[2,48,256]{2,1,0:T(8,128)(2,1)S(1)}, u32[]{:S(2)}, u32[]{:S(2)}) collective-permute-start(bf16[2,48,256]{2,1,0:T(8,128)(2,1)S(1)} %get-tuple-element.61), channel_id=1, source_target_pairs={{0,2},{1,3},{2,0},{3,1},{4,6},{5,7},{6,4},{7,5},{8,10},{9,11},{10,... | collective-permute-start | bytes 147464 | tf_op jit(solution)/shard_map/ppermute | solution.py:477
  20.8 0.1 collective-permute-start.6
  20.9 0.6 turn.1
  21.5 1.7 %collective-permute-done.5.m2 = bf16[2,48,256]{2,1,0:T(8,128)(2,1)S(1)} collective-permute-done((bf16[2,48,256]{2,1,0:T(8,128)(2,1)S(1)}, bf16[2,48,256]{2,1,0:T(8,128)(2,1)S(1)}, u32[]{:S(2)}, u32[]{:S(2)}) %collective-permute-start.5) | collective-permute-done | bytes 49184 | tf_op jit(solution)/shard_map/ppermute | solution.py:477
  23.3 0.8 collective-permute-done.6.m3
  24.0 2.7 %mlp.1 = (bf16[96,256]{1,0:T(8,128)(2,1)S(1)}, bf16[96,256]{1,0:T(8,128)(2,1)S(1)}, bf16[96,256]{1,0:T(8,128)(2,1)S(1)}, bf16[96,256]{1,0:T(8,128)(2,1)S(1)}, bf...) custom-call(bf16[2,48,256]{2,1,0:T(8,128)(2,1)S(1)} %get-tuple-eleme, ...), custom_call_target="tpu_custom_call" | custom-call | tf_op jit(solution)/shard_map/mlp/pallas_call | solution.py:456
  26.8 1.7 %collective-permute-start.10 = (bf16[4,288,128]{2,1,0:T(8,128)(2,1)S(1)}, bf16[4,288,128]{2,1,0:T(8,128)(2,1)S(1)}, u32[]{:S(2)}, u32[]{:S(2)}) collective-permute-start(bf16[4,288,128]{2,1,0:T(8,128)(2,1)S(1)} %get-tuple-element.80), channel_id=1, source_target_pairs={{0,4},{4,0},{1,5},{5,1},{2,6},{6,2},{3,7},{7,3},{8,12},{12,8},{9,1... | collective-permute-start | bytes 884744 | tf_op jit(solution)/shard_map/ppermute | solution.py:495
  28.4 0.0 collective-permute-start.11
  28.4 2.5 %collective-permute-start.12 = (bf16[96,256]{1,0:T(8,128)(2,1)S(1)}, bf16[96,256]{1,0:T(8,128)(2,1)S(1)}, u32[]{:S(2)}, u32[]{:S(2)}) collective-permute-start(bf16[96,256]{1,0:T(8,128)(2,1)S(1)} %get-tuple-element.83), channel_id=1, source_target_pairs={{0,2},{1,3},{2,0},{3,1},{4,6},{5,7},{6,4},{7,5},{8,10},{9,11},{10,... | collective-permute-start | bytes 147464 | tf_op jit(solution)/shard_map/ppermute | solution.py:477
  31.0 0.8 collective-permute-start.13
  31.7 0.8 merge.1
  32.5 3.5 %all-to-all-start = ((bf16[4,288,128]{2,1,0:T(8,128)(2,1)}), bf16[4,288,128]{2,1,0:T(8,128)(2,1)S(1)}, u32[]{:S(2)}, u32[]{:S(2)}) async-start(bf16[4,288,128]{2,1,0:T(8,128)(2,1)} %merge.1), calls=%async_computation | async-start | bytes 589824 | tf_op jit(solution)/shard_map/all_to_all | solution.py:572
  36.0 1.2 %collective-permute-start.14 = (bf16[8,48,256]{2,1,0:T(8,128)(2,1)S(1)}, bf16[8,48,256]{2,1,0:T(8,128)(2,1)S(1)}, u32[]{:S(2)}, u32[]{:S(2)}) collective-permute-start(bf16[8,48,256]{2,1,0:T(8,128)(2,1)S(1)} %land.1.grad_ref.own_ref), channel_id=1, source_target_pairs={{0,4},{4,0},{1,5},{5,1},{2,6},{6,2},{3,7},{7,3},{8,12},{12,8},{9,1... | collective-permute-start | bytes 589832 | tf_op jit(solution)/shard_map/ppermute | solution.py:495
  37.2 2.0 %tap_sums.1.taps_ref = f32[64,128]{1,0:T(8,128)S(1)} custom-call(bf16[8,48,256]{2,1,0:T(8,128)(2,1)S(1)} %land.1.grad_ref.own_ref, bf16[3,528,128]{2,1,0:T(8,128)(2,1)S(1)} %get-tuple-element.85.pad_ref, f32[128,384]{1,0:T(8,128)S(1)} %get-tuple-element.86.fold), custom_call_target="tpu_custom_call" | custom-call | tf_op jit(solution)/shard_map/tap_sums/pallas_call | solution.py:456
  39.3 0.1 edges.1
  39.4 2.9 %collective-permute-start.15 = (bf16[8,48,128]{2,1,0:T(8,128)(2,1)S(1)}, bf16[8,48,128]{2,1,0:T(8,128)(2,1)S(1)}, u32[]{:S(2)}, u32[]{:S(2)}) collective-permute-start(bf16[8,48,128]{2,1,0:T(8,128)(2,1)S(1)} %edges.1), channel_id=1, source_target_pairs={{4,8},{8,4},{12,16},{16,12},{20,24},{24,20},{28,32},{32,28},{36,40... | collective-permute-start | bytes 294920 | tf_op jit(solution)/shard_map/ppermute | solution.py:499
  42.4 0.8 pieces.1
  43.2 12.2 %all-to-all-start.1 = ((bf16[32,16,128]{2,1,0:T(8,128)(2,1)}), bf16[32,16,128]{2,1,0:T(8,128)(2,1)S(1)}, u32[]{:S(2)}, u32[]{:S(2)}) async-start(bf16[32,16,128]{2,1,0:T(8,128)(2,1)} %pieces.1), calls=%async_computation.1 | async-start | bytes 262144 | tf_op jit(solution)/shard_map/all_to_all | solution.py:599
  55.4 2.1 %collective-permute-start.16 = (bf16[8,48,128]{2,1,0:T(8,128)(2,1)S(1)}, bf16[8,48,128]{2,1,0:T(8,128)(2,1)S(1)}, u32[]{:S(2)}, u32[]{:S(2)}) collective-permute-start(bf16[8,48,128]{2,1,0:T(8,128)(2,1)S(1)} %collective-permute-done.15.near_ref), channel_id=1, source_target_pairs={{0,4},{4,0},{1,5},{5,1},{2,6},{6,2},{3,7},{7,3},{8,12},{12,8},{9,1... | collective-permute-start | bytes 294920 | tf_op jit(solution)/shard_map/ppermute | solution.py:495
  57.5 0.9 %collective-permute-done.16.far_ref = bf16[8,48,128]{2,1,0:T(8,128)(2,1)S(1)} collective-permute-done((bf16[8,48,128]{2,1,0:T(8,128)(2,1)S(1)}, bf16[8,48,128]{2,1,0:T(8,128)(2,1)S(1)}, u32[]{:S(2)}, u32[]{:S(2)}) %collective-permute-start.16) | collective-permute-done | bytes 98336 | tf_op jit(solution)/shard_map/ppermute | solution.py:495
  58.5 1.4 %surround.1.pad = f32[3,528,128]{2,1,0:T(8,128)S(1)} custom-call(s32[8,8]{1,0:T(8,128)S(1)} %copy-done.2, bf16[8,48,256]{2,1,0:T(8,128)(2,1)S(1)} %land.1.grad_ref.own_ref, bf16[8,48,256]{2,1,0:T(8,128)(2,1)S(1)} %collective-permute-done.14.par_ref, bf16[8,48,128]{2,1,0:T(8,128)(2,1)S(1)} %collective-permute-done.15.near_ref, ...), custom_call_target="tpu_custom_call" | custom-call | flops 700000000 | bytes 2583000 | tf_op jit(solution)/shard_map/surround/pallas_call | solution.py:456
  59.9 4.9 %all-to-all-done.1.in_ref = bf16[32,16,128]{2,1,0:T(8,128)(2,1)S(1)} async-done(((bf16[32,16,128]{2,1,0:T(8,128)(2,1)}), bf16[32,16,128]{2,1,0:T(8,128)(2,1)S(1)}, u32[]{:S(2)}, u32[]{:S(2)}) %all-to-all-start.1) | async-done | bytes 131104 | tf_op jit(solution)/shard_map/all_to_all | solution.py:599
  64.8 0.7 totals.1
  65.5 4.8 %all-to-all-start.2 = ((bf16[32,16,128]{2,1,0:T(8,128)(2,1)}), bf16[32,16,128]{2,1,0:T(8,128)(2,1)S(1)}, u32[]{:S(2)}, u32[]{:S(2)}) async-start(bf16[32,16,128]{2,1,0:T(8,128)(2,1)} %totals.1), calls=%async_computation.2 | async-start | bytes 262144 | tf_op jit(solution)/shard_map/all_to_all | solution.py:618
  70.3 0.0 copy-start.3
  70.3 1.0 %collective-permute-start.17 = (bf16[96,256]{1,0:T(8,128)(2,1)S(1)}, bf16[96,256]{1,0:T(8,128)(2,1)S(1)}, u32[]{:S(2)}, u32[]{:S(2)}) collective-permute-start(bf16[96,256]{1,0:T(8,128)(2,1)S(1)} %get-tuple-element.98), channel_id=1, source_target_pairs={{0,1},{1,2},{2,3},{3,0},{4,5},{5,6},{6,7},{7,4},{8,9},{9,10},{10,1... | collective-permute-start | bytes 147464 | tf_op jit(solution)/shard_map/ppermute | solution.py:477
  71.3 2.9 %collective-permute-start.18 = (bf16[96,256]{1,0:T(8,128)(2,1)S(1)}, bf16[96,256]{1,0:T(8,128)(2,1)S(1)}, u32[]{:S(2)}, u32[]{:S(2)}) collective-permute-start(bf16[96,256]{1,0:T(8,128)(2,1)S(1)} %get-tuple-element.99), channel_id=1, source_target_pairs={{0,2},{1,3},{2,0},{3,1},{4,6},{5,7},{6,4},{7,5},{8,10},{9,11},{10,... | collective-permute-start | bytes 147464 | tf_op jit(solution)/shard_map/ppermute | solution.py:477
  74.2 1.2 %collective-permute-start.19 = (bf16[96,256]{1,0:T(8,128)(2,1)S(1)}, bf16[96,256]{1,0:T(8,128)(2,1)S(1)}, u32[]{:S(2)}, u32[]{:S(2)}) collective-permute-start(bf16[96,256]{1,0:T(8,128)(2,1)S(1)} %get-tuple-element.100), channel_id=1, source_target_pairs={{0,3},{1,0},{2,1},{3,2},{4,7},{5,4},{6,5},{7,6},{8,11},{9,8},{10,9... | collective-permute-start | bytes 147464 | tf_op jit(solution)/shard_map/ppermute | solution.py:477
  75.4 0.8 collective-permute-done.18.r2
  76.2 1.2 %collective-permute-done.19.r3 = bf16[96,256]{1,0:T(8,128)(2,1)S(1)} collective-permute-done((bf16[96,256]{1,0:T(8,128)(2,1)S(1)}, bf16[96,256]{1,0:T(8,128)(2,1)S(1)}, u32[]{:S(2)}, u32[]{:S(2)}) %collective-permute-start.19) | collective-permute-done | bytes 49184 | tf_op jit(solution)/shard_map/ppermute | solution.py:477
  77.5 2.8 %unmix.1 = (bf16[8,48,256]{2,1,0:T(8,128)(2,1)}, bf16[8,48,256]{2,1,0:T(8,128)(2,1)}) custom-call(f32[3,528,128]{2,1,0:T(8,128)S(1)} %surround.1.pad, bf16[8,48,256]{2,1,0:T(8,128)(2,1)S(1)} %copy-done.1, f32[56,384]{1,0:T(8,128)S(1)} %get-tuple-element.58.taps, bf16[8,48,256]{2,1,0:T(8,128)(2,1)S(1)} %get-tuple-element.90.owned_ref, f32[1,48]{1,0:T(1,128)S(1)} %bitcast.3, ...), custom_call_target="tpu_custom_call" | custom-call | tf_op jit(solution)/shard_map/unmix/pallas_call | solution.py:456
  80.2 3.1 %collective-permute-start.20 = (bf16[32,16,128]{2,1,0:T(8,128)(2,1)S(1)}, bf16[32,16,128]{2,1,0:T(8,128)(2,1)S(1)}, u32[]{:S(2)}, u32[]{:S(2)}) collective-permute-start(bf16[32,16,128]{2,1,0:T(8,128)(2,1)S(1)} %all-to-all-done.2.in_ref), channel_id=1, source_target_pairs={{0,4},{4,0},{1,5},{5,1},{2,6},{6,2},{3,7},{7,3},{8,12},{12,8},{9,1... | collective-permute-start | bytes 393224 | tf_op jit(solution)/shard_map/ppermute | solution.py:495
  83.3 1.0 %collective-permute-done.20.other_ref = bf16[32,16,128]{2,1,0:T(8,128)(2,1)S(1)} collective-permute-done((bf16[32,16,128]{2,1,0:T(8,128)(2,1)S(1)}, bf16[32,16,128]{2,1,0:T(8,128)(2,1)S(1)}, u32[]{:S(2)}, u32[]{:S(2)}) %collective-permute-start.20) | collective-permute-done | bytes 131104 | tf_op jit(solution)/shard_map/ppermute | solution.py:495
  84.3 1.1 %finish.1 = (f32[48,49]{1,0:T(8,128)}, f32[192,192]{1,0:T(8,128)}, f32[192,192]{1,0:T(8,128)}) custom-call(bf16[32,16,128]{2,1,0:T(8,128)(2,1)S(1)} %all-to-all-done.2.in_ref, bf16[32,16,128]{2,1,0:T(8,128)(2,1)S(1)} %collective-permute-done.20.other_ref), custom_call_target="tpu_custom_call" | custom-call | tf_op jit(solution)/shard_map/finish/pallas_call | solution.py:456
  (23 shorter events, 0.1 us)
Async XLA Ops:
  0.6 12.8 %copy-start = (bf16[528,768]{1,0:T(8,128)(2,1)S(1)}, bf16[528,768]{1,0:T(8,128)(2,1)}, u32[]{:S(2)}) copy-start(bf16[528,768]{1,0:T(8,128)(2,1)} %constant.4.clone.maps) | copy-start | bytes 2433028
  0.6 12.8 %collective-permute-start.1 = (bf16[16,48,256]{2,1,0:T(8,128)(2,1)}, bf16[16,48,256]{2,1,0:T(8,128)(2,1)S(1)}, u32[]{:S(2)}, u32[]{:S(2)}) collective-permute-start(bf16[16,48,256]{2,1,0:T(8,128)(2,1)} %x_hbm.1), channel_id=1, source_target_pairs={{0,4},{4,0},{1,5},{5,1},{2,6},{6,2},{3,7},{7,3},{8,12},{12,8},{9,1... | collective-permute-start | bytes 1179656 | tf_op jit(solution)/shard_map/ppermute | solution.py:495
  5.7 4.3 %copy-start.4 = (s32[16]{0:T(128)S(1)}, s32[16]{0:T(128)}, u32[]{:S(2)}) copy-start(s32[16]{0:T(128)} %own_slots.1) | copy-start | bytes 196
  5.7 6.2 %collective-permute-start.2 = (bf16[8,48,128]{2,1,0:T(8,128)(2,1)S(1)}, bf16[8,48,128]{2,1,0:T(8,128)(2,1)S(1)}, u32[]{:S(2)}, u32[]{:S(2)}) collective-permute-start(bf16[8,48,128]{2,1,0:T(8,128)(2,1)S(1)} %get-tuple-element.57), channel_id=1, source_target_pairs={{4,8},{8,4},{12,16},{16,12},{20,24},{24,20},{28,32},{32,28},{36,40... | collective-permute-start | bytes 294920 | tf_op jit(solution)/shard_map/ppermute | solution.py:499
  7.6 5.9 %copy-start.2 = (s32[8,8]{1,0:T(8,128)S(1)}, s32[8,8]{1,0:T(8,128)}, u32[]{:S(2)}) copy-start(s32[8,8]{1,0:T(8,128)} %adj.3) | copy-start | bytes 772
  7.6 13.1 %collective-permute-start.8 = (bf16[400,256]{1,0:T(8,128)(2,1)S(1)}, bf16[400,256]{1,0:T(8,128)(2,1)S(1)}, u32[]{:S(2)}, u32[]{:S(2)}) collective-permute-start(bf16[400,256]{1,0:T(8,128)(2,1)S(1)} %get-tuple-element.66), channel_id=1, source_target_pairs={{0,2},{1,3},{2,0},{3,1},{4,6},{5,7},{6,4},{7,5},{8,10},{9,11},{10,... | collective-permute-start | bytes 614408 | tf_op jit(solution)/shard_map/ppermute | solution.py:477
  10.0 1.1 %collective-permute-start = (s32[16]{0:T(128)S(1)}, s32[16]{0:T(128)S(1)}, u32[]{:S(2)}, u32[]{:S(2)}) collective-permute-start(s32[16]{0:T(128)S(1)} %copy-done.4), channel_id=1, source_target_pairs={{0,4},{4,0},{1,5},{5,1},{2,6},{6,2},{3,7},{7,3},{8,12},{12,8},{9,1... | collective-permute-start | bytes 200 | tf_op jit(solution)/shard_map/ppermute | solution.py:495
  10.0 10.9 %collective-permute-start.9 = (bf16[400,256]{1,0:T(8,128)(2,1)S(1)}, bf16[400,256]{1,0:T(8,128)(2,1)S(1)}, u32[]{:S(2)}, u32[]{:S(2)}) collective-permute-start(bf16[400,256]{1,0:T(8,128)(2,1)S(1)} %get-tuple-element.67), channel_id=1, source_target_pairs={{0,3},{1,0},{2,1},{3,2},{4,7},{5,4},{6,5},{7,6},{8,11},{9,8},{10,9... | collective-permute-start | bytes 614408 | tf_op jit(solution)/shard_map/ppermute | solution.py:477
  11.9 9.0 %collective-permute-start.7 = (bf16[400,256]{1,0:T(8,128)(2,1)S(1)}, bf16[400,256]{1,0:T(8,128)(2,1)S(1)}, u32[]{:S(2)}, u32[]{:S(2)}) collective-permute-start(bf16[400,256]{1,0:T(8,128)(2,1)S(1)} %get-tuple-element.65), channel_id=1, source_target_pairs={{0,1},{1,2},{2,3},{3,0},{4,5},{5,6},{6,7},{7,4},{8,9},{9,10},{10,1... | collective-permute-start | bytes 614408 | tf_op jit(solution)/shard_map/ppermute | solution.py:477
  11.9 1.5 %collective-permute-start.3 = (bf16[8,48,128]{2,1,0:T(8,128)(2,1)S(1)}, bf16[8,48,128]{2,1,0:T(8,128)(2,1)S(1)}, u32[]{:S(2)}, u32[]{:S(2)}) collective-permute-start(bf16[8,48,128]{2,1,0:T(8,128)(2,1)S(1)} %collective-permute-done.2.near_ref), channel_id=1, source_target_pairs={{0,4},{4,0},{1,5},{5,1},{2,6},{6,2},{3,7},{7,3},{8,12},{12,8},{9,1... | collective-permute-start | bytes 294920 | tf_op jit(solution)/shard_map/ppermute | solution.py:495
  17.1 4.5 %collective-permute-start.4 = (bf16[2,48,256]{2,1,0:T(8,128)(2,1)S(1)}, bf16[2,48,256]{2,1,0:T(8,128)(2,1)S(1)}, u32[]{:S(2)}, u32[]{:S(2)}) collective-permute-start(bf16[2,48,256]{2,1,0:T(8,128)(2,1)S(1)} %get-tuple-element.60), channel_id=1, source_target_pairs={{0,1},{1,2},{2,3},{3,0},{4,5},{5,6},{6,7},{7,4},{8,9},{9,10},{10,1... | collective-permute-start | bytes 147464 | tf_op jit(solution)/shard_map/ppermute | solution.py:477
  17.6 5.7 %collective-permute-start.5 = (bf16[2,48,256]{2,1,0:T(8,128)(2,1)S(1)}, bf16[2,48,256]{2,1,0:T(8,128)(2,1)S(1)}, u32[]{:S(2)}, u32[]{:S(2)}) collective-permute-start(bf16[2,48,256]{2,1,0:T(8,128)(2,1)S(1)} %get-tuple-element.61), channel_id=1, source_target_pairs={{0,2},{1,3},{2,0},{3,1},{4,6},{5,7},{6,4},{7,5},{8,10},{9,11},{10,... | collective-permute-start | bytes 147464 | tf_op jit(solution)/shard_map/ppermute | solution.py:477
  20.8 3.2 %collective-permute-start.6 = (bf16[2,48,256]{2,1,0:T(8,128)(2,1)S(1)}, bf16[2,48,256]{2,1,0:T(8,128)(2,1)S(1)}, u32[]{:S(2)}, u32[]{:S(2)}) collective-permute-start(bf16[2,48,256]{2,1,0:T(8,128)(2,1)S(1)} %get-tuple-element.62), channel_id=1, source_target_pairs={{0,3},{1,0},{2,1},{3,2},{4,7},{5,4},{6,5},{7,6},{8,11},{9,8},{10,9... | collective-permute-start | bytes 147464 | tf_op jit(solution)/shard_map/ppermute | solution.py:477
  26.8 5.0 %collective-permute-start.10 = (bf16[4,288,128]{2,1,0:T(8,128)(2,1)S(1)}, bf16[4,288,128]{2,1,0:T(8,128)(2,1)S(1)}, u32[]{:S(2)}, u32[]{:S(2)}) collective-permute-start(bf16[4,288,128]{2,1,0:T(8,128)(2,1)S(1)} %get-tuple-element.80), channel_id=1, source_target_pairs={{0,4},{4,0},{1,5},{5,1},{2,6},{6,2},{3,7},{7,3},{8,12},{12,8},{9,1... | collective-permute-start | bytes 884744 | tf_op jit(solution)/shard_map/ppermute | solution.py:495
  28.4 7.5 %collective-permute-start.11 = (bf16[96,256]{1,0:T(8,128)(2,1)S(1)}, bf16[96,256]{1,0:T(8,128)(2,1)S(1)}, u32[]{:S(2)}, u32[]{:S(2)}) collective-permute-start(bf16[96,256]{1,0:T(8,128)(2,1)S(1)} %get-tuple-element.82), channel_id=1, source_target_pairs={{0,1},{1,2},{2,3},{3,0},{4,5},{5,6},{6,7},{7,4},{8,9},{9,10},{10,1... | collective-permute-start | bytes 147464 | tf_op jit(solution)/shard_map/ppermute | solution.py:477
  28.4 7.5 %collective-permute-start.12 = (bf16[96,256]{1,0:T(8,128)(2,1)S(1)}, bf16[96,256]{1,0:T(8,128)(2,1)S(1)}, u32[]{:S(2)}, u32[]{:S(2)}) collective-permute-start(bf16[96,256]{1,0:T(8,128)(2,1)S(1)} %get-tuple-element.83), channel_id=1, source_target_pairs={{0,2},{1,3},{2,0},{3,1},{4,6},{5,7},{6,4},{7,5},{8,10},{9,11},{10,... | collective-permute-start | bytes 147464 | tf_op jit(solution)/shard_map/ppermute | solution.py:477
  31.0 5.0 %collective-permute-start.13 = (bf16[96,256]{1,0:T(8,128)(2,1)S(1)}, bf16[96,256]{1,0:T(8,128)(2,1)S(1)}, u32[]{:S(2)}, u32[]{:S(2)}) collective-permute-start(bf16[96,256]{1,0:T(8,128)(2,1)S(1)} %get-tuple-element.84), channel_id=1, source_target_pairs={{0,3},{1,0},{2,1},{3,2},{4,7},{5,4},{6,5},{7,6},{8,11},{9,8},{10,9... | collective-permute-start | bytes 147464 | tf_op jit(solution)/shard_map/ppermute | solution.py:477
  32.5 9.8 %all-to-all-start = ((bf16[4,288,128]{2,1,0:T(8,128)(2,1)}), bf16[4,288,128]{2,1,0:T(8,128)(2,1)S(1)}, u32[]{:S(2)}, u32[]{:S(2)}) async-start(bf16[4,288,128]{2,1,0:T(8,128)(2,1)} %merge.1), calls=%async_computation | async-start | bytes 589824 | tf_op jit(solution)/shard_map/all_to_all | solution.py:572
  36.0 3.2 %collective-permute-start.14 = (bf16[8,48,256]{2,1,0:T(8,128)(2,1)S(1)}, bf16[8,48,256]{2,1,0:T(8,128)(2,1)S(1)}, u32[]{:S(2)}, u32[]{:S(2)}) collective-permute-start(bf16[8,48,256]{2,1,0:T(8,128)(2,1)S(1)} %land.1.grad_ref.own_ref), channel_id=1, source_target_pairs={{0,4},{4,0},{1,5},{5,1},{2,6},{6,2},{3,7},{7,3},{8,12},{12,8},{9,1... | collective-permute-start | bytes 589832 | tf_op jit(solution)/shard_map/ppermute | solution.py:495
  39.4 16.0 %collective-permute-start.15 = (bf16[8,48,128]{2,1,0:T(8,128)(2,1)S(1)}, bf16[8,48,128]{2,1,0:T(8,128)(2,1)S(1)}, u32[]{:S(2)}, u32[]{:S(2)}) collective-permute-start(bf16[8,48,128]{2,1,0:T(8,128)(2,1)S(1)} %edges.1), channel_id=1, source_target_pairs={{4,8},{8,4},{12,16},{16,12},{20,24},{24,20},{28,32},{32,28},{36,40... | collective-permute-start | bytes 294920 | tf_op jit(solution)/shard_map/ppermute | solution.py:499
  43.2 21.6 %all-to-all-start.1 = ((bf16[32,16,128]{2,1,0:T(8,128)(2,1)}), bf16[32,16,128]{2,1,0:T(8,128)(2,1)S(1)}, u32[]{:S(2)}, u32[]{:S(2)}) async-start(bf16[32,16,128]{2,1,0:T(8,128)(2,1)} %pieces.1), calls=%async_computation.1 | async-start | bytes 262144 | tf_op jit(solution)/shard_map/all_to_all | solution.py:599
  55.4 3.0 %collective-permute-start.16 = (bf16[8,48,128]{2,1,0:T(8,128)(2,1)S(1)}, bf16[8,48,128]{2,1,0:T(8,128)(2,1)S(1)}, u32[]{:S(2)}, u32[]{:S(2)}) collective-permute-start(bf16[8,48,128]{2,1,0:T(8,128)(2,1)S(1)} %collective-permute-done.15.near_ref), channel_id=1, source_target_pairs={{0,4},{4,0},{1,5},{5,1},{2,6},{6,2},{3,7},{7,3},{8,12},{12,8},{9,1... | collective-permute-start | bytes 294920 | tf_op jit(solution)/shard_map/ppermute | solution.py:495
  65.5 12.0 %copy-start.1 = (bf16[8,48,256]{2,1,0:T(8,128)(2,1)S(1)}, bf16[8,48,256]{2,1,0:T(8,128)(2,1)}, u32[]{:S(2)}) copy-start(bf16[8,48,256]{2,1,0:T(8,128)(2,1)} %cot_ref.1) | copy-start | bytes 589828
  65.5 14.8 %all-to-all-start.2 = ((bf16[32,16,128]{2,1,0:T(8,128)(2,1)}), bf16[32,16,128]{2,1,0:T(8,128)(2,1)S(1)}, u32[]{:S(2)}, u32[]{:S(2)}) async-start(bf16[32,16,128]{2,1,0:T(8,128)(2,1)} %totals.1), calls=%async_computation.2 | async-start | bytes 262144 | tf_op jit(solution)/shard_map/all_to_all | solution.py:618
  70.3 7.2 %copy-start.3 = (f32[48]{0:T(128)S(1)}, f32[48]{0:T(128)}, u32[]{:S(2)}) copy-start(f32[48]{0:T(128)} %param.21) | copy-start | bytes 580
  70.3 5.1 %collective-permute-start.17 = (bf16[96,256]{1,0:T(8,128)(2,1)S(1)}, bf16[96,256]{1,0:T(8,128)(2,1)S(1)}, u32[]{:S(2)}, u32[]{:S(2)}) collective-permute-start(bf16[96,256]{1,0:T(8,128)(2,1)S(1)} %get-tuple-element.98), channel_id=1, source_target_pairs={{0,1},{1,2},{2,3},{3,0},{4,5},{5,6},{6,7},{7,4},{8,9},{9,10},{10,1... | collective-permute-start | bytes 147464 | tf_op jit(solution)/shard_map/ppermute | solution.py:477
  71.3 4.9 %collective-permute-start.18 = (bf16[96,256]{1,0:T(8,128)(2,1)S(1)}, bf16[96,256]{1,0:T(8,128)(2,1)S(1)}, u32[]{:S(2)}, u32[]{:S(2)}) collective-permute-start(bf16[96,256]{1,0:T(8,128)(2,1)S(1)} %get-tuple-element.99), channel_id=1, source_target_pairs={{0,2},{1,3},{2,0},{3,1},{4,6},{5,7},{6,4},{7,5},{8,10},{9,11},{10,... | collective-permute-start | bytes 147464 | tf_op jit(solution)/shard_map/ppermute | solution.py:477
  74.2 3.2 %collective-permute-start.19 = (bf16[96,256]{1,0:T(8,128)(2,1)S(1)}, bf16[96,256]{1,0:T(8,128)(2,1)S(1)}, u32[]{:S(2)}, u32[]{:S(2)}) collective-permute-start(bf16[96,256]{1,0:T(8,128)(2,1)S(1)} %get-tuple-element.100), channel_id=1, source_target_pairs={{0,3},{1,0},{2,1},{3,2},{4,7},{5,4},{6,5},{7,6},{8,11},{9,8},{10,9... | collective-permute-start | bytes 147464 | tf_op jit(solution)/shard_map/ppermute | solution.py:477
  80.2 4.1 %collective-permute-start.20 = (bf16[32,16,128]{2,1,0:T(8,128)(2,1)S(1)}, bf16[32,16,128]{2,1,0:T(8,128)(2,1)S(1)}, u32[]{:S(2)}, u32[]{:S(2)}) collective-permute-start(bf16[32,16,128]{2,1,0:T(8,128)(2,1)S(1)} %all-to-all-done.2.in_ref), channel_id=1, source_target_pairs={{0,4},{4,0},{1,5},{5,1},{2,6},{6,2},{3,7},{7,3},{8,12},{12,8},{9,1... | collective-permute-start | bytes 393224 | tf_op jit(solution)/shard_map/ppermute | solution.py:495

commit v9 on v7

--- a/solution.py
+++ b/solution.py
@@ -203,8 +203,8 @@
 
 def mix_kernel(
     own_slots, par_slots, adj, x_ref, par_ref, near_ref, far_ref, taps, maps,
-    owned_ref, pad_out, m0, m1, m2, m3,
-    place, table, up_g, mid_g, down_g, pad, result, flat,
+    owned_ref, pad, m0, m1, m2, m3,
+    place, table, up_g, mid_g, down_g, result, flat,
 ):
     me = my_owner()
     odd = lax.axis_index("core")
@@ -231,7 +231,6 @@
         gather_tile(table, up_g, mid_g, down_g, t, center, entries)
     owned_ref[...] = mid_g[:, 0:256].reshape(8, 48, 256)
     build_padded(pad, up_g, mid_g, down_g, maps)
-    pad_out[...] = pad[...].astype(BF16)
     convolve(pad, taps, result, False)
     flat[...] = result[...].T.astype(BF16).reshape(8, 48, 256)
     for j, out in enumerate((m0, m1, m2, m3)):
@@ -290,11 +289,12 @@
     for j in range(4):
         preact = dot(in_t[j], normed, NN) + across(bias[j])
         square = preact * preact
-        tangent = jnp.tanh(GELU_SCALE * (preact + GELU_CUBIC * square * preact))
-        half = 0.5 * (1.0 + tangent)
-        act = (preact * half).astype(BF16)
-        slope = half + 0.5 * preact * (1.0 - tangent * tangent) * (
-            GELU_SCALE * (1.0 + 3.0 * GELU_CUBIC * square)
+        tangent = jnp.tanh(preact * (GELU_SCALE + (GELU_SCALE * GELU_CUBIC) * square))
+        half = 0.5 + 0.5 * tangent
+        value = preact * half
+        act = value.astype(BF16)
+        slope = half + value * (1.0 - tangent) * (
+            GELU_SCALE + (3.0 * GELU_SCALE * GELU_CUBIC) * square
         )
         branch = branch + dot(out_t[j], act, NN)
         pre_grad = (dot(w_out[j], dbranch, NN) * slope).astype(BF16)
@@ -333,8 +333,7 @@
         out_ref[(mine + 4 - j) & 3] = both.astype(BF16)
 
 
-def taps_kernel(grad_ref, pad_ref, fold, out_ref, pad, grad_t, sums):
-    pad[...] = pad_ref[...].astype(F32)
+def taps_kernel(grad_ref, pad, fold, out_ref, grad_t, sums):
     grad_t[...] = grad_ref[...].reshape(384, 256).astype(F32).T
     sums[...] = jnp.zeros((64, 384), F32)
 
@@ -529,13 +528,13 @@
         pltpu.VMEM((384, 384), BF16),
         pltpu.VMEM((384, 768), BF16),
         pltpu.VMEM((384, 384), BF16),
-        pltpu.VMEM((3, 22 * WIDE, 128), F32),
-        pltpu.VMEM((256, 384), F32),
     ]
     mix = call(
         mix_kernel,
-        [shape(8, 48, 256), shape(3, 22 * WIDE, 128)] + [tile_chunk] * 4,
-        scratch=[pltpu.SMEM((8,), jnp.int32)] + grid_scratch(65) + [pltpu.VMEM((8, 48, 256), BF16)],
+        [held(8, 48, 256), held(3, 22 * WIDE, 128, dtype=F32)] + [tile_chunk] * 4,
+        scratch=[pltpu.SMEM((8,), jnp.int32)]
+        + grid_scratch(65)
+        + [pltpu.VMEM((256, 384), F32), pltpu.VMEM((8, 48, 256), BF16)],
         smem=3,
         n_in=9,
         name="mix",
@@ -575,14 +574,10 @@
     tap_sums = call(
         taps_kernel,
         held(64, 128, dtype=F32),
-        scratch=[
-            pltpu.VMEM((3, 22 * WIDE, 128), F32),
-            pltpu.VMEM((256, 384), F32),
-            pltpu.VMEM((64, 384), F32),
-        ],
+        scratch=[pltpu.VMEM((256, 384), F32), pltpu.VMEM((64, 384), F32)],
         n_in=3,
         name="tap_sums",
-        near=(0, 2),
+        near=(0, 1, 2),
     )(grads, padded, fold)
     edges = call(edges_kernel, held(8, 48, 128), n_in=2, name="edges", near=(0, 1))(
         after(grads, tap_sums), par_grads
@@ -603,7 +598,7 @@
     surrounded = call(
         surround_kernel,
         held(3, 22 * WIDE, 128, dtype=F32),
-        scratch=grid_scratch(49)[0:4],
+        scratch=grid_scratch(49),
         smem=1,
         n_in=6,
         name="surround",

time: 85.7 us -> 85.6 us (level)
  no operation moved by 1% of the time
where the time goes in v9:
time: 85.6 us; the launch traced here: 85.3 us
  starting transfers between devices  47.3 us (55%)
  Pallas kernels  18.4 us (21%)
  waiting for transfers between devices  18.1 us (21%)
    pallas_call x12, Pallas kernels, run(): inner(*(pltpu.with_memory_space_constraint(a, pltpu.VMEM) if i in near el...  16.7 us
    all_to_all x1, starting transfers between devices, body(): arrived = lax.all_to_all(after(pieces, edges), 'chip', 0, 0, tiled=True)  12.5 us
    ppermute x7, starting transfers between devices, partner(): return lax.ppermute(value, 'core', [(0, 1), (1, 0)])  12.1 us
    ppermute x9, starting transfers between devices, along_chan(): lax.ppermute(values[j], 'chan', [(i, (i + j) % 4) for i in range(4)])  10.3 us
    all_to_all x1, waiting for transfers between devices, body(): spread = lax.all_to_all(totals, 'chip', 0, 0, tiled=True)  5.92 us
    all_to_all x1, waiting for transfers between devices, body(): arrived = lax.all_to_all(after(pieces, edges), 'chip', 0, 0, tiled=True)  5.55 us
    ppermute x2, starting transfers between devices, next_chip(): lax.ppermute(value, owners, [p for p in pairs if 0 <= p[1] < devices])  4.85 us
    all_to_all x1, starting transfers between devices, body(): spread = lax.all_to_all(totals, 'chip', 0, 0, tiled=True)  4.09 us
  transfers between devices with their start and end apart: 21, of which 10 were waited for; matrix products, arithmetic and copies ran while one was open for 0% of the time, Pallas kernels for 16%

profile of v9, /device:TPU:1, one launch (start us, length us, event | category | flops | bytes accessed | tf_op | source)
XLA Modules:
  0.0 85.3 jit_solution(17153030559948439013)
XLA Ops:
  0.6 0.0 copy-start
  0.6 3.3 %collective-permute-start.1 = (bf16[16,48,256]{2,1,0:T(8,128)(2,1)}, bf16[16,48,256]{2,1,0:T(8,128)(2,1)S(1)}, u32[]{:S(2)}, u32[]{:S(2)}) collective-permute-start(bf16[16,48,256]{2,1,0:T(8,128)(2,1)} %x_hbm.1), channel_id=1, source_target_pairs={{0,4},{4,0},{1,5},{5,1},{2,6},{6,2},{3,7},{7,3},{8,12},{12,8},{9,1... | collective-permute-start | bytes 1179656 | tf_op jit(solution)/shard_map/ppermute | solution.py:494
  4.0 1.7 %open.1 = (bf16[8,48,128]{2,1,0:T(8,128)(2,1)S(1)}, bf16[400,256]{1,0:T(8,128)(2,1)S(1)}, bf16[400,256]{1,0:T(8,128)(2,1)S(1)}, bf16[400,256]{1,0:T(8,128)(2,1)S...) custom-call(bf16[16,48,256]{2,1,0:T(8,128)(2,1)} %x_hbm.1, ...), custom_call_target="tpu_custom_call" | custom-call | tf_op jit(solution)/shard_map/open/pallas_call | solution.py:506
  5.7 0.0 copy-start.4
  5.7 1.9 %collective-permute-start.2 = (bf16[8,48,128]{2,1,0:T(8,128)(2,1)S(1)}, bf16[8,48,128]{2,1,0:T(8,128)(2,1)S(1)}, u32[]{:S(2)}, u32[]{:S(2)}) collective-permute-start(bf16[8,48,128]{2,1,0:T(8,128)(2,1)S(1)} %get-tuple-element.49), channel_id=1, source_target_pairs={{4,8},{8,4},{12,16},{16,12},{20,24},{24,20},{28,32},{32,28},{36,40... | collective-permute-start | bytes 294920 | tf_op jit(solution)/shard_map/ppermute | solution.py:498
  7.6 0.0 copy-start.2
  7.6 2.3 %collective-permute-start.8 = (bf16[400,256]{1,0:T(8,128)(2,1)S(1)}, bf16[400,256]{1,0:T(8,128)(2,1)S(1)}, u32[]{:S(2)}, u32[]{:S(2)}) collective-permute-start(bf16[400,256]{1,0:T(8,128)(2,1)S(1)} %get-tuple-element.58), channel_id=1, source_target_pairs={{0,2},{1,3},{2,0},{3,1},{4,6},{5,7},{6,4},{7,5},{8,10},{9,11},{10,... | collective-permute-start | bytes 614408 | tf_op jit(solution)/shard_map/ppermute | solution.py:476
  10.0 0.0 collective-permute-start
  10.0 0.9 %collective-permute-start.9 = (bf16[400,256]{1,0:T(8,128)(2,1)S(1)}, bf16[400,256]{1,0:T(8,128)(2,1)S(1)}, u32[]{:S(2)}, u32[]{:S(2)}) collective-permute-start(bf16[400,256]{1,0:T(8,128)(2,1)S(1)} %get-tuple-element.59), channel_id=1, source_target_pairs={{0,3},{1,0},{2,1},{3,2},{4,7},{5,4},{6,5},{7,6},{8,11},{9,8},{10,9... | collective-permute-start | bytes 614408 | tf_op jit(solution)/shard_map/ppermute | solution.py:476
  10.8 0.3 collective-permute-done.par_slots
  11.1 0.8 collective-permute-done.2.near_ref
  11.9 0.6 collective-permute-start.3
  12.5 0.9 %collective-permute-done.3.far_ref = bf16[8,48,128]{2,1,0:T(8,128)(2,1)S(1)} collective-permute-done((bf16[8,48,128]{2,1,0:T(8,128)(2,1)S(1)}, bf16[8,48,128]{2,1,0:T(8,128)(2,1)S(1)}, u32[]{:S(2)}, u32[]{:S(2)}) %collective-permute-start.3) | collective-permute-done | bytes 98336 | tf_op jit(solution)/shard_map/ppermute | solution.py:494
  13.5 3.6 %mix.1 = (bf16[8,48,256]{2,1,0:T(8,128)(2,1)S(1)}, f32[3,528,128]{2,1,0:T(8,128)S(1)}, bf16[2,48,256]{2,1,0:T(8,128)(2,1)S(1)}, bf16[2,48,256]{2,1,0:T(8,128)(2,...) custom-call(s32[16]{0:T(128)S(1)} %copy-done.4, s32[16]{0:T(128)S(1)} %collective-permute-done.par_slots, ...), custom_call_target="tpu_custom_call" | custom-call | tf_op jit(solution)/shard_map/mix/pallas_call | solution.py:455
  17.1 0.5 collective-permute-start.4
  17.6 3.2 %collective-permute-start.5 = (bf16[2,48,256]{2,1,0:T(8,128)(2,1)S(1)}, bf16[2,48,256]{2,1,0:T(8,128)(2,1)S(1)}, u32[]{:S(2)}, u32[]{:S(2)}) collective-permute-start(bf16[2,48,256]{2,1,0:T(8,128)(2,1)S(1)} %get-tuple-element.53), channel_id=1, source_target_pairs={{0,2},{1,3},{2,0},{3,1},{4,6},{5,7},{6,4},{7,5},{8,10},{9,11},{10,... | collective-permute-start | bytes 147464 | tf_op jit(solution)/shard_map/ppermute | solution.py:476
  20.8 0.0 collective-permute-done.8.p2
  20.8 0.1 collective-permute-start.6
  20.9 0.6 turn.1
  21.5 1.7 %collective-permute-done.5.m2 = bf16[2,48,256]{2,1,0:T(8,128)(2,1)S(1)} collective-permute-done((bf16[2,48,256]{2,1,0:T(8,128)(2,1)S(1)}, bf16[2,48,256]{2,1,0:T(8,128)(2,1)S(1)}, u32[]{:S(2)}, u32[]{:S(2)}) %collective-permute-start.5) | collective-permute-done | bytes 49184 | tf_op jit(solution)/shard_map/ppermute | solution.py:476
  23.3 0.8 collective-permute-done.6.m3
  24.0 2.7 %mlp.1 = (bf16[192,256]{1,0:T(8,128)(2,1)S(1)}, bf16[192,256]{1,0:T(8,128)(2,1)S(1)}, bf16[192,256]{1,0:T(8,128)(2,1)S(1)}, bf16[192,256]{1,0:T(8,128)(2,1)S(1)}...) custom-call(bf16[2,48,256]{2,1,0:T(8,128)(2,1)S(1)} %get-tuple-element.51.m0, ...), custom_call_target="tpu_custom_call" | custom-call | tf_op jit(solution)/shard_map/mlp/pallas_call | solution.py:455
  26.8 1.7 %collective-permute-start.10 = (bf16[4,288,128]{2,1,0:T(8,128)(2,1)S(1)}, bf16[4,288,128]{2,1,0:T(8,128)(2,1)S(1)}, u32[]{:S(2)}, u32[]{:S(2)}) collective-permute-start(bf16[4,288,128]{2,1,0:T(8,128)(2,1)S(1)} %get-tuple-element.72), channel_id=1, source_target_pairs={{0,4},{4,0},{1,5},{5,1},{2,6},{6,2},{3,7},{7,3},{8,12},{12,8},{9,1... | collective-permute-start | bytes 884744 | tf_op jit(solution)/shard_map/ppermute | solution.py:494
  28.4 0.0 collective-permute-start.11
  28.4 2.5 %collective-permute-start.12 = (bf16[192,256]{1,0:T(8,128)(2,1)S(1)}, bf16[192,256]{1,0:T(8,128)(2,1)S(1)}, u32[]{:S(2)}, u32[]{:S(2)}) collective-permute-start(bf16[192,256]{1,0:T(8,128)(2,1)S(1)} %get-tuple-element.75), channel_id=1, source_target_pairs={{0,2},{1,3},{2,0},{3,1},{4,6},{5,7},{6,4},{7,5},{8,10},{9,11},{10,... | collective-permute-start | bytes 294920 | tf_op jit(solution)/shard_map/ppermute | solution.py:476
  31.0 0.8 collective-permute-start.13
  31.7 0.8 merge.1
  32.5 3.5 %all-to-all-start = ((bf16[4,288,128]{2,1,0:T(8,128)(2,1)}), bf16[4,288,128]{2,1,0:T(8,128)(2,1)S(1)}, u32[]{:S(2)}, u32[]{:S(2)}) async-start(bf16[4,288,128]{2,1,0:T(8,128)(2,1)} %merge.1), calls=%async_computation | async-start | bytes 589824 | tf_op jit(solution)/shard_map/all_to_all | solution.py:571
  36.0 0.1 collective-permute-done.13.g3.r3
  36.1 1.5 %collective-permute-start.14 = (bf16[8,48,256]{2,1,0:T(8,128)(2,1)S(1)}, bf16[8,48,256]{2,1,0:T(8,128)(2,1)S(1)}, u32[]{:S(2)}, u32[]{:S(2)}) collective-permute-start(bf16[8,48,256]{2,1,0:T(8,128)(2,1)S(1)} %land.1.grad_ref.own_ref), channel_id=1, source_target_pairs={{0,4},{4,0},{1,5},{5,1},{2,6},{6,2},{3,7},{7,3},{8,12},{12,8},{9,1... | collective-permute-start | bytes 589832 | tf_op jit(solution)/shard_map/ppermute | solution.py:494
  37.6 2.0 %tap_sums.1.taps_ref = f32[64,128]{1,0:T(8,128)S(1)} custom-call(bf16[8,48,256]{2,1,0:T(8,128)(2,1)S(1)} %land.1.grad_ref.own_ref, f32[3,528,128]{2,1,0:T(8,128)S(1)} %get-tuple-element.77.pad, f32[128,384]{1,0:T(8,128)S(1)} %get-tuple-element.78.fold), custom_call_target="tpu_custom_call" | custom-call | tf_op jit(solution)/shard_map/tap_sums/pallas_call | solution.py:455
  39.7 0.1 edges.1
  39.8 2.9 %collective-permute-start.15 = (bf16[8,48,128]{2,1,0:T(8,128)(2,1)S(1)}, bf16[8,48,128]{2,1,0:T(8,128)(2,1)S(1)}, u32[]{:S(2)}, u32[]{:S(2)}) collective-permute-start(bf16[8,48,128]{2,1,0:T(8,128)(2,1)S(1)} %edges.1), channel_id=1, source_target_pairs={{4,8},{8,4},{12,16},{16,12},{20,24},{24,20},{28,32},{32,28},{36,40... | collective-permute-start | bytes 294920 | tf_op jit(solution)/shard_map/ppermute | solution.py:498
  42.8 0.8 pieces.1
  43.6 12.5 %all-to-all-start.1 = ((bf16[32,16,128]{2,1,0:T(8,128)(2,1)}), bf16[32,16,128]{2,1,0:T(8,128)(2,1)S(1)}, u32[]{:S(2)}, u32[]{:S(2)}) async-start(bf16[32,16,128]{2,1,0:T(8,128)(2,1)} %pieces.1), calls=%async_computation.1 | async-start | bytes 262144 | tf_op jit(solution)/shard_map/all_to_all | solution.py:594
  56.1 1.4 %collective-permute-start.16 = (bf16[8,48,128]{2,1,0:T(8,128)(2,1)S(1)}, bf16[8,48,128]{2,1,0:T(8,128)(2,1)S(1)}, u32[]{:S(2)}, u32[]{:S(2)}) collective-permute-start(bf16[8,48,128]{2,1,0:T(8,128)(2,1)S(1)} %collective-permute-done.15.near_ref), channel_id=1, source_target_pairs={{0,4},{4,0},{1,5},{5,1},{2,6},{6,2},{3,7},{7,3},{8,12},{12,8},{9,1... | collective-permute-start | bytes 294920 | tf_op jit(solution)/shard_map/ppermute | solution.py:494
  57.5 0.9 %collective-permute-done.16.far_ref = bf16[8,48,128]{2,1,0:T(8,128)(2,1)S(1)} collective-permute-done((bf16[8,48,128]{2,1,0:T(8,128)(2,1)S(1)}, bf16[8,48,128]{2,1,0:T(8,128)(2,1)S(1)}, u32[]{:S(2)}, u32[]{:S(2)}) %collective-permute-start.16) | collective-permute-done | bytes 98336 | tf_op jit(solution)/shard_map/ppermute | solution.py:494
  58.4 1.4 %surround.1.pad = f32[3,528,128]{2,1,0:T(8,128)S(1)} custom-call(s32[8,8]{1,0:T(8,128)S(1)} %copy-done.2, bf16[8,48,256]{2,1,0:T(8,128)(2,1)S(1)} %land.1.grad_ref.own_ref, bf16[8,48,256]{2,1,0:T(8,128)(2,1)S(1)} %collective-permute-done.14.par_ref, bf16[8,48,128]{2,1,0:T(8,128)(2,1)S(1)} %collective-permute-done.15.near_ref, ...), custom_call_target="tpu_custom_call" | custom-call | flops 700000000 | bytes 2583000 | tf_op jit(solution)/shard_map/surround/pallas_call | solution.py:455
  59.9 5.5 %all-to-all-done.1.in_ref = bf16[32,16,128]{2,1,0:T(8,128)(2,1)S(1)} async-done(((bf16[32,16,128]{2,1,0:T(8,128)(2,1)}), bf16[32,16,128]{2,1,0:T(8,128)(2,1)S(1)}, u32[]{:S(2)}, u32[]{:S(2)}) %all-to-all-start.1) | async-done | bytes 131104 | tf_op jit(solution)/shard_map/all_to_all | solution.py:594
  65.4 0.7 totals.1
  66.1 4.1 %all-to-all-start.2 = ((bf16[32,16,128]{2,1,0:T(8,128)(2,1)}), bf16[32,16,128]{2,1,0:T(8,128)(2,1)S(1)}, u32[]{:S(2)}, u32[]{:S(2)}) async-start(bf16[32,16,128]{2,1,0:T(8,128)(2,1)} %totals.1), calls=%async_computation.2 | async-start | bytes 262144 | tf_op jit(solution)/shard_map/all_to_all | solution.py:612
  70.2 0.0 copy-start.3
  70.2 0.6 copy-done.3
  70.9 2.8 %unmix.1 = (bf16[8,48,256]{2,1,0:T(8,128)(2,1)}, bf16[8,48,256]{2,1,0:T(8,128)(2,1)}) custom-call(f32[3,528,128]{2,1,0:T(8,128)S(1)} %surround.1.pad, bf16[8,48,256]{2,1,0:T(8,128)(2,1)S(1)} %copy-done.1, f32[56,384]{1,0:T(8,128)S(1)} %get-tuple-element.50.taps, bf16[8,48,256]{2,1,0:T(8,128)(2,1)S(1)} %get-tuple-element.82.owned_ref, f32[1,48]{1,0:T(1,128)S(1)} %bitcast.3, ...), custom_call_target="tpu_custom_call" | custom-call | tf_op jit(solution)/shard_map/unmix/pallas_call | solution.py:455
  73.7 5.9 %all-to-all-done.2.in_ref = bf16[32,16,128]{2,1,0:T(8,128)(2,1)S(1)} async-done(((bf16[32,16,128]{2,1,0:T(8,128)(2,1)}), bf16[32,16,128]{2,1,0:T(8,128)(2,1)S(1)}, u32[]{:S(2)}, u32[]{:S(2)}) %all-to-all-start.2) | async-done | bytes 131104 | tf_op jit(solution)/shard_map/all_to_all | solution.py:612
  79.6 3.6 %collective-permute-start.17 = (bf16[32,16,128]{2,1,0:T(8,128)(2,1)S(1)}, bf16[32,16,128]{2,1,0:T(8,128)(2,1)S(1)}, u32[]{:S(2)}, u32[]{:S(2)}) collective-permute-start(bf16[32,16,128]{2,1,0:T(8,128)(2,1)S(1)} %all-to-all-done.2.in_ref), channel_id=1, source_target_pairs={{0,4},{4,0},{1,5},{5,1},{2,6},{6,2},{3,7},{7,3},{8,12},{12,8},{9,1... | collective-permute-start | bytes 393224 | tf_op jit(solution)/shard_map/ppermute | solution.py:494
  83.2 1.0 %collective-permute-done.17.other_ref = bf16[32,16,128]{2,1,0:T(8,128)(2,1)S(1)} collective-permute-done((bf16[32,16,128]{2,1,0:T(8,128)(2,1)S(1)}, bf16[32,16,128]{2,1,0:T(8,128)(2,1)S(1)}, u32[]{:S(2)}, u32[]{:S(2)}) %collective-permute-start.17) | collective-permute-done | bytes 131104 | tf_op jit(solution)/shard_map/ppermute | solution.py:494
  84.2 1.1 %finish.1 = (f32[48,49]{1,0:T(8,128)}, f32[192,192]{1,0:T(8,128)}, f32[192,192]{1,0:T(8,128)}) custom-call(bf16[32,16,128]{2,1,0:T(8,128)(2,1)S(1)} %all-to-all-done.2.in_ref, bf16[32,16,128]{2,1,0:T(8,128)(2,1)S(1)} %collective-permute-done.17.other_ref), custom_call_target="tpu_custom_call" | custom-call | tf_op jit(solution)/shard_map/finish/pallas_call | solution.py:455
  (17 shorter events, 0.1 us)
Async XLA Ops:
  0.6 12.8 %copy-start = (bf16[528,768]{1,0:T(8,128)(2,1)S(1)}, bf16[528,768]{1,0:T(8,128)(2,1)}, u32[]{:S(2)}) copy-start(bf16[528,768]{1,0:T(8,128)(2,1)} %constant.4.clone.maps) | copy-start | bytes 2433028
  0.6 12.8 %collective-permute-start.1 = (bf16[16,48,256]{2,1,0:T(8,128)(2,1)}, bf16[16,48,256]{2,1,0:T(8,128)(2,1)S(1)}, u32[]{:S(2)}, u32[]{:S(2)}) collective-permute-start(bf16[16,48,256]{2,1,0:T(8,128)(2,1)} %x_hbm.1), channel_id=1, source_target_pairs={{0,4},{4,0},{1,5},{5,1},{2,6},{6,2},{3,7},{7,3},{8,12},{12,8},{9,1... | collective-permute-start | bytes 1179656 | tf_op jit(solution)/shard_map/ppermute | solution.py:494
  5.7 4.3 %copy-start.4 = (s32[16]{0:T(128)S(1)}, s32[16]{0:T(128)}, u32[]{:S(2)}) copy-start(s32[16]{0:T(128)} %own_slots.1) | copy-start | bytes 196
  5.7 6.2 %collective-permute-start.2 = (bf16[8,48,128]{2,1,0:T(8,128)(2,1)S(1)}, bf16[8,48,128]{2,1,0:T(8,128)(2,1)S(1)}, u32[]{:S(2)}, u32[]{:S(2)}) collective-permute-start(bf16[8,48,128]{2,1,0:T(8,128)(2,1)S(1)} %get-tuple-element.49), channel_id=1, source_target_pairs={{4,8},{8,4},{12,16},{16,12},{20,24},{24,20},{28,32},{32,28},{36,40... | collective-permute-start | bytes 294920 | tf_op jit(solution)/shard_map/ppermute | solution.py:498
  7.6 5.9 %copy-start.2 = (s32[8,8]{1,0:T(8,128)S(1)}, s32[8,8]{1,0:T(8,128)}, u32[]{:S(2)}) copy-start(s32[8,8]{1,0:T(8,128)} %adj.3) | copy-start | bytes 772
  7.6 13.1 %collective-permute-start.8 = (bf16[400,256]{1,0:T(8,128)(2,1)S(1)}, bf16[400,256]{1,0:T(8,128)(2,1)S(1)}, u32[]{:S(2)}, u32[]{:S(2)}) collective-permute-start(bf16[400,256]{1,0:T(8,128)(2,1)S(1)} %get-tuple-element.58), channel_id=1, source_target_pairs={{0,2},{1,3},{2,0},{3,1},{4,6},{5,7},{6,4},{7,5},{8,10},{9,11},{10,... | collective-permute-start | bytes 614408 | tf_op jit(solution)/shard_map/ppermute | solution.py:476
  10.0 1.1 %collective-permute-start = (s32[16]{0:T(128)S(1)}, s32[16]{0:T(128)S(1)}, u32[]{:S(2)}, u32[]{:S(2)}) collective-permute-start(s32[16]{0:T(128)S(1)} %copy-done.4), channel_id=1, source_target_pairs={{0,4},{4,0},{1,5},{5,1},{2,6},{6,2},{3,7},{7,3},{8,12},{12,8},{9,1... | collective-permute-start | bytes 200 | tf_op jit(solution)/shard_map/ppermute | solution.py:494
  10.0 10.9 %collective-permute-start.9 = (bf16[400,256]{1,0:T(8,128)(2,1)S(1)}, bf16[400,256]{1,0:T(8,128)(2,1)S(1)}, u32[]{:S(2)}, u32[]{:S(2)}) collective-permute-start(bf16[400,256]{1,0:T(8,128)(2,1)S(1)} %get-tuple-element.59), channel_id=1, source_target_pairs={{0,3},{1,0},{2,1},{3,2},{4,7},{5,4},{6,5},{7,6},{8,11},{9,8},{10,9... | collective-permute-start | bytes 614408 | tf_op jit(solution)/shard_map/ppermute | solution.py:476
  11.9 9.0 %collective-permute-start.7 = (bf16[400,256]{1,0:T(8,128)(2,1)S(1)}, bf16[400,256]{1,0:T(8,128)(2,1)S(1)}, u32[]{:S(2)}, u32[]{:S(2)}) collective-permute-start(bf16[400,256]{1,0:T(8,128)(2,1)S(1)} %get-tuple-element.57), channel_id=1, source_target_pairs={{0,1},{1,2},{2,3},{3,0},{4,5},{5,6},{6,7},{7,4},{8,9},{9,10},{10,1... | collective-permute-start | bytes 614408 | tf_op jit(solution)/shard_map/ppermute | solution.py:476
  11.9 1.5 %collective-permute-start.3 = (bf16[8,48,128]{2,1,0:T(8,128)(2,1)S(1)}, bf16[8,48,128]{2,1,0:T(8,128)(2,1)S(1)}, u32[]{:S(2)}, u32[]{:S(2)}) collective-permute-start(bf16[8,48,128]{2,1,0:T(8,128)(2,1)S(1)} %collective-permute-done.2.near_ref), channel_id=1, source_target_pairs={{0,4},{4,0},{1,5},{5,1},{2,6},{6,2},{3,7},{7,3},{8,12},{12,8},{9,1... | collective-permute-start | bytes 294920 | tf_op jit(solution)/shard_map/ppermute | solution.py:494
  17.1 4.5 %collective-permute-start.4 = (bf16[2,48,256]{2,1,0:T(8,128)(2,1)S(1)}, bf16[2,48,256]{2,1,0:T(8,128)(2,1)S(1)}, u32[]{:S(2)}, u32[]{:S(2)}) collective-permute-start(bf16[2,48,256]{2,1,0:T(8,128)(2,1)S(1)} %get-tuple-element.52), channel_id=1, source_target_pairs={{0,1},{1,2},{2,3},{3,0},{4,5},{5,6},{6,7},{7,4},{8,9},{9,10},{10,1... | collective-permute-start | bytes 147464 | tf_op jit(solution)/shard_map/ppermute | solution.py:476
  17.6 5.7 %collective-permute-start.5 = (bf16[2,48,256]{2,1,0:T(8,128)(2,1)S(1)}, bf16[2,48,256]{2,1,0:T(8,128)(2,1)S(1)}, u32[]{:S(2)}, u32[]{:S(2)}) collective-permute-start(bf16[2,48,256]{2,1,0:T(8,128)(2,1)S(1)} %get-tuple-element.53), channel_id=1, source_target_pairs={{0,2},{1,3},{2,0},{3,1},{4,6},{5,7},{6,4},{7,5},{8,10},{9,11},{10,... | collective-permute-start | bytes 147464 | tf_op jit(solution)/shard_map/ppermute | solution.py:476
  20.8 3.2 %collective-permute-start.6 = (bf16[2,48,256]{2,1,0:T(8,128)(2,1)S(1)}, bf16[2,48,256]{2,1,0:T(8,128)(2,1)S(1)}, u32[]{:S(2)}, u32[]{:S(2)}) collective-permute-start(bf16[2,48,256]{2,1,0:T(8,128)(2,1)S(1)} %get-tuple-element.54), channel_id=1, source_target_pairs={{0,3},{1,0},{2,1},{3,2},{4,7},{5,4},{6,5},{7,6},{8,11},{9,8},{10,9... | collective-permute-start | bytes 147464 | tf_op jit(solution)/shard_map/ppermute | solution.py:476
  26.8 5.0 %collective-permute-start.10 = (bf16[4,288,128]{2,1,0:T(8,128)(2,1)S(1)}, bf16[4,288,128]{2,1,0:T(8,128)(2,1)S(1)}, u32[]{:S(2)}, u32[]{:S(2)}) collective-permute-start(bf16[4,288,128]{2,1,0:T(8,128)(2,1)S(1)} %get-tuple-element.72), channel_id=1, source_target_pairs={{0,4},{4,0},{1,5},{5,1},{2,6},{6,2},{3,7},{7,3},{8,12},{12,8},{9,1... | collective-permute-start | bytes 884744 | tf_op jit(solution)/shard_map/ppermute | solution.py:494
  28.4 7.5 %collective-permute-start.11 = (bf16[192,256]{1,0:T(8,128)(2,1)S(1)}, bf16[192,256]{1,0:T(8,128)(2,1)S(1)}, u32[]{:S(2)}, u32[]{:S(2)}) collective-permute-start(bf16[192,256]{1,0:T(8,128)(2,1)S(1)} %get-tuple-element.74), channel_id=1, source_target_pairs={{0,1},{1,2},{2,3},{3,0},{4,5},{5,6},{6,7},{7,4},{8,9},{9,10},{10,1... | collective-permute-start | bytes 294920 | tf_op jit(solution)/shard_map/ppermute | solution.py:476
  28.4 7.5 %collective-permute-start.12 = (bf16[192,256]{1,0:T(8,128)(2,1)S(1)}, bf16[192,256]{1,0:T(8,128)(2,1)S(1)}, u32[]{:S(2)}, u32[]{:S(2)}) collective-permute-start(bf16[192,256]{1,0:T(8,128)(2,1)S(1)} %get-tuple-element.75), channel_id=1, source_target_pairs={{0,2},{1,3},{2,0},{3,1},{4,6},{5,7},{6,4},{7,5},{8,10},{9,11},{10,... | collective-permute-start | bytes 294920 | tf_op jit(solution)/shard_map/ppermute | solution.py:476
  31.0 5.2 %collective-permute-start.13 = (bf16[192,256]{1,0:T(8,128)(2,1)S(1)}, bf16[192,256]{1,0:T(8,128)(2,1)S(1)}, u32[]{:S(2)}, u32[]{:S(2)}) collective-permute-start(bf16[192,256]{1,0:T(8,128)(2,1)S(1)} %get-tuple-element.76), channel_id=1, source_target_pairs={{0,3},{1,0},{2,1},{3,2},{4,7},{5,4},{6,5},{7,6},{8,11},{9,8},{10,9... | collective-permute-start | bytes 294920 | tf_op jit(solution)/shard_map/ppermute | solution.py:476
  32.5 10.3 %all-to-all-start = ((bf16[4,288,128]{2,1,0:T(8,128)(2,1)}), bf16[4,288,128]{2,1,0:T(8,128)(2,1)S(1)}, u32[]{:S(2)}, u32[]{:S(2)}) async-start(bf16[4,288,128]{2,1,0:T(8,128)(2,1)} %merge.1), calls=%async_computation | async-start | bytes 589824 | tf_op jit(solution)/shard_map/all_to_all | solution.py:571
  36.1 3.5 %collective-permute-start.14 = (bf16[8,48,256]{2,1,0:T(8,128)(2,1)S(1)}, bf16[8,48,256]{2,1,0:T(8,128)(2,1)S(1)}, u32[]{:S(2)}, u32[]{:S(2)}) collective-permute-start(bf16[8,48,256]{2,1,0:T(8,128)(2,1)S(1)} %land.1.grad_ref.own_ref), channel_id=1, source_target_pairs={{0,4},{4,0},{1,5},{5,1},{2,6},{6,2},{3,7},{7,3},{8,12},{12,8},{9,1... | collective-permute-start | bytes 589832 | tf_op jit(solution)/shard_map/ppermute | solution.py:494
  39.8 16.3 %collective-permute-start.15 = (bf16[8,48,128]{2,1,0:T(8,128)(2,1)S(1)}, bf16[8,48,128]{2,1,0:T(8,128)(2,1)S(1)}, u32[]{:S(2)}, u32[]{:S(2)}) collective-permute-start(bf16[8,48,128]{2,1,0:T(8,128)(2,1)S(1)} %edges.1), channel_id=1, source_target_pairs={{4,8},{8,4},{12,16},{16,12},{20,24},{24,20},{28,32},{32,28},{36,40... | collective-permute-start | bytes 294920 | tf_op jit(solution)/shard_map/ppermute | solution.py:498
  43.6 21.8 %all-to-all-start.1 = ((bf16[32,16,128]{2,1,0:T(8,128)(2,1)}), bf16[32,16,128]{2,1,0:T(8,128)(2,1)S(1)}, u32[]{:S(2)}, u32[]{:S(2)}) async-start(bf16[32,16,128]{2,1,0:T(8,128)(2,1)} %pieces.1), calls=%async_computation.1 | async-start | bytes 262144 | tf_op jit(solution)/shard_map/all_to_all | solution.py:594
  56.1 2.3 %collective-permute-start.16 = (bf16[8,48,128]{2,1,0:T(8,128)(2,1)S(1)}, bf16[8,48,128]{2,1,0:T(8,128)(2,1)S(1)}, u32[]{:S(2)}, u32[]{:S(2)}) collective-permute-start(bf16[8,48,128]{2,1,0:T(8,128)(2,1)S(1)} %collective-permute-done.15.near_ref), channel_id=1, source_target_pairs={{0,4},{4,0},{1,5},{5,1},{2,6},{6,2},{3,7},{7,3},{8,12},{12,8},{9,1... | collective-permute-start | bytes 294920 | tf_op jit(solution)/shard_map/ppermute | solution.py:494
  66.1 4.1 %copy-start.1 = (bf16[8,48,256]{2,1,0:T(8,128)(2,1)S(1)}, bf16[8,48,256]{2,1,0:T(8,128)(2,1)}, u32[]{:S(2)}) copy-start(bf16[8,48,256]{2,1,0:T(8,128)(2,1)} %cot_ref.1) | copy-start | bytes 589828
  66.1 13.4 %all-to-all-start.2 = ((bf16[32,16,128]{2,1,0:T(8,128)(2,1)}), bf16[32,16,128]{2,1,0:T(8,128)(2,1)S(1)}, u32[]{:S(2)}, u32[]{:S(2)}) async-start(bf16[32,16,128]{2,1,0:T(8,128)(2,1)} %totals.1), calls=%async_computation.2 | async-start | bytes 262144 | tf_op jit(solution)/shard_map/all_to_all | solution.py:612
  70.2 0.7 copy-start.3
  79.6 4.6 %collective-permute-start.17 = (bf16[32,16,128]{2,1,0:T(8,128)(2,1)S(1)}, bf16[32,16,128]{2,1,0:T(8,128)(2,1)S(1)}, u32[]{:S(2)}, u32[]{:S(2)}) collective-permute-start(bf16[32,16,128]{2,1,0:T(8,128)(2,1)S(1)} %all-to-all-done.2.in_ref), channel_id=1, source_target_pairs={{0,4},{4,0},{1,5},{5,1},{2,6},{6,2},{3,7},{7,3},{8,12},{12,8},{9,1... | collective-permute-start | bytes 393224 | tf_op jit(solution)/shard_map/ppermute | solution.py:494
